TPU v7x, 32 devices: a whole 2x2x4 slice. The times are simulated.
32 devices in a mesh: dp: 8 (over z, y), row: 2 (over x), col: 2 (over core).
Axes of the slice: x: 2, y: 2, z: 4, core: 2. Of those that a mesh axis runs over, the one named last changes fastest.
Arguments:
- tokens: bfloat16 [12288, 1024], P('dp', 'row'), may hold values from -6 to 6
- gain_attn: float32 [1024], replicated, may hold values from 0.5 to 1.5
- w_qkv: float32 [1024, 16, 192], P('row', 'col'), may hold values from -0.1875 to 0.1875
- w_out: float32 [1024, 1024], P('col', 'row'), may hold values from -3 to 3
- gain_mlp: float32 [1024], replicated, may hold values from 0.5 to 1.5
- w_in: float32 [1024, 2, 2624], P('row', None, 'col'), may hold values from -0.1875 to 0.1875
- w_down: float32 [2624, 1024], P('col', 'row'), may hold values from -0.125 to 0.125
- cotangent: bfloat16 [12288, 1024], P('dp', 'row'), may hold values from -6 to 6
- seq_lengths: int32 [16], replicated, may hold values from 256 to 1024, as said below
- seq_offsets: int32 [16], replicated, may hold values from 0 to 11264, as said below
- deal: int32 [16], replicated, may hold values from 0 to 15, as said below
Outputs:
- layer_out: bfloat16 [12288, 1024], P('dp', 'row')
- tokens_grad: bfloat16 [12288, 1024], P('dp', 'row')
- gain_attn_grad: float32 [1024], P(('dp', 'row'))
- w_qkv_grad: float32 [1024, 16, 192], P(('dp', 'row'), 'col')
- w_out_grad: float32 [1024, 1024], P('col', ('dp', 'row'))
- gain_mlp_grad: float32 [1024], P(('dp', 'row'))
- w_in_grad: float32 [1024, 2, 2624], P(('dp', 'row'), None, 'col')
- w_down_grad: float32 [2624, 1024], P('col', ('dp', 'row'))
Inputs may be any that keep to these rules, and one draw needn't show every extreme that they name: `seq_lengths`: each group holds one sequence of 1024 tokens, its others have at most half of 1024, and some group fills all 1536 slots. Sequence 16 - 1 has 1024 tokens. Sequences 0 to 14 lie end to end in index order from place 0: seq_offsets[s] is the sum of the lengths of sequences 0 to s - 1. Sequence 16 - 1 ends at the last token place; places between belong to no sequence. `deal`: A permutation of the 16 sequences.
All inputs are finite; a program needn't handle non-finite values.
Results may differ from a plain program's by a relative error of at most 0.017.
Values may be sent and summed in bfloat16 or wider, within the bound.
No kernel may reach another device: no remote copies, remote signals or barrier semaphores. Data moves between devices by JAX's collectives and lax.ppermute only.
A program may use at most 192 MiB of HBM per device.

v0:
```python
import functools
import math

import jax
import jax.numpy as jnp
from jax import lax
from jax.experimental import pallas as pl
from jax.experimental.pallas import tpu as pltpu
from jax.sharding import PartitionSpec as P

LONGEST = 1024
BQ = 256
BK = 256
NEG = -1e30
FAR = 1e30
epsilon = 1e-05
rope_base = 160000.0
bf16 = jnp.bfloat16
f32 = jnp.float32
SWAP = [(0, 1), (1, 0)]


def nt(a, b):
    return lax.dot_general(a, b, (((1,), (1,)), ((), ())), preferred_element_type=f32)


def tn(a, b):
    return lax.dot_general(a, b, (((0,), (0,)), ((), ())), preferred_element_type=f32)


def nn(a, b):
    return jnp.dot(a, b, preferred_element_type=f32)


def after(a, *others):
    return lax.optimization_barrier((a, *others))[0]


def half_mask(width, heads, head):
    lane = lax.broadcasted_iota(jnp.int32, (1, width), 1)
    half = width // 2
    lane = jnp.where(lane >= half, lane - half, lane)
    step = half // heads
    return (lane >= head * step) & (lane < (head + 1) * step)


def whole_mask(width, heads, head):
    lane = lax.broadcasted_iota(jnp.int32, (1, width), 1)
    step = width // heads
    return (lane >= head * step) & (lane < (head + 1) * step)


def stack_heads(block, heads, mask_of):
    zero = jnp.zeros_like(block)
    width = block.shape[1]
    return jnp.concatenate(
        [jnp.where(mask_of(width, heads, h), block, zero) for h in range(heads)], axis=0
    )


def same_segment(key_seg, query_seg, heads):
    tile = key_seg
    lanes = query_seg.shape[1]
    if lanes > tile.shape[1]:
        tile = jnp.concatenate([tile] * (lanes // tile.shape[1]), axis=1)
    same = tile == query_seg
    return jnp.concatenate([same] * heads, axis=1) if heads > 1 else same


def forward_kernel(heads, sets, final, bounds, *refs):
    refs = list(refs)
    q_ref, sq_ref = refs[:2]
    kv_refs = refs[2 : 2 + sets]
    sk_refs = refs[2 + sets : 2 + 2 * sets]
    rest = refs[2 + 2 * sets :]
    if final:
        acc_in, ml_in, o_ref, lse_ref = rest[:4]
        acc, m_ref, l_ref = rest[4:7]
        vt_refs = rest[7:]
    else:
        acc, ml_ref = rest[:2]
        m_ref, l_ref = rest[2:4]
        vt_refs = rest[4:]
    step = pl.program_id(0)
    rows, width = q_ref.shape
    each = width // heads

    @pl.when(step == 0)
    def _():
        for kv, vt in zip(kv_refs, vt_refs):
            for j in range(kv.shape[0] // BK):
                vt[:, j * BK : (j + 1) * BK] = kv[j * BK : (j + 1) * BK, width:].T

    if final:
        acc[...] = acc_in[0]
        m_ref[...] = ml_in[0, 0:1]
        l_ref[...] = ml_in[0, 1:2]
    else:
        acc[...] = jnp.zeros_like(acc)
        m_ref[...] = jnp.full_like(m_ref, NEG)
        l_ref[...] = jnp.zeros_like(l_ref)
    queries = stack_heads(q_ref[...], heads, half_mask)
    query_seg = sq_ref[0]
    target = acc if final else acc.at[0]

    for s in range(sets):
        kv, sk, vt = kv_refs[s], sk_refs[s], vt_refs[s]

        def body(j, carry):
            first = pl.multiple_of(j * BK, BK)
            keys = kv[pl.ds(first, BK), 0:width]
            scores = nt(keys, queries)
            same = same_segment(sk[pl.ds(first, BK), :], query_seg, heads)
            scores = jnp.where(same, scores, NEG)
            before = m_ref[...]
            top = jnp.maximum(before, jnp.max(scores, axis=0, keepdims=True))
            raised = jnp.exp(scores - top)
            shrink = jnp.exp(before - top)
            m_ref[...] = top
            l_ref[...] = l_ref[...] * shrink + jnp.sum(raised, axis=0, keepdims=True)
            low = raised.astype(bf16)
            for h in range(heads):
                part = nn(
                    vt[h * each : (h + 1) * each, pl.ds(first, BK)],
                    low[:, h * rows : (h + 1) * rows],
                )
                hold = target[h * each : (h + 1) * each, :]
                target[h * each : (h + 1) * each, :] = (
                    hold * shrink[:, h * rows : (h + 1) * rows] + part
                )
            return carry

        lax.fori_loop(
            bounds[(step * sets + s) * 2], bounds[(step * sets + s) * 2 + 1], body, 0
        )

    if final:
        live = query_seg >= 0
        total = l_ref[...]
        live_all = jnp.concatenate([live] * heads, axis=1) if heads > 1 else live
        total = jnp.where(live_all, total, 1.0)
        inverse = jnp.where(live_all, 1.0 / total, 0.0)
        for h in range(heads):
            acc[h * each : (h + 1) * each, :] = (
                acc[h * each : (h + 1) * each, :] * inverse[:, h * rows : (h + 1) * rows]
            )
        o_ref[...] = acc[...].T.astype(bf16)
        lse_ref[0] = jnp.where(live_all, m_ref[...] + jnp.log(total), FAR)
    else:
        ml_ref[0, 0:1] = m_ref[...]
        ml_ref[0, 1:2] = l_ref[...]


def cost(products, q, kvs):
    pairs = q.shape[0]
    return pl.CostEstimate(
        flops=4 * products * pairs * q.shape[1],
        bytes_accessed=2 * sum(a.size for a in kvs) + 4 * q.size,
        transcendentals=4 * pairs,
    )


def whole(shape):
    zeros = (0,) * len(shape)
    return pl.BlockSpec(shape, lambda i, *_: zeros)


def attend_call(bounds, q, sq, kvs, sks, heads, state=None):
    count = q.shape[0] // BQ
    width = q.shape[1]
    sets = len(kvs)
    final = state is not None
    row_spec = pl.BlockSpec((BQ, width), lambda i, *_: (i, 0))
    acc_spec = pl.BlockSpec((1, width, BQ), lambda i, *_: (i, 0, 0))
    ml_spec = pl.BlockSpec((1, 2, heads * BQ), lambda i, *_: (i, 0, 0))
    in_specs = [row_spec, pl.BlockSpec((1, 1, BQ), lambda i, *_: (i, 0, 0))]
    in_specs += [whole(a.shape) for a in kvs] + [whole(a.shape) for a in sks]
    scratch = [pltpu.VMEM((1, heads * BQ), f32)] * 2
    scratch += [pltpu.VMEM((width, a.shape[0]), bf16) for a in kvs]
    if final:
        in_specs += [acc_spec, ml_spec]
        out_specs = [row_spec, pl.BlockSpec((1, 1, heads * BQ), lambda i, *_: (i, 0, 0))]
        out_shape = [
            jax.ShapeDtypeStruct(q.shape, bf16),
            jax.ShapeDtypeStruct((count, 1, heads * BQ), f32),
        ]
        scratch = [pltpu.VMEM((width, BQ), f32)] + scratch
    else:
        out_specs = [acc_spec, ml_spec]
        out_shape = [
            jax.ShapeDtypeStruct((count, width, BQ), f32),
            jax.ShapeDtypeStruct((count, 2, heads * BQ), f32),
        ]
    return pl.pallas_call(
        functools.partial(forward_kernel, heads, sets, final),
        grid_spec=pltpu.PrefetchScalarGridSpec(
            num_scalar_prefetch=1,
            grid=(count,),
            in_specs=in_specs,
            out_specs=out_specs,
            scratch_shapes=scratch,
        ),
        out_shape=out_shape,
        cost_estimate=cost(4, q, kvs),
        name="attend_final" if final else "attend_own",
    )(bounds, q, sq, *kvs, *sks, *(state or ()))


def backward_kernel(heads, sets, final, bounds, *refs):
    refs = list(refs)
    q_ref, do_ref, o_ref, lse_ref, sq_ref = refs[:5]
    kv_refs = refs[5 : 5 + sets]
    sk_refs = refs[5 + sets : 5 + 2 * sets]
    rest = refs[5 + 2 * sets :]
    if final:
        dq_in, dq_ref = rest[0], rest[1]
        dkv_refs = rest[2 : 2 + sets]
        dq_acc = rest[2 + sets]
        kt_refs = rest[3 + sets : 3 + 2 * sets]
        sums = dkv_refs
    else:
        dq_ref = rest[0]
        dkv_refs = rest[1 : 1 + sets]
        dq_acc = rest[1 + sets]
        kt_refs = rest[2 + sets : 2 + 2 * sets]
        sums = rest[2 + 2 * sets :]
    step = pl.program_id(0)
    rows, width = q_ref.shape
    each = width // heads
    half = width // 2
    piece = half // heads

    @pl.when(step == 0)
    def _():
        for kv, kt, total in zip(kv_refs, kt_refs, sums):
            total[...] = jnp.zeros_like(total)
            for j in range(kv.shape[0] // BK):
                kt[:, j * BK : (j + 1) * BK] = kv[j * BK : (j + 1) * BK, :width].T

    if final:
        dq_acc[...] = dq_in[0]
    else:
        dq_acc[...] = jnp.zeros_like(dq_acc)
    grads = do_ref[...]
    queries = stack_heads(q_ref[...], heads, half_mask)
    outs = stack_heads(grads, heads, whole_mask)
    query_seg = sq_ref[0]
    lse = lse_ref[0]
    product = (grads.astype(f32) * o_ref[...].astype(f32)).T
    delta = jnp.concatenate(
        [
            jnp.sum(product[h * each : (h + 1) * each], axis=0, keepdims=True)
            for h in range(heads)
        ],
        axis=1,
    )

    for s in range(sets):
        kv, sk, kt, total = kv_refs[s], sk_refs[s], kt_refs[s], sums[s]

        def body(j, carry):
            first = pl.multiple_of(j * BK, BK)
            keys = kv[pl.ds(first, BK), 0:width]
            values = kv[pl.ds(first, BK), width : 2 * width]
            scores = nt(keys, queries)
            same = same_segment(sk[pl.ds(first, BK), :], query_seg, heads)
            probs = jnp.where(same, jnp.exp(scores - lse), 0.0)
            grad_probs = nt(values, outs)
            grad_scores = (probs * (grad_probs - delta)).astype(bf16)
            low = probs.astype(bf16)
            total[pl.ds(first, BK), width : 2 * width] += nn(low, outs)
            total[pl.ds(first, BK), 0:width] += nn(grad_scores, queries)
            for h in range(heads):
                column = grad_scores[:, h * rows : (h + 1) * rows]
                for lead in (h * piece, half + h * piece):
                    dq_acc[lead : lead + piece, :] += nn(
                        kt[lead : lead + piece, pl.ds(first, BK)], column
                    )
            return carry

        lax.fori_loop(
            bounds[(step * sets + s) * 2], bounds[(step * sets + s) * 2 + 1], body, 0
        )

    if final:
        dq_ref[...] = dq_acc[...].T
    else:
        dq_ref[0] = dq_acc[...]

        @pl.when(step == pl.num_programs(0) - 1)
        def _():
            for total, out in zip(sums, dkv_refs):
                out[...] = total[...].astype(bf16)


def attend_back_call(bounds, q, do, o, lse, sq, kvs, sks, heads, state=None):
    count = q.shape[0] // BQ
    width = q.shape[1]
    sets = len(kvs)
    final = state is not None
    row_spec = pl.BlockSpec((BQ, width), lambda i, *_: (i, 0))
    acc_spec = pl.BlockSpec((1, width, BQ), lambda i, *_: (i, 0, 0))
    in_specs = [row_spec] * 3 + [
        pl.BlockSpec((1, 1, heads * BQ), lambda i, *_: (i, 0, 0)),
        pl.BlockSpec((1, 1, BQ), lambda i, *_: (i, 0, 0)),
    ]
    in_specs += [whole(a.shape) for a in kvs] + [whole(a.shape) for a in sks]
    scratch = [pltpu.VMEM((width, BQ), f32)]
    scratch += [pltpu.VMEM((width, a.shape[0]), bf16) for a in kvs]
    if final:
        in_specs += [acc_spec]
        out_specs = [row_spec]
        out_shape = [jax.ShapeDtypeStruct(q.shape, f32)]
    else:
        out_specs = [acc_spec]
        out_shape = [jax.ShapeDtypeStruct((count, width, BQ), f32)]
        scratch += [pltpu.VMEM(a.shape, f32) for a in kvs]
    out_specs += [whole(a.shape) for a in kvs]
    out_shape += [jax.ShapeDtypeStruct(a.shape, f32 if final else bf16) for a in kvs]
    return pl.pallas_call(
        functools.partial(backward_kernel, heads, sets, final),
        grid_spec=pltpu.PrefetchScalarGridSpec(
            num_scalar_prefetch=1,
            grid=(count,),
            in_specs=in_specs,
            out_specs=out_specs,
            scratch_shapes=scratch,
        ),
        out_shape=out_shape,
        cost_estimate=cost(10, q, kvs),
        name="back_own" if final else "back_halo",
    )(bounds, q, do, o, lse, sq, *kvs, *sks, *(state or ()))


def place_tables(seq_lengths, seq_offsets, first, count):
    place = first + jnp.arange(count, dtype=jnp.int32)
    ends = seq_offsets + seq_lengths
    inside = (place[:, None] >= seq_offsets[None, :]) & (place[:, None] < ends[None, :])
    live = jnp.any(inside, axis=1)
    index = jnp.arange(seq_offsets.shape[0], dtype=jnp.int32)
    segment = jnp.sum(jnp.where(inside, index[None, :], 0), axis=1)
    start = jnp.sum(jnp.where(inside, seq_offsets[None, :], 0), axis=1)
    end = jnp.sum(jnp.where(inside, ends[None, :], 0), axis=1)
    return live, segment, start, end, place


def qkv_order(heads, head_width):
    width = heads * head_width
    half = head_width // 2
    new = jnp.arange(3 * width, dtype=jnp.int32)
    kind = new // width
    inner = new % width
    side = inner // (width // 2)
    pair_head = (inner % (width // 2)) // half
    pair_old = pair_head * 3 * head_width + kind * head_width + side * half + inner % half
    value_old = (inner // head_width) * 3 * head_width + 2 * head_width + inner % head_width
    old = jnp.where(kind == 2, value_old, pair_old)
    return (old[None, :] == new[:, None]).astype(bf16)


def local(
    tokens,
    gain_attn,
    w_qkv,
    w_out,
    gain_mlp,
    w_in,
    w_down,
    cotangent,
    seq_lengths,
    seq_offsets,
    deal,
):
    R, C, B = lax.axis_size("row"), lax.axis_size("col"), lax.axis_size("dp")
    r, c, b = lax.axis_index("row"), lax.axis_index("col"), lax.axis_index("dp")
    S, Dl = tokens.shape
    D = Dl * R
    two = R == 2 and C == 2 and B == 8
    heads = w_qkv.shape[1] // R
    head_width = w_qkv.shape[2] // 3
    W = heads * head_width
    F = w_down.shape[0]
    H = LONGEST
    Sr = S // R
    zrow, zcol = (r == 0), (c == 0)

    def to_row(a):
        return lax.ppermute(a, "row", SWAP)

    def to_col(a):
        return lax.ppermute(a, "col", SWAP)

    def ordered(flag, mine, theirs, axis):
        return jnp.where(
            flag,
            jnp.concatenate([mine, theirs], axis=axis),
            jnp.concatenate([theirs, mine], axis=axis),
        )

    def own_first(a, axis):
        if not two:
            return a
        n = a.shape[axis] // 2
        return jnp.where(zrow, a, jnp.roll(a, n, axis=axis))

    def take(a, index, size, axis=0):
        return lax.dynamic_slice_in_dim(a, index * size, size, axis)

    def partner(a):
        n = a.shape[0] // 2
        got = to_row(take(a, c, n))
        return ordered(zcol, got, to_col(got), 0)

    def gather(a, axis):
        if two:
            return jnp.concatenate([a, to_row(a)], axis=axis)
        return lax.all_gather(a, "row", axis=axis, tiled=True)

    def col_sum(a):
        return a + to_col(a.astype(bf16)).astype(f32) if C == 2 else lax.psum(a, "col")

    live_x, seg_x, start_x, end_x, place_x = place_tables(seq_lengths, seq_offsets, b * S - H, S + 2 * H)
    key_seg = jnp.broadcast_to(jnp.where(live_x, seg_x, -2)[:, None], (S + 2 * H, 128))
    sk_left, sk_own, sk_right = key_seg[:H], key_seg[H : H + S], key_seg[H + S :]
    live = live_x[H : H + S]
    nq = S // BQ
    sq = jnp.where(live, seg_x[H : H + S], -1).reshape(nq, 1, BQ)
    first = jnp.min(jnp.where(live, start_x[H : H + S] - b * S, 4 * S).reshape(nq, BQ), axis=1)
    last = jnp.max(jnp.where(live, end_x[H : H + S] - b * S, -4 * S).reshape(nq, BQ), axis=1)
    own_low = jnp.clip(first, 0, S) // BK
    own_high = (jnp.clip(last, 0, S) + BK - 1) // BK
    left_low = jnp.clip(first + H, 0, H) // BK
    right_high = (jnp.clip(last - S, 0, H) + BK - 1) // BK
    own_bounds = jnp.stack([own_low, own_high], axis=1).reshape(-1).astype(jnp.int32)
    zero = jnp.zeros_like(left_low)
    halo_bounds = (
        jnp.stack([left_low, zero + H // BK, zero, right_high], axis=1).reshape(-1).astype(jnp.int32)
    )
    position = jnp.where(live, place_x[H : H + S] - start_x[H : H + S], 0)
    freq = rope_base ** (-(jnp.arange(0, head_width, 2, dtype=f32) / head_width))
    angle = position.astype(f32)[:, None] * jnp.tile(freq, heads)[None, :]
    cosine, sine = lax.optimization_barrier((jnp.cos(angle), jnp.sin(angle)))

    live_column = live[:, None]
    if two:
        x_got = partner(tokens)
        x_low = jnp.where(live_column, jnp.concatenate([tokens, x_got], axis=1), 0)
    else:
        own_x = jnp.where(live_column, tokens, 0)
        x_low = lax.all_gather(own_x, "row", axis=1, tiled=True)

    wq_low = w_qkv.reshape(Dl, R * 3 * W).astype(bf16)
    if two:
        wq_mine = take(wq_low, r, 3 * W, 1)
        wq_got = to_row(take(wq_low, 1 - r, 3 * W, 1))
    else:
        wq = lax.all_to_all(wq_low, "row", split_axis=1, concat_axis=0, tiled=True)
    order = qkv_order(heads, head_width)

    gain_one = own_first(gain_attn, 0)
    gain_two = own_first(gain_mlp, 0)

    x = x_low.astype(f32)
    center = x - jnp.mean(x, axis=-1, keepdims=True)
    inverse_one = lax.rsqrt(jnp.mean(center * center, axis=-1, keepdims=True) + epsilon)
    mean_one = jnp.mean(x, axis=-1, keepdims=True)
    h1 = (center * inverse_one * gain_one).astype(bf16)
    if two:
        h1, wq_mine, wq_got = lax.optimization_barrier((h1, wq_mine, wq_got))
        wq = jnp.concatenate([wq_mine, wq_got], axis=0)
    wq = nn(wq, order).astype(bf16)

    half = W // 2

    def turn(t, sign):
        first_half, second_half = t[:, :half], t[:, half:]
        s = sine * sign
        return jnp.concatenate(
            [first_half * cosine - second_half * s, second_half * cosine + first_half * s], axis=1
        )

    kv_raw = nn(h1, wq[:, W:])
    kv = jnp.concatenate([turn(kv_raw[:, :W], 1.0), kv_raw[:, W:]], axis=1).astype(bf16)
    up = [(i, i + 1) for i in range(B - 1)]
    down = [(i + 1, i) for i in range(B - 1)]
    kv_left = lax.ppermute(kv[S - H :], "dp", up)
    kv_right = lax.ppermute(kv[:H], "dp", down)
    q = (turn(nn(h1, wq[:, :W]), 1.0) * (1.0 / math.sqrt(head_width))).astype(bf16)
    wo_low, wd_low = w_out.astype(bf16), w_down.astype(bf16)
    act_low, lin_low = w_in[:, 0].astype(bf16), w_in[:, 1].astype(bf16)
    if two:
        act_got = to_row(act_low)
        q, act_got = lax.optimization_barrier((q, act_got))
        lin_got = to_row(after(lin_low, act_got))
    state = attend_call(own_bounds, q, sq, [kv], [sk_own], heads)
    if two:
        state, lin_got = lax.optimization_barrier((state, lin_got))
        wo_got = to_row(after(wo_low, lin_got))
    o, lse = attend_call(
        halo_bounds, q, sq, [kv_left, kv_right], [sk_left, sk_right], heads, state
    )

    if two:
        o, wo_got = lax.optimization_barrier((o, wo_got))
        wo = own_first(jnp.concatenate([wo_low, wo_got], axis=1), 0)
    else:
        wo = gather(wo_low, 1)

    if two:
        o_got = to_row(take(o, 1 - r, Sr))
        o_rows = jnp.concatenate([take(o, r, Sr), o_got], axis=1)
        g_send, wd_send = after((take(cotangent, 1 - r, Sr), wd_low), o_got)
        wd_got = to_row(wd_send)
        g_low = jnp.concatenate([take(cotangent, r, Sr), partner(g_send)], axis=1)
        g_low = jnp.where(take(live, r, Sr)[:, None], g_low, 0)
        wds = [wd_low, wd_got]
        acts, lins = [act_low, act_got], [lin_low, lin_got]
    else:
        o_rows = lax.all_to_all(o, "row", split_axis=0, concat_axis=1, tiled=True)
        own_g = jnp.where(live_column, cotangent, 0)
        g_low = lax.all_to_all(own_g, "row", split_axis=0, concat_axis=1, tiled=True)
        wds, acts, lins = [gather(wd_low, 1)], [gather(act_low, 0)], [gather(lin_low, 0)]

    def split_nn(a, parts):
        n = a.shape[1] // len(parts)
        return sum(nn(a[:, i * n : (i + 1) * n], w) for i, w in enumerate(parts))

    def split_nt(a, parts):
        n = a.shape[1] // len(parts)
        return sum(nt(a[:, i * n : (i + 1) * n], w) for i, w in enumerate(parts))

    def wide(parts):
        return parts[0] if len(parts) == 1 else jnp.concatenate(parts, axis=1)

    x_rows = take(x_low, r, Sr).astype(f32)
    if C == 2:
        o_all = jnp.concatenate([o_rows, to_col(o_rows)], axis=1)
        wo_all = jnp.concatenate([wo, to_col(wo)], axis=0)
        x1 = x_rows + nn(o_all, wo_all)
    else:
        x1 = x_rows + lax.psum(nn(o_rows, wo), "col")

    center = x1 - jnp.mean(x1, axis=-1, keepdims=True)
    inverse_two = lax.rsqrt(jnp.mean(center * center, axis=-1, keepdims=True) + epsilon)
    n2 = center * inverse_two
    h2 = (n2 * gain_two).astype(bf16)
    a = split_nn(h2, acts)
    u = split_nn(h2, lins)
    phi = 0.5 + 0.5 * lax.erf(a * math.sqrt(0.5))
    gelu = a * phi
    slope = phi + a * jnp.exp(-0.5 * a * a) * (1.0 / math.sqrt(2.0 * math.pi))
    m = (gelu * u).astype(bf16)
    y_part = wide([nn(m, w) for w in wds])
    if two:
        n = Sr // 2
        y_half = (
            take(x1, c, n) + take(y_part, c, n) + to_col(take(y_part, 1 - c, n).astype(bf16)).astype(f32)
        ).astype(bf16)
        y_got = to_row(y_half[:, Dl:])
    else:
        y = (x1 + col_sum(y_part)).astype(bf16)
        layer_out = lax.all_to_all(y, "row", split_axis=1, concat_axis=0, tiled=True)

    dm = split_nt(g_low, wds)
    da = (dm * u * slope).astype(bf16)
    du = (dm * gelu).astype(bf16)
    dh2 = col_sum(wide([nt(da, v) + nt(du, w) for v, w in zip(acts, lins)]))
    e2 = dh2 * gain_two
    dx1 = g_low.astype(f32) + inverse_two * (
        e2
        - jnp.mean(e2, axis=-1, keepdims=True)
        - n2 * jnp.mean(e2 * n2, axis=-1, keepdims=True)
    )
    dx_low = dx1.astype(bf16)
    do_rows = nt(dx_low, wo).astype(bf16)
    if two:
        do_got = to_row(do_rows[:, W:])
        do = ordered(zrow, do_rows[:, :W], do_got, 0)
        pair = ordered(zrow, y_half[None, :, :Dl], y_got[None], 0)
        layer_out = ordered(zcol, pair[:, None], to_col(pair)[:, None], 1).reshape(S, Dl)
    else:
        do = lax.all_to_all(do_rows, "row", split_axis=1, concat_axis=0, tiled=True)

    Db = D // B
    Dd = D // (B * R)
    if two:
        y_bit, z_bits = b % 2, b // 2

        def relative(a, bits):
            n = jnp.arange(D, dtype=jnp.int32)
            rel = {"w": 0 * n, "x": 0 * n}
            for i, bit in enumerate(bits):
                rel[bit] = n // (D >> (i + 1)) % 2
            z_rel = 2 * rel["Z"] + rel["z"]
            column = ((z_bits ^ z_rel) * 2 + (y_bit ^ rel["y"])) * Db + n % Dd
            column = column + (rel["w"] if "w" in bits else r ^ rel["x"]) * Dd
            column = column ^ (r * (D // 2))
            return nn(a, (n[:, None] == column[None, :]).astype(bf16)).astype(bf16)

        def to_y(a):
            return lax.ppermute(a, "dp", [(i, i ^ 1) for i in range(B)])

        def to_z(a, j):
            return lax.ppermute(a, "dp", [(i, i ^ (2 * j)) for i in range(B)])

        def first(a):
            return a[:, : a.shape[1] // 2]

        def second(a):
            return a[:, a.shape[1] // 2 :].astype(bf16)

        def product(left, right):
            return tn(left, second(right)).astype(bf16)

        def halved(left, right, got):
            return tn(left, first(right)) + got.astype(f32)

        def joined(part, got):
            return first(part).astype(f32) + got.astype(f32)

        o_heads = own_first(o_rows, 1)
        g_y, dx_y = relative(g_low, "yzZx"), relative(dx_low, "yzZx")
        h_act, h_lin = relative(h2, "xzZy"), relative(h2, "xyzZ")
        lower_got = to_y(product(m, g_y))
        lower_got = after(lower_got, do_rows)
        lower = halved(m, g_y, lower_got)
        lower_got = to_z(second(lower), 1)
        proj_got = to_y(product(o_heads, dx_y))
        gate_send = jnp.concatenate([product(da, h_act), product(du, h_lin)], axis=0)
        gate_got = to_row(after(gate_send, do_got))
        do, lower, layer_out = lax.optimization_barrier((do, lower, layer_out))

    dq_part, dkv_left, dkv_right = attend_back_call(
        halo_bounds, q, do, o, lse, sq, [kv_left, kv_right], [sk_left, sk_right], heads
    )
    from_right = lax.ppermute(dkv_left, "dp", down)
    from_left = lax.ppermute(dkv_right, "dp", up)
    if two:
        dq_part, lower_got = lax.optimization_barrier((dq_part, lower_got))
    dq, dkv = attend_back_call(own_bounds, q, do, o, lse, sq, [kv], [sk_own], heads, [dq_part])
    if two:
        dkv, from_right, from_left, gate_got, proj_got = lax.optimization_barrier(
            (dkv, from_right, from_left, gate_got, proj_got)
        )
    pad = jnp.zeros((S - H, 2 * W), bf16)
    dkv = (
        dkv
        + jnp.concatenate([pad, from_right], axis=0).astype(f32)
        + jnp.concatenate([from_left, pad], axis=0).astype(f32)
    )
    dq = turn(dq * (1.0 / math.sqrt(head_width)), -1.0)
    dt = jnp.concatenate([dq, turn(dkv[:, :W], -1.0), dkv[:, W:]], axis=1).astype(bf16)
    dh1_part = nt(dt, wq)

    if two:
        n = S // 2
        kept = take(dh1_part, c, n) + to_col(take(dh1_part, 1 - c, n).astype(bf16)).astype(f32)
        xs = take(x_low, c, n).astype(f32)
        inv, mean = take(inverse_one, c, n), take(mean_one, c, n)
        n1 = (xs - mean) * inv
        e1 = kept * gain_one
        sums = jnp.stack([jnp.sum(e1, axis=-1), jnp.sum(e1 * n1, axis=-1)])
        sums = (sums + to_row(sums)) * (1.0 / D)
        mine = (kept[:, :Dl] + to_row(kept[:, Dl:].astype(bf16)).astype(f32)) * gain_one[:Dl]
        moved = lax.ppermute(after(dx_low[:, Dl:], from_left), ("row", "col"), [(0, 2), (3, 1)])
        base = jnp.where(r == c, dx1[:, :Dl], moved.astype(f32))
        dx = base + inv * (mine - sums[0][:, None] - n1[:, :Dl] * sums[1][:, None])
        dx = dx.astype(bf16)
        tokens_grad = ordered(zcol, dx, to_col(dx), 0)
    else:
        dh1 = lax.psum_scatter(col_sum(dh1_part), "row", scatter_dimension=1, tiled=True)
        xs = own_x.astype(f32)
        n1 = (xs - mean_one) * inverse_one
        e1 = dh1 * take(gain_attn, r, Dl)
        sums = lax.psum(jnp.stack([jnp.sum(e1, axis=-1), jnp.sum(e1 * n1, axis=-1)]), "row") / D
        base = lax.all_to_all(dx_low, "row", split_axis=1, concat_axis=0, tiled=True).astype(f32)
        tokens_grad = (
            base + inverse_one * (e1 - sums[0][:, None] - n1 * sums[1][:, None])
        ).astype(bf16)

    if two:
        h1_y = relative(h1, "yzZw")
        query = halved(dt, h1_y, after(to_y(product(dt, h1_y)), kept))
        lower_got = after(lower_got, from_left)
        n = F
        lower = joined(lower, lower_got)
        lower_got = after(to_z(second(lower), 2), kept)
        act = halved(da, h_act, gate_got[:n])
        lin = halved(du, h_lin, gate_got[n:])
        proj = halved(o_heads, dx_y, proj_got)
        both_got = after(to_z(jnp.concatenate([second(act), second(proj)], axis=0), 1), kept)
        lin = joined(lin, after(to_y(second(lin)), kept))
        act, proj = joined(act, both_got[:n]), joined(proj, both_got[n:])
        both_got = to_z(jnp.concatenate([second(act), second(proj)], axis=0), 2)
        lin = joined(lin, to_z(second(lin), 1))
        act, proj = joined(act, both_got[:n]), joined(proj, both_got[n:])
        lower = joined(lower, lower_got)
        last_got = to_row(jnp.concatenate([second(lower), second(proj)], axis=0))
        lower, proj = joined(lower, last_got[:n]), joined(proj, last_got[n:])
        act = joined(act, to_y(second(act)))
        lin = joined(lin, to_z(second(lin), 2))
        gate = jnp.stack([act.T, lin.T])
        query = joined(query, to_z(second(query), 1))
        query = joined(query, to_z(second(query), 2)).T
        wq_rows = take(wq, b ^ (4 * r), Db)
        place = (2 * b + r) ^ (8 * r)
        side, inner = place // 8, place % 8
        wi_rows = jnp.stack(
            [take(jnp.where(side == 0, w[0], w[1]), inner, Dd) for w in (acts, lins)]
        )
    else:

        def scatter(grad):
            return lax.psum_scatter(grad, ("dp", "row"), scatter_dimension=1, tiled=True).astype(f32)

        gate = jnp.stack([scatter(tn(da, h2).astype(bf16)).T, scatter(tn(du, h2).astype(bf16)).T])
        proj = scatter(tn(o_rows, dx_low).astype(bf16))
        lower = scatter(tn(m, g_low).astype(bf16))
        query = lax.psum_scatter(
            tn(h1, dt).astype(bf16), "dp", scatter_dimension=0, tiled=True
        ).astype(f32)
        wq_rows = take(wq, b, Db)
        wi_rows = jnp.stack([take(acts[0], b * R + r, Dd), take(lins[0], b * R + r, Dd)])

    one_part = jnp.sum(query * wq_rows.astype(f32), axis=1)
    two_part = jnp.sum(jnp.sum(gate * wi_rows.astype(f32), axis=2), axis=0)
    natural = lax.dot_general(
        query, order.astype(f32), (((1,), (1,)), ((), ())),
        precision=lax.Precision.HIGHEST, preferred_element_type=f32,
    )
    if two:
        one_part = one_part + to_row(one_part)
        one_part = take(one_part, r, Dd)
        pair = natural.reshape(2, Dd, 3 * W)
        mine = lax.dynamic_index_in_dim(pair, r, 0, keepdims=False)
        theirs = to_row(lax.dynamic_index_in_dim(pair, 1 - r, 0, keepdims=False))
        query_out = ordered(zrow, mine, theirs, 1)
    else:
        one_part = take(lax.psum(one_part, "row"), r, Dd)
        query_out = lax.all_to_all(natural, "row", split_axis=0, concat_axis=1, tiled=True)
    gains = jnp.stack([one_part, two_part])
    gains = gains + to_col(gains) if C == 2 else lax.psum(gains, "col")
    gain_attn_grad = gains[0] / take(gain_attn, b * R + r, Dd)
    gain_mlp_grad = gains[1] / take(gain_mlp, b * R + r, Dd)
    return (
        layer_out,
        tokens_grad,
        gain_attn_grad,
        query_out.reshape(Dd, R * heads, 3 * head_width),
        proj,
        gain_mlp_grad,
        jnp.swapaxes(gate, 0, 1),
        lower,
    )


def solution(mesh):
    return jax.shard_map(
        local,
        mesh=mesh,
        in_specs=(
            P("dp", "row"),
            P(),
            P("row", "col", None),
            P("col", "row"),
            P(),
            P("row", None, "col"),
            P("col", "row"),
            P("dp", "row"),
            P(),
            P(),
            P(),
        ),
        out_specs=(
            P("dp", "row"),
            P("dp", "row"),
            P(("dp", "row")),
            P(("dp", "row"), "col", None),
            P("col", ("dp", "row")),
            P(("dp", "row")),
            P(("dp", "row"), None, "col"),
            P("col", ("dp", "row")),
        ),
        check_vma=False,
    )
```

profile of v0, /device:TPU:3, one launch (start us, length us, event | category | flops | bytes accessed | tf_op | source)
XLA Modules:
  0.0 463.8 jit_solution(2630976583025522936)
XLA Ops:
  13.8 7.6 %collective-permute-done = bf16[768,512]{1,0:T(8,128)(2,1)} collective-permute-done((bf16[768,512]{1,0:T(8,128)(2,1)}, bf16[768,512]{1,0:T(8,128)(2,1)}, u32[]{:S(2)}, u32[]{:S(2)}) %collective-permute-start) | collective-permute-done | bytes 786464 | tf_op jit(solution)/shard_map/ppermute | solution.py:388
  24.1 4.3 multiply_sine_fusion
  46.7 20.4 %collective-permute-done.3 = bf16[512,1312]{0,1:T(8,128)(2,1)} collective-permute-done((bf16[512,1312]{0,1:T(8,128)(2,1)}, bf16[512,1312]{0,1:T(8,128)(2,1)}, u32[]{:S(2)}, u32[]{:S(2)}) %collective-permute-start.3) | collective-permute-done | bytes 1343520 | tf_op jit(solution)/shard_map/ppermute | solution.py:388
  73.8 4.1 collective-permute-start.4
  87.4 25.4 %attend_own.1 = (f32[6,256,256]{2,1,0:T(8,128)}, f32[6,2,1024]{2,1,0:T(2,128)}) custom-call(s32[12]{0:T(128)} %reshape.725.bounds, bf16[1536,256]{1,0:T(8,128)(2,1)} %fusion.53.refs_0_, s32[6,1,256]{2,1,0:T(1,128)} %select_n.637.refs_1_.refs_4_, bf16[1536,512]{1,0:T(8,128)(2,1)} %copy-done, s32[1536,128]{1,0:T(8,128)} %broadcast_in_dim.128.refs_3_.refs_6_), custom_call_target="tpu_custom_call" | custom-call | flops 6291456 | bytes 3145728 | tf_op jit(solution)/shard_map/attend_own/pallas_call | solution.py:194
  114.7 5.7 %collective-permute-done.4.refs_2_.refs_5_ = bf16[1024,512]{1,0:T(8,128)(2,1)} collective-permute-done((bf16[1024,512]{1,0:T(8,128)(2,1)}, bf16[1024,512]{1,0:T(8,128)(2,1)}, u32[]{:S(2)}, u32[]{:S(2)}) %collective-permute-start.4) | collective-permute-done | bytes 1048608 | tf_op jit(solution)/shard_map/ppermute | solution.py:486
  122.4 8.0 %attend_final.1 = (bf16[1536,256]{1,0:T(8,128)(2,1)}, f32[6,1,1024]{2,1,0:T(1,128)}) custom-call(s32[24]{0:T(128)} %reshape.724.bounds, bf16[1536,256]{1,0:T(8,128)(2,1)} %fusion.53.refs_0_, s32[6,1,256]{2,1,0:T(1,128)} %select_n.637.refs_1_.refs_4_, bf16[1024,512]{1,0:T(8,128)(2,1)} %collective-permute-done.4.refs_2_.refs_5_, ...), custom_call_target="tpu_custom_call" | custom-call | flops 6291456 | bytes 3670016 | tf_op jit(solution)/shard_map/attend_final/pallas_call | solution.py:194
  133.7 3.0 convert_element_type.219
  139.7 3.0 collective-permute-start.12
  145.4 5.0 %fusion.16 = bf16[1536,1024]{1,0:T(8,128)(2,1)} fusion(bf16[1536,1024]{1,0:T(8,128)(2,1)S(1)} %copy-done.16, s32[1024]{0:T(1024)S(1)} %add_xor_fusion), kind=kOutput, calls=%fused_computation.29 | convolution fusion | flops 3223846912 | bytes 6295552 | tf_op jit(solution)/shard_map/dot_general | solution.py:32
  156.2 5.0 %collective-permute-done.9 = bf16[384,512]{1,0:T(8,128)(2,1)S(1)} collective-permute-done((bf16[384,512]{1,0:T(8,128)(2,1)S(1)}, bf16[384,512]{1,0:T(8,128)(2,1)S(1)}, u32[]{:S(2)}, u32[]{:S(2)}) %collective-permute-start.9) | collective-permute-done | bytes 393248 | tf_op jit(solution)/shard_map/ppermute | solution.py:388
  171.6 3.0 fusion.30
  174.6 3.0 fusion.31
  181.6 12.9 %fusion.32 = bf16[768,1024]{1,0:T(8,128)(2,1)} fusion(bf16[768,1024]{1,0:T(8,128)(2,1)S(1)} %maximum_select_fusion.2, s32[1024]{0:T(1024)S(1)} %copy-done.41), kind=kOutput, calls=%fused_computation.72 | convolution fusion | flops 1612447744 | bytes 3149824 | tf_op jit(solution)/shard_map/dot_general | solution.py:32
  195.8 5.3 %multiply_convert_fusion = (bf16[768,1312]{0,1:T(8,128)(2,1)}, bf16[768,1312]{0,1:T(8,128)(2,1)S(1)}, bf16[768,1312]{0,1:T(8,128)(2,1)S(1)}) fusion(f32[768,1312]{0,1:T(8,128)S(1)} %convolution_add_fusion, f32[768,1312]{0,1:T(8,128)S(1)} %convolution_add_fusion.2, f32[768,1312]{0,1:T(8,128)S(1)} %fusion.91, bf16[512,1312]{0,1:T(8,128)(2,1)} %collective-permute-done.6, ...), kind=kOutput, calls=%fused_computation.26 | convolution fusion | flops 1048928256 | bytes 20267008 | tf_op jit(solution)/shard_map/dot_general | solution.py:32
  219.4 4.2 collective-permute-start.16
  228.4 7.5 %collective-permute-done.18 = bf16[384,512]{1,0:T(8,128)(2,1)S(1)} collective-permute-done((bf16[384,512]{1,0:T(8,128)(2,1)S(1)}, bf16[384,512]{1,0:T(8,128)(2,1)S(1)}, u32[]{:S(2)}, u32[]{:S(2)}) %collective-permute-start.18) | collective-permute-done | bytes 393248 | tf_op jit(solution)/shard_map/ppermute | solution.py:388
  244.2 9.3 %collective-permute-done.16 = bf16[1312,512]{1,0:T(8,128)(2,1)S(1)} collective-permute-done((bf16[1312,512]{1,0:T(8,128)(2,1)S(1)}, bf16[1312,512]{1,0:T(8,128)(2,1)S(1)}, u32[]{:S(2)}, u32[]{:S(2)}) %collective-permute-start.16) | collective-permute-done | bytes 1343520 | tf_op jit(solution)/shard_map/ppermute | solution.py:601
  255.9 8.4 %collective-permute-start.20 = (bf16[1312,256]{1,0:T(8,128)(2,1)}, bf16[1312,256]{1,0:T(8,128)(2,1)}, u32[]{:S(2)}, u32[]{:S(2)}) collective-permute-start(bf16[1312,256]{1,0:T(8,128)(2,1)} %slice.727), channel_id=1, source_target_pairs={{0,8},{4,12},{8,0},{12,4},{16,24},{20,28},{24,16},{28,20},{1,9},{5... | collective-permute-start | bytes 2015240 | tf_op jit(solution)/shard_map/ppermute | solution.py:604
  267.4 3.1 convolution_convert_fusion.4
  273.6 9.5 %back_halo.1 = (f32[6,256,256]{2,1,0:T(8,128)}, bf16[1024,512]{1,0:T(8,128)(2,1)}, bf16[1024,512]{1,0:T(8,128)(2,1)}) custom-call(s32[24]{0:T(128)} %reshape.724.bounds, bf16[1536,256]{1,0:T(8,128)(2,1)} %fusion.53.refs_0_, bf16[1536,256]{1,0:T(8,128)(2,1)} %maximum_select_fusion.6.refs_1_, bf16[1536,256]{1,0:T(8,128)(2,1)} %get-tuple-element.66.refs_2_, ...), custom_call_target="tpu_custom_call" | custom-call | flops 15728640 | bytes 3670016 | tf_op jit(solution)/shard_map/back_halo/pallas_call | solution.py:320
  284.4 7.3 %collective-permute-start.22 = (bf16[1024,512]{1,0:T(8,128)(2,1)}, bf16[1024,512]{1,0:T(8,128)(2,1)}, u32[]{:S(2)}, u32[]{:S(2)}) collective-permute-start(bf16[1024,512]{1,0:T(8,128)(2,1)} %get-tuple-element.78), channel_id=1, source_target_pairs={{0,4},{4,8},{8,12},{12,16},{16,20},{20,24},{24,28},{1,5},{5,9},{9,... | collective-permute-start | bytes 3145736 | tf_op jit(solution)/shard_map/ppermute | solution.py:637
  291.7 33.9 %back_own.1 = (f32[1536,256]{1,0:T(8,128)}, f32[1536,512]{1,0:T(8,128)}) custom-call(s32[12]{0:T(128)} %reshape.725.bounds, bf16[1536,256]{1,0:T(8,128)(2,1)} %fusion.53.refs_0_, bf16[1536,256]{1,0:T(8,128)(2,1)} %maximum_select_fusion.6.refs_1_, bf16[1536,256]{1,0:T(8,128)(2,1)} %get-tuple-element.66.refs_2_, f32[6,1,1024]{2,1,0:T(1,128)} %get-tuple-element.73.refs_3_, ...), custom_call_target="tpu_custom_call" | custom-call | flops 15728640 | bytes 3145728 | tf_op jit(solution)/shard_map/back_own/pallas_call | solution.py:320
  328.0 6.7 %collective-permute-done.22 = bf16[1024,512]{1,0:T(8,128)(2,1)} collective-permute-done((bf16[1024,512]{1,0:T(8,128)(2,1)}, bf16[1024,512]{1,0:T(8,128)(2,1)}, u32[]{:S(2)}, u32[]{:S(2)}) %collective-permute-start.22) | collective-permute-done | bytes 1048608 | tf_op jit(solution)/shard_map/ppermute | solution.py:637
  336.3 3.3 collective-permute-start.42
  364.5 3.2 collective-permute-start.25
  370.6 5.9 %collective-permute-done.34 = bf16[1824,256]{1,0:T(8,128)(2,1)S(1)} collective-permute-done((bf16[1824,256]{1,0:T(8,128)(2,1)S(1)}, bf16[1824,256]{1,0:T(8,128)(2,1)S(1)}, u32[]{:S(2)}, u32[]{:S(2)}) %collective-permute-start.34) | collective-permute-done | bytes 933920 | tf_op jit(solution)/shard_map/ppermute | solution.py:604
  382.6 12.0 %collective-permute-done.37 = bf16[1312,256]{1,0:T(8,128)(2,1)S(1)} collective-permute-done((bf16[1312,256]{1,0:T(8,128)(2,1)S(1)}, bf16[1312,256]{1,0:T(8,128)(2,1)S(1)}, u32[]{:S(2)}, u32[]{:S(2)}) %collective-permute-start.37) | collective-permute-done | bytes 671776 | tf_op jit(solution)/shard_map/ppermute | solution.py:601
  398.6 10.5 %collective-permute-done.38 = bf16[1312,128]{1,0:T(8,128)(2,1)S(1)} collective-permute-done((bf16[1312,128]{1,0:T(8,128)(2,1)S(1)}, bf16[1312,128]{1,0:T(8,128)(2,1)S(1)}, u32[]{:S(2)}, u32[]{:S(2)}) %collective-permute-start.38) | collective-permute-done | bytes 335904 | tf_op jit(solution)/shard_map/ppermute | solution.py:604
  413.4 17.8 %collective-permute-done.39 = bf16[1312,64]{1,0:T(8,128)(2,1)S(1)} collective-permute-done((bf16[1312,64]{1,0:T(8,128)(2,1)S(1)}, bf16[1312,64]{1,0:T(8,128)(2,1)S(1)}, u32[]{:S(2)}, u32[]{:S(2)}) %collective-permute-start.39) | collective-permute-done | bytes 167968 | tf_op jit(solution)/shard_map/ppermute | solution.py:604
  450.5 3.9 fusion.47
  460.5 3.1 maximum_select_fusion.4
  (375 shorter events, 196.0 us)
Async XLA Ops:
  2.7 18.7 %collective-permute-start = (bf16[768,512]{1,0:T(8,128)(2,1)}, bf16[768,512]{1,0:T(8,128)(2,1)}, u32[]{:S(2)}, u32[]{:S(2)}) collective-permute-start(bf16[768,512]{1,0:T(8,128)(2,1)} %constant_dynamic-slice_fusion.6), channel_id=1, source_target_pairs={{0,2},{2,0},{1,3},{3,1},{4,6},{6,4},{5,7},{7,5},{8,10},{10,8},{9,1... | collective-permute-start | bytes 2359304 | tf_op jit(solution)/shard_map/ppermute | solution.py:388
  6.0 32.3 %collective-permute-start.2 = (bf16[512,768]{0,1:T(8,128)(2,1)}, bf16[512,768]{0,1:T(8,128)(2,1)}, u32[]{:S(2)}, u32[]{:S(2)}) collective-permute-start(bf16[512,768]{0,1:T(8,128)(2,1)} %get-tuple-element.148), channel_id=1, source_target_pairs={{0,2},{2,0},{1,3},{3,1},{4,6},{6,4},{5,7},{7,5},{8,10},{10,8},{9,1... | collective-permute-start | bytes 2359304 | tf_op jit(solution)/shard_map/ppermute | solution.py:388
  12.7 54.4 %collective-permute-start.3 = (bf16[512,1312]{0,1:T(8,128)(2,1)}, bf16[512,1312]{0,1:T(8,128)(2,1)}, u32[]{:S(2)}, u32[]{:S(2)}) collective-permute-start(bf16[512,1312]{0,1:T(8,128)(2,1)} %get-tuple-element.141), channel_id=1, source_target_pairs={{0,2},{2,0},{1,3},{3,1},{4,6},{6,4},{5,7},{7,5},{8,10},{10,8},{9,1... | collective-permute-start | bytes 4030472 | tf_op jit(solution)/shard_map/ppermute | solution.py:388
  67.1 45.7 %collective-permute-start.6 = (bf16[512,1312]{0,1:T(8,128)(2,1)}, bf16[512,1312]{0,1:T(8,128)(2,1)}, u32[]{:S(2)}, u32[]{:S(2)}) collective-permute-start(bf16[512,1312]{0,1:T(8,128)(2,1)} %get-tuple-element.60), channel_id=1, source_target_pairs={{0,2},{2,0},{1,3},{3,1},{4,6},{6,4},{5,7},{7,5},{8,10},{10,8},{9,1... | collective-permute-start | bytes 4030472 | tf_op jit(solution)/shard_map/ppermute | solution.py:388
  73.8 46.6 %collective-permute-start.4 = (bf16[1024,512]{1,0:T(8,128)(2,1)}, bf16[1024,512]{1,0:T(8,128)(2,1)}, u32[]{:S(2)}, u32[]{:S(2)}) collective-permute-start(bf16[1024,512]{1,0:T(8,128)(2,1)} %get-tuple-element.145), channel_id=1, source_target_pairs={{0,4},{4,8},{8,12},{12,16},{16,20},{20,24},{24,28},{1,5},{5,9},{9,... | collective-permute-start | bytes 3145736 | tf_op jit(solution)/shard_map/ppermute | solution.py:486
  77.9 42.5 %collective-permute-start.5 = (bf16[1024,512]{1,0:T(8,128)(2,1)}, bf16[1024,512]{1,0:T(8,128)(2,1)}, u32[]{:S(2)}, u32[]{:S(2)}) collective-permute-start(bf16[1024,512]{1,0:T(8,128)(2,1)} %get-tuple-element.144), channel_id=1, source_target_pairs={{4,0},{8,4},{12,8},{16,12},{20,16},{24,20},{28,24},{5,1},{9,5},{13... | collective-permute-start | bytes 3145736 | tf_op jit(solution)/shard_map/ppermute | solution.py:487
  112.8 17.7 %collective-permute-start.7 = (bf16[512,512]{1,0:T(8,128)(2,1)}, bf16[512,512]{1,0:T(8,128)(2,1)}, u32[]{:S(2)}, u32[]{:S(2)}) collective-permute-start(bf16[512,512]{1,0:T(8,128)(2,1)} %convert_element_type.229), channel_id=1, source_target_pairs={{0,2},{2,0},{1,3},{3,1},{4,6},{6,4},{5,7},{7,5},{8,10},{10,8},{9,1... | collective-permute-start | bytes 1572872 | tf_op jit(solution)/shard_map/ppermute | solution.py:388
  139.7 23.0 %collective-permute-start.12 = (bf16[512,1024]{1,0:T(8,128)(2,1)S(1)}, bf16[512,1024]{1,0:T(8,128)(2,1)S(1)}, u32[]{:S(2)}, u32[]{:S(2)}) collective-permute-start(bf16[512,1024]{1,0:T(8,128)(2,1)S(1)} %fusion.65), channel_id=1, source_target_pairs={{0,1},{1,0},{2,3},{3,2},{4,5},{5,4},{6,7},{7,6},{8,9},{9,8},{10,11... | collective-permute-start | bytes 3145736 | tf_op jit(solution)/shard_map/ppermute | solution.py:391
  143.8 18.9 %collective-permute-start.11 = (bf16[768,512]{1,0:T(8,128)(2,1)S(1)}, bf16[768,512]{1,0:T(8,128)(2,1)S(1)}, u32[]{:S(2)}, u32[]{:S(2)}) collective-permute-start(bf16[768,512]{1,0:T(8,128)(2,1)S(1)} %pad_maximum_fusion.6), channel_id=1, source_target_pairs={{0,1},{1,0},{2,3},{3,2},{4,5},{5,4},{6,7},{7,6},{8,9},{9,8},{10,11... | collective-permute-start | bytes 2359304 | tf_op jit(solution)/shard_map/ppermute | solution.py:391
  156.0 38.6 %collective-permute-start.13 = (bf16[1312,512]{1,0:T(8,128)(2,1)S(1)}, bf16[1312,512]{1,0:T(8,128)(2,1)S(1)}, u32[]{:S(2)}, u32[]{:S(2)}) collective-permute-start(bf16[1312,512]{1,0:T(8,128)(2,1)S(1)} %copy-done.11), channel_id=1, source_target_pairs={{0,2},{2,0},{1,3},{3,1},{4,6},{6,4},{5,7},{7,5},{8,10},{10,8},{9,1... | collective-permute-start | bytes 4030472 | tf_op jit(solution)/shard_map/ppermute | solution.py:388
  161.2 17.7 %collective-permute-start.10 = (bf16[384,512]{1,0:T(8,128)(2,1)S(1)}, bf16[384,512]{1,0:T(8,128)(2,1)S(1)}, u32[]{:S(2)}, u32[]{:S(2)}) collective-permute-start(bf16[384,512]{1,0:T(8,128)(2,1)S(1)} %collective-permute-done.9), channel_id=1, source_target_pairs={{0,1},{1,0},{2,3},{3,2},{4,5},{5,4},{6,7},{7,6},{8,9},{9,8},{10,11... | collective-permute-start | bytes 1179656 | tf_op jit(solution)/shard_map/ppermute | solution.py:391
  209.7 27.7 %collective-permute-start.14 = (bf16[768,1024]{1,0:T(8,128)(2,1)S(1)}, bf16[768,1024]{1,0:T(8,128)(2,1)S(1)}, u32[]{:S(2)}, u32[]{:S(2)}) collective-permute-start(bf16[768,1024]{1,0:T(8,128)(2,1)S(1)} %fusion.17), channel_id=1, source_target_pairs={{0,1},{1,0},{2,3},{3,2},{4,5},{5,4},{6,7},{7,6},{8,9},{9,8},{10,11... | collective-permute-start | bytes 4718600 | tf_op jit(solution)/shard_map/ppermute | solution.py:391
  219.4 34.0 %collective-permute-start.16 = (bf16[1312,512]{1,0:T(8,128)(2,1)S(1)}, bf16[1312,512]{1,0:T(8,128)(2,1)S(1)}, u32[]{:S(2)}, u32[]{:S(2)}) collective-permute-start(bf16[1312,512]{1,0:T(8,128)(2,1)S(1)} %convolution_convert_fusion.2), channel_id=1, source_target_pairs={{0,4},{4,0},{8,12},{12,8},{16,20},{20,16},{24,28},{28,24},{1,5},{5... | collective-permute-start | bytes 4030472 | tf_op jit(solution)/shard_map/ppermute | solution.py:601
  236.0 34.8 %collective-permute-start.19 = (bf16[2,384,512]{2,1,0:T(8,128)(2,1)S(1)}, bf16[2,384,512]{2,1,0:T(8,128)(2,1)S(1)}, u32[]{:S(2)}, u32[]{:S(2)}) collective-permute-start(bf16[2,384,512]{2,1,0:T(8,128)(2,1)S(1)} %maximum_select_fusion.8), channel_id=1, source_target_pairs={{0,1},{1,0},{2,3},{3,2},{4,5},{5,4},{6,7},{7,6},{8,9},{9,8},{10,11... | collective-permute-start | bytes 2359304 | tf_op jit(solution)/shard_map/ppermute | solution.py:391
  242.9 21.5 %collective-permute-start.15 = (bf16[768,256]{1,0:T(8,128)(2,1)S(1)}, bf16[768,256]{1,0:T(8,128)(2,1)S(1)}, u32[]{:S(2)}, u32[]{:S(2)}) collective-permute-start(bf16[768,256]{1,0:T(8,128)(2,1)S(1)} %get-tuple-element.158), channel_id=1, source_target_pairs={{0,2},{2,0},{1,3},{3,1},{4,6},{6,4},{5,7},{7,5},{8,10},{10,8},{9,1... | collective-permute-start | bytes 1179656 | tf_op jit(solution)/shard_map/ppermute | solution.py:388
  255.9 35.9 %collective-permute-start.20 = (bf16[1312,256]{1,0:T(8,128)(2,1)}, bf16[1312,256]{1,0:T(8,128)(2,1)}, u32[]{:S(2)}, u32[]{:S(2)}) collective-permute-start(bf16[1312,256]{1,0:T(8,128)(2,1)} %slice.727), channel_id=1, source_target_pairs={{0,8},{4,12},{8,0},{12,4},{16,24},{20,28},{24,16},{28,20},{1,9},{5... | collective-permute-start | bytes 2015240 | tf_op jit(solution)/shard_map/ppermute | solution.py:604
  264.3 70.4 %collective-permute-start.23 = (bf16[2624,512]{1,0:T(8,128)(2,1)}, bf16[2624,512]{1,0:T(8,128)(2,1)}, u32[]{:S(2)}, u32[]{:S(2)}) collective-permute-start(bf16[2624,512]{1,0:T(8,128)(2,1)} %pad_maximum_fusion.1), channel_id=1, source_target_pairs={{0,2},{2,0},{1,3},{3,1},{4,6},{6,4},{5,7},{7,5},{8,10},{10,8},{9,1... | collective-permute-start | bytes 8060936 | tf_op jit(solution)/shard_map/ppermute | solution.py:388
  270.5 57.5 %collective-permute-start.24 = (bf16[512,512]{1,0:T(8,128)(2,1)}, bf16[512,512]{1,0:T(8,128)(2,1)}, u32[]{:S(2)}, u32[]{:S(2)}) collective-permute-start(bf16[512,512]{1,0:T(8,128)(2,1)} %convolution_convert_fusion.4), channel_id=1, source_target_pairs={{0,4},{4,0},{8,12},{12,8},{16,20},{20,16},{24,28},{28,24},{1,5},{5... | collective-permute-start | bytes 1572872 | tf_op jit(solution)/shard_map/ppermute | solution.py:601
  283.1 44.9 %collective-permute-start.21 = (bf16[1024,512]{1,0:T(8,128)(2,1)}, bf16[1024,512]{1,0:T(8,128)(2,1)}, u32[]{:S(2)}, u32[]{:S(2)}) collective-permute-start(bf16[1024,512]{1,0:T(8,128)(2,1)} %get-tuple-element.77), channel_id=1, source_target_pairs={{4,0},{8,4},{12,8},{16,12},{20,16},{24,20},{28,24},{5,1},{9,5},{13... | collective-permute-start | bytes 3145736 | tf_op jit(solution)/shard_map/ppermute | solution.py:636
  284.4 50.4 %collective-permute-start.22 = (bf16[1024,512]{1,0:T(8,128)(2,1)}, bf16[1024,512]{1,0:T(8,128)(2,1)}, u32[]{:S(2)}, u32[]{:S(2)}) collective-permute-start(bf16[1024,512]{1,0:T(8,128)(2,1)} %get-tuple-element.78), channel_id=1, source_target_pairs={{0,4},{4,8},{8,12},{12,16},{16,20},{20,24},{24,28},{1,5},{5,9},{9,... | collective-permute-start | bytes 3145736 | tf_op jit(solution)/shard_map/ppermute | solution.py:637
  336.3 34.3 %collective-permute-start.42 = (bf16[1312,128]{1,0:T(8,128)(2,1)S(1)}, bf16[1312,128]{1,0:T(8,128)(2,1)S(1)}, u32[]{:S(2)}, u32[]{:S(2)}) collective-permute-start(bf16[1312,128]{1,0:T(8,128)(2,1)S(1)} %slice.730), channel_id=1, source_target_pairs={{0,16},{4,20},{8,24},{12,28},{16,0},{20,4},{24,8},{28,12},{1,17},{... | collective-permute-start | bytes 1007624 | tf_op jit(solution)/shard_map/ppermute | solution.py:604
  346.3 18.2 %collective-permute-start.26 = (bf16[768,1024]{1,0:T(8,128)(2,1)S(1)}, bf16[768,1024]{1,0:T(8,128)(2,1)S(1)}, u32[]{:S(2)}, u32[]{:S(2)}) collective-permute-start(bf16[768,1024]{1,0:T(8,128)(2,1)S(1)} %dynamic-slice_convert_fusion), channel_id=1, source_target_pairs={{0,1},{1,0},{2,3},{3,2},{4,5},{5,4},{6,7},{7,6},{8,9},{9,8},{10,11... | collective-permute-start | bytes 4718600 | tf_op jit(solution)/shard_map/ppermute | solution.py:391
  353.2 23.3 %collective-permute-start.34 = (bf16[1824,256]{1,0:T(8,128)(2,1)S(1)}, bf16[1824,256]{1,0:T(8,128)(2,1)S(1)}, u32[]{:S(2)}, u32[]{:S(2)}) collective-permute-start(bf16[1824,256]{1,0:T(8,128)(2,1)S(1)} %pad_maximum_fusion.5), channel_id=1, source_target_pairs={{0,8},{4,12},{8,0},{12,4},{16,24},{20,28},{24,16},{28,20},{1,9},{5... | collective-permute-start | bytes 2801672 | tf_op jit(solution)/shard_map/ppermute | solution.py:604
  360.7 19.6 %collective-permute-start.30 = (bf16[768,512]{1,0:T(8,128)(2,1)}, bf16[768,512]{1,0:T(8,128)(2,1)S(1)}, u32[]{:S(2)}, u32[]{:S(2)}) collective-permute-start(bf16[768,512]{1,0:T(8,128)(2,1)} %fusion.59), channel_id=1, source_target_pairs={{0,4},{4,0},{8,12},{12,8},{16,20},{20,16},{24,28},{28,24},{1,5},{5... | collective-permute-start | bytes 2359304 | tf_op jit(solution)/shard_map/ppermute | solution.py:601
  363.0 31.6 %collective-permute-start.37 = (bf16[1312,256]{1,0:T(8,128)(2,1)S(1)}, bf16[1312,256]{1,0:T(8,128)(2,1)S(1)}, u32[]{:S(2)}, u32[]{:S(2)}) collective-permute-start(bf16[1312,256]{1,0:T(8,128)(2,1)S(1)} %slice.725), channel_id=1, source_target_pairs={{0,4},{4,0},{8,12},{12,8},{16,20},{20,16},{24,28},{28,24},{1,5},{5... | collective-permute-start | bytes 2015240 | tf_op jit(solution)/shard_map/ppermute | solution.py:601
  364.5 85.9 %collective-permute-start.25 = (bf16[768,512]{1,0:T(8,128)(2,1)}, bf16[768,512]{1,0:T(8,128)(2,1)}, u32[]{:S(2)}, u32[]{:S(2)}) collective-permute-start(bf16[768,512]{1,0:T(8,128)(2,1)} %slice.493), channel_id=1, source_target_pairs={{0,2},{3,1},{4,6},{7,5},{8,10},{11,9},{12,14},{15,13},{16,18},{19,... | collective-permute-start | bytes 2359304 | tf_op jit(solution)/shard_map/ppermute | solution.py:665
  378.2 33.8 %collective-permute-start.35 = (bf16[1824,128]{1,0:T(8,128)(2,1)S(1)}, bf16[1824,128]{1,0:T(8,128)(2,1)S(1)}, u32[]{:S(2)}, u32[]{:S(2)}) collective-permute-start(bf16[1824,128]{1,0:T(8,128)(2,1)S(1)} %pad_maximum_fusion.7), channel_id=1, source_target_pairs={{0,16},{4,20},{8,24},{12,28},{16,0},{20,4},{24,8},{28,12},{1,17},{... | collective-permute-start | bytes 1400840 | tf_op jit(solution)/shard_map/ppermute | solution.py:604
  380.6 29.5 %collective-permute-start.31 = (bf16[768,256]{1,0:T(8,128)(2,1)S(1)}, bf16[768,256]{1,0:T(8,128)(2,1)S(1)}, u32[]{:S(2)}, u32[]{:S(2)}) collective-permute-start(bf16[768,256]{1,0:T(8,128)(2,1)S(1)} %slice.728), channel_id=1, source_target_pairs={{0,8},{4,12},{8,0},{12,4},{16,24},{20,28},{24,16},{28,20},{1,9},{5... | collective-permute-start | bytes 1179656 | tf_op jit(solution)/shard_map/ppermute | solution.py:604
  397.5 52.9 %collective-permute-start.27 = (bf16[768,512]{1,0:T(8,128)(2,1)}, bf16[768,512]{1,0:T(8,128)(2,1)}, u32[]{:S(2)}, u32[]{:S(2)}) collective-permute-start(bf16[768,512]{1,0:T(8,128)(2,1)} %slice.723), channel_id=1, source_target_pairs={{0,2},{2,0},{1,3},{3,1},{4,6},{6,4},{5,7},{7,5},{8,10},{10,8},{9,1... | collective-permute-start | bytes 2359304 | tf_op jit(solution)/shard_map/ppermute | solution.py:388
  409.4 21.8 %collective-permute-start.39 = (bf16[1312,64]{1,0:T(8,128)(2,1)S(1)}, bf16[1312,64]{1,0:T(8,128)(2,1)S(1)}, u32[]{:S(2)}, u32[]{:S(2)}) collective-permute-start(bf16[1312,64]{1,0:T(8,128)(2,1)S(1)} %slice.731), channel_id=1, source_target_pairs={{0,16},{4,20},{8,24},{12,28},{16,0},{20,4},{24,8},{28,12},{1,17},{... | collective-permute-start | bytes 503816 | tf_op jit(solution)/shard_map/ppermute | solution.py:604
  410.3 25.1 %collective-permute-start.32 = (bf16[768,128]{1,0:T(8,128)(2,1)S(1)}, bf16[768,128]{1,0:T(8,128)(2,1)S(1)}, u32[]{:S(2)}, u32[]{:S(2)}) collective-permute-start(bf16[768,128]{1,0:T(8,128)(2,1)S(1)} %slice.736), channel_id=1, source_target_pairs={{0,16},{4,20},{8,24},{12,28},{16,0},{20,4},{24,8},{28,12},{1,17},{... | collective-permute-start | bytes 589832 | tf_op jit(solution)/shard_map/ppermute | solution.py:604
  413.1 41.6 %collective-permute-start.43 = (bf16[1824,64]{1,0:T(8,128)(2,1)}, bf16[1824,64]{1,0:T(8,128)(2,1)}, u32[]{:S(2)}, u32[]{:S(2)}) collective-permute-start(bf16[1824,64]{1,0:T(8,128)(2,1)} %pad_maximum_fusion.8), channel_id=1, source_target_pairs={{0,2},{2,0},{1,3},{3,1},{4,6},{6,4},{5,7},{7,5},{8,10},{10,8},{9,1... | collective-permute-start | bytes 700424 | tf_op jit(solution)/shard_map/ppermute | solution.py:388
  (77 other events, 492.8 us)
where the time goes:
time: 471 us; the launch traced here: 464 us
  waiting for transfers between devices  116 us (25%)
  matrix products  82.2 us (17%)
  Pallas kernels  76.8 us (16%)
  starting transfers between devices  74.6 us (16%)
  other arithmetic  71.9 us (15%)
  local copies, waits for them, and re-layouts  40.2 us (9%)
    dot_general x15, matrix products, nn(): return jnp.dot(a, b, preferred_element_type=f32)  47.4 us
    pallas_call x2, Pallas kernels, attend_back_call(): pl.pallas_call(functools.partial(backward_kernel, heads, sets, final), gr...  43.4 us
    ppermute x16, waiting for transfers between devices, to_row(): return lax.ppermute(a, 'row', SWAP)  43.2 us
    ppermute x8, waiting for transfers between devices, to_z(): return lax.ppermute(a, 'dp', [(i, i ^ 2 * j) for i in range(B)])  35.9 us
    pallas_call x2, Pallas kernels, attend_call(): pl.pallas_call(functools.partial(forward_kernel, heads, sets, final), gri...  33.4 us
    ppermute x5, waiting for transfers between devices, to_y(): return lax.ppermute(a, 'dp', [(i, i ^ 1) for i in range(B)])  24.3 us
    ppermute x8, starting transfers between devices, to_z(): return lax.ppermute(a, 'dp', [(i, i ^ 2 * j) for i in range(B)])  22.7 us
    dot_general x10, matrix products, tn(): lax.dot_general(a, b, (((0,), (0,)), ((), ())), preferred_element_type=f32)  18.8 us
  transfers between devices with their start and end apart: 44, of which 17 were waited for; matrix products, arithmetic and copies ran while one was open for 35% of the time, Pallas kernels for 17%

commit v1 on v0

--- a/solution.py
+++ b/solution.py
@@ -489,19 +489,26 @@
     wo_low, wd_low = w_out.astype(bf16), w_down.astype(bf16)
     act_low, lin_low = w_in[:, 0].astype(bf16), w_in[:, 1].astype(bf16)
     if two:
-        act_got = to_row(act_low)
-        q, act_got = lax.optimization_barrier((q, act_got))
-        lin_got = to_row(after(lin_low, act_got))
+        even = (b // 2) % 2 == 0
+        in_got, wo_got = to_row(jnp.where(even, act_low, lin_low)), to_row(wo_low)
+        g_got = to_row(take(take(cotangent, 1 - r, Sr), c, Sr // 2))
+        wd_half = take(wd_low, (b // 2) % 2, F // 2)
+
+        def to_z(a, j):
+            return lax.ppermute(a, "dp", [(i, i ^ (2 * j)) for i in range(B)])
+
     state = attend_call(own_bounds, q, sq, [kv], [sk_own], heads)
     if two:
-        state, lin_got = lax.optimization_barrier((state, lin_got))
-        wo_got = to_row(after(wo_low, lin_got))
+        kv_left, kv_right, in_got, wo_got, g_got, wd_half = after(
+            (kv_left, kv_right, in_got, wo_got, g_got, wd_half), state
+        )
+        in_other, wd_got = to_z(in_got, 1), to_row(wd_half)
     o, lse = attend_call(
         halo_bounds, q, sq, [kv_left, kv_right], [sk_left, sk_right], heads, state
     )
 
     if two:
-        o, wo_got = lax.optimization_barrier((o, wo_got))
+        o, wd_got = lax.optimization_barrier((o, wd_got))
         wo = own_first(jnp.concatenate([wo_low, wo_got], axis=1), 0)
     else:
         wo = gather(wo_low, 1)
@@ -509,9 +516,11 @@
     if two:
         o_got = to_row(take(o, 1 - r, Sr))
         o_rows = jnp.concatenate([take(o, r, Sr), o_got], axis=1)
-        g_send, wd_send = after((take(cotangent, 1 - r, Sr), wd_low), o_got)
-        wd_got = to_row(wd_send)
-        g_low = jnp.concatenate([take(cotangent, r, Sr), partner(g_send)], axis=1)
+        wd_other, in_other = to_z(wd_got, 1), after(in_other, o_got)
+        act_got, lin_got = jnp.where(even, in_got, in_other), jnp.where(even, in_other, in_got)
+        wd_got = ordered(even, wd_got, wd_other, 0)
+        g_got = ordered(zcol, g_got, to_col(g_got), 0)
+        g_low = jnp.concatenate([take(cotangent, r, Sr), g_got], axis=1)
         g_low = jnp.where(take(live, r, Sr)[:, None], g_low, 0)
         wds = [wd_low, wd_got]
         acts, lins = [act_low, act_got], [lin_low, lin_got]
@@ -539,6 +548,40 @@
         x1 = x_rows + nn(o_all, wo_all)
     else:
         x1 = x_rows + lax.psum(nn(o_rows, wo), "col")
+
+    Db = D // B
+    Dd = D // (B * R)
+    if two:
+        y_bit, z_bits = b % 2, b // 2
+
+        def relative(a, bits):
+            n = jnp.arange(D, dtype=jnp.int32)
+            rel = {"w": 0 * n, "x": 0 * n}
+            for i, bit in enumerate(bits):
+                rel[bit] = n // (D >> (i + 1)) % 2
+            z_rel = 2 * rel["Z"] + rel["z"]
+            column = ((z_bits ^ z_rel) * 2 + (y_bit ^ rel["y"])) * Db + n % Dd
+            column = column + (rel["w"] if "w" in bits else r ^ rel["x"]) * Dd
+            column = column ^ (r * (D // 2))
+            return nn(a, (n[:, None] == column[None, :]).astype(bf16)).astype(bf16)
+
+        def to_y(a):
+            return lax.ppermute(a, "dp", [(i, i ^ 1) for i in range(B)])
+
+        def first(a):
+            return a[:, : a.shape[1] // 2]
+
+        def second(a):
+            return a[:, a.shape[1] // 2 :].astype(bf16)
+
+        def product(left, right):
+            return tn(left, second(right)).astype(bf16)
+
+        def halved(left, right, got):
+            return tn(left, first(right)) + got.astype(f32)
+
+        def joined(part, got):
+            return first(part).astype(f32) + got.astype(f32)
 
     center = x1 - jnp.mean(x1, axis=-1, keepdims=True)
     inverse_two = lax.rsqrt(jnp.mean(center * center, axis=-1, keepdims=True) + epsilon)
@@ -565,6 +608,10 @@
     da = (dm * u * slope).astype(bf16)
     du = (dm * gelu).astype(bf16)
     dh2 = col_sum(wide([nt(da, v) + nt(du, w) for v, w in zip(acts, lins)]))
+    if two:
+        g_y = relative(g_low, "yzZx")
+        lower_got = to_y(product(m, g_y))
+        dh2, lower_got = lax.optimization_barrier((dh2, lower_got))
     e2 = dh2 * gain_two
     dx1 = g_low.astype(f32) + inverse_two * (
         e2
@@ -576,53 +623,15 @@
     if two:
         do_got = to_row(do_rows[:, W:])
         do = ordered(zrow, do_rows[:, :W], do_got, 0)
-        pair = ordered(zrow, y_half[None, :, :Dl], y_got[None], 0)
+        pair = ordered(zrow, y_half[None, :, :Dl], after(y_got, dx_low)[None], 0)
         layer_out = ordered(zcol, pair[:, None], to_col(pair)[:, None], 1).reshape(S, Dl)
     else:
         do = lax.all_to_all(do_rows, "row", split_axis=1, concat_axis=0, tiled=True)
 
-    Db = D // B
-    Dd = D // (B * R)
-    if two:
-        y_bit, z_bits = b % 2, b // 2
-
-        def relative(a, bits):
-            n = jnp.arange(D, dtype=jnp.int32)
-            rel = {"w": 0 * n, "x": 0 * n}
-            for i, bit in enumerate(bits):
-                rel[bit] = n // (D >> (i + 1)) % 2
-            z_rel = 2 * rel["Z"] + rel["z"]
-            column = ((z_bits ^ z_rel) * 2 + (y_bit ^ rel["y"])) * Db + n % Dd
-            column = column + (rel["w"] if "w" in bits else r ^ rel["x"]) * Dd
-            column = column ^ (r * (D // 2))
-            return nn(a, (n[:, None] == column[None, :]).astype(bf16)).astype(bf16)
-
-        def to_y(a):
-            return lax.ppermute(a, "dp", [(i, i ^ 1) for i in range(B)])
-
-        def to_z(a, j):
-            return lax.ppermute(a, "dp", [(i, i ^ (2 * j)) for i in range(B)])
-
-        def first(a):
-            return a[:, : a.shape[1] // 2]
-
-        def second(a):
-            return a[:, a.shape[1] // 2 :].astype(bf16)
-
-        def product(left, right):
-            return tn(left, second(right)).astype(bf16)
-
-        def halved(left, right, got):
-            return tn(left, first(right)) + got.astype(f32)
-
-        def joined(part, got):
-            return first(part).astype(f32) + got.astype(f32)
-
+    if two:
         o_heads = own_first(o_rows, 1)
-        g_y, dx_y = relative(g_low, "yzZx"), relative(dx_low, "yzZx")
+        dx_y = relative(dx_low, "yzZx")
         h_act, h_lin = relative(h2, "xzZy"), relative(h2, "xyzZ")
-        lower_got = to_y(product(m, g_y))
-        lower_got = after(lower_got, do_rows)
         lower = halved(m, g_y, lower_got)
         lower_got = to_z(second(lower), 1)
         proj_got = to_y(product(o_heads, dx_y))
@@ -661,8 +670,9 @@
         e1 = kept * gain_one
         sums = jnp.stack([jnp.sum(e1, axis=-1), jnp.sum(e1 * n1, axis=-1)])
         sums = (sums + to_row(sums)) * (1.0 / D)
-        mine = (kept[:, :Dl] + to_row(kept[:, Dl:].astype(bf16)).astype(f32)) * gain_one[:Dl]
         moved = lax.ppermute(after(dx_low[:, Dl:], from_left), ("row", "col"), [(0, 2), (3, 1)])
+        kept_send, moved = lax.optimization_barrier((kept[:, Dl:].astype(bf16), moved))
+        mine = (kept[:, :Dl] + to_row(kept_send).astype(f32)) * gain_one[:Dl]
         base = jnp.where(r == c, dx1[:, :Dl], moved.astype(f32))
         dx = base + inv * (mine - sums[0][:, None] - n1[:, :Dl] * sums[1][:, None])
         dx = dx.astype(bf16)
@@ -695,18 +705,17 @@
         lin = joined(lin, to_z(second(lin), 1))
         act, proj = joined(act, both_got[:n]), joined(proj, both_got[n:])
         lower = joined(lower, lower_got)
-        last_got = to_row(jnp.concatenate([second(lower), second(proj)], axis=0))
+        last_got = after(to_row(jnp.concatenate([second(lower), second(proj)], axis=0)), dx)
         lower, proj = joined(lower, last_got[:n]), joined(proj, last_got[n:])
         act = joined(act, to_y(second(act)))
-        lin = joined(lin, to_z(second(lin), 2))
+        lin = joined(lin, after(to_z(second(lin), 2), dx))
         gate = jnp.stack([act.T, lin.T])
         query = joined(query, to_z(second(query), 1))
-        query = joined(query, to_z(second(query), 2)).T
+        query = joined(query, after(to_z(second(query), 2), dx)).T
         wq_rows = take(wq, b ^ (4 * r), Db)
         place = (2 * b + r) ^ (8 * r)
-        side, inner = place // 8, place % 8
         wi_rows = jnp.stack(
-            [take(jnp.where(side == 0, w[0], w[1]), inner, Dd) for w in (acts, lins)]
+            [jnp.where(place < 8, *(take(w, place % 8, Dd) for w in ws)) for ws in (acts, lins)]
         )
     else:
 

time: 471 us -> 429 us (0.911)
  Pallas kernels: 76.8 us -> 63.7 us
  other arithmetic: 71.9 us -> 62.9 us
  matrix products: 82.2 us -> 73.7 us
  local copies, waits for them, and re-layouts: 40.2 us -> 33.1 us
    ppermute x16 -> x15, waiting for transfers between devices: 43.2 us -> 23.5 us  [to_row(): return lax.ppermute(a, 'row', SWAP)]
    dot_general x15, matrix products: 47.4 us -> 34 us  [nn(): return jnp.dot(a, b, preferred_element_type=f32)]
    ppermute x8 -> x10, waiting for transfers between devices: 35.9 us -> 47.1 us  [to_z(): return lax.ppermute(a, 'dp', [(i, i ^ 2 * j) for i in range(B)])]
    ppermute x1, waiting for transfers between devices: 6.74 us -> 14.9 us  [local(): from_left = lax.ppermute(dkv_right, 'dp', up)]
    pallas_call x2, Pallas kernels: 43.4 us -> 35.9 us  [attend_back_call(): pl.pallas_call(functools.partial(backward_kernel, heads, sets, final), gr...]
    pallas_call x2, Pallas kernels: 33.4 us -> 27.8 us  [attend_call(): pl.pallas_call(functools.partial(forward_kernel, heads, sets, final), gri...]
    ppermute x5, starting transfers between devices: 9.15 us -> 4.08 us  [to_y(): return lax.ppermute(a, 'dp', [(i, i ^ 1) for i in range(B)])]
    unnamed x129 -> x125, local copies, waits for them, and re-layouts: 11.6 us -> 9.24 us
  transfers between devices with their start and end apart: 44 -> 45, of which waited for: 17 -> 16; matrix products, arithmetic and copies ran while one was open for 35% -> 30% of each run, Pallas kernels for 17% -> 15%
where the time goes in v1:
time: 429 us; the launch traced here: 423 us
  waiting for transfers between devices  116 us (27%)
  matrix products  73.7 us (17%)
  starting transfers between devices  70.4 us (16%)
  Pallas kernels  63.7 us (15%)
  other arithmetic  62.9 us (15%)
  local copies, waits for them, and re-layouts  33.1 us (8%)
    ppermute x10, waiting for transfers between devices, to_z(): return lax.ppermute(a, 'dp', [(i, i ^ 2 * j) for i in range(B)])  47.1 us
    pallas_call x2, Pallas kernels, attend_back_call(): pl.pallas_call(functools.partial(backward_kernel, heads, sets, final), gr...  35.9 us
    dot_general x15, matrix products, nn(): return jnp.dot(a, b, preferred_element_type=f32)  34 us
    pallas_call x2, Pallas kernels, attend_call(): pl.pallas_call(functools.partial(forward_kernel, heads, sets, final), gri...  27.8 us
    ppermute x15, waiting for transfers between devices, to_row(): return lax.ppermute(a, 'row', SWAP)  23.5 us
    ppermute x10, starting transfers between devices, to_z(): return lax.ppermute(a, 'dp', [(i, i ^ 2 * j) for i in range(B)])  23.4 us
    ppermute x5, waiting for transfers between devices, to_y(): return lax.ppermute(a, 'dp', [(i, i ^ 1) for i in range(B)])  23 us
    dot_general x10, matrix products, tn(): lax.dot_general(a, b, (((0,), (0,)), ((), ())), preferred_element_type=f32)  19.2 us
  transfers between devices with their start and end apart: 45, of which 16 were waited for; matrix products, arithmetic and copies ran while one was open for 30% of the time, Pallas kernels for 15%

profile of v1, /device:TPU:3, one launch (start us, length us, event | category | flops | bytes accessed | tf_op | source)
XLA Modules:
  0.0 422.7 jit_solution(8031635314147896003)
XLA Ops:
  7.7 2.9 convert.78
  19.9 2.8 multiply_sine_fusion
  33.2 5.2 %collective-permute-done.2 = bf16[512,768]{0,1:T(8,128)(2,1)} collective-permute-done((bf16[512,768]{0,1:T(8,128)(2,1)}, bf16[512,768]{0,1:T(8,128)(2,1)}, u32[]{:S(2)}, u32[]{:S(2)}) %collective-permute-start.2) | collective-permute-done | bytes 786464 | tf_op jit(solution)/shard_map/ppermute | solution.py:388
  47.8 3.3 collective-permute-start.3
  59.8 19.5 %attend_own.1 = (f32[6,256,256]{2,1,0:T(8,128)}, f32[6,2,1024]{2,1,0:T(2,128)}) custom-call(s32[12]{0:T(128)} %reshape.726.bounds, bf16[1536,256]{1,0:T(8,128)(2,1)} %fusion.53.refs_0_, s32[6,1,256]{2,1,0:T(1,128)} %select_n.689.refs_1_.refs_4_, bf16[1536,512]{1,0:T(8,128)(2,1)} %copy-done.7, s32[1536,128]{1,0:T(8,128)} %broadcast_in_dim.126.refs_3_.refs_6_), custom_call_target="tpu_custom_call" | custom-call | flops 6291456 | bytes 3145728 | tf_op jit(solution)/shard_map/attend_own/pallas_call | solution.py:194
  79.3 7.6 %collective-permute-done.7 = bf16[384,512]{1,0:T(8,128)(2,1)} collective-permute-done((bf16[384,512]{1,0:T(8,128)(2,1)}, bf16[384,512]{1,0:T(8,128)(2,1)}, u32[]{:S(2)}, u32[]{:S(2)}) %collective-permute-start.7) | collective-permute-done | bytes 393248 | tf_op jit(solution)/shard_map/ppermute | solution.py:388
  86.9 6.8 %collective-permute-done.3.refs_2_.refs_5_ = bf16[1024,512]{1,0:T(8,128)(2,1)S(1)} collective-permute-done((bf16[1024,512]{1,0:T(8,128)(2,1)}, bf16[1024,512]{1,0:T(8,128)(2,1)S(1)}, u32[]{:S(2)}, u32[]{:S(2)}) %collective-permute-start.3) | collective-permute-done | bytes 1048608 | tf_op jit(solution)/shard_map/ppermute | solution.py:486
  93.7 3.5 collective-permute-start.8
  97.2 6.8 %fusion.16 = bf16[1536,1024]{1,0:T(8,128)(2,1)} fusion(bf16[1536,1024]{1,0:T(8,128)(2,1)} %copy-done.23, s32[1024]{0:T(1024)S(1)} %add_xor_fusion), kind=kOutput, calls=%fused_computation.29 | convolution fusion | flops 3223846912 | bytes 6295552 | tf_op jit(solution)/shard_map/dot_general | solution.py:32
  109.1 2.8 collective-permute-start.14
  113.9 8.3 %attend_final.1 = (bf16[1536,256]{1,0:T(8,128)(2,1)}, f32[6,1,1024]{2,1,0:T(1,128)}) custom-call(s32[24]{0:T(128)} %reshape.727.bounds, bf16[1536,256]{1,0:T(8,128)(2,1)} %fusion.53.refs_0_, s32[6,1,256]{2,1,0:T(1,128)} %select_n.689.refs_1_.refs_4_, bf16[1024,512]{1,0:T(8,128)(2,1)} %copy-done.18, bf16[1024,512]{1,0:T(8,128)(2,1)} %collective-permute-done.4.refs_3_.refs_6_, ...), custom_call_target="tpu_custom_call" | custom-call | flops 6291456 | bytes 3670016 | tf_op jit(solution)/shard_map/attend_final/pallas_call | solution.py:194
  125.5 3.0 fusion.32
  129.7 5.0 %collective-permute-start.13 = (bf16[656,512]{1,0:T(8,128)(2,1)}, bf16[656,512]{1,0:T(8,128)(2,1)}, u32[]{:S(2)}, u32[]{:S(2)}) collective-permute-start(bf16[656,512]{1,0:T(8,128)(2,1)} %collective-permute-done.9), channel_id=1, source_target_pairs={{0,8},{4,12},{8,0},{12,4},{16,24},{20,28},{24,16},{28,20},{1,9},{5... | collective-permute-start | bytes 2015240 | tf_op jit(solution)/shard_map/ppermute | solution.py:498
  135.9 6.0 %collective-permute-done.14 = bf16[512,1312]{0,1:T(8,128)(2,1)} collective-permute-done((bf16[512,1312]{0,1:T(8,128)(2,1)}, bf16[512,1312]{0,1:T(8,128)(2,1)}, u32[]{:S(2)}, u32[]{:S(2)}) %collective-permute-start.14) | collective-permute-done | bytes 1343520 | tf_op jit(solution)/shard_map/ppermute | solution.py:498
  147.9 3.4 fusion.178
  158.9 7.1 %multiply_convert_fusion = (bf16[768,1312]{0,1:T(8,128)(2,1)}, bf16[768,1312]{0,1:T(8,128)(2,1)}, bf16[768,1312]{0,1:T(8,128)(2,1)}) fusion(f32[768,1312]{0,1:T(8,128)S(1)} %convolution_add_fusion.1, f32[768,1312]{0,1:T(8,128)S(1)} %convolution_add_fusion, f32[768,1312]{0,1:T(8,128)S(1)} %fusion.92, bf16[656,512]{1,0:T(8,128)(2,1)} %collective-permute-done.13, ...), kind=kOutput, calls=%fused_computation.26 | convolution fusion | flops 1054973952 | bytes 20267008 | tf_op jit(solution)/shard_map/dot_general | solution.py:24
  166.0 3.1 convolution_convert_fusion.2
  180.0 3.1 fusion.111
  194.4 15.6 %collective-permute-done.16 = bf16[1312,512]{1,0:T(8,128)(2,1)S(1)} collective-permute-done((bf16[1312,512]{1,0:T(8,128)(2,1)S(1)}, bf16[1312,512]{1,0:T(8,128)(2,1)S(1)}, u32[]{:S(2)}, u32[]{:S(2)}) %collective-permute-start.16) | collective-permute-done | bytes 1343520 | tf_op jit(solution)/shard_map/ppermute | solution.py:569
  219.1 6.6 %collective-permute-done.17 = bf16[768,256]{1,0:T(8,128)(2,1)S(1)} collective-permute-done((bf16[768,256]{1,0:T(8,128)(2,1)S(1)}, bf16[768,256]{1,0:T(8,128)(2,1)S(1)}, u32[]{:S(2)}, u32[]{:S(2)}) %collective-permute-start.17) | collective-permute-done | bytes 393248 | tf_op jit(solution)/shard_map/ppermute | solution.py:388
  237.3 9.5 %back_halo.1 = (f32[6,256,256]{2,1,0:T(8,128)}, bf16[1024,512]{1,0:T(8,128)(2,1)}, bf16[1024,512]{1,0:T(8,128)(2,1)}) custom-call(s32[24]{0:T(128)} %reshape.727.bounds, bf16[1536,256]{1,0:T(8,128)(2,1)} %fusion.53.refs_0_, bf16[1536,256]{1,0:T(8,128)(2,1)} %maximum_select_fusion.7.refs_1_, bf16[1536,256]{1,0:T(8,128)(2,1)} %get-tuple-element.68.refs_2_, ...), custom_call_target="tpu_custom_call" | custom-call | flops 15728640 | bytes 3670016 | tf_op jit(solution)/shard_map/back_halo/pallas_call | solution.py:320
  248.2 9.3 %collective-permute-start.23 = (bf16[1024,512]{1,0:T(8,128)(2,1)}, bf16[1024,512]{1,0:T(8,128)(2,1)}, u32[]{:S(2)}, u32[]{:S(2)}) collective-permute-start(bf16[1024,512]{1,0:T(8,128)(2,1)} %get-tuple-element.84), channel_id=1, source_target_pairs={{0,4},{4,8},{8,12},{12,16},{16,20},{20,24},{24,28},{1,5},{5,9},{9,... | collective-permute-start | bytes 3145736 | tf_op jit(solution)/shard_map/ppermute | solution.py:646
  257.5 26.4 %back_own.1 = (f32[1536,256]{1,0:T(8,128)}, f32[1536,512]{1,0:T(8,128)}) custom-call(s32[12]{0:T(128)} %reshape.726.bounds, bf16[1536,256]{1,0:T(8,128)(2,1)} %fusion.53.refs_0_, bf16[1536,256]{1,0:T(8,128)(2,1)} %maximum_select_fusion.7.refs_1_, bf16[1536,256]{1,0:T(8,128)(2,1)} %get-tuple-element.68.refs_2_, f32[6,1,1024]{2,1,0:T(1,128)} %get-tuple-element.78.refs_3_, ...), custom_call_target="tpu_custom_call" | custom-call | flops 15728640 | bytes 3145728 | tf_op jit(solution)/shard_map/back_own/pallas_call | solution.py:320
  286.2 14.9 %collective-permute-done.23 = bf16[1024,512]{1,0:T(8,128)(2,1)} collective-permute-done((bf16[1024,512]{1,0:T(8,128)(2,1)}, bf16[1024,512]{1,0:T(8,128)(2,1)}, u32[]{:S(2)}, u32[]{:S(2)}) %collective-permute-start.23) | collective-permute-done | bytes 1048608 | tf_op jit(solution)/shard_map/ppermute | solution.py:646
  330.7 5.6 %collective-permute-start.43 = (bf16[1312,128]{1,0:T(8,128)(2,1)}, bf16[1312,128]{1,0:T(8,128)(2,1)S(1)}, u32[]{:S(2)}, u32[]{:S(2)}) collective-permute-start(bf16[1312,128]{1,0:T(8,128)(2,1)} %slice.740), channel_id=1, source_target_pairs={{0,16},{4,20},{8,24},{12,28},{16,0},{20,4},{24,8},{28,12},{1,17},{... | collective-permute-start | bytes 1007624 | tf_op jit(solution)/shard_map/ppermute | solution.py:498
  340.7 11.9 %collective-permute-done.35 = bf16[1824,256]{1,0:T(8,128)(2,1)S(1)} collective-permute-done((bf16[1824,256]{1,0:T(8,128)(2,1)S(1)}, bf16[1824,256]{1,0:T(8,128)(2,1)S(1)}, u32[]{:S(2)}, u32[]{:S(2)}) %collective-permute-start.35) | collective-permute-done | bytes 933920 | tf_op jit(solution)/shard_map/ppermute | solution.py:498
  353.1 5.7 %collective-permute-start.36 = (bf16[1824,128]{1,0:T(8,128)(2,1)S(1)}, bf16[1824,128]{1,0:T(8,128)(2,1)S(1)}, u32[]{:S(2)}, u32[]{:S(2)}) collective-permute-start(bf16[1824,128]{1,0:T(8,128)(2,1)S(1)} %pad_maximum_fusion.7), channel_id=1, source_target_pairs={{0,16},{4,20},{8,24},{12,28},{16,0},{20,4},{24,8},{28,12},{1,17},{... | collective-permute-start | bytes 1400840 | tf_op jit(solution)/shard_map/ppermute | solution.py:498
  360.7 7.8 %collective-permute-done.39 = bf16[1312,128]{1,0:T(8,128)(2,1)S(1)} collective-permute-done((bf16[1312,128]{1,0:T(8,128)(2,1)S(1)}, bf16[1312,128]{1,0:T(8,128)(2,1)S(1)}, u32[]{:S(2)}, u32[]{:S(2)}) %collective-permute-start.39) | collective-permute-done | bytes 335904 | tf_op jit(solution)/shard_map/ppermute | solution.py:498
  368.8 16.2 %collective-permute-done.32 = bf16[768,256]{1,0:T(8,128)(2,1)S(1)} collective-permute-done((bf16[768,256]{1,0:T(8,128)(2,1)S(1)}, bf16[768,256]{1,0:T(8,128)(2,1)S(1)}, u32[]{:S(2)}, u32[]{:S(2)}) %collective-permute-start.32) | collective-permute-done | bytes 393248 | tf_op jit(solution)/shard_map/ppermute | solution.py:498
  386.1 7.4 %collective-permute-done.37 = bf16[1312,64]{1,0:T(8,128)(2,1)S(1)} collective-permute-done((bf16[1312,64]{1,0:T(8,128)(2,1)S(1)}, bf16[1312,64]{1,0:T(8,128)(2,1)S(1)}, u32[]{:S(2)}, u32[]{:S(2)}) %collective-permute-start.37) | collective-permute-done | bytes 167968 | tf_op jit(solution)/shard_map/ppermute | solution.py:569
  398.1 4.0 collective-permute-done.33
  419.4 3.1 maximum_select_fusion.4
  (377 shorter events, 176.0 us)
Async XLA Ops:
  2.8 19.9 %collective-permute-start = (bf16[768,512]{1,0:T(8,128)(2,1)}, bf16[768,512]{1,0:T(8,128)(2,1)}, u32[]{:S(2)}, u32[]{:S(2)}) collective-permute-start(bf16[768,512]{1,0:T(8,128)(2,1)} %constant_dynamic-slice_fusion.7), channel_id=1, source_target_pairs={{0,2},{2,0},{1,3},{3,1},{4,6},{6,4},{5,7},{7,5},{8,10},{10,8},{9,1... | collective-permute-start | bytes 2359304 | tf_op jit(solution)/shard_map/ppermute | solution.py:388
  6.2 32.2 %collective-permute-start.2 = (bf16[512,768]{0,1:T(8,128)(2,1)}, bf16[512,768]{0,1:T(8,128)(2,1)}, u32[]{:S(2)}, u32[]{:S(2)}) collective-permute-start(bf16[512,768]{0,1:T(8,128)(2,1)} %get-tuple-element.158), channel_id=1, source_target_pairs={{0,2},{2,0},{1,3},{3,1},{4,6},{6,4},{5,7},{7,5},{8,10},{10,8},{9,1... | collective-permute-start | bytes 2359304 | tf_op jit(solution)/shard_map/ppermute | solution.py:388
  12.6 74.3 %collective-permute-start.5 = (bf16[512,1312]{0,1:T(8,128)(2,1)}, bf16[512,1312]{0,1:T(8,128)(2,1)}, u32[]{:S(2)}, u32[]{:S(2)}) collective-permute-start(bf16[512,1312]{0,1:T(8,128)(2,1)} %bitcast_select_fusion), channel_id=1, source_target_pairs={{0,2},{2,0},{1,3},{3,1},{4,6},{6,4},{5,7},{7,5},{8,10},{10,8},{9,1... | collective-permute-start | bytes 4030472 | tf_op jit(solution)/shard_map/ppermute | solution.py:388
  13.5 73.4 %collective-permute-start.6 = (bf16[512,512]{1,0:T(8,128)(2,1)}, bf16[512,512]{1,0:T(8,128)(2,1)}, u32[]{:S(2)}, u32[]{:S(2)}) collective-permute-start(bf16[512,512]{1,0:T(8,128)(2,1)} %convert_element_type.227), channel_id=1, source_target_pairs={{0,2},{2,0},{1,3},{3,1},{4,6},{6,4},{5,7},{7,5},{8,10},{10,8},{9,1... | collective-permute-start | bytes 1572872 | tf_op jit(solution)/shard_map/ppermute | solution.py:388
  15.8 71.1 %collective-permute-start.7 = (bf16[384,512]{1,0:T(8,128)(2,1)}, bf16[384,512]{1,0:T(8,128)(2,1)}, u32[]{:S(2)}, u32[]{:S(2)}) collective-permute-start(bf16[384,512]{1,0:T(8,128)(2,1)} %constant_dynamic-slice_fusion.4), channel_id=1, source_target_pairs={{0,2},{2,0},{1,3},{3,1},{4,6},{6,4},{5,7},{7,5},{8,10},{10,8},{9,1... | collective-permute-start | bytes 1179656 | tf_op jit(solution)/shard_map/ppermute | solution.py:388
  47.8 45.9 %collective-permute-start.3 = (bf16[1024,512]{1,0:T(8,128)(2,1)}, bf16[1024,512]{1,0:T(8,128)(2,1)S(1)}, u32[]{:S(2)}, u32[]{:S(2)}) collective-permute-start(bf16[1024,512]{1,0:T(8,128)(2,1)} %get-tuple-element.157), channel_id=1, source_target_pairs={{0,4},{4,8},{8,12},{12,16},{16,20},{20,24},{24,28},{1,5},{5,9},{9,... | collective-permute-start | bytes 3145736 | tf_op jit(solution)/shard_map/ppermute | solution.py:486
  51.1 42.6 %collective-permute-start.4 = (bf16[1024,512]{1,0:T(8,128)(2,1)}, bf16[1024,512]{1,0:T(8,128)(2,1)}, u32[]{:S(2)}, u32[]{:S(2)}) collective-permute-start(bf16[1024,512]{1,0:T(8,128)(2,1)} %get-tuple-element.156), channel_id=1, source_target_pairs={{4,0},{8,4},{12,8},{16,12},{20,16},{24,20},{28,24},{5,1},{9,5},{13... | collective-permute-start | bytes 3145736 | tf_op jit(solution)/shard_map/ppermute | solution.py:487
  93.7 28.6 %collective-permute-start.8 = (bf16[384,512]{1,0:T(8,128)(2,1)}, bf16[384,512]{1,0:T(8,128)(2,1)S(1)}, u32[]{:S(2)}, u32[]{:S(2)}) collective-permute-start(bf16[384,512]{1,0:T(8,128)(2,1)} %collective-permute-done.7), channel_id=1, source_target_pairs={{0,1},{1,0},{2,3},{3,2},{4,5},{5,4},{6,7},{7,6},{8,9},{9,8},{10,11... | collective-permute-start | bytes 1179656 | tf_op jit(solution)/shard_map/ppermute | solution.py:391
  104.2 19.9 %collective-permute-start.9 = (bf16[656,512]{1,0:T(8,128)(2,1)S(1)}, bf16[656,512]{1,0:T(8,128)(2,1)}, u32[]{:S(2)}, u32[]{:S(2)}) collective-permute-start(bf16[656,512]{1,0:T(8,128)(2,1)S(1)} %copy-done.29), channel_id=1, source_target_pairs={{0,2},{2,0},{1,3},{3,1},{4,6},{6,4},{5,7},{7,5},{8,10},{10,8},{9,1... | collective-permute-start | bytes 2015240 | tf_op jit(solution)/shard_map/ppermute | solution.py:388
  108.4 39.5 %collective-permute-start.12 = (bf16[512,1024]{1,0:T(8,128)(2,1)}, bf16[512,1024]{1,0:T(8,128)(2,1)}, u32[]{:S(2)}, u32[]{:S(2)}) collective-permute-start(bf16[512,1024]{1,0:T(8,128)(2,1)} %fusion.72), channel_id=1, source_target_pairs={{0,1},{1,0},{2,3},{3,2},{4,5},{5,4},{6,7},{7,6},{8,9},{9,8},{10,11... | collective-permute-start | bytes 3145736 | tf_op jit(solution)/shard_map/ppermute | solution.py:391
  109.1 32.8 %collective-permute-start.14 = (bf16[512,1312]{0,1:T(8,128)(2,1)}, bf16[512,1312]{0,1:T(8,128)(2,1)}, u32[]{:S(2)}, u32[]{:S(2)}) collective-permute-start(bf16[512,1312]{0,1:T(8,128)(2,1)} %collective-permute-done.5), channel_id=1, source_target_pairs={{0,8},{4,12},{8,0},{12,4},{16,24},{20,28},{24,16},{28,20},{1,9},{5... | collective-permute-start | bytes 4030472 | tf_op jit(solution)/shard_map/ppermute | solution.py:498
  129.7 29.1 %collective-permute-start.13 = (bf16[656,512]{1,0:T(8,128)(2,1)}, bf16[656,512]{1,0:T(8,128)(2,1)}, u32[]{:S(2)}, u32[]{:S(2)}) collective-permute-start(bf16[656,512]{1,0:T(8,128)(2,1)} %collective-permute-done.9), channel_id=1, source_target_pairs={{0,8},{4,12},{8,0},{12,4},{16,24},{20,28},{24,16},{28,20},{1,9},{5... | collective-permute-start | bytes 2015240 | tf_op jit(solution)/shard_map/ppermute | solution.py:498
  179.1 31.0 %collective-permute-start.16 = (bf16[1312,512]{1,0:T(8,128)(2,1)S(1)}, bf16[1312,512]{1,0:T(8,128)(2,1)S(1)}, u32[]{:S(2)}, u32[]{:S(2)}) collective-permute-start(bf16[1312,512]{1,0:T(8,128)(2,1)S(1)} %convolution_convert_fusion.2), channel_id=1, source_target_pairs={{0,4},{4,0},{8,12},{12,8},{16,20},{20,16},{24,28},{28,24},{1,5},{5... | collective-permute-start | bytes 4030472 | tf_op jit(solution)/shard_map/ppermute | solution.py:569
  192.5 24.6 %collective-permute-start.19 = (bf16[384,512]{1,0:T(8,128)(2,1)S(1)}, bf16[384,512]{1,0:T(8,128)(2,1)S(1)}, u32[]{:S(2)}, u32[]{:S(2)}) collective-permute-start(bf16[384,512]{1,0:T(8,128)(2,1)S(1)} %get-tuple-element.166), channel_id=1, source_target_pairs={{0,2},{2,0},{1,3},{3,1},{4,6},{6,4},{5,7},{7,5},{8,10},{10,8},{9,1... | collective-permute-start | bytes 1179656 | tf_op jit(solution)/shard_map/ppermute | solution.py:388
  217.3 18.5 %collective-permute-start.20 = (bf16[2,384,512]{2,1,0:T(8,128)(2,1)S(1)}, bf16[2,384,512]{2,1,0:T(8,128)(2,1)S(1)}, u32[]{:S(2)}, u32[]{:S(2)}) collective-permute-start(bf16[2,384,512]{2,1,0:T(8,128)(2,1)S(1)} %maximum_select_fusion.9), channel_id=1, source_target_pairs={{0,1},{1,0},{2,3},{3,2},{4,5},{5,4},{6,7},{7,6},{8,9},{9,8},{10,11... | collective-permute-start | bytes 2359304 | tf_op jit(solution)/shard_map/ppermute | solution.py:391
  225.7 75.4 %collective-permute-start.24 = (bf16[2624,512]{1,0:T(8,128)(2,1)}, bf16[2624,512]{1,0:T(8,128)(2,1)}, u32[]{:S(2)}, u32[]{:S(2)}) collective-permute-start(bf16[2624,512]{1,0:T(8,128)(2,1)} %pad_maximum_fusion.1), channel_id=1, source_target_pairs={{0,2},{2,0},{1,3},{3,1},{4,6},{6,4},{5,7},{7,5},{8,10},{10,8},{9,1... | collective-permute-start | bytes 8060936 | tf_op jit(solution)/shard_map/ppermute | solution.py:388
  229.8 17.1 %collective-permute-start.21 = (bf16[1312,256]{1,0:T(8,128)(2,1)}, bf16[1312,256]{1,0:T(8,128)(2,1)}, u32[]{:S(2)}, u32[]{:S(2)}) collective-permute-start(bf16[1312,256]{1,0:T(8,128)(2,1)} %slice.737), channel_id=1, source_target_pairs={{0,8},{4,12},{8,0},{12,4},{16,24},{20,28},{24,16},{28,20},{1,9},{5... | collective-permute-start | bytes 2015240 | tf_op jit(solution)/shard_map/ppermute | solution.py:498
  233.9 52.2 %collective-permute-start.25 = (bf16[512,512]{1,0:T(8,128)(2,1)}, bf16[512,512]{1,0:T(8,128)(2,1)}, u32[]{:S(2)}, u32[]{:S(2)}) collective-permute-start(bf16[512,512]{1,0:T(8,128)(2,1)} %convolution_convert_fusion.4), channel_id=1, source_target_pairs={{0,4},{4,0},{8,12},{12,8},{16,20},{20,16},{24,28},{28,24},{1,5},{5... | collective-permute-start | bytes 1572872 | tf_op jit(solution)/shard_map/ppermute | solution.py:569
  246.9 39.3 %collective-permute-start.22 = (bf16[1024,512]{1,0:T(8,128)(2,1)}, bf16[1024,512]{1,0:T(8,128)(2,1)}, u32[]{:S(2)}, u32[]{:S(2)}) collective-permute-start(bf16[1024,512]{1,0:T(8,128)(2,1)} %get-tuple-element.83), channel_id=1, source_target_pairs={{4,0},{8,4},{12,8},{16,12},{20,16},{24,20},{28,24},{5,1},{9,5},{13... | collective-permute-start | bytes 3145736 | tf_op jit(solution)/shard_map/ppermute | solution.py:645
  248.2 52.9 %collective-permute-start.23 = (bf16[1024,512]{1,0:T(8,128)(2,1)}, bf16[1024,512]{1,0:T(8,128)(2,1)}, u32[]{:S(2)}, u32[]{:S(2)}) collective-permute-start(bf16[1024,512]{1,0:T(8,128)(2,1)} %get-tuple-element.84), channel_id=1, source_target_pairs={{0,4},{4,8},{8,12},{12,16},{16,20},{20,24},{24,28},{1,5},{5,9},{9,... | collective-permute-start | bytes 3145736 | tf_op jit(solution)/shard_map/ppermute | solution.py:646
  313.3 17.4 %collective-permute-start.26 = (bf16[768,1024]{1,0:T(8,128)(2,1)S(1)}, bf16[768,1024]{1,0:T(8,128)(2,1)S(1)}, u32[]{:S(2)}, u32[]{:S(2)}) collective-permute-start(bf16[768,1024]{1,0:T(8,128)(2,1)S(1)} %dynamic-slice_convert_fusion), channel_id=1, source_target_pairs={{0,1},{1,0},{2,3},{3,2},{4,5},{5,4},{6,7},{7,6},{8,9},{9,8},{10,11... | collective-permute-start | bytes 4718600 | tf_op jit(solution)/shard_map/ppermute | solution.py:391
  313.8 23.9 %collective-permute-start.27 = (bf16[768,512]{1,0:T(8,128)(2,1)}, bf16[768,512]{1,0:T(8,128)(2,1)S(1)}, u32[]{:S(2)}, u32[]{:S(2)}) collective-permute-start(bf16[768,512]{1,0:T(8,128)(2,1)} %slice.503), channel_id=1, source_target_pairs={{0,2},{3,1},{4,6},{7,5},{8,10},{11,9},{12,14},{15,13},{16,18},{19,... | collective-permute-start | bytes 2359304 | tf_op jit(solution)/shard_map/ppermute | solution.py:673
  317.1 20.7 %collective-permute-start.38 = (bf16[1312,256]{1,0:T(8,128)(2,1)}, bf16[1312,256]{1,0:T(8,128)(2,1)}, u32[]{:S(2)}, u32[]{:S(2)}) collective-permute-start(bf16[1312,256]{1,0:T(8,128)(2,1)} %slice.735), channel_id=1, source_target_pairs={{0,4},{4,0},{8,12},{12,8},{16,20},{20,16},{24,28},{28,24},{1,5},{5... | collective-permute-start | bytes 2015240 | tf_op jit(solution)/shard_map/ppermute | solution.py:569
  322.2 30.4 %collective-permute-start.35 = (bf16[1824,256]{1,0:T(8,128)(2,1)S(1)}, bf16[1824,256]{1,0:T(8,128)(2,1)S(1)}, u32[]{:S(2)}, u32[]{:S(2)}) collective-permute-start(bf16[1824,256]{1,0:T(8,128)(2,1)S(1)} %pad_maximum_fusion.5), channel_id=1, source_target_pairs={{0,8},{4,12},{8,0},{12,4},{16,24},{20,28},{24,16},{28,20},{1,9},{5... | collective-permute-start | bytes 2801672 | tf_op jit(solution)/shard_map/ppermute | solution.py:498
  326.8 26.2 %collective-permute-start.31 = (bf16[768,512]{1,0:T(8,128)(2,1)}, bf16[768,512]{1,0:T(8,128)(2,1)}, u32[]{:S(2)}, u32[]{:S(2)}) collective-permute-start(bf16[768,512]{1,0:T(8,128)(2,1)} %fusion.59), channel_id=1, source_target_pairs={{0,4},{4,0},{8,12},{12,8},{16,20},{20,16},{24,28},{28,24},{1,5},{5... | collective-permute-start | bytes 2359304 | tf_op jit(solution)/shard_map/ppermute | solution.py:569
  330.7 29.6 %collective-permute-start.43 = (bf16[1312,128]{1,0:T(8,128)(2,1)}, bf16[1312,128]{1,0:T(8,128)(2,1)S(1)}, u32[]{:S(2)}, u32[]{:S(2)}) collective-permute-start(bf16[1312,128]{1,0:T(8,128)(2,1)} %slice.740), channel_id=1, source_target_pairs={{0,16},{4,20},{8,24},{12,28},{16,0},{20,4},{24,8},{28,12},{1,17},{... | collective-permute-start | bytes 1007624 | tf_op jit(solution)/shard_map/ppermute | solution.py:498
  337.7 55.9 %collective-permute-start.28 = (bf16[768,512]{1,0:T(8,128)(2,1)S(1)}, bf16[768,512]{1,0:T(8,128)(2,1)S(1)}, u32[]{:S(2)}, u32[]{:S(2)}) collective-permute-start(bf16[768,512]{1,0:T(8,128)(2,1)S(1)} %slice.733), channel_id=1, source_target_pairs={{0,2},{2,0},{1,3},{3,1},{4,6},{6,4},{5,7},{7,5},{8,10},{10,8},{9,1... | collective-permute-start | bytes 2359304 | tf_op jit(solution)/shard_map/ppermute | solution.py:388
  337.9 22.7 %collective-permute-start.29 = (f32[2,768]{1,0:T(2,128)S(1)}, f32[2,768]{1,0:T(2,128)S(1)}, u32[]{:S(2)}, u32[]{:S(2)}) collective-permute-start(f32[2,768]{1,0:T(2,128)S(1)} %pad_maximum_fusion.11), channel_id=1, source_target_pairs={{0,2},{2,0},{1,3},{3,1},{4,6},{6,4},{5,7},{7,5},{8,10},{10,8},{9,1... | collective-permute-start | bytes 18440 | tf_op jit(solution)/shard_map/ppermute | solution.py:388
  353.1 32.1 %collective-permute-start.36 = (bf16[1824,128]{1,0:T(8,128)(2,1)S(1)}, bf16[1824,128]{1,0:T(8,128)(2,1)S(1)}, u32[]{:S(2)}, u32[]{:S(2)}) collective-permute-start(bf16[1824,128]{1,0:T(8,128)(2,1)S(1)} %pad_maximum_fusion.7), channel_id=1, source_target_pairs={{0,16},{4,20},{8,24},{12,28},{16,0},{20,4},{24,8},{28,12},{1,17},{... | collective-permute-start | bytes 1400840 | tf_op jit(solution)/shard_map/ppermute | solution.py:498
  360.3 24.7 %collective-permute-start.32 = (bf16[768,256]{1,0:T(8,128)(2,1)S(1)}, bf16[768,256]{1,0:T(8,128)(2,1)S(1)}, u32[]{:S(2)}, u32[]{:S(2)}) collective-permute-start(bf16[768,256]{1,0:T(8,128)(2,1)S(1)} %slice.738), channel_id=1, source_target_pairs={{0,8},{4,12},{8,0},{12,4},{16,24},{20,28},{24,16},{28,20},{1,9},{5... | collective-permute-start | bytes 1179656 | tf_op jit(solution)/shard_map/ppermute | solution.py:498
  368.7 29.2 %collective-permute-start.40 = (bf16[1312,64]{1,0:T(8,128)(2,1)S(1)}, bf16[1312,64]{1,0:T(8,128)(2,1)S(1)}, u32[]{:S(2)}, u32[]{:S(2)}) collective-permute-start(bf16[1312,64]{1,0:T(8,128)(2,1)S(1)} %slice.741), channel_id=1, source_target_pairs={{0,16},{4,20},{8,24},{12,28},{16,0},{20,4},{24,8},{28,12},{1,17},{... | collective-permute-start | bytes 503816 | tf_op jit(solution)/shard_map/ppermute | solution.py:498
  394.3 25.2 %collective-permute-start.30 = (bf16[768,512]{1,0:T(8,128)(2,1)S(1)}, bf16[768,512]{1,0:T(8,128)(2,1)}, u32[]{:S(2)}, u32[]{:S(2)}) collective-permute-start(bf16[768,512]{1,0:T(8,128)(2,1)S(1)} %fusion.47), channel_id=1, source_target_pairs={{0,1},{1,0},{2,3},{3,2},{4,5},{5,4},{6,7},{7,6},{8,9},{9,8},{10,11... | collective-permute-start | bytes 2359304 | tf_op jit(solution)/shard_map/ppermute | solution.py:391
  (76 other events, 823.9 us)

commit v2 on v1

--- a/solution.py
+++ b/solution.py
@@ -460,95 +460,6 @@
     gain_one = own_first(gain_attn, 0)
     gain_two = own_first(gain_mlp, 0)
 
-    x = x_low.astype(f32)
-    center = x - jnp.mean(x, axis=-1, keepdims=True)
-    inverse_one = lax.rsqrt(jnp.mean(center * center, axis=-1, keepdims=True) + epsilon)
-    mean_one = jnp.mean(x, axis=-1, keepdims=True)
-    h1 = (center * inverse_one * gain_one).astype(bf16)
-    if two:
-        h1, wq_mine, wq_got = lax.optimization_barrier((h1, wq_mine, wq_got))
-        wq = jnp.concatenate([wq_mine, wq_got], axis=0)
-    wq = nn(wq, order).astype(bf16)
-
-    half = W // 2
-
-    def turn(t, sign):
-        first_half, second_half = t[:, :half], t[:, half:]
-        s = sine * sign
-        return jnp.concatenate(
-            [first_half * cosine - second_half * s, second_half * cosine + first_half * s], axis=1
-        )
-
-    kv_raw = nn(h1, wq[:, W:])
-    kv = jnp.concatenate([turn(kv_raw[:, :W], 1.0), kv_raw[:, W:]], axis=1).astype(bf16)
-    up = [(i, i + 1) for i in range(B - 1)]
-    down = [(i + 1, i) for i in range(B - 1)]
-    kv_left = lax.ppermute(kv[S - H :], "dp", up)
-    kv_right = lax.ppermute(kv[:H], "dp", down)
-    q = (turn(nn(h1, wq[:, :W]), 1.0) * (1.0 / math.sqrt(head_width))).astype(bf16)
-    wo_low, wd_low = w_out.astype(bf16), w_down.astype(bf16)
-    act_low, lin_low = w_in[:, 0].astype(bf16), w_in[:, 1].astype(bf16)
-    if two:
-        even = (b // 2) % 2 == 0
-        in_got, wo_got = to_row(jnp.where(even, act_low, lin_low)), to_row(wo_low)
-        g_got = to_row(take(take(cotangent, 1 - r, Sr), c, Sr // 2))
-        wd_half = take(wd_low, (b // 2) % 2, F // 2)
-
-        def to_z(a, j):
-            return lax.ppermute(a, "dp", [(i, i ^ (2 * j)) for i in range(B)])
-
-    state = attend_call(own_bounds, q, sq, [kv], [sk_own], heads)
-    if two:
-        kv_left, kv_right, in_got, wo_got, g_got, wd_half = after(
-            (kv_left, kv_right, in_got, wo_got, g_got, wd_half), state
-        )
-        in_other, wd_got = to_z(in_got, 1), to_row(wd_half)
-    o, lse = attend_call(
-        halo_bounds, q, sq, [kv_left, kv_right], [sk_left, sk_right], heads, state
-    )
-
-    if two:
-        o, wd_got = lax.optimization_barrier((o, wd_got))
-        wo = own_first(jnp.concatenate([wo_low, wo_got], axis=1), 0)
-    else:
-        wo = gather(wo_low, 1)
-
-    if two:
-        o_got = to_row(take(o, 1 - r, Sr))
-        o_rows = jnp.concatenate([take(o, r, Sr), o_got], axis=1)
-        wd_other, in_other = to_z(wd_got, 1), after(in_other, o_got)
-        act_got, lin_got = jnp.where(even, in_got, in_other), jnp.where(even, in_other, in_got)
-        wd_got = ordered(even, wd_got, wd_other, 0)
-        g_got = ordered(zcol, g_got, to_col(g_got), 0)
-        g_low = jnp.concatenate([take(cotangent, r, Sr), g_got], axis=1)
-        g_low = jnp.where(take(live, r, Sr)[:, None], g_low, 0)
-        wds = [wd_low, wd_got]
-        acts, lins = [act_low, act_got], [lin_low, lin_got]
-    else:
-        o_rows = lax.all_to_all(o, "row", split_axis=0, concat_axis=1, tiled=True)
-        own_g = jnp.where(live_column, cotangent, 0)
-        g_low = lax.all_to_all(own_g, "row", split_axis=0, concat_axis=1, tiled=True)
-        wds, acts, lins = [gather(wd_low, 1)], [gather(act_low, 0)], [gather(lin_low, 0)]
-
-    def split_nn(a, parts):
-        n = a.shape[1] // len(parts)
-        return sum(nn(a[:, i * n : (i + 1) * n], w) for i, w in enumerate(parts))
-
-    def split_nt(a, parts):
-        n = a.shape[1] // len(parts)
-        return sum(nt(a[:, i * n : (i + 1) * n], w) for i, w in enumerate(parts))
-
-    def wide(parts):
-        return parts[0] if len(parts) == 1 else jnp.concatenate(parts, axis=1)
-
-    x_rows = take(x_low, r, Sr).astype(f32)
-    if C == 2:
-        o_all = jnp.concatenate([o_rows, to_col(o_rows)], axis=1)
-        wo_all = jnp.concatenate([wo, to_col(wo)], axis=0)
-        x1 = x_rows + nn(o_all, wo_all)
-    else:
-        x1 = x_rows + lax.psum(nn(o_rows, wo), "col")
-
     Db = D // B
     Dd = D // (B * R)
     if two:
@@ -568,6 +479,9 @@
         def to_y(a):
             return lax.ppermute(a, "dp", [(i, i ^ 1) for i in range(B)])
 
+        def to_z(a, j):
+            return lax.ppermute(a, "dp", [(i, i ^ (2 * j)) for i in range(B)])
+
         def first(a):
             return a[:, : a.shape[1] // 2]
 
@@ -582,6 +496,95 @@
 
         def joined(part, got):
             return first(part).astype(f32) + got.astype(f32)
+
+    x = x_low.astype(f32)
+    center = x - jnp.mean(x, axis=-1, keepdims=True)
+    inverse_one = lax.rsqrt(jnp.mean(center * center, axis=-1, keepdims=True) + epsilon)
+    mean_one = jnp.mean(x, axis=-1, keepdims=True)
+    h1 = (center * inverse_one * gain_one).astype(bf16)
+    if two:
+        h1_y = relative(h1, "yzZw")
+        h1, h1_y, wq_mine, wq_got = lax.optimization_barrier((h1, h1_y, wq_mine, wq_got))
+        wq = jnp.concatenate([wq_mine, wq_got], axis=0)
+    wq = nn(wq, order).astype(bf16)
+
+    half = W // 2
+
+    def turn(t, sign):
+        first_half, second_half = t[:, :half], t[:, half:]
+        s = sine * sign
+        return jnp.concatenate(
+            [first_half * cosine - second_half * s, second_half * cosine + first_half * s], axis=1
+        )
+
+    kv_raw = nn(h1, wq[:, W:])
+    kv = jnp.concatenate([turn(kv_raw[:, :W], 1.0), kv_raw[:, W:]], axis=1).astype(bf16)
+    up = [(i, i + 1) for i in range(B - 1)]
+    down = [(i + 1, i) for i in range(B - 1)]
+    kv_left = lax.ppermute(kv[S - H :], "dp", up)
+    kv_right = lax.ppermute(kv[:H], "dp", down)
+    q = (turn(nn(h1, wq[:, :W]), 1.0) * (1.0 / math.sqrt(head_width))).astype(bf16)
+    wo_low, wd_low = w_out.astype(bf16), w_down.astype(bf16)
+    act_low, lin_low = w_in[:, 0].astype(bf16), w_in[:, 1].astype(bf16)
+    if two:
+        even = (b // 2) % 2 == 0
+        in_got, wo_got = to_row(jnp.where(even, act_low, lin_low)), to_row(wo_low)
+        g_got = to_row(take(take(cotangent, 1 - r, Sr), c, Sr // 2))
+        wd_half = take(wd_low, (b // 2) % 2, F // 2)
+
+    state = attend_call(own_bounds, q, sq, [kv], [sk_own], heads)
+    if two:
+        kv_left, kv_right, sk_left, sk_right, in_got, wo_got, g_got, wd_half = after(
+            (kv_left, kv_right, sk_left, sk_right, in_got, wo_got, g_got, wd_half), state
+        )
+        in_other, wd_got = to_z(in_got, 1), to_row(wd_half)
+    o, lse = attend_call(
+        halo_bounds, q, sq, [kv_left, kv_right], [sk_left, sk_right], heads, state
+    )
+
+    if two:
+        o, wd_got, wo_got, g_got = lax.optimization_barrier((o, wd_got, wo_got, g_got))
+        wo = own_first(jnp.concatenate([wo_low, wo_got], axis=1), 0)
+    else:
+        wo = gather(wo_low, 1)
+
+    if two:
+        o_got = to_row(take(o, 1 - r, Sr))
+        o_rows = jnp.concatenate([take(o, r, Sr), o_got], axis=1)
+        wd_other = to_z(wd_got, 1)
+        wd_got = ordered(even, wd_got, wd_other, 0)
+        g_got = ordered(zcol, g_got, to_col(g_got), 0)
+        g_low = jnp.concatenate([take(cotangent, r, Sr), g_got], axis=1)
+        g_low = jnp.where(take(live, r, Sr)[:, None], g_low, 0)
+        wds = [wd_low, wd_got]
+    else:
+        o_rows = lax.all_to_all(o, "row", split_axis=0, concat_axis=1, tiled=True)
+        own_g = jnp.where(live_column, cotangent, 0)
+        g_low = lax.all_to_all(own_g, "row", split_axis=0, concat_axis=1, tiled=True)
+        wds, acts, lins = [gather(wd_low, 1)], [gather(act_low, 0)], [gather(lin_low, 0)]
+
+    def split_nn(a, parts):
+        n = a.shape[1] // len(parts)
+        return sum(nn(a[:, i * n : (i + 1) * n], w) for i, w in enumerate(parts))
+
+    def split_nt(a, parts):
+        n = a.shape[1] // len(parts)
+        return sum(nt(a[:, i * n : (i + 1) * n], w) for i, w in enumerate(parts))
+
+    def wide(parts):
+        return parts[0] if len(parts) == 1 else jnp.concatenate(parts, axis=1)
+
+    x_rows = take(x_low, r, Sr).astype(f32)
+    if C == 2:
+        o_all = jnp.concatenate([o_rows, to_col(o_rows)], axis=1)
+        wo_all = jnp.concatenate([wo, to_col(wo)], axis=0)
+        x1 = x_rows + nn(o_all, wo_all)
+    else:
+        x1 = x_rows + lax.psum(nn(o_rows, wo), "col")
+    if two:
+        in_got, in_other = after((in_got, in_other), o_got)
+        act_got, lin_got = jnp.where(even, in_got, in_other), jnp.where(even, in_other, in_got)
+        acts, lins = [act_low, act_got], [lin_low, lin_got]
 
     center = x1 - jnp.mean(x1, axis=-1, keepdims=True)
     inverse_two = lax.rsqrt(jnp.mean(center * center, axis=-1, keepdims=True) + epsilon)
@@ -611,7 +614,6 @@
     if two:
         g_y = relative(g_low, "yzZx")
         lower_got = to_y(product(m, g_y))
-        dh2, lower_got = lax.optimization_barrier((dh2, lower_got))
     e2 = dh2 * gain_two
     dx1 = g_low.astype(f32) + inverse_two * (
         e2
@@ -629,14 +631,14 @@
         do = lax.all_to_all(do_rows, "row", split_axis=1, concat_axis=0, tiled=True)
 
     if two:
-        o_heads = own_first(o_rows, 1)
-        dx_y = relative(dx_low, "yzZx")
+        h2, da, du, o_heads, dx_late = after((h2, da, du, own_first(o_rows, 1), dx_low), do_rows)
+        dx_y = relative(dx_late, "yzZx")
         h_act, h_lin = relative(h2, "xzZy"), relative(h2, "xyzZ")
-        lower = halved(m, g_y, lower_got)
-        lower_got = to_z(second(lower), 1)
         proj_got = to_y(product(o_heads, dx_y))
         gate_send = jnp.concatenate([product(da, h_act), product(du, h_lin)], axis=0)
         gate_got = to_row(after(gate_send, do_got))
+        lower = halved(m, g_y, after(lower_got, gate_send))
+        lower_got = to_z(second(lower), 1)
         do, lower, layer_out = lax.optimization_barrier((do, lower, layer_out))
 
     dq_part, dkv_left, dkv_right = attend_back_call(
@@ -645,11 +647,13 @@
     from_right = lax.ppermute(dkv_left, "dp", down)
     from_left = lax.ppermute(dkv_right, "dp", up)
     if two:
-        dq_part, lower_got = lax.optimization_barrier((dq_part, lower_got))
+        lower = joined(lower, after(lower_got, dq_part))
+        lower_got = to_z(second(lower), 2)
+        dq_part, lower = lax.optimization_barrier((dq_part, lower))
     dq, dkv = attend_back_call(own_bounds, q, do, o, lse, sq, [kv], [sk_own], heads, [dq_part])
     if two:
-        dkv, from_right, from_left, gate_got, proj_got = lax.optimization_barrier(
-            (dkv, from_right, from_left, gate_got, proj_got)
+        dkv, from_right, from_left, gate_got, proj_got, lower_got = lax.optimization_barrier(
+            (dkv, from_right, from_left, gate_got, proj_got, lower_got)
         )
     pad = jnp.zeros((S - H, 2 * W), bf16)
     dkv = (
@@ -660,6 +664,9 @@
     dq = turn(dq * (1.0 / math.sqrt(head_width)), -1.0)
     dt = jnp.concatenate([dq, turn(dkv[:, :W], -1.0), dkv[:, W:]], axis=1).astype(bf16)
     dh1_part = nt(dt, wq)
+    if two:
+        query_send = product(dt, h1_y)
+        gate_got, proj_got, lower_got = after((gate_got, proj_got, lower_got), query_send, dh1_part)
 
     if two:
         n = S // 2
@@ -689,12 +696,8 @@
         ).astype(bf16)
 
     if two:
-        h1_y = relative(h1, "yzZw")
-        query = halved(dt, h1_y, after(to_y(product(dt, h1_y)), kept))
-        lower_got = after(lower_got, from_left)
+        query = halved(dt, h1_y, after(to_y(query_send), kept))
         n = F
-        lower = joined(lower, lower_got)
-        lower_got = after(to_z(second(lower), 2), kept)
         act = halved(da, h_act, gate_got[:n])
         lin = halved(du, h_lin, gate_got[n:])
         proj = halved(o_heads, dx_y, proj_got)
@@ -715,7 +718,7 @@
         wq_rows = take(wq, b ^ (4 * r), Db)
         place = (2 * b + r) ^ (8 * r)
         wi_rows = jnp.stack(
-            [jnp.where(place < 8, *(take(w, place % 8, Dd) for w in ws)) for ws in (acts, lins)]
+            [jnp.where(place < 8, *(take(w, place % 8, Dd) for w in ws)) for ws in after((acts, lins), kept)]
         )
     else:
 
@@ -738,12 +741,13 @@
         precision=lax.Precision.HIGHEST, preferred_element_type=f32,
     )
     if two:
-        one_part = one_part + to_row(one_part)
-        one_part = take(one_part, r, Dd)
-        pair = natural.reshape(2, Dd, 3 * W)
+        pair = jnp.concatenate([natural, jnp.broadcast_to(one_part[:, None], (Db, 128))], axis=1)
+        pair = pair.reshape(2, Dd, 3 * W + 128)
         mine = lax.dynamic_index_in_dim(pair, r, 0, keepdims=False)
         theirs = to_row(lax.dynamic_index_in_dim(pair, 1 - r, 0, keepdims=False))
-        query_out = ordered(zrow, mine, theirs, 1)
+        theirs = after(theirs, tokens_grad)
+        one_part = mine[:, 3 * W] + theirs[:, 3 * W]
+        query_out = ordered(zrow, mine[:, : 3 * W], theirs[:, : 3 * W], 1)
     else:
         one_part = take(lax.psum(one_part, "row"), r, Dd)
         query_out = lax.all_to_all(natural, "row", split_axis=0, concat_axis=1, tiled=True)

time: 429 us -> 416 us (0.970)
  waiting for transfers between devices: 116 us -> 80.9 us
  other arithmetic: 62.9 us -> 73.7 us
  local copies, waits for them, and re-layouts: 33.1 us -> 41.1 us
    ppermute x15 -> x14, waiting for transfers between devices: 23.5 us -> 4.14 us  [to_row(): return lax.ppermute(a, 'row', SWAP)]
    ppermute x10, waiting for transfers between devices: 47.1 us -> 28.8 us  [to_z(): return lax.ppermute(a, 'dp', [(i, i ^ 2 * j) for i in range(B)])]
    ppermute x1, waiting for transfers between devices: 14.9 us -> 1.39 us  [local(): from_left = lax.ppermute(dkv_right, 'dp', up)]
    ppermute x1, waiting for transfers between devices: 6.78 us -> 15.4 us  [local(): kv_left = lax.ppermute(kv[S - H:], 'dp', up)]
    ppermute x10, starting transfers between devices: 23.4 us -> 31.6 us  [to_z(): return lax.ppermute(a, 'dp', [(i, i ^ 2 * j) for i in range(B)])]
    ppermute x5, waiting for transfers between devices: 23 us -> 31.1 us  [to_y(): return lax.ppermute(a, 'dp', [(i, i ^ 1) for i in range(B)])]
    ppermute x10, starting transfers between devices: 15.4 us -> 10.2 us  [to_col(): return lax.ppermute(a, 'col', SWAP)]
    dot_general x15, matrix products: 34 us -> 29.2 us  [nn(): return jnp.dot(a, b, preferred_element_type=f32)]
  transfers between devices with their start and end apart: 45 -> 44, of which waited for: 16 -> 13; matrix products, arithmetic and copies ran while one was open for 30% -> 37% of each run, Pallas kernels for 15% -> 17%
where the time goes in v2:
time: 416 us; the launch traced here: 408 us
  waiting for transfers between devices  80.9 us (19%)
  other arithmetic  73.7 us (18%)
  starting transfers between devices  71.5 us (17%)
  matrix products  70.8 us (17%)
  Pallas kernels  67.9 us (16%)
  local copies, waits for them, and re-layouts  41.1 us (10%)
    pallas_call x2, Pallas kernels, attend_back_call(): pl.pallas_call(functools.partial(backward_kernel, heads, sets, final), gr...  38.4 us
    ppermute x10, starting transfers between devices, to_z(): return lax.ppermute(a, 'dp', [(i, i ^ 2 * j) for i in range(B)])  31.6 us
    ppermute x5, waiting for transfers between devices, to_y(): return lax.ppermute(a, 'dp', [(i, i ^ 1) for i in range(B)])  31.1 us
    pallas_call x2, Pallas kernels, attend_call(): pl.pallas_call(functools.partial(forward_kernel, heads, sets, final), gri...  29.4 us
    dot_general x15, matrix products, nn(): return jnp.dot(a, b, preferred_element_type=f32)  29.2 us
    ppermute x10, waiting for transfers between devices, to_z(): return lax.ppermute(a, 'dp', [(i, i ^ 2 * j) for i in range(B)])  28.8 us
    dot_general x8, matrix products, nt(): lax.dot_general(a, b, (((1,), (1,)), ((), ())), preferred_element_type=f32)  21.9 us
    dot_general x10, matrix products, tn(): lax.dot_general(a, b, (((0,), (0,)), ((), ())), preferred_element_type=f32)  18.1 us
  transfers between devices with their start and end apart: 44, of which 13 were waited for; matrix products, arithmetic and copies ran while one was open for 37% of the time, Pallas kernels for 17%

profile of v2, /device:TPU:3, one launch (start us, length us, event | category | flops | bytes accessed | tf_op | source)
XLA Modules:
  0.0 408.1 jit_solution(8015419214739610551)
XLA Ops:
  7.7 2.9 convert.78
  20.5 3.5 multiply_sine_fusion
  39.1 5.0 %fusion.16 = bf16[1536,1024]{1,0:T(8,128)(2,1)} fusion(bf16[1536,1024]{1,0:T(8,128)(2,1)S(1)} %fusion.4, s32[1024]{0:T(1024)S(1)} %add_xor_fusion.3), kind=kOutput, calls=%fused_computation.29 | convolution fusion | flops 3223846912 | bytes 6295552 | tf_op jit(solution)/shard_map/dot_general | solution.py:32
  53.3 4.7 %collective-permute-start.3 = (bf16[1024,512]{1,0:T(8,128)(2,1)}, bf16[1024,512]{1,0:T(8,128)(2,1)}, u32[]{:S(2)}, u32[]{:S(2)}) collective-permute-start(bf16[1024,512]{1,0:T(8,128)(2,1)} %get-tuple-element.199), channel_id=1, source_target_pairs={{0,4},{4,8},{8,12},{12,16},{16,20},{20,24},{24,28},{1,5},{5,9},{9,... | collective-permute-start | bytes 3145736 | tf_op jit(solution)/shard_map/ppermute | solution.py:524
  67.1 19.3 %attend_own.1 = (f32[6,256,256]{2,1,0:T(8,128)}, f32[6,2,1024]{2,1,0:T(2,128)}) custom-call(s32[12]{0:T(128)} %reshape.742.bounds, bf16[1536,256]{1,0:T(8,128)(2,1)} %fusion.49.refs_0_, s32[6,1,256]{2,1,0:T(1,128)} %select_n.689.refs_1_.refs_4_, bf16[1536,512]{1,0:T(8,128)(2,1)} %copy-done.7, s32[1536,128]{1,0:T(8,128)} %broadcast_in_dim.134.refs_3_.refs_6_), custom_call_target="tpu_custom_call" | custom-call | flops 6291456 | bytes 3145728 | tf_op jit(solution)/shard_map/attend_own/pallas_call | solution.py:194
  86.8 15.4 %collective-permute-done.3.refs_2_.refs_5_ = bf16[1024,512]{1,0:T(8,128)(2,1)} collective-permute-done((bf16[1024,512]{1,0:T(8,128)(2,1)}, bf16[1024,512]{1,0:T(8,128)(2,1)}, u32[]{:S(2)}, u32[]{:S(2)}) %collective-permute-start.3) | collective-permute-done | bytes 1048608 | tf_op jit(solution)/shard_map/ppermute | solution.py:524
  107.1 3.4 slice_bitcast_fusion
  110.5 3.6 collective-permute-start.14
  114.0 10.2 %attend_final.1 = (bf16[1536,256]{1,0:T(8,128)(2,1)}, f32[6,1,1024]{2,1,0:T(1,128)}) custom-call(s32[24]{0:T(128)} %reshape.741.bounds, bf16[1536,256]{1,0:T(8,128)(2,1)} %fusion.49.refs_0_, s32[6,1,256]{2,1,0:T(1,128)} %select_n.689.refs_1_.refs_4_, bf16[1024,512]{1,0:T(8,128)(2,1)} %collective-permute-done.3.refs_2_.refs_5_, ...), custom_call_target="tpu_custom_call" | custom-call | flops 6291456 | bytes 3670016 | tf_op jit(solution)/shard_map/attend_final/pallas_call | solution.py:194
  132.4 3.7 collective-permute-done.10
  138.9 3.2 fusion.81
  154.7 3.1 collective-permute-done.13
  157.9 7.1 %multiply_convert_fusion = (bf16[768,1312]{0,1:T(8,128)(2,1)S(1)}, bf16[768,1312]{0,1:T(8,128)(2,1)S(1)}, bf16[768,1312]{0,1:T(8,128)(2,1)}) fusion(f32[768,1312]{0,1:T(8,128)S(1)} %convolution_add_fusion.1, f32[768,1312]{0,1:T(8,128)S(1)} %convolution_add_fusion, f32[768,1312]{0,1:T(8,128)} %fusion.81, bf16[656,512]{1,0:T(8,128)(2,1)} %collective-permute-done.13, ...), kind=kOutput, calls=%fused_computation.26 | convolution fusion | flops 1054973952 | bytes 20267008 | tf_op jit(solution)/shard_map/dot_general | solution.py:24
  165.0 3.7 fusion.164
  176.1 3.2 fusion.100
  186.3 2.9 fusion.157
  199.4 13.7 %collective-permute-done.17 = bf16[1312,512]{1,0:T(8,128)(2,1)S(1)} collective-permute-done((bf16[1312,512]{1,0:T(8,128)(2,1)S(1)}, bf16[1312,512]{1,0:T(8,128)(2,1)S(1)}, u32[]{:S(2)}, u32[]{:S(2)}) %collective-permute-start.17) | collective-permute-done | bytes 1343520 | tf_op jit(solution)/shard_map/ppermute | solution.py:480
  224.4 12.5 %back_halo.1 = (f32[6,256,256]{2,1,0:T(8,128)}, bf16[1024,512]{1,0:T(8,128)(2,1)}, bf16[1024,512]{1,0:T(8,128)(2,1)}) custom-call(s32[24]{0:T(128)} %reshape.741.bounds, bf16[1536,256]{1,0:T(8,128)(2,1)} %fusion.49.refs_0_, bf16[1536,256]{1,0:T(8,128)(2,1)} %maximum_select_fusion.7.refs_1_, bf16[1536,256]{1,0:T(8,128)(2,1)} %get-tuple-element.90.refs_2_, ...), custom_call_target="tpu_custom_call" | custom-call | flops 15728640 | bytes 3670016 | tf_op jit(solution)/shard_map/back_halo/pallas_call | solution.py:320
  240.5 5.0 %collective-permute-start.23 = (bf16[1024,512]{1,0:T(8,128)(2,1)}, bf16[1024,512]{1,0:T(8,128)(2,1)}, u32[]{:S(2)}, u32[]{:S(2)}) collective-permute-start(bf16[1024,512]{1,0:T(8,128)(2,1)} %get-tuple-element.111), channel_id=1, source_target_pairs={{0,4},{4,8},{8,12},{12,16},{16,20},{20,24},{24,28},{1,5},{5,9},{9,... | collective-permute-start | bytes 3145736 | tf_op jit(solution)/shard_map/ppermute | solution.py:648
  245.4 7.0 %collective-permute-start.26 = (bf16[1312,128]{1,0:T(8,128)(2,1)}, bf16[1312,128]{1,0:T(8,128)(2,1)}, u32[]{:S(2)}, u32[]{:S(2)}) collective-permute-start(bf16[1312,128]{1,0:T(8,128)(2,1)} %slice.753), channel_id=1, source_target_pairs={{0,16},{4,20},{8,24},{12,28},{16,0},{20,4},{24,8},{28,12},{1,17},{... | collective-permute-start | bytes 1007624 | tf_op jit(solution)/shard_map/ppermute | solution.py:483
  252.4 26.0 %back_own.1 = (f32[1536,256]{1,0:T(8,128)}, f32[1536,512]{1,0:T(8,128)}) custom-call(s32[12]{0:T(128)} %reshape.742.bounds, bf16[1536,256]{1,0:T(8,128)(2,1)} %fusion.49.refs_0_, bf16[1536,256]{1,0:T(8,128)(2,1)} %maximum_select_fusion.7.refs_1_, bf16[1536,256]{1,0:T(8,128)(2,1)} %get-tuple-element.90.refs_2_, f32[6,1,1024]{2,1,0:T(1,128)} %get-tuple-element.103.refs_3_, ...), custom_call_target="tpu_custom_call" | custom-call | flops 15728640 | bytes 3145728 | tf_op jit(solution)/shard_map/back_own/pallas_call | solution.py:320
  280.7 6.9 %collective-permute-done.26 = bf16[1312,128]{1,0:T(8,128)(2,1)} collective-permute-done((bf16[1312,128]{1,0:T(8,128)(2,1)}, bf16[1312,128]{1,0:T(8,128)(2,1)}, u32[]{:S(2)}, u32[]{:S(2)}) %collective-permute-start.26) | collective-permute-done | bytes 335904 | tf_op jit(solution)/shard_map/ppermute | solution.py:483
  292.4 2.6 fusion.166
  295.9 3.6 collective-permute-start.28
  313.3 7.1 %collective-permute-start.36 = (bf16[1824,256]{1,0:T(8,128)(2,1)S(1)}, bf16[1824,256]{1,0:T(8,128)(2,1)S(1)}, u32[]{:S(2)}, u32[]{:S(2)}) collective-permute-start(bf16[1824,256]{1,0:T(8,128)(2,1)S(1)} %pad_maximum_fusion.5), channel_id=1, source_target_pairs={{0,8},{4,12},{8,0},{12,4},{16,24},{20,28},{24,16},{28,20},{1,9},{5... | collective-permute-start | bytes 2801672 | tf_op jit(solution)/shard_map/ppermute | solution.py:483
  324.9 10.2 %collective-permute-done.39 = bf16[1312,256]{1,0:T(8,128)(2,1)S(1)} collective-permute-done((bf16[1312,256]{1,0:T(8,128)(2,1)}, bf16[1312,256]{1,0:T(8,128)(2,1)S(1)}, u32[]{:S(2)}, u32[]{:S(2)}) %collective-permute-start.39) | collective-permute-done | bytes 671776 | tf_op jit(solution)/shard_map/ppermute | solution.py:480
  335.3 7.1 %collective-permute-start.40 = (bf16[1312,128]{1,0:T(8,128)(2,1)S(1)}, bf16[1312,128]{1,0:T(8,128)(2,1)S(1)}, u32[]{:S(2)}, u32[]{:S(2)}) collective-permute-start(bf16[1312,128]{1,0:T(8,128)(2,1)S(1)} %slice.750), channel_id=1, source_target_pairs={{0,8},{4,12},{8,0},{12,4},{16,24},{20,28},{24,16},{28,20},{1,9},{5... | collective-permute-start | bytes 1007624 | tf_op jit(solution)/shard_map/ppermute | solution.py:483
  351.3 2.8 collective-permute-done.40
  356.1 13.8 %collective-permute-done.33 = bf16[768,256]{1,0:T(8,128)(2,1)S(1)} collective-permute-done((bf16[768,256]{1,0:T(8,128)(2,1)S(1)}, bf16[768,256]{1,0:T(8,128)(2,1)S(1)}, u32[]{:S(2)}, u32[]{:S(2)}) %collective-permute-start.33) | collective-permute-done | bytes 393248 | tf_op jit(solution)/shard_map/ppermute | solution.py:483
  372.4 3.3 collective-permute-start.38
  376.7 7.2 %collective-permute-done.38 = bf16[1312,64]{1,0:T(8,128)(2,1)S(1)} collective-permute-done((bf16[1312,64]{1,0:T(8,128)(2,1)S(1)}, bf16[1312,64]{1,0:T(8,128)(2,1)S(1)}, u32[]{:S(2)}, u32[]{:S(2)}) %collective-permute-start.38) | collective-permute-done | bytes 167968 | tf_op jit(solution)/shard_map/ppermute | solution.py:480
  399.1 3.4 maximum_select_fusion.4
  (384 shorter events, 178.7 us)
Async XLA Ops:
  2.8 21.2 %collective-permute-start = (bf16[768,512]{1,0:T(8,128)(2,1)}, bf16[768,512]{1,0:T(8,128)(2,1)}, u32[]{:S(2)}, u32[]{:S(2)}) collective-permute-start(bf16[768,512]{1,0:T(8,128)(2,1)} %constant_dynamic-slice_fusion.6), channel_id=1, source_target_pairs={{0,2},{2,0},{1,3},{3,1},{4,6},{6,4},{5,7},{7,5},{8,10},{10,8},{9,1... | collective-permute-start | bytes 2359304 | tf_op jit(solution)/shard_map/ppermute | solution.py:388
  6.2 37.9 %collective-permute-start.2 = (bf16[512,768]{0,1:T(8,128)(2,1)}, bf16[512,768]{0,1:T(8,128)(2,1)}, u32[]{:S(2)}, u32[]{:S(2)}) collective-permute-start(bf16[512,768]{0,1:T(8,128)(2,1)} %get-tuple-element.202), channel_id=1, source_target_pairs={{0,2},{2,0},{1,3},{3,1},{4,6},{6,4},{5,7},{7,5},{8,10},{10,8},{9,1... | collective-permute-start | bytes 2359304 | tf_op jit(solution)/shard_map/ppermute | solution.py:388
  12.6 74.2 %collective-permute-start.5 = (bf16[512,1312]{0,1:T(8,128)(2,1)}, bf16[512,1312]{0,1:T(8,128)(2,1)}, u32[]{:S(2)}, u32[]{:S(2)}) collective-permute-start(bf16[512,1312]{0,1:T(8,128)(2,1)} %broadcast_select_fusion.2), channel_id=1, source_target_pairs={{0,2},{2,0},{1,3},{3,1},{4,6},{6,4},{5,7},{7,5},{8,10},{10,8},{9,1... | collective-permute-start | bytes 4030472 | tf_op jit(solution)/shard_map/ppermute | solution.py:388
  13.6 73.2 %collective-permute-start.6 = (bf16[512,512]{1,0:T(8,128)(2,1)}, bf16[512,512]{1,0:T(8,128)(2,1)}, u32[]{:S(2)}, u32[]{:S(2)}) collective-permute-start(bf16[512,512]{1,0:T(8,128)(2,1)} %convert_element_type.229), channel_id=1, source_target_pairs={{0,2},{2,0},{1,3},{3,1},{4,6},{6,4},{5,7},{7,5},{8,10},{10,8},{9,1... | collective-permute-start | bytes 1572872 | tf_op jit(solution)/shard_map/ppermute | solution.py:388
  15.9 70.9 %collective-permute-start.7 = (bf16[384,512]{1,0:T(8,128)(2,1)}, bf16[384,512]{1,0:T(8,128)(2,1)S(1)}, u32[]{:S(2)}, u32[]{:S(2)}) collective-permute-start(bf16[384,512]{1,0:T(8,128)(2,1)} %constant_dynamic-slice_fusion.3), channel_id=1, source_target_pairs={{0,2},{2,0},{1,3},{3,1},{4,6},{6,4},{5,7},{7,5},{8,10},{10,8},{9,1... | collective-permute-start | bytes 1179656 | tf_op jit(solution)/shard_map/ppermute | solution.py:388
  53.3 48.9 %collective-permute-start.3 = (bf16[1024,512]{1,0:T(8,128)(2,1)}, bf16[1024,512]{1,0:T(8,128)(2,1)}, u32[]{:S(2)}, u32[]{:S(2)}) collective-permute-start(bf16[1024,512]{1,0:T(8,128)(2,1)} %get-tuple-element.199), channel_id=1, source_target_pairs={{0,4},{4,8},{8,12},{12,16},{16,20},{20,24},{24,28},{1,5},{5,9},{9,... | collective-permute-start | bytes 3145736 | tf_op jit(solution)/shard_map/ppermute | solution.py:524
  58.0 44.2 %collective-permute-start.4 = (bf16[1024,512]{1,0:T(8,128)(2,1)}, bf16[1024,512]{1,0:T(8,128)(2,1)}, u32[]{:S(2)}, u32[]{:S(2)}) collective-permute-start(bf16[1024,512]{1,0:T(8,128)(2,1)} %get-tuple-element.198), channel_id=1, source_target_pairs={{4,0},{8,4},{12,8},{16,12},{20,16},{24,20},{28,24},{5,1},{9,5},{13... | collective-permute-start | bytes 3145736 | tf_op jit(solution)/shard_map/ppermute | solution.py:525
  104.2 20.0 %collective-permute-start.8 = (bf16[656,512]{1,0:T(8,128)(2,1)}, bf16[656,512]{1,0:T(8,128)(2,1)}, u32[]{:S(2)}, u32[]{:S(2)}) collective-permute-start(bf16[656,512]{1,0:T(8,128)(2,1)} %constant_dynamic-slice_fusion.2), channel_id=1, source_target_pairs={{0,2},{2,0},{1,3},{3,1},{4,6},{6,4},{5,7},{7,5},{8,10},{10,8},{9,1... | collective-permute-start | bytes 2015240 | tf_op jit(solution)/shard_map/ppermute | solution.py:388
  110.5 33.0 %collective-permute-start.14 = (bf16[512,1312]{0,1:T(8,128)(2,1)}, bf16[512,1312]{0,1:T(8,128)(2,1)}, u32[]{:S(2)}, u32[]{:S(2)}) collective-permute-start(bf16[512,1312]{0,1:T(8,128)(2,1)} %collective-permute-done.5), channel_id=1, source_target_pairs={{0,8},{4,12},{8,0},{12,4},{16,24},{20,28},{24,16},{28,20},{1,9},{5... | collective-permute-start | bytes 4030472 | tf_op jit(solution)/shard_map/ppermute | solution.py:483
  131.1 26.8 %collective-permute-start.13 = (bf16[656,512]{1,0:T(8,128)(2,1)}, bf16[656,512]{1,0:T(8,128)(2,1)}, u32[]{:S(2)}, u32[]{:S(2)}) collective-permute-start(bf16[656,512]{1,0:T(8,128)(2,1)} %collective-permute-done.8), channel_id=1, source_target_pairs={{0,8},{4,12},{8,0},{12,4},{16,24},{20,28},{24,16},{28,20},{1,9},{5... | collective-permute-start | bytes 2015240 | tf_op jit(solution)/shard_map/ppermute | solution.py:483
  182.6 30.6 %collective-permute-start.17 = (bf16[1312,512]{1,0:T(8,128)(2,1)S(1)}, bf16[1312,512]{1,0:T(8,128)(2,1)S(1)}, u32[]{:S(2)}, u32[]{:S(2)}) collective-permute-start(bf16[1312,512]{1,0:T(8,128)(2,1)S(1)} %convolution_convert_fusion.2), channel_id=1, source_target_pairs={{0,4},{4,0},{8,12},{12,8},{16,20},{20,16},{24,28},{28,24},{1,5},{5... | collective-permute-start | bytes 4030472 | tf_op jit(solution)/shard_map/ppermute | solution.py:480
  184.5 28.7 %collective-permute-start.19 = (bf16[384,512]{1,0:T(8,128)(2,1)S(1)}, bf16[384,512]{1,0:T(8,128)(2,1)S(1)}, u32[]{:S(2)}, u32[]{:S(2)}) collective-permute-start(bf16[384,512]{1,0:T(8,128)(2,1)S(1)} %get-tuple-element.210), channel_id=1, source_target_pairs={{0,2},{2,0},{1,3},{3,1},{4,6},{6,4},{5,7},{7,5},{8,10},{10,8},{9,1... | collective-permute-start | bytes 1179656 | tf_op jit(solution)/shard_map/ppermute | solution.py:388
  190.3 31.0 %collective-permute-start.16 = (bf16[768,256]{1,0:T(8,128)(2,1)S(1)}, bf16[768,256]{1,0:T(8,128)(2,1)S(1)}, u32[]{:S(2)}, u32[]{:S(2)}) collective-permute-start(bf16[768,256]{1,0:T(8,128)(2,1)S(1)} %get-tuple-element.214), channel_id=1, source_target_pairs={{0,2},{2,0},{1,3},{3,1},{4,6},{6,4},{5,7},{7,5},{8,10},{10,8},{9,1... | collective-permute-start | bytes 1179656 | tf_op jit(solution)/shard_map/ppermute | solution.py:388
  216.3 20.5 %collective-permute-start.21 = (bf16[1312,256]{1,0:T(8,128)(2,1)}, bf16[1312,256]{1,0:T(8,128)(2,1)S(1)}, u32[]{:S(2)}, u32[]{:S(2)}) collective-permute-start(bf16[1312,256]{1,0:T(8,128)(2,1)} %slice.746), channel_id=1, source_target_pairs={{0,8},{4,12},{8,0},{12,4},{16,24},{20,28},{24,16},{28,20},{1,9},{5... | collective-permute-start | bytes 2015240 | tf_op jit(solution)/shard_map/ppermute | solution.py:483
  221.2 59.5 %collective-permute-start.25 = (bf16[512,512]{1,0:T(8,128)(2,1)}, bf16[512,512]{1,0:T(8,128)(2,1)}, u32[]{:S(2)}, u32[]{:S(2)}) collective-permute-start(bf16[512,512]{1,0:T(8,128)(2,1)} %convolution_convert_fusion.4), channel_id=1, source_target_pairs={{0,4},{4,0},{8,12},{12,8},{16,20},{20,16},{24,28},{28,24},{1,5},{5... | collective-permute-start | bytes 1572872 | tf_op jit(solution)/shard_map/ppermute | solution.py:480
  221.2 67.8 %collective-permute-start.24 = (bf16[2624,512]{1,0:T(8,128)(2,1)}, bf16[2624,512]{1,0:T(8,128)(2,1)}, u32[]{:S(2)}, u32[]{:S(2)}) collective-permute-start(bf16[2624,512]{1,0:T(8,128)(2,1)} %pad_maximum_fusion.1), channel_id=1, source_target_pairs={{0,2},{2,0},{1,3},{3,1},{4,6},{6,4},{5,7},{7,5},{8,10},{10,8},{9,1... | collective-permute-start | bytes 8060936 | tf_op jit(solution)/shard_map/ppermute | solution.py:388
  239.2 48.4 %collective-permute-start.22 = (bf16[1024,512]{1,0:T(8,128)(2,1)}, bf16[1024,512]{1,0:T(8,128)(2,1)S(1)}, u32[]{:S(2)}, u32[]{:S(2)}) collective-permute-start(bf16[1024,512]{1,0:T(8,128)(2,1)} %get-tuple-element.110), channel_id=1, source_target_pairs={{4,0},{8,4},{12,8},{16,12},{20,16},{24,20},{28,24},{5,1},{9,5},{13... | collective-permute-start | bytes 3145736 | tf_op jit(solution)/shard_map/ppermute | solution.py:647
  240.5 48.5 %collective-permute-start.23 = (bf16[1024,512]{1,0:T(8,128)(2,1)}, bf16[1024,512]{1,0:T(8,128)(2,1)}, u32[]{:S(2)}, u32[]{:S(2)}) collective-permute-start(bf16[1024,512]{1,0:T(8,128)(2,1)} %get-tuple-element.111), channel_id=1, source_target_pairs={{0,4},{4,8},{8,12},{12,16},{16,20},{20,24},{24,28},{1,5},{5,9},{9,... | collective-permute-start | bytes 3145736 | tf_op jit(solution)/shard_map/ppermute | solution.py:648
  245.4 42.2 %collective-permute-start.26 = (bf16[1312,128]{1,0:T(8,128)(2,1)}, bf16[1312,128]{1,0:T(8,128)(2,1)}, u32[]{:S(2)}, u32[]{:S(2)}) collective-permute-start(bf16[1312,128]{1,0:T(8,128)(2,1)} %slice.753), channel_id=1, source_target_pairs={{0,16},{4,20},{8,24},{12,28},{16,0},{20,4},{24,8},{28,12},{1,17},{... | collective-permute-start | bytes 1007624 | tf_op jit(solution)/shard_map/ppermute | solution.py:483
  295.3 26.4 %collective-permute-start.27 = (bf16[768,1024]{1,0:T(8,128)(2,1)S(1)}, bf16[768,1024]{1,0:T(8,128)(2,1)S(1)}, u32[]{:S(2)}, u32[]{:S(2)}) collective-permute-start(bf16[768,1024]{1,0:T(8,128)(2,1)S(1)} %dynamic-slice_convert_fusion), channel_id=1, source_target_pairs={{0,1},{1,0},{2,3},{3,2},{4,5},{5,4},{6,7},{7,6},{8,9},{9,8},{10,11... | collective-permute-start | bytes 4718600 | tf_op jit(solution)/shard_map/ppermute | solution.py:391
  295.9 27.4 %collective-permute-start.28 = (bf16[768,512]{1,0:T(8,128)(2,1)S(1)}, bf16[768,512]{1,0:T(8,128)(2,1)S(1)}, u32[]{:S(2)}, u32[]{:S(2)}) collective-permute-start(bf16[768,512]{1,0:T(8,128)(2,1)S(1)} %slice.520), channel_id=1, source_target_pairs={{0,2},{3,1},{4,6},{7,5},{8,10},{11,9},{12,14},{15,13},{16,18},{19,... | collective-permute-start | bytes 2359304 | tf_op jit(solution)/shard_map/ppermute | solution.py:680
  301.8 41.2 %collective-permute-start.32 = (bf16[768,512]{1,0:T(8,128)(2,1)}, bf16[768,512]{1,0:T(8,128)(2,1)}, u32[]{:S(2)}, u32[]{:S(2)}) collective-permute-start(bf16[768,512]{1,0:T(8,128)(2,1)} %fusion.61), channel_id=1, source_target_pairs={{0,4},{4,0},{8,12},{12,8},{16,20},{20,16},{24,28},{28,24},{1,5},{5... | collective-permute-start | bytes 2359304 | tf_op jit(solution)/shard_map/ppermute | solution.py:480
  307.5 27.5 %collective-permute-start.39 = (bf16[1312,256]{1,0:T(8,128)(2,1)}, bf16[1312,256]{1,0:T(8,128)(2,1)S(1)}, u32[]{:S(2)}, u32[]{:S(2)}) collective-permute-start(bf16[1312,256]{1,0:T(8,128)(2,1)} %slice.744), channel_id=1, source_target_pairs={{0,4},{4,0},{8,12},{12,8},{16,20},{20,16},{24,28},{28,24},{1,5},{5... | collective-permute-start | bytes 2015240 | tf_op jit(solution)/shard_map/ppermute | solution.py:480
  313.3 29.1 %collective-permute-start.36 = (bf16[1824,256]{1,0:T(8,128)(2,1)S(1)}, bf16[1824,256]{1,0:T(8,128)(2,1)S(1)}, u32[]{:S(2)}, u32[]{:S(2)}) collective-permute-start(bf16[1824,256]{1,0:T(8,128)(2,1)S(1)} %pad_maximum_fusion.5), channel_id=1, source_target_pairs={{0,8},{4,12},{8,0},{12,4},{16,24},{20,28},{24,16},{28,20},{1,9},{5... | collective-permute-start | bytes 2801672 | tf_op jit(solution)/shard_map/ppermute | solution.py:483
  323.2 61.6 %collective-permute-start.29 = (bf16[768,512]{1,0:T(8,128)(2,1)S(1)}, bf16[768,512]{1,0:T(8,128)(2,1)S(1)}, u32[]{:S(2)}, u32[]{:S(2)}) collective-permute-start(bf16[768,512]{1,0:T(8,128)(2,1)S(1)} %slice.742), channel_id=1, source_target_pairs={{0,2},{2,0},{1,3},{3,1},{4,6},{6,4},{5,7},{7,5},{8,10},{10,8},{9,1... | collective-permute-start | bytes 2359304 | tf_op jit(solution)/shard_map/ppermute | solution.py:388
  323.4 27.9 %collective-permute-start.30 = (f32[2,768]{1,0:T(2,128)S(1)}, f32[2,768]{1,0:T(2,128)S(1)}, u32[]{:S(2)}, u32[]{:S(2)}) collective-permute-start(f32[2,768]{1,0:T(2,128)S(1)} %pad_maximum_fusion.10), channel_id=1, source_target_pairs={{0,2},{2,0},{1,3},{3,1},{4,6},{6,4},{5,7},{7,5},{8,10},{10,8},{9,1... | collective-permute-start | bytes 18440 | tf_op jit(solution)/shard_map/ppermute | solution.py:388
  335.3 18.8 %collective-permute-start.40 = (bf16[1312,128]{1,0:T(8,128)(2,1)S(1)}, bf16[1312,128]{1,0:T(8,128)(2,1)S(1)}, u32[]{:S(2)}, u32[]{:S(2)}) collective-permute-start(bf16[1312,128]{1,0:T(8,128)(2,1)S(1)} %slice.750), channel_id=1, source_target_pairs={{0,8},{4,12},{8,0},{12,4},{16,24},{20,28},{24,16},{28,20},{1,9},{5... | collective-permute-start | bytes 1007624 | tf_op jit(solution)/shard_map/ppermute | solution.py:483
  342.9 29.2 %collective-permute-start.37 = (bf16[1824,128]{1,0:T(8,128)(2,1)S(1)}, bf16[1824,128]{1,0:T(8,128)(2,1)S(1)}, u32[]{:S(2)}, u32[]{:S(2)}) collective-permute-start(bf16[1824,128]{1,0:T(8,128)(2,1)S(1)} %pad_maximum_fusion.7), channel_id=1, source_target_pairs={{0,16},{4,20},{8,24},{12,28},{16,0},{20,4},{24,8},{28,12},{1,17},{... | collective-permute-start | bytes 1400840 | tf_op jit(solution)/shard_map/ppermute | solution.py:483
  347.7 22.2 %collective-permute-start.33 = (bf16[768,256]{1,0:T(8,128)(2,1)S(1)}, bf16[768,256]{1,0:T(8,128)(2,1)S(1)}, u32[]{:S(2)}, u32[]{:S(2)}) collective-permute-start(bf16[768,256]{1,0:T(8,128)(2,1)S(1)} %slice.747), channel_id=1, source_target_pairs={{0,8},{4,12},{8,0},{12,4},{16,24},{20,28},{24,16},{28,20},{1,9},{5... | collective-permute-start | bytes 1179656 | tf_op jit(solution)/shard_map/ppermute | solution.py:483
  354.4 32.6 %collective-permute-start.41 = (bf16[1312,64]{1,0:T(8,128)(2,1)S(1)}, bf16[1312,64]{1,0:T(8,128)(2,1)S(1)}, u32[]{:S(2)}, u32[]{:S(2)}) collective-permute-start(bf16[1312,64]{1,0:T(8,128)(2,1)S(1)} %slice.749), channel_id=1, source_target_pairs={{0,16},{4,20},{8,24},{12,28},{16,0},{20,4},{24,8},{28,12},{1,17},{... | collective-permute-start | bytes 503816 | tf_op jit(solution)/shard_map/ppermute | solution.py:483
  370.1 18.6 %collective-permute-start.34 = (bf16[768,128]{1,0:T(8,128)(2,1)S(1)}, bf16[768,128]{1,0:T(8,128)(2,1)S(1)}, u32[]{:S(2)}, u32[]{:S(2)}) collective-permute-start(bf16[768,128]{1,0:T(8,128)(2,1)S(1)} %slice.755), channel_id=1, source_target_pairs={{0,16},{4,20},{8,24},{12,28},{16,0},{20,4},{24,8},{28,12},{1,17},{... | collective-permute-start | bytes 589832 | tf_op jit(solution)/shard_map/ppermute | solution.py:483
  376.7 15.7 %collective-permute-start.43 = (bf16[1824,64]{1,0:T(8,128)(2,1)}, bf16[1824,64]{1,0:T(8,128)(2,1)}, u32[]{:S(2)}, u32[]{:S(2)}) collective-permute-start(bf16[1824,64]{1,0:T(8,128)(2,1)} %pad_maximum_fusion.8), channel_id=1, source_target_pairs={{0,2},{2,0},{1,3},{3,1},{4,6},{6,4},{5,7},{7,5},{8,10},{10,8},{9,1... | collective-permute-start | bytes 700424 | tf_op jit(solution)/shard_map/ppermute | solution.py:388
  (79 other events, 712.7 us)

commit v3 on v2

--- a/solution.py
+++ b/solution.py
@@ -503,8 +503,7 @@
     mean_one = jnp.mean(x, axis=-1, keepdims=True)
     h1 = (center * inverse_one * gain_one).astype(bf16)
     if two:
-        h1_y = relative(h1, "yzZw")
-        h1, h1_y, wq_mine, wq_got = lax.optimization_barrier((h1, h1_y, wq_mine, wq_got))
+        h1, wq_mine, wq_got = lax.optimization_barrier((h1, wq_mine, wq_got))
         wq = jnp.concatenate([wq_mine, wq_got], axis=0)
     wq = nn(wq, order).astype(bf16)
 
@@ -531,11 +530,15 @@
         in_got, wo_got = to_row(jnp.where(even, act_low, lin_low)), to_row(wo_low)
         g_got = to_row(take(take(cotangent, 1 - r, Sr), c, Sr // 2))
         wd_half = take(wd_low, (b // 2) % 2, F // 2)
+        h1_y = relative(after(h1, kv), "yzZw")
+        q, h1_y, sk_left, sk_right, act_low, lin_low, wd_half = lax.optimization_barrier(
+            (q, h1_y, sk_left, sk_right, act_low, lin_low, wd_half)
+        )
 
     state = attend_call(own_bounds, q, sq, [kv], [sk_own], heads)
     if two:
-        kv_left, kv_right, sk_left, sk_right, in_got, wo_got, g_got, wd_half = after(
-            (kv_left, kv_right, sk_left, sk_right, in_got, wo_got, g_got, wd_half), state
+        kv_left, kv_right, in_got, wo_got, g_got, wd_half = after(
+            (kv_left, kv_right, in_got, wo_got, g_got, wd_half), state
         )
         in_other, wd_got = to_z(in_got, 1), to_row(wd_half)
     o, lse = attend_call(
@@ -648,8 +651,9 @@
     from_left = lax.ppermute(dkv_right, "dp", up)
     if two:
         lower = joined(lower, after(lower_got, dq_part))
-        lower_got = to_z(second(lower), 2)
-        dq_part, lower = lax.optimization_barrier((dq_part, lower))
+        proj = halved(o_heads, dx_y, after(proj_got, dq_part))
+        lower_got, proj_got = to_z(second(lower), 2), to_z(second(proj), 1)
+        dq_part, lower, proj = lax.optimization_barrier((dq_part, lower, proj))
     dq, dkv = attend_back_call(own_bounds, q, do, o, lse, sq, [kv], [sk_own], heads, [dq_part])
     if two:
         dkv, from_right, from_left, gate_got, proj_got, lower_got = lax.optimization_barrier(
@@ -700,21 +704,20 @@
         n = F
         act = halved(da, h_act, gate_got[:n])
         lin = halved(du, h_lin, gate_got[n:])
-        proj = halved(o_heads, dx_y, proj_got)
-        both_got = after(to_z(jnp.concatenate([second(act), second(proj)], axis=0), 1), kept)
+        act_got = after(to_z(second(act), 1), kept)
         lin = joined(lin, after(to_y(second(lin)), kept))
-        act, proj = joined(act, both_got[:n]), joined(proj, both_got[n:])
+        act, proj = joined(act, act_got), joined(proj, proj_got)
         both_got = to_z(jnp.concatenate([second(act), second(proj)], axis=0), 2)
         lin = joined(lin, to_z(second(lin), 1))
         act, proj = joined(act, both_got[:n]), joined(proj, both_got[n:])
         lower = joined(lower, lower_got)
-        last_got = after(to_row(jnp.concatenate([second(lower), second(proj)], axis=0)), dx)
+        query = joined(query, after(to_z(second(query), 1), dx))
+        last_got = after(to_row(jnp.concatenate([second(lower), second(proj)], axis=0)), query)
         lower, proj = joined(lower, last_got[:n]), joined(proj, last_got[n:])
-        act = joined(act, to_y(second(act)))
-        lin = joined(lin, after(to_z(second(lin), 2), dx))
+        act = joined(act, after(to_y(second(act)), query))
+        lin = joined(lin, after(to_z(second(lin), 2), query))
         gate = jnp.stack([act.T, lin.T])
-        query = joined(query, to_z(second(query), 1))
-        query = joined(query, after(to_z(second(query), 2), dx)).T
+        query = joined(query, to_z(second(query), 2)).T
         wq_rows = take(wq, b ^ (4 * r), Db)
         place = (2 * b + r) ^ (8 * r)
         wi_rows = jnp.stack(

time: 416 us -> 428 us (1.029)
  Pallas kernels: 67.9 us -> 82 us
  other arithmetic: 73.7 us -> 68.5 us
    ppermute x14, waiting for transfers between devices: 4.14 us -> 27.8 us  [to_row(): return lax.ppermute(a, 'row', SWAP)]
    ppermute x10 -> x11, starting transfers between devices: 31.6 us -> 16 us  [to_z(): return lax.ppermute(a, 'dp', [(i, i ^ 2 * j) for i in range(B)])]
    ppermute x5, waiting for transfers between devices: 31.1 us -> 15.9 us  [to_y(): return lax.ppermute(a, 'dp', [(i, i ^ 1) for i in range(B)])]
    ppermute x10, starting transfers between devices: 10.2 us -> 24.5 us  [to_col(): return lax.ppermute(a, 'col', SWAP)]
    pallas_call x2, Pallas kernels: 38.4 us -> 46.2 us  [attend_back_call(): pl.pallas_call(functools.partial(backward_kernel, heads, sets, final), gr...]
    ppermute x1, waiting for transfers between devices: 15.4 us -> 8.73 us  [local(): kv_left = lax.ppermute(kv[S - H:], 'dp', up)]
    pallas_call x2, Pallas kernels: 29.4 us -> 35.8 us  [attend_call(): pl.pallas_call(functools.partial(forward_kernel, heads, sets, final), gri...]
    ppermute x10 -> x11, waiting for transfers between devices: 28.8 us -> 22.6 us  [to_z(): return lax.ppermute(a, 'dp', [(i, i ^ 2 * j) for i in range(B)])]
  transfers between devices with their start and end apart: 44 -> 45, of which waited for: 13 -> 16; matrix products, arithmetic and copies ran while one was open for 37% -> 35% of each run, Pallas kernels for 17% -> 20%
where the time goes in v3:
time: 428 us; the launch traced here: 420 us
  Pallas kernels  82 us (19%)
  waiting for transfers between devices  81.7 us (19%)
  starting transfers between devices  74.2 us (17%)
  other arithmetic  68.5 us (16%)
  matrix products  68.4 us (16%)
  local copies, waits for them, and re-layouts  42.3 us (10%)
    pallas_call x2, Pallas kernels, attend_back_call(): pl.pallas_call(functools.partial(backward_kernel, heads, sets, final), gr...  46.2 us
    pallas_call x2, Pallas kernels, attend_call(): pl.pallas_call(functools.partial(forward_kernel, heads, sets, final), gri...  35.8 us
    dot_general x15, matrix products, nn(): return jnp.dot(a, b, preferred_element_type=f32)  31.2 us
    ppermute x14, waiting for transfers between devices, to_row(): return lax.ppermute(a, 'row', SWAP)  27.8 us
    ppermute x10, starting transfers between devices, to_col(): return lax.ppermute(a, 'col', SWAP)  24.5 us
    ppermute x11, waiting for transfers between devices, to_z(): return lax.ppermute(a, 'dp', [(i, i ^ 2 * j) for i in range(B)])  22.6 us
    dot_general x8, matrix products, nt(): lax.dot_general(a, b, (((1,), (1,)), ((), ())), preferred_element_type=f32)  17.9 us
    dot_general x10, matrix products, tn(): lax.dot_general(a, b, (((0,), (0,)), ((), ())), preferred_element_type=f32)  16.9 us
  transfers between devices with their start and end apart: 45, of which 16 were waited for; matrix products, arithmetic and copies ran while one was open for 35% of the time, Pallas kernels for 20%

profile of v3, /device:TPU:3, one launch (start us, length us, event | category | flops | bytes accessed | tf_op | source)
XLA Modules:
  0.0 419.8 jit_solution(8555133280645009186)
XLA Ops:
  12.2 2.9 convert.78
  22.1 3.5 multiply_sine_fusion
  28.9 3.0 convert_element_type.229
  34.7 6.6 %collective-permute-done = bf16[768,512]{1,0:T(8,128)(2,1)} collective-permute-done((bf16[768,512]{1,0:T(8,128)(2,1)}, bf16[768,512]{1,0:T(8,128)(2,1)}, u32[]{:S(2)}, u32[]{:S(2)}) %collective-permute-start) | collective-permute-done | bytes 786464 | tf_op jit(solution)/shard_map/ppermute | solution.py:388
  44.0 3.6 slice_bitcast_fusion
  53.7 4.5 %collective-permute-done.2 = bf16[512,768]{0,1:T(8,128)(2,1)} collective-permute-done((bf16[512,768]{0,1:T(8,128)(2,1)}, bf16[512,768]{0,1:T(8,128)(2,1)}, u32[]{:S(2)}, u32[]{:S(2)}) %collective-permute-start.2) | collective-permute-done | bytes 786464 | tf_op jit(solution)/shard_map/ppermute | solution.py:388
  67.6 5.0 %collective-permute-start.3 = (bf16[1024,512]{1,0:T(8,128)(2,1)}, bf16[1024,512]{1,0:T(8,128)(2,1)}, u32[]{:S(2)}, u32[]{:S(2)}) collective-permute-start(bf16[1024,512]{1,0:T(8,128)(2,1)} %get-tuple-element.215), channel_id=1, source_target_pairs={{0,4},{4,8},{8,12},{12,16},{16,20},{20,24},{24,28},{1,5},{5,9},{9,... | collective-permute-start | bytes 3145736 | tf_op jit(solution)/shard_map/ppermute | solution.py:523
  72.6 5.0 %fusion.16 = bf16[1536,1024]{1,0:T(8,128)(2,1)} fusion(bf16[1536,1024]{1,0:T(8,128)(2,1)S(1)} %fusion.4, s32[1024]{0:T(1024)S(1)} %add_xor_fusion.3), kind=kOutput, calls=%fused_computation.29 | convolution fusion | flops 3223846912 | bytes 6295552 | tf_op jit(solution)/shard_map/dot_general | solution.py:32
  81.8 25.4 %attend_own.1 = (f32[6,256,256]{2,1,0:T(8,128)}, f32[6,2,1024]{2,1,0:T(2,128)}) custom-call(s32[12]{0:T(128)} %reshape.742.bounds, bf16[1536,256]{1,0:T(8,128)(2,1)} %fusion.49.refs_0_, s32[6,1,256]{2,1,0:T(1,128)} %select_n.692.refs_1_.refs_4_, bf16[1536,512]{1,0:T(8,128)(2,1)} %copy-done.4, s32[1536,128]{1,0:T(8,128)} %broadcast_in_dim.134.refs_3_.refs_6_), custom_call_target="tpu_custom_call" | custom-call | flops 6291456 | bytes 3145728 | tf_op jit(solution)/shard_map/attend_own/pallas_call | solution.py:194
  107.3 8.7 %collective-permute-done.3.refs_2_.refs_5_ = bf16[1024,512]{1,0:T(8,128)(2,1)} collective-permute-done((bf16[1024,512]{1,0:T(8,128)(2,1)}, bf16[1024,512]{1,0:T(8,128)(2,1)}, u32[]{:S(2)}, u32[]{:S(2)}) %collective-permute-start.3) | collective-permute-done | bytes 1048608 | tf_op jit(solution)/shard_map/ppermute | solution.py:523
  119.3 10.4 %attend_final.1 = (bf16[1536,256]{1,0:T(8,128)(2,1)}, f32[6,1,1024]{2,1,0:T(1,128)}) custom-call(s32[24]{0:T(128)} %reshape.741.bounds, bf16[1536,256]{1,0:T(8,128)(2,1)} %fusion.49.refs_0_, s32[6,1,256]{2,1,0:T(1,128)} %select_n.692.refs_1_.refs_4_, bf16[1024,512]{1,0:T(8,128)(2,1)} %collective-permute-done.3.refs_2_.refs_5_, bf16[1024,512]{1,0:T(8,128)(2,1)} %copy-done.18, ...), custom_call_target="tpu_custom_call" | custom-call | flops 6291456 | bytes 3670016 | tf_op jit(solution)/shard_map/attend_final/pallas_call | solution.py:194
  129.6 2.8 collective-permute-done.8
  160.1 2.8 collective-permute-done.13
  162.9 7.3 %multiply_convert_fusion = (bf16[768,1312]{0,1:T(8,128)(2,1)}, bf16[768,1312]{0,1:T(8,128)(2,1)}, bf16[768,1312]{0,1:T(8,128)(2,1)}) fusion(f32[768,1312]{0,1:T(8,128)S(1)} %convolution_add_fusion.1, f32[768,1312]{0,1:T(8,128)S(1)} %convolution_add_fusion, f32[768,1312]{0,1:T(8,128)S(1)} %fusion.80, bf16[656,512]{1,0:T(8,128)(2,1)} %collective-permute-done.13, ...), kind=kOutput, calls=%fused_computation.26 | convolution fusion | flops 1054973952 | bytes 20267008 | tf_op jit(solution)/shard_map/dot_general | solution.py:24
  170.3 3.1 fusion.164
  173.4 3.2 fusion.99
  196.5 2.9 fusion.155
  218.2 2.9 collective-permute-done.17
  230.3 12.7 %back_halo.1 = (f32[6,256,256]{2,1,0:T(8,128)}, bf16[1024,512]{1,0:T(8,128)(2,1)}, bf16[1024,512]{1,0:T(8,128)(2,1)}) custom-call(s32[24]{0:T(128)} %reshape.741.bounds, bf16[1536,256]{1,0:T(8,128)(2,1)} %fusion.49.refs_0_, bf16[1536,256]{1,0:T(8,128)(2,1)} %maximum_select_fusion.7.refs_1_, bf16[1536,256]{1,0:T(8,128)(2,1)} %get-tuple-element.101.refs_2_, ...), custom_call_target="tpu_custom_call" | custom-call | flops 15728640 | bytes 3670016 | tf_op jit(solution)/shard_map/back_halo/pallas_call | solution.py:320
  249.0 3.9 collective-permute-start.26
  256.1 5.0 %collective-permute-start.24 = (bf16[1024,512]{1,0:T(8,128)(2,1)}, bf16[1024,512]{1,0:T(8,128)(2,1)}, u32[]{:S(2)}, u32[]{:S(2)}) collective-permute-start(bf16[1024,512]{1,0:T(8,128)(2,1)} %get-tuple-element.127), channel_id=1, source_target_pairs={{0,4},{4,8},{8,12},{12,16},{16,20},{20,24},{24,28},{1,5},{5,9},{9,... | collective-permute-start | bytes 3145736 | tf_op jit(solution)/shard_map/ppermute | solution.py:651
  261.1 33.5 %back_own.1 = (f32[1536,256]{1,0:T(8,128)}, f32[1536,512]{1,0:T(8,128)}) custom-call(s32[12]{0:T(128)} %reshape.742.bounds, bf16[1536,256]{1,0:T(8,128)(2,1)} %fusion.49.refs_0_, bf16[1536,256]{1,0:T(8,128)(2,1)} %maximum_select_fusion.7.refs_1_, bf16[1536,256]{1,0:T(8,128)(2,1)} %get-tuple-element.101.refs_2_, f32[6,1,1024]{2,1,0:T(1,128)} %get-tuple-element.116.refs_3_, ...), custom_call_target="tpu_custom_call" | custom-call | flops 15728640 | bytes 3145728 | tf_op jit(solution)/shard_map/back_own/pallas_call | solution.py:320
  297.0 6.6 %collective-permute-done.24 = bf16[1024,512]{1,0:T(8,128)(2,1)} collective-permute-done((bf16[1024,512]{1,0:T(8,128)(2,1)}, bf16[1024,512]{1,0:T(8,128)(2,1)}, u32[]{:S(2)}, u32[]{:S(2)}) %collective-permute-start.24) | collective-permute-done | bytes 1048608 | tf_op jit(solution)/shard_map/ppermute | solution.py:651
  314.5 3.2 collective-permute-start.29
  332.0 12.9 %collective-permute-done.40 = bf16[1312,256]{1,0:T(8,128)(2,1)S(1)} collective-permute-done((bf16[1312,256]{1,0:T(8,128)(2,1)}, bf16[1312,256]{1,0:T(8,128)(2,1)S(1)}, u32[]{:S(2)}, u32[]{:S(2)}) %collective-permute-start.40) | collective-permute-done | bytes 671776 | tf_op jit(solution)/shard_map/ppermute | solution.py:480
  356.6 14.0 %collective-permute-done.38 = bf16[1824,128]{1,0:T(8,128)(2,1)S(1)} collective-permute-done((bf16[1824,128]{1,0:T(8,128)(2,1)S(1)}, bf16[1824,128]{1,0:T(8,128)(2,1)S(1)}, u32[]{:S(2)}, u32[]{:S(2)}) %collective-permute-start.38) | collective-permute-done | bytes 466976 | tf_op jit(solution)/shard_map/ppermute | solution.py:483
  370.9 2.8 collective-permute-start.39
  375.9 5.7 %collective-permute-done.44 = bf16[1824,64]{1,0:T(8,128)(2,1)S(1)} collective-permute-done((bf16[1824,64]{1,0:T(8,128)(2,1)S(1)}, bf16[1824,64]{1,0:T(8,128)(2,1)S(1)}, u32[]{:S(2)}, u32[]{:S(2)}) %collective-permute-start.44) | collective-permute-done | bytes 233504 | tf_op jit(solution)/shard_map/ppermute | solution.py:388
  384.5 10.4 %collective-permute-start.32 = (bf16[768,512]{1,0:T(8,128)(2,1)S(1)}, bf16[768,512]{1,0:T(8,128)(2,1)}, u32[]{:S(2)}, u32[]{:S(2)}) collective-permute-start(bf16[768,512]{1,0:T(8,128)(2,1)S(1)} %fusion.43), channel_id=1, source_target_pairs={{0,1},{1,0},{2,3},{3,2},{4,5},{5,4},{6,7},{7,6},{8,9},{9,8},{10,11... | collective-permute-start | bytes 2359304 | tf_op jit(solution)/shard_map/ppermute | solution.py:391
  400.9 3.6 collective-permute-done.35
  409.4 3.1 maximum_select_fusion.4
  412.5 2.8 collective-permute-done.36
  (381 shorter events, 193.3 us)
Async XLA Ops:
  2.9 104.3 %collective-permute-start.7 = (bf16[384,512]{1,0:T(8,128)(2,1)}, bf16[384,512]{1,0:T(8,128)(2,1)S(1)}, u32[]{:S(2)}, u32[]{:S(2)}) collective-permute-start(bf16[384,512]{1,0:T(8,128)(2,1)} %constant_dynamic-slice_fusion.2), channel_id=1, source_target_pairs={{0,2},{2,0},{1,3},{3,1},{4,6},{6,4},{5,7},{7,5},{8,10},{10,8},{9,1... | collective-permute-start | bytes 1179656 | tf_op jit(solution)/shard_map/ppermute | solution.py:388
  5.0 102.3 %collective-permute-start.6 = (bf16[512,512]{1,0:T(8,128)(2,1)}, bf16[512,512]{1,0:T(8,128)(2,1)}, u32[]{:S(2)}, u32[]{:S(2)}) collective-permute-start(bf16[512,512]{1,0:T(8,128)(2,1)} %convert_element_type.230), channel_id=1, source_target_pairs={{0,2},{2,0},{1,3},{3,1},{4,6},{6,4},{5,7},{7,5},{8,10},{10,8},{9,1... | collective-permute-start | bytes 1572872 | tf_op jit(solution)/shard_map/ppermute | solution.py:388
  7.4 33.9 %collective-permute-start = (bf16[768,512]{1,0:T(8,128)(2,1)}, bf16[768,512]{1,0:T(8,128)(2,1)}, u32[]{:S(2)}, u32[]{:S(2)}) collective-permute-start(bf16[768,512]{1,0:T(8,128)(2,1)} %constant_dynamic-slice_fusion.6), channel_id=1, source_target_pairs={{0,2},{2,0},{1,3},{3,1},{4,6},{6,4},{5,7},{7,5},{8,10},{10,8},{9,1... | collective-permute-start | bytes 2359304 | tf_op jit(solution)/shard_map/ppermute | solution.py:388
  10.8 47.4 %collective-permute-start.2 = (bf16[512,768]{0,1:T(8,128)(2,1)}, bf16[512,768]{0,1:T(8,128)(2,1)}, u32[]{:S(2)}, u32[]{:S(2)}) collective-permute-start(bf16[512,768]{0,1:T(8,128)(2,1)} %get-tuple-element.218), channel_id=1, source_target_pairs={{0,2},{2,0},{1,3},{3,1},{4,6},{6,4},{5,7},{7,5},{8,10},{10,8},{9,1... | collective-permute-start | bytes 2359304 | tf_op jit(solution)/shard_map/ppermute | solution.py:388
  17.9 89.3 %collective-permute-start.5 = (bf16[512,1312]{0,1:T(8,128)(2,1)}, bf16[512,1312]{0,1:T(8,128)(2,1)}, u32[]{:S(2)}, u32[]{:S(2)}) collective-permute-start(bf16[512,1312]{0,1:T(8,128)(2,1)} %broadcast_select_fusion.2), channel_id=1, source_target_pairs={{0,2},{2,0},{1,3},{3,1},{4,6},{6,4},{5,7},{7,5},{8,10},{10,8},{9,1... | collective-permute-start | bytes 4030472 | tf_op jit(solution)/shard_map/ppermute | solution.py:388
  66.3 40.9 %collective-permute-start.4 = (bf16[1024,512]{1,0:T(8,128)(2,1)}, bf16[1024,512]{1,0:T(8,128)(2,1)S(1)}, u32[]{:S(2)}, u32[]{:S(2)}) collective-permute-start(bf16[1024,512]{1,0:T(8,128)(2,1)} %get-tuple-element.214), channel_id=1, source_target_pairs={{4,0},{8,4},{12,8},{16,12},{20,16},{24,20},{28,24},{5,1},{9,5},{13... | collective-permute-start | bytes 3145736 | tf_op jit(solution)/shard_map/ppermute | solution.py:524
  67.6 48.4 %collective-permute-start.3 = (bf16[1024,512]{1,0:T(8,128)(2,1)}, bf16[1024,512]{1,0:T(8,128)(2,1)}, u32[]{:S(2)}, u32[]{:S(2)}) collective-permute-start(bf16[1024,512]{1,0:T(8,128)(2,1)} %get-tuple-element.215), channel_id=1, source_target_pairs={{0,4},{4,8},{8,12},{12,16},{16,20},{20,24},{24,28},{1,5},{5,9},{9,... | collective-permute-start | bytes 3145736 | tf_op jit(solution)/shard_map/ppermute | solution.py:523
  116.0 16.5 %collective-permute-start.8 = (bf16[656,512]{1,0:T(8,128)(2,1)}, bf16[656,512]{1,0:T(8,128)(2,1)}, u32[]{:S(2)}, u32[]{:S(2)}) collective-permute-start(bf16[656,512]{1,0:T(8,128)(2,1)} %constant_dynamic-slice_fusion.3), channel_id=1, source_target_pairs={{0,2},{2,0},{1,3},{3,1},{4,6},{6,4},{5,7},{7,5},{8,10},{10,8},{9,1... | collective-permute-start | bytes 2015240 | tf_op jit(solution)/shard_map/ppermute | solution.py:388
  117.9 30.6 %collective-permute-start.14 = (bf16[512,1312]{0,1:T(8,128)(2,1)}, bf16[512,1312]{0,1:T(8,128)(2,1)}, u32[]{:S(2)}, u32[]{:S(2)}) collective-permute-start(bf16[512,1312]{0,1:T(8,128)(2,1)} %collective-permute-done.5), channel_id=1, source_target_pairs={{0,8},{4,12},{8,0},{12,4},{16,24},{20,28},{24,16},{28,20},{1,9},{5... | collective-permute-start | bytes 4030472 | tf_op jit(solution)/shard_map/ppermute | solution.py:483
  134.3 12.1 %collective-permute-start.9 = (bf16[384,512]{1,0:T(8,128)(2,1)S(1)}, bf16[384,512]{1,0:T(8,128)(2,1)S(1)}, u32[]{:S(2)}, u32[]{:S(2)}) collective-permute-start(bf16[384,512]{1,0:T(8,128)(2,1)S(1)} %copy-done.37), channel_id=1, source_target_pairs={{0,1},{1,0},{2,3},{3,2},{4,5},{5,4},{6,7},{7,6},{8,9},{9,8},{10,11... | collective-permute-start | bytes 1179656 | tf_op jit(solution)/shard_map/ppermute | solution.py:391
  135.9 27.0 %collective-permute-start.13 = (bf16[656,512]{1,0:T(8,128)(2,1)}, bf16[656,512]{1,0:T(8,128)(2,1)}, u32[]{:S(2)}, u32[]{:S(2)}) collective-permute-start(bf16[656,512]{1,0:T(8,128)(2,1)} %collective-permute-done.8), channel_id=1, source_target_pairs={{0,8},{4,12},{8,0},{12,4},{16,24},{20,28},{24,16},{28,20},{1,9},{5... | collective-permute-start | bytes 2015240 | tf_op jit(solution)/shard_map/ppermute | solution.py:483
  176.7 15.7 %collective-permute-start.18 = (bf16[384,1024]{1,0:T(8,128)(2,1)S(1)}, bf16[384,1024]{1,0:T(8,128)(2,1)S(1)}, u32[]{:S(2)}, u32[]{:S(2)}) collective-permute-start(bf16[384,1024]{1,0:T(8,128)(2,1)S(1)} %fusion.35), channel_id=1, source_target_pairs={{0,1},{1,0},{2,3},{3,2},{4,5},{5,4},{6,7},{7,6},{8,9},{9,8},{10,11... | collective-permute-start | bytes 2359304 | tf_op jit(solution)/shard_map/ppermute | solution.py:391
  189.0 32.1 %collective-permute-start.17 = (bf16[1312,512]{1,0:T(8,128)(2,1)S(1)}, bf16[1312,512]{1,0:T(8,128)(2,1)S(1)}, u32[]{:S(2)}, u32[]{:S(2)}) collective-permute-start(bf16[1312,512]{1,0:T(8,128)(2,1)S(1)} %convolution_convert_fusion.2), channel_id=1, source_target_pairs={{0,4},{4,0},{8,12},{12,8},{16,20},{20,16},{24,28},{28,24},{1,5},{5... | collective-permute-start | bytes 4030472 | tf_op jit(solution)/shard_map/ppermute | solution.py:480
  204.2 21.5 %collective-permute-start.16 = (bf16[768,256]{1,0:T(8,128)(2,1)S(1)}, bf16[768,256]{1,0:T(8,128)(2,1)S(1)}, u32[]{:S(2)}, u32[]{:S(2)}) collective-permute-start(bf16[768,256]{1,0:T(8,128)(2,1)S(1)} %get-tuple-element.230), channel_id=1, source_target_pairs={{0,2},{2,0},{1,3},{3,1},{4,6},{6,4},{5,7},{7,5},{8,10},{10,8},{9,1... | collective-permute-start | bytes 1179656 | tf_op jit(solution)/shard_map/ppermute | solution.py:388
  205.5 23.3 %collective-permute-start.20 = (bf16[2,384,512]{2,1,0:T(8,128)(2,1)S(1)}, bf16[2,384,512]{2,1,0:T(8,128)(2,1)S(1)}, u32[]{:S(2)}, u32[]{:S(2)}) collective-permute-start(bf16[2,384,512]{2,1,0:T(8,128)(2,1)S(1)} %maximum_select_fusion.10), channel_id=1, source_target_pairs={{0,1},{1,0},{2,3},{3,2},{4,5},{5,4},{6,7},{7,6},{8,9},{9,8},{10,11... | collective-permute-start | bytes 2359304 | tf_op jit(solution)/shard_map/ppermute | solution.py:391
  210.3 32.7 %collective-permute-start.22 = (bf16[512,512]{1,0:T(8,128)(2,1)}, bf16[512,512]{1,0:T(8,128)(2,1)}, u32[]{:S(2)}, u32[]{:S(2)}) collective-permute-start(bf16[512,512]{1,0:T(8,128)(2,1)} %convolution_convert_fusion.4), channel_id=1, source_target_pairs={{0,4},{4,0},{8,12},{12,8},{16,20},{20,16},{24,28},{28,24},{1,5},{5... | collective-permute-start | bytes 1572872 | tf_op jit(solution)/shard_map/ppermute | solution.py:480
  222.6 23.1 %collective-permute-start.21 = (bf16[1312,256]{1,0:T(8,128)(2,1)}, bf16[1312,256]{1,0:T(8,128)(2,1)}, u32[]{:S(2)}, u32[]{:S(2)}) collective-permute-start(bf16[1312,256]{1,0:T(8,128)(2,1)} %slice.729), channel_id=1, source_target_pairs={{0,8},{4,12},{8,0},{12,4},{16,24},{20,28},{24,16},{28,20},{1,9},{5... | collective-permute-start | bytes 2015240 | tf_op jit(solution)/shard_map/ppermute | solution.py:483
  225.7 77.9 %collective-permute-start.25 = (bf16[2624,512]{1,0:T(8,128)(2,1)}, bf16[2624,512]{1,0:T(8,128)(2,1)}, u32[]{:S(2)}, u32[]{:S(2)}) collective-permute-start(bf16[2624,512]{1,0:T(8,128)(2,1)} %pad_maximum_fusion.1), channel_id=1, source_target_pairs={{0,2},{2,0},{1,3},{3,1},{4,6},{6,4},{5,7},{7,5},{8,10},{10,8},{9,1... | collective-permute-start | bytes 8060936 | tf_op jit(solution)/shard_map/ppermute | solution.py:388
  249.0 48.0 %collective-permute-start.26 = (bf16[512,256]{1,0:T(8,128)(2,1)}, bf16[512,256]{1,0:T(8,128)(2,1)}, u32[]{:S(2)}, u32[]{:S(2)}) collective-permute-start(bf16[512,256]{1,0:T(8,128)(2,1)} %slice.737), channel_id=1, source_target_pairs={{0,8},{4,12},{8,0},{12,4},{16,24},{20,28},{24,16},{28,20},{1,9},{5... | collective-permute-start | bytes 786440 | tf_op jit(solution)/shard_map/ppermute | solution.py:483
  252.8 44.1 %collective-permute-start.27 = (bf16[1312,128]{1,0:T(8,128)(2,1)}, bf16[1312,128]{1,0:T(8,128)(2,1)S(1)}, u32[]{:S(2)}, u32[]{:S(2)}) collective-permute-start(bf16[1312,128]{1,0:T(8,128)(2,1)} %slice.736), channel_id=1, source_target_pairs={{0,16},{4,20},{8,24},{12,28},{16,0},{20,4},{24,8},{28,12},{1,17},{... | collective-permute-start | bytes 1007624 | tf_op jit(solution)/shard_map/ppermute | solution.py:483
  254.8 42.1 %collective-permute-start.23 = (bf16[1024,512]{1,0:T(8,128)(2,1)}, bf16[1024,512]{1,0:T(8,128)(2,1)}, u32[]{:S(2)}, u32[]{:S(2)}) collective-permute-start(bf16[1024,512]{1,0:T(8,128)(2,1)} %get-tuple-element.126), channel_id=1, source_target_pairs={{4,0},{8,4},{12,8},{16,12},{20,16},{24,20},{28,24},{5,1},{9,5},{13... | collective-permute-start | bytes 3145736 | tf_op jit(solution)/shard_map/ppermute | solution.py:650
  256.1 47.5 %collective-permute-start.24 = (bf16[1024,512]{1,0:T(8,128)(2,1)}, bf16[1024,512]{1,0:T(8,128)(2,1)}, u32[]{:S(2)}, u32[]{:S(2)}) collective-permute-start(bf16[1024,512]{1,0:T(8,128)(2,1)} %get-tuple-element.127), channel_id=1, source_target_pairs={{0,4},{4,8},{8,12},{12,16},{16,20},{20,24},{24,28},{1,5},{5,9},{9,... | collective-permute-start | bytes 3145736 | tf_op jit(solution)/shard_map/ppermute | solution.py:651
  312.3 33.1 %collective-permute-start.33 = (bf16[768,512]{1,0:T(8,128)(2,1)}, bf16[768,512]{1,0:T(8,128)(2,1)}, u32[]{:S(2)}, u32[]{:S(2)}) collective-permute-start(bf16[768,512]{1,0:T(8,128)(2,1)} %fusion.59), channel_id=1, source_target_pairs={{0,4},{4,0},{8,12},{12,8},{16,20},{20,16},{24,28},{28,24},{1,5},{5... | collective-permute-start | bytes 2359304 | tf_op jit(solution)/shard_map/ppermute | solution.py:480
  314.5 36.5 %collective-permute-start.29 = (bf16[768,512]{1,0:T(8,128)(2,1)}, bf16[768,512]{1,0:T(8,128)(2,1)}, u32[]{:S(2)}, u32[]{:S(2)}) collective-permute-start(bf16[768,512]{1,0:T(8,128)(2,1)} %slice.514), channel_id=1, source_target_pairs={{0,2},{3,1},{4,6},{7,5},{8,10},{11,9},{12,14},{15,13},{16,18},{19,... | collective-permute-start | bytes 2359304 | tf_op jit(solution)/shard_map/ppermute | solution.py:684
  327.6 17.3 %collective-permute-start.40 = (bf16[1312,256]{1,0:T(8,128)(2,1)}, bf16[1312,256]{1,0:T(8,128)(2,1)S(1)}, u32[]{:S(2)}, u32[]{:S(2)}) collective-permute-start(bf16[1312,256]{1,0:T(8,128)(2,1)} %slice.727), channel_id=1, source_target_pairs={{0,4},{4,0},{8,12},{12,8},{16,20},{20,16},{24,28},{28,24},{1,5},{5... | collective-permute-start | bytes 2015240 | tf_op jit(solution)/shard_map/ppermute | solution.py:480
  327.6 17.5 %collective-permute-start.37 = (bf16[1312,256]{1,0:T(8,128)(2,1)S(1)}, bf16[1312,256]{1,0:T(8,128)(2,1)S(1)}, u32[]{:S(2)}, u32[]{:S(2)}) collective-permute-start(bf16[1312,256]{1,0:T(8,128)(2,1)S(1)} %slice.728), channel_id=1, source_target_pairs={{0,8},{4,12},{8,0},{12,4},{16,24},{20,28},{24,16},{28,20},{1,9},{5... | collective-permute-start | bytes 2015240 | tf_op jit(solution)/shard_map/ppermute | solution.py:483
  349.1 26.6 %collective-permute-start.34 = (bf16[768,256]{1,0:T(8,128)(2,1)S(1)}, bf16[768,256]{1,0:T(8,128)(2,1)S(1)}, u32[]{:S(2)}, u32[]{:S(2)}) collective-permute-start(bf16[768,256]{1,0:T(8,128)(2,1)S(1)} %slice.730), channel_id=1, source_target_pairs={{0,8},{4,12},{8,0},{12,4},{16,24},{20,28},{24,16},{28,20},{1,9},{5... | collective-permute-start | bytes 1179656 | tf_op jit(solution)/shard_map/ppermute | solution.py:483
  349.4 21.2 %collective-permute-start.38 = (bf16[1824,128]{1,0:T(8,128)(2,1)S(1)}, bf16[1824,128]{1,0:T(8,128)(2,1)S(1)}, u32[]{:S(2)}, u32[]{:S(2)}) collective-permute-start(bf16[1824,128]{1,0:T(8,128)(2,1)S(1)} %pad_maximum_fusion.6), channel_id=1, source_target_pairs={{0,16},{4,20},{8,24},{12,28},{16,0},{20,4},{24,8},{28,12},{1,17},{... | collective-permute-start | bytes 1400840 | tf_op jit(solution)/shard_map/ppermute | solution.py:483
  351.1 22.9 %collective-permute-start.30 = (bf16[768,512]{1,0:T(8,128)(2,1)S(1)}, bf16[768,512]{1,0:T(8,128)(2,1)S(1)}, u32[]{:S(2)}, u32[]{:S(2)}) collective-permute-start(bf16[768,512]{1,0:T(8,128)(2,1)S(1)} %slice.725), channel_id=1, source_target_pairs={{0,2},{2,0},{1,3},{3,1},{4,6},{6,4},{5,7},{7,5},{8,10},{10,8},{9,1... | collective-permute-start | bytes 2359304 | tf_op jit(solution)/shard_map/ppermute | solution.py:388
  355.2 28.5 %collective-permute-start.42 = (bf16[1312,64]{1,0:T(8,128)(2,1)S(1)}, bf16[1312,64]{1,0:T(8,128)(2,1)S(1)}, u32[]{:S(2)}, u32[]{:S(2)}) collective-permute-start(bf16[1312,64]{1,0:T(8,128)(2,1)S(1)} %slice.732), channel_id=1, source_target_pairs={{0,16},{4,20},{8,24},{12,28},{16,0},{20,4},{24,8},{28,12},{1,17},{... | collective-permute-start | bytes 503816 | tf_op jit(solution)/shard_map/ppermute | solution.py:483
  370.9 24.0 %collective-permute-start.39 = (bf16[1312,64]{1,0:T(8,128)(2,1)S(1)}, bf16[1312,64]{1,0:T(8,128)(2,1)S(1)}, u32[]{:S(2)}, u32[]{:S(2)}) collective-permute-start(bf16[1312,64]{1,0:T(8,128)(2,1)S(1)} %slice.734), channel_id=1, source_target_pairs={{0,4},{4,0},{8,12},{12,8},{16,20},{20,16},{24,28},{28,24},{1,5},{5... | collective-permute-start | bytes 503816 | tf_op jit(solution)/shard_map/ppermute | solution.py:480
  384.5 24.8 %collective-permute-start.32 = (bf16[768,512]{1,0:T(8,128)(2,1)S(1)}, bf16[768,512]{1,0:T(8,128)(2,1)}, u32[]{:S(2)}, u32[]{:S(2)}) collective-permute-start(bf16[768,512]{1,0:T(8,128)(2,1)S(1)} %fusion.43), channel_id=1, source_target_pairs={{0,1},{1,0},{2,3},{3,2},{4,5},{5,4},{6,7},{7,6},{8,9},{9,8},{10,11... | collective-permute-start | bytes 2359304 | tf_op jit(solution)/shard_map/ppermute | solution.py:391
  (77 other events, 665.8 us)

commit v4 on v2

--- a/solution.py
+++ b/solution.py
@@ -503,8 +503,7 @@
     mean_one = jnp.mean(x, axis=-1, keepdims=True)
     h1 = (center * inverse_one * gain_one).astype(bf16)
     if two:
-        h1_y = relative(h1, "yzZw")
-        h1, h1_y, wq_mine, wq_got = lax.optimization_barrier((h1, h1_y, wq_mine, wq_got))
+        h1, wq_mine, wq_got = lax.optimization_barrier((h1, wq_mine, wq_got))
         wq = jnp.concatenate([wq_mine, wq_got], axis=0)
     wq = nn(wq, order).astype(bf16)
 
@@ -528,14 +527,21 @@
     act_low, lin_low = w_in[:, 0].astype(bf16), w_in[:, 1].astype(bf16)
     if two:
         even = (b // 2) % 2 == 0
-        in_got, wo_got = to_row(jnp.where(even, act_low, lin_low)), to_row(wo_low)
-        g_got = to_row(take(take(cotangent, 1 - r, Sr), c, Sr // 2))
+        in_send, wo_send, g_send = after(
+            (jnp.where(even, act_low, lin_low), wo_low, take(take(cotangent, 1 - r, Sr), c, Sr // 2)),
+            cosine,
+        )
+        in_got, wo_got, g_got = to_row(in_send), to_row(wo_send), to_row(g_send)
         wd_half = take(wd_low, (b // 2) % 2, F // 2)
+        h1_y = relative(after(h1, kv), "yzZw")
+        q, h1_y, sk_left, sk_right, act_low, lin_low, wd_half = lax.optimization_barrier(
+            (q, h1_y, sk_left, sk_right, act_low, lin_low, wd_half)
+        )
 
     state = attend_call(own_bounds, q, sq, [kv], [sk_own], heads)
     if two:
-        kv_left, kv_right, sk_left, sk_right, in_got, wo_got, g_got, wd_half = after(
-            (kv_left, kv_right, sk_left, sk_right, in_got, wo_got, g_got, wd_half), state
+        kv_left, kv_right, in_got, wo_got, g_got, wd_half = after(
+            (kv_left, kv_right, in_got, wo_got, g_got, wd_half), state
         )
         in_other, wd_got = to_z(in_got, 1), to_row(wd_half)
     o, lse = attend_call(

time: 416 us -> 423 us (1.017)
  waiting for transfers between devices: 80.9 us -> 103 us
  starting transfers between devices: 71.5 us -> 62.8 us
  other arithmetic: 73.7 us -> 69.2 us
    ppermute x10, starting transfers between devices: 31.6 us -> 10.4 us  [to_z(): return lax.ppermute(a, 'dp', [(i, i ^ 2 * j) for i in range(B)])]
    ppermute x1, waiting for transfers between devices: 1.39 us -> 15.2 us  [local(): from_left = lax.ppermute(dkv_right, 'dp', up)]
    ppermute x14, waiting for transfers between devices: 4.14 us -> 12 us  [to_row(): return lax.ppermute(a, 'row', SWAP)]
    ppermute x10, waiting for transfers between devices: 28.8 us -> 34.3 us  [to_z(): return lax.ppermute(a, 'dp', [(i, i ^ 2 * j) for i in range(B)])]
    ppermute x10, starting transfers between devices: 10.2 us -> 15 us  [to_col(): return lax.ppermute(a, 'col', SWAP)]
    ppermute x5, waiting for transfers between devices: 31.1 us -> 26.5 us  [to_y(): return lax.ppermute(a, 'dp', [(i, i ^ 1) for i in range(B)])]
    unnamed x133 -> x135, local copies, waits for them, and re-layouts: 10.3 us -> 9.74 us
  transfers between devices with their start and end apart: 44 -> 44, of which waited for: 13 -> 16; matrix products, arithmetic and copies ran while one was open for 37% -> 36% of each run, Pallas kernels for 17% -> 16%
where the time goes in v4:
time: 423 us; the launch traced here: 416 us
  waiting for transfers between devices  103 us (24%)
  other arithmetic  69.2 us (16%)
  matrix products  68.9 us (16%)
  Pallas kernels  67.5 us (16%)
  starting transfers between devices  62.8 us (15%)
  local copies, waits for them, and re-layouts  41.1 us (10%)
    pallas_call x2, Pallas kernels, attend_back_call(): pl.pallas_call(functools.partial(backward_kernel, heads, sets, final), gr...  38.3 us
    ppermute x10, waiting for transfers between devices, to_z(): return lax.ppermute(a, 'dp', [(i, i ^ 2 * j) for i in range(B)])  34.3 us
    dot_general x15, matrix products, nn(): return jnp.dot(a, b, preferred_element_type=f32)  31.2 us
    pallas_call x2, Pallas kernels, attend_call(): pl.pallas_call(functools.partial(forward_kernel, heads, sets, final), gri...  29.3 us
    ppermute x5, waiting for transfers between devices, to_y(): return lax.ppermute(a, 'dp', [(i, i ^ 1) for i in range(B)])  26.5 us
    dot_general x8, matrix products, nt(): lax.dot_general(a, b, (((1,), (1,)), ((), ())), preferred_element_type=f32)  17.9 us
    dot_general x10, matrix products, tn(): lax.dot_general(a, b, (((0,), (0,)), ((), ())), preferred_element_type=f32)  17.3 us
    ppermute x1, waiting for transfers between devices, local(): from_left = lax.ppermute(dkv_right, 'dp', up)  15.2 us
  transfers between devices with their start and end apart: 44, of which 16 were waited for; matrix products, arithmetic and copies ran while one was open for 36% of the time, Pallas kernels for 16%

profile of v4, /device:TPU:3, one launch (start us, length us, event | category | flops | bytes accessed | tf_op | source)
XLA Modules:
  0.0 415.7 jit_solution(8628622431768055106)
XLA Ops:
  10.9 2.8 multiply_sine_fusion
  13.7 4.9 %convert.78 = bf16[512,2,1312]{0,2,1:T(8,128)(2,1)} convert(f32[512,2,1312]{0,2,1:T(8,128)} %param.16) | non-fusion elementwise | flops 1343488 | bytes 8060928 | tf_op jit(solution)/shard_map/convert.22
  19.5 3.0 broadcast_select_fusion.2
  32.5 3.0 convert_element_type.229
  40.2 3.4 slice_bitcast_fusion
  59.2 5.2 %collective-permute-start.3 = (bf16[1024,512]{1,0:T(8,128)(2,1)}, bf16[1024,512]{1,0:T(8,128)(2,1)}, u32[]{:S(2)}, u32[]{:S(2)}) collective-permute-start(bf16[1024,512]{1,0:T(8,128)(2,1)} %get-tuple-element.215), channel_id=1, source_target_pairs={{0,4},{4,8},{8,12},{12,16},{16,20},{20,24},{24,28},{1,5},{5,9},{9,... | collective-permute-start | bytes 3145736 | tf_op jit(solution)/shard_map/ppermute | solution.py:523
  64.5 5.0 %fusion.16 = bf16[1536,1024]{1,0:T(8,128)(2,1)} fusion(bf16[1536,1024]{1,0:T(8,128)(2,1)S(1)} %fusion.4, s32[1024]{0:T(1024)S(1)} %add_xor_fusion.3), kind=kOutput, calls=%fused_computation.29 | convolution fusion | flops 3223846912 | bytes 6295552 | tf_op jit(solution)/shard_map/dot_general | solution.py:32
  73.6 19.3 %attend_own.1 = (f32[6,256,256]{2,1,0:T(8,128)}, f32[6,2,1024]{2,1,0:T(2,128)}) custom-call(s32[12]{0:T(128)} %reshape.742.bounds, bf16[1536,256]{1,0:T(8,128)(2,1)} %fusion.49.refs_0_, s32[6,1,256]{2,1,0:T(1,128)} %select_n.692.refs_1_.refs_4_, bf16[1536,512]{1,0:T(8,128)(2,1)} %copy-done.4, s32[1536,128]{1,0:T(8,128)} %broadcast_in_dim.134.refs_3_.refs_6_), custom_call_target="tpu_custom_call" | custom-call | flops 6291456 | bytes 3145728 | tf_op jit(solution)/shard_map/attend_own/pallas_call | solution.py:194
  93.0 15.2 %collective-permute-done.3.refs_2_.refs_5_ = bf16[1024,512]{1,0:T(8,128)(2,1)} collective-permute-done((bf16[1024,512]{1,0:T(8,128)(2,1)}, bf16[1024,512]{1,0:T(8,128)(2,1)}, u32[]{:S(2)}, u32[]{:S(2)}) %collective-permute-start.3) | collective-permute-done | bytes 1048608 | tf_op jit(solution)/shard_map/ppermute | solution.py:523
  113.0 10.0 %attend_final.1 = (bf16[1536,256]{1,0:T(8,128)(2,1)}, f32[6,1,1024]{2,1,0:T(1,128)}) custom-call(s32[24]{0:T(128)} %reshape.741.bounds, bf16[1536,256]{1,0:T(8,128)(2,1)} %fusion.49.refs_0_, s32[6,1,256]{2,1,0:T(1,128)} %select_n.692.refs_1_.refs_4_, bf16[1024,512]{1,0:T(8,128)(2,1)} %collective-permute-done.3.refs_2_.refs_5_, bf16[1024,512]{1,0:T(8,128)(2,1)} %copy-done.18, ...), custom_call_target="tpu_custom_call" | custom-call | flops 6291456 | bytes 3670016 | tf_op jit(solution)/shard_map/attend_final/pallas_call | solution.py:194
  153.9 2.8 collective-permute-done.13
  156.7 7.3 %multiply_convert_fusion = (bf16[768,1312]{0,1:T(8,128)(2,1)}, bf16[768,1312]{0,1:T(8,128)(2,1)}, bf16[768,1312]{0,1:T(8,128)(2,1)}) fusion(f32[768,1312]{0,1:T(8,128)S(1)} %convolution_add_fusion.1, f32[768,1312]{0,1:T(8,128)S(1)} %convolution_add_fusion, f32[768,1312]{0,1:T(8,128)S(1)} %fusion.79, bf16[656,512]{1,0:T(8,128)(2,1)} %collective-permute-done.13, ...), kind=kOutput, calls=%fused_computation.26 | convolution fusion | flops 1054973952 | bytes 20267008 | tf_op jit(solution)/shard_map/dot_general | solution.py:24
  164.1 3.1 fusion.163
  167.2 3.3 fusion.98
  189.1 2.9 fusion.154
  193.1 4.2 %collective-permute-done.19 = bf16[384,512]{1,0:T(8,128)(2,1)S(1)} collective-permute-done((bf16[384,512]{1,0:T(8,128)(2,1)S(1)}, bf16[384,512]{1,0:T(8,128)(2,1)S(1)}, u32[]{:S(2)}, u32[]{:S(2)}) %collective-permute-start.19) | collective-permute-done | bytes 393248 | tf_op jit(solution)/shard_map/ppermute | solution.py:388
  207.5 7.4 %collective-permute-done.17 = bf16[1312,512]{1,0:T(8,128)(2,1)S(1)} collective-permute-done((bf16[1312,512]{1,0:T(8,128)(2,1)S(1)}, bf16[1312,512]{1,0:T(8,128)(2,1)S(1)}, u32[]{:S(2)}, u32[]{:S(2)}) %collective-permute-start.17) | collective-permute-done | bytes 1343520 | tf_op jit(solution)/shard_map/ppermute | solution.py:480
  226.7 12.3 %back_halo.1 = (f32[6,256,256]{2,1,0:T(8,128)}, bf16[1024,512]{1,0:T(8,128)(2,1)}, bf16[1024,512]{1,0:T(8,128)(2,1)}) custom-call(s32[24]{0:T(128)} %reshape.741.bounds, bf16[1536,256]{1,0:T(8,128)(2,1)} %fusion.49.refs_0_, bf16[1536,256]{1,0:T(8,128)(2,1)} %maximum_select_fusion.7.refs_1_, bf16[1536,256]{1,0:T(8,128)(2,1)} %get-tuple-element.104.refs_2_, ...), custom_call_target="tpu_custom_call" | custom-call | flops 15728640 | bytes 3670016 | tf_op jit(solution)/shard_map/back_halo/pallas_call | solution.py:320
  245.0 7.5 %collective-permute-start.23 = (bf16[1024,512]{1,0:T(8,128)(2,1)}, bf16[1024,512]{1,0:T(8,128)(2,1)}, u32[]{:S(2)}, u32[]{:S(2)}) collective-permute-start(bf16[1024,512]{1,0:T(8,128)(2,1)} %get-tuple-element.127), channel_id=1, source_target_pairs={{0,4},{4,8},{8,12},{12,16},{16,20},{20,24},{24,28},{1,5},{5,9},{9,... | collective-permute-start | bytes 3145736 | tf_op jit(solution)/shard_map/ppermute | solution.py:654
  252.5 26.0 %back_own.1 = (f32[1536,256]{1,0:T(8,128)}, f32[1536,512]{1,0:T(8,128)}) custom-call(s32[12]{0:T(128)} %reshape.742.bounds, bf16[1536,256]{1,0:T(8,128)(2,1)} %fusion.49.refs_0_, bf16[1536,256]{1,0:T(8,128)(2,1)} %maximum_select_fusion.7.refs_1_, bf16[1536,256]{1,0:T(8,128)(2,1)} %get-tuple-element.104.refs_2_, f32[6,1,1024]{2,1,0:T(1,128)} %get-tuple-element.119.refs_3_, ...), custom_call_target="tpu_custom_call" | custom-call | flops 15728640 | bytes 3145728 | tf_op jit(solution)/shard_map/back_own/pallas_call | solution.py:320
  280.8 15.2 %collective-permute-done.23 = bf16[1024,512]{1,0:T(8,128)(2,1)} collective-permute-done((bf16[1024,512]{1,0:T(8,128)(2,1)}, bf16[1024,512]{1,0:T(8,128)(2,1)}, u32[]{:S(2)}, u32[]{:S(2)}) %collective-permute-start.23) | collective-permute-done | bytes 1048608 | tf_op jit(solution)/shard_map/ppermute | solution.py:654
  307.0 3.0 collective-permute-start.28
  313.6 2.7 convolution_add_fusion.4
  324.5 14.5 %collective-permute-done.39 = bf16[1312,256]{1,0:T(8,128)(2,1)} collective-permute-done((bf16[1312,256]{1,0:T(8,128)(2,1)}, bf16[1312,256]{1,0:T(8,128)(2,1)}, u32[]{:S(2)}, u32[]{:S(2)}) %collective-permute-start.39) | collective-permute-done | bytes 671776 | tf_op jit(solution)/shard_map/ppermute | solution.py:480
  342.1 3.1 collective-permute-start.30
  353.4 10.4 %collective-permute-done.40 = bf16[1312,128]{1,0:T(8,128)(2,1)S(1)} collective-permute-done((bf16[1312,128]{1,0:T(8,128)(2,1)S(1)}, bf16[1312,128]{1,0:T(8,128)(2,1)S(1)}, u32[]{:S(2)}, u32[]{:S(2)}) %collective-permute-start.40) | collective-permute-done | bytes 335904 | tf_op jit(solution)/shard_map/ppermute | solution.py:483
  364.2 8.2 %collective-permute-done.33 = bf16[768,256]{1,0:T(8,128)(2,1)S(1)} collective-permute-done((bf16[768,256]{1,0:T(8,128)(2,1)S(1)}, bf16[768,256]{1,0:T(8,128)(2,1)S(1)}, u32[]{:S(2)}, u32[]{:S(2)}) %collective-permute-start.33) | collective-permute-done | bytes 393248 | tf_op jit(solution)/shard_map/ppermute | solution.py:483
  376.5 4.5 %collective-permute-done.38 = bf16[1312,64]{1,0:T(8,128)(2,1)S(1)} collective-permute-done((bf16[1312,64]{1,0:T(8,128)(2,1)S(1)}, bf16[1312,64]{1,0:T(8,128)(2,1)S(1)}, u32[]{:S(2)}, u32[]{:S(2)}) %collective-permute-start.38) | collective-permute-done | bytes 167968 | tf_op jit(solution)/shard_map/ppermute | solution.py:480
  381.7 3.2 collective-permute-start.31
  384.9 9.2 %collective-permute-done.41 = bf16[1312,64]{1,0:T(8,128)(2,1)S(1)} collective-permute-done((bf16[1312,64]{1,0:T(8,128)(2,1)S(1)}, bf16[1312,64]{1,0:T(8,128)(2,1)S(1)}, u32[]{:S(2)}, u32[]{:S(2)}) %collective-permute-start.41) | collective-permute-done | bytes 167968 | tf_op jit(solution)/shard_map/ppermute | solution.py:483
  404.4 3.1 maximum_select_fusion.4
  407.6 3.5 collective-permute-done.35
  (387 shorter events, 183.5 us)
Async XLA Ops:
  2.8 35.5 %collective-permute-start = (bf16[768,512]{1,0:T(8,128)(2,1)}, bf16[768,512]{1,0:T(8,128)(2,1)}, u32[]{:S(2)}, u32[]{:S(2)}) collective-permute-start(bf16[768,512]{1,0:T(8,128)(2,1)} %constant_dynamic-slice_fusion.6), channel_id=1, source_target_pairs={{0,2},{2,0},{1,3},{3,1},{4,6},{6,4},{5,7},{7,5},{8,10},{10,8},{9,1... | collective-permute-start | bytes 2359304 | tf_op jit(solution)/shard_map/ppermute | solution.py:388
  6.2 43.5 %collective-permute-start.2 = (bf16[512,768]{0,1:T(8,128)(2,1)}, bf16[512,768]{0,1:T(8,128)(2,1)}, u32[]{:S(2)}, u32[]{:S(2)}) collective-permute-start(bf16[512,768]{0,1:T(8,128)(2,1)} %get-tuple-element.218), channel_id=1, source_target_pairs={{0,2},{2,0},{1,3},{3,1},{4,6},{6,4},{5,7},{7,5},{8,10},{10,8},{9,1... | collective-permute-start | bytes 2359304 | tf_op jit(solution)/shard_map/ppermute | solution.py:388
  22.5 70.4 %collective-permute-start.7 = (bf16[384,512]{1,0:T(8,128)(2,1)}, bf16[384,512]{1,0:T(8,128)(2,1)S(1)}, u32[]{:S(2)}, u32[]{:S(2)}) collective-permute-start(bf16[384,512]{1,0:T(8,128)(2,1)} %constant_dynamic-slice_fusion.2), channel_id=1, source_target_pairs={{0,2},{2,0},{1,3},{3,1},{4,6},{6,4},{5,7},{7,5},{8,10},{10,8},{9,1... | collective-permute-start | bytes 1179656 | tf_op jit(solution)/shard_map/ppermute | solution.py:388
  22.5 70.4 %collective-permute-start.6 = (bf16[512,512]{1,0:T(8,128)(2,1)}, bf16[512,512]{1,0:T(8,128)(2,1)}, u32[]{:S(2)}, u32[]{:S(2)}) collective-permute-start(bf16[512,512]{1,0:T(8,128)(2,1)} %convert_element_type.230), channel_id=1, source_target_pairs={{0,2},{2,0},{1,3},{3,1},{4,6},{6,4},{5,7},{7,5},{8,10},{10,8},{9,1... | collective-permute-start | bytes 1572872 | tf_op jit(solution)/shard_map/ppermute | solution.py:388
  24.0 69.0 %collective-permute-start.5 = (bf16[512,1312]{0,1:T(8,128)(2,1)}, bf16[512,1312]{0,1:T(8,128)(2,1)}, u32[]{:S(2)}, u32[]{:S(2)}) collective-permute-start(bf16[512,1312]{0,1:T(8,128)(2,1)} %broadcast_select_fusion.2), channel_id=1, source_target_pairs={{0,2},{2,0},{1,3},{3,1},{4,6},{6,4},{5,7},{7,5},{8,10},{10,8},{9,1... | collective-permute-start | bytes 4030472 | tf_op jit(solution)/shard_map/ppermute | solution.py:388
  57.9 35.0 %collective-permute-start.4 = (bf16[1024,512]{1,0:T(8,128)(2,1)}, bf16[1024,512]{1,0:T(8,128)(2,1)S(1)}, u32[]{:S(2)}, u32[]{:S(2)}) collective-permute-start(bf16[1024,512]{1,0:T(8,128)(2,1)} %get-tuple-element.214), channel_id=1, source_target_pairs={{4,0},{8,4},{12,8},{16,12},{20,16},{24,20},{28,24},{5,1},{9,5},{13... | collective-permute-start | bytes 3145736 | tf_op jit(solution)/shard_map/ppermute | solution.py:524
  59.2 49.0 %collective-permute-start.3 = (bf16[1024,512]{1,0:T(8,128)(2,1)}, bf16[1024,512]{1,0:T(8,128)(2,1)}, u32[]{:S(2)}, u32[]{:S(2)}) collective-permute-start(bf16[1024,512]{1,0:T(8,128)(2,1)} %get-tuple-element.215), channel_id=1, source_target_pairs={{0,4},{4,8},{8,12},{12,16},{16,20},{20,24},{24,28},{1,5},{5,9},{9,... | collective-permute-start | bytes 3145736 | tf_op jit(solution)/shard_map/ppermute | solution.py:523
  108.2 17.2 %collective-permute-start.8 = (bf16[656,512]{1,0:T(8,128)(2,1)}, bf16[656,512]{1,0:T(8,128)(2,1)}, u32[]{:S(2)}, u32[]{:S(2)}) collective-permute-start(bf16[656,512]{1,0:T(8,128)(2,1)} %constant_dynamic-slice_fusion.3), channel_id=1, source_target_pairs={{0,2},{2,0},{1,3},{3,1},{4,6},{6,4},{5,7},{7,5},{8,10},{10,8},{9,1... | collective-permute-start | bytes 2015240 | tf_op jit(solution)/shard_map/ppermute | solution.py:388
  111.7 30.7 %collective-permute-start.14 = (bf16[512,1312]{0,1:T(8,128)(2,1)}, bf16[512,1312]{0,1:T(8,128)(2,1)}, u32[]{:S(2)}, u32[]{:S(2)}) collective-permute-start(bf16[512,1312]{0,1:T(8,128)(2,1)} %collective-permute-done.5), channel_id=1, source_target_pairs={{0,8},{4,12},{8,0},{12,4},{16,24},{20,28},{24,16},{28,20},{1,9},{5... | collective-permute-start | bytes 4030472 | tf_op jit(solution)/shard_map/ppermute | solution.py:483
  129.7 27.0 %collective-permute-start.13 = (bf16[656,512]{1,0:T(8,128)(2,1)}, bf16[656,512]{1,0:T(8,128)(2,1)}, u32[]{:S(2)}, u32[]{:S(2)}) collective-permute-start(bf16[656,512]{1,0:T(8,128)(2,1)} %collective-permute-done.8), channel_id=1, source_target_pairs={{0,8},{4,12},{8,0},{12,4},{16,24},{20,28},{24,16},{28,20},{1,9},{5... | collective-permute-start | bytes 2015240 | tf_op jit(solution)/shard_map/ppermute | solution.py:483
  170.6 15.7 %collective-permute-start.18 = (bf16[384,1024]{1,0:T(8,128)(2,1)S(1)}, bf16[384,1024]{1,0:T(8,128)(2,1)S(1)}, u32[]{:S(2)}, u32[]{:S(2)}) collective-permute-start(bf16[384,1024]{1,0:T(8,128)(2,1)S(1)} %fusion.35), channel_id=1, source_target_pairs={{0,1},{1,0},{2,3},{3,2},{4,5},{5,4},{6,7},{7,6},{8,9},{9,8},{10,11... | collective-permute-start | bytes 2359304 | tf_op jit(solution)/shard_map/ppermute | solution.py:391
  182.8 32.1 %collective-permute-start.17 = (bf16[1312,512]{1,0:T(8,128)(2,1)S(1)}, bf16[1312,512]{1,0:T(8,128)(2,1)S(1)}, u32[]{:S(2)}, u32[]{:S(2)}) collective-permute-start(bf16[1312,512]{1,0:T(8,128)(2,1)S(1)} %convolution_convert_fusion.2), channel_id=1, source_target_pairs={{0,4},{4,0},{8,12},{12,8},{16,20},{20,16},{24,28},{28,24},{1,5},{5... | collective-permute-start | bytes 4030472 | tf_op jit(solution)/shard_map/ppermute | solution.py:480
  197.3 25.9 %collective-permute-start.16 = (bf16[768,256]{1,0:T(8,128)(2,1)S(1)}, bf16[768,256]{1,0:T(8,128)(2,1)S(1)}, u32[]{:S(2)}, u32[]{:S(2)}) collective-permute-start(bf16[768,256]{1,0:T(8,128)(2,1)S(1)} %get-tuple-element.230), channel_id=1, source_target_pairs={{0,2},{2,0},{1,3},{3,1},{4,6},{6,4},{5,7},{7,5},{8,10},{10,8},{9,1... | collective-permute-start | bytes 1179656 | tf_op jit(solution)/shard_map/ppermute | solution.py:388
  198.1 27.1 %collective-permute-start.20 = (bf16[2,384,512]{2,1,0:T(8,128)(2,1)S(1)}, bf16[2,384,512]{2,1,0:T(8,128)(2,1)S(1)}, u32[]{:S(2)}, u32[]{:S(2)}) collective-permute-start(bf16[2,384,512]{2,1,0:T(8,128)(2,1)S(1)} %maximum_select_fusion.10), channel_id=1, source_target_pairs={{0,1},{1,0},{2,3},{3,2},{4,5},{5,4},{6,7},{7,6},{8,9},{9,8},{10,11... | collective-permute-start | bytes 2359304 | tf_op jit(solution)/shard_map/ppermute | solution.py:391
  218.3 20.7 %collective-permute-start.21 = (bf16[1312,256]{1,0:T(8,128)(2,1)}, bf16[1312,256]{1,0:T(8,128)(2,1)}, u32[]{:S(2)}, u32[]{:S(2)}) collective-permute-start(bf16[1312,256]{1,0:T(8,128)(2,1)} %slice.740), channel_id=1, source_target_pairs={{0,8},{4,12},{8,0},{12,4},{16,24},{20,28},{24,16},{28,20},{1,9},{5... | collective-permute-start | bytes 2015240 | tf_op jit(solution)/shard_map/ppermute | solution.py:483
  222.0 58.7 %collective-permute-start.25 = (bf16[512,512]{1,0:T(8,128)(2,1)}, bf16[512,512]{1,0:T(8,128)(2,1)}, u32[]{:S(2)}, u32[]{:S(2)}) collective-permute-start(bf16[512,512]{1,0:T(8,128)(2,1)} %convolution_convert_fusion.4), channel_id=1, source_target_pairs={{0,4},{4,0},{8,12},{12,8},{16,20},{20,16},{24,28},{28,24},{1,5},{5... | collective-permute-start | bytes 1572872 | tf_op jit(solution)/shard_map/ppermute | solution.py:480
  223.2 72.8 %collective-permute-start.24 = (bf16[2624,512]{1,0:T(8,128)(2,1)}, bf16[2624,512]{1,0:T(8,128)(2,1)}, u32[]{:S(2)}, u32[]{:S(2)}) collective-permute-start(bf16[2624,512]{1,0:T(8,128)(2,1)} %pad_maximum_fusion.1), channel_id=1, source_target_pairs={{0,2},{2,0},{1,3},{3,1},{4,6},{6,4},{5,7},{7,5},{8,10},{10,8},{9,1... | collective-permute-start | bytes 8060936 | tf_op jit(solution)/shard_map/ppermute | solution.py:388
  242.5 38.2 %collective-permute-start.26 = (bf16[1312,128]{1,0:T(8,128)(2,1)}, bf16[1312,128]{1,0:T(8,128)(2,1)S(1)}, u32[]{:S(2)}, u32[]{:S(2)}) collective-permute-start(bf16[1312,128]{1,0:T(8,128)(2,1)} %slice.747), channel_id=1, source_target_pairs={{0,16},{4,20},{8,24},{12,28},{16,0},{20,4},{24,8},{28,12},{1,17},{... | collective-permute-start | bytes 1007624 | tf_op jit(solution)/shard_map/ppermute | solution.py:483
  243.7 37.1 %collective-permute-start.22 = (bf16[1024,512]{1,0:T(8,128)(2,1)}, bf16[1024,512]{1,0:T(8,128)(2,1)}, u32[]{:S(2)}, u32[]{:S(2)}) collective-permute-start(bf16[1024,512]{1,0:T(8,128)(2,1)} %get-tuple-element.126), channel_id=1, source_target_pairs={{4,0},{8,4},{12,8},{16,12},{20,16},{24,20},{28,24},{5,1},{9,5},{13... | collective-permute-start | bytes 3145736 | tf_op jit(solution)/shard_map/ppermute | solution.py:653
  245.0 51.0 %collective-permute-start.23 = (bf16[1024,512]{1,0:T(8,128)(2,1)}, bf16[1024,512]{1,0:T(8,128)(2,1)}, u32[]{:S(2)}, u32[]{:S(2)}) collective-permute-start(bf16[1024,512]{1,0:T(8,128)(2,1)} %get-tuple-element.127), channel_id=1, source_target_pairs={{0,4},{4,8},{8,12},{12,16},{16,20},{20,24},{24,28},{1,5},{5,9},{9,... | collective-permute-start | bytes 3145736 | tf_op jit(solution)/shard_map/ppermute | solution.py:654
  304.8 37.3 %collective-permute-start.32 = (bf16[768,512]{1,0:T(8,128)(2,1)}, bf16[768,512]{1,0:T(8,128)(2,1)}, u32[]{:S(2)}, u32[]{:S(2)}) collective-permute-start(bf16[768,512]{1,0:T(8,128)(2,1)} %fusion.59), channel_id=1, source_target_pairs={{0,4},{4,0},{8,12},{12,8},{16,20},{20,16},{24,28},{28,24},{1,5},{5... | collective-permute-start | bytes 2359304 | tf_op jit(solution)/shard_map/ppermute | solution.py:480
  307.0 43.6 %collective-permute-start.28 = (bf16[768,512]{1,0:T(8,128)(2,1)S(1)}, bf16[768,512]{1,0:T(8,128)(2,1)S(1)}, u32[]{:S(2)}, u32[]{:S(2)}) collective-permute-start(bf16[768,512]{1,0:T(8,128)(2,1)S(1)} %copy-done.31), channel_id=1, source_target_pairs={{0,2},{3,1},{4,6},{7,5},{8,10},{11,9},{12,14},{15,13},{16,18},{19,... | collective-permute-start | bytes 2359304 | tf_op jit(solution)/shard_map/ppermute | solution.py:686
  319.9 19.1 %collective-permute-start.39 = (bf16[1312,256]{1,0:T(8,128)(2,1)}, bf16[1312,256]{1,0:T(8,128)(2,1)}, u32[]{:S(2)}, u32[]{:S(2)}) collective-permute-start(bf16[1312,256]{1,0:T(8,128)(2,1)} %slice.738), channel_id=1, source_target_pairs={{0,4},{4,0},{8,12},{12,8},{16,20},{20,16},{24,28},{28,24},{1,5},{5... | collective-permute-start | bytes 2015240 | tf_op jit(solution)/shard_map/ppermute | solution.py:480
  320.3 21.6 %collective-permute-start.36 = (bf16[1824,256]{1,0:T(8,128)(2,1)S(1)}, bf16[1824,256]{1,0:T(8,128)(2,1)S(1)}, u32[]{:S(2)}, u32[]{:S(2)}) collective-permute-start(bf16[1824,256]{1,0:T(8,128)(2,1)S(1)} %pad_maximum_fusion.5), channel_id=1, source_target_pairs={{0,8},{4,12},{8,0},{12,4},{16,24},{20,28},{24,16},{28,20},{1,9},{5... | collective-permute-start | bytes 2801672 | tf_op jit(solution)/shard_map/ppermute | solution.py:483
  345.5 18.4 %collective-permute-start.40 = (bf16[1312,128]{1,0:T(8,128)(2,1)S(1)}, bf16[1312,128]{1,0:T(8,128)(2,1)S(1)}, u32[]{:S(2)}, u32[]{:S(2)}) collective-permute-start(bf16[1312,128]{1,0:T(8,128)(2,1)S(1)} %slice.744), channel_id=1, source_target_pairs={{0,8},{4,12},{8,0},{12,4},{16,24},{20,28},{24,16},{28,20},{1,9},{5... | collective-permute-start | bytes 1007624 | tf_op jit(solution)/shard_map/ppermute | solution.py:483
  348.2 24.2 %collective-permute-start.33 = (bf16[768,256]{1,0:T(8,128)(2,1)S(1)}, bf16[768,256]{1,0:T(8,128)(2,1)S(1)}, u32[]{:S(2)}, u32[]{:S(2)}) collective-permute-start(bf16[768,256]{1,0:T(8,128)(2,1)S(1)} %slice.741), channel_id=1, source_target_pairs={{0,8},{4,12},{8,0},{12,4},{16,24},{20,28},{24,16},{28,20},{1,9},{5... | collective-permute-start | bytes 1179656 | tf_op jit(solution)/shard_map/ppermute | solution.py:483
  348.6 24.8 %collective-permute-start.37 = (bf16[1824,128]{1,0:T(8,128)(2,1)S(1)}, bf16[1824,128]{1,0:T(8,128)(2,1)S(1)}, u32[]{:S(2)}, u32[]{:S(2)}) collective-permute-start(bf16[1824,128]{1,0:T(8,128)(2,1)S(1)} %pad_maximum_fusion.7), channel_id=1, source_target_pairs={{0,16},{4,20},{8,24},{12,28},{16,0},{20,4},{24,8},{28,12},{1,17},{... | collective-permute-start | bytes 1400840 | tf_op jit(solution)/shard_map/ppermute | solution.py:483
  350.7 30.4 %collective-permute-start.29 = (bf16[768,512]{1,0:T(8,128)(2,1)S(1)}, bf16[768,512]{1,0:T(8,128)(2,1)S(1)}, u32[]{:S(2)}, u32[]{:S(2)}) collective-permute-start(bf16[768,512]{1,0:T(8,128)(2,1)S(1)} %slice.736), channel_id=1, source_target_pairs={{0,2},{2,0},{1,3},{3,1},{4,6},{6,4},{5,7},{7,5},{8,10},{10,8},{9,1... | collective-permute-start | bytes 2359304 | tf_op jit(solution)/shard_map/ppermute | solution.py:388
  364.1 30.0 %collective-permute-start.41 = (bf16[1312,64]{1,0:T(8,128)(2,1)S(1)}, bf16[1312,64]{1,0:T(8,128)(2,1)S(1)}, u32[]{:S(2)}, u32[]{:S(2)}) collective-permute-start(bf16[1312,64]{1,0:T(8,128)(2,1)S(1)} %slice.743), channel_id=1, source_target_pairs={{0,16},{4,20},{8,24},{12,28},{16,0},{20,4},{24,8},{28,12},{1,17},{... | collective-permute-start | bytes 503816 | tf_op jit(solution)/shard_map/ppermute | solution.py:483
  373.3 25.1 %collective-permute-start.34 = (bf16[768,128]{1,0:T(8,128)(2,1)}, bf16[768,128]{1,0:T(8,128)(2,1)}, u32[]{:S(2)}, u32[]{:S(2)}) collective-permute-start(bf16[768,128]{1,0:T(8,128)(2,1)} %slice.749), channel_id=1, source_target_pairs={{0,16},{4,20},{8,24},{12,28},{16,0},{20,4},{24,8},{28,12},{1,17},{... | collective-permute-start | bytes 589832 | tf_op jit(solution)/shard_map/ppermute | solution.py:483
  376.2 22.3 %collective-permute-start.43 = (bf16[1824,64]{1,0:T(8,128)(2,1)}, bf16[1824,64]{1,0:T(8,128)(2,1)S(1)}, u32[]{:S(2)}, u32[]{:S(2)}) collective-permute-start(bf16[1824,64]{1,0:T(8,128)(2,1)} %pad_maximum_fusion.8), channel_id=1, source_target_pairs={{0,2},{2,0},{1,3},{3,1},{4,6},{6,4},{5,7},{7,5},{8,10},{10,8},{9,1... | collective-permute-start | bytes 700424 | tf_op jit(solution)/shard_map/ppermute | solution.py:388
  381.7 22.7 %collective-permute-start.31 = (bf16[768,512]{1,0:T(8,128)(2,1)S(1)}, bf16[768,512]{1,0:T(8,128)(2,1)}, u32[]{:S(2)}, u32[]{:S(2)}) collective-permute-start(bf16[768,512]{1,0:T(8,128)(2,1)S(1)} %fusion.43), channel_id=1, source_target_pairs={{0,1},{1,0},{2,3},{3,2},{4,5},{5,4},{6,7},{7,6},{8,9},{9,8},{10,11... | collective-permute-start | bytes 2359304 | tf_op jit(solution)/shard_map/ppermute | solution.py:391
  (80 other events, 666.8 us)

commit v5 on v4

--- a/solution.py
+++ b/solution.py
@@ -451,8 +451,8 @@
 
     wq_low = w_qkv.reshape(Dl, R * 3 * W).astype(bf16)
     if two:
-        wq_mine = take(wq_low, r, 3 * W, 1)
-        wq_got = to_row(take(wq_low, 1 - r, 3 * W, 1))
+        wq_mine, wq_send = take(wq_low, r, 3 * W, 1), take(wq_low, 1 - r, 3 * W, 1)
+        wq_got = to_row(wq_send)
     else:
         wq = lax.all_to_all(wq_low, "row", split_axis=1, concat_axis=0, tiled=True)
     order = qkv_order(heads, head_width)
@@ -523,13 +523,20 @@
     kv_left = lax.ppermute(kv[S - H :], "dp", up)
     kv_right = lax.ppermute(kv[:H], "dp", down)
     q = (turn(nn(h1, wq[:, :W]), 1.0) * (1.0 / math.sqrt(head_width))).astype(bf16)
-    wo_low, wd_low = w_out.astype(bf16), w_down.astype(bf16)
-    act_low, lin_low = w_in[:, 0].astype(bf16), w_in[:, 1].astype(bf16)
+    wo_low = w_out.astype(bf16)
+    w_in_late, w_down_late = after((w_in, w_down), kv)
+    wd_low = w_down_late.astype(bf16)
+    act_low, lin_low = w_in_late[:, 0].astype(bf16), w_in_late[:, 1].astype(bf16)
     if two:
         even = (b // 2) % 2 == 0
         in_send, wo_send, g_send = after(
-            (jnp.where(even, act_low, lin_low), wo_low, take(take(cotangent, 1 - r, Sr), c, Sr // 2)),
+            (
+                lax.dynamic_index_in_dim(w_in, (b // 2) % 2, 1, keepdims=False).astype(bf16),
+                wo_low,
+                take(cotangent, 2 * (1 - r) + c, Sr // 2),
+            ),
             cosine,
+            wq_send,
         )
         in_got, wo_got, g_got = to_row(in_send), to_row(wo_send), to_row(g_send)
         wd_half = take(wd_low, (b // 2) % 2, F // 2)
@@ -616,9 +623,10 @@
     dm = split_nt(g_low, wds)
     da = (dm * u * slope).astype(bf16)
     du = (dm * gelu).astype(bf16)
-    dh2 = col_sum(wide([nt(da, v) + nt(du, w) for v, w in zip(acts, lins)]))
-    if two:
-        g_y = relative(g_low, "yzZx")
+    dh2_part = wide([nt(da, v) + nt(du, w) for v, w in zip(acts, lins)])
+    dh2 = col_sum(dh2_part)
+    if two:
+        g_y = relative(after(g_low, dh2_part), "yzZx")
         lower_got = to_y(product(m, g_y))
     e2 = dh2 * gain_two
     dx1 = g_low.astype(f32) + inverse_two * (
@@ -631,8 +639,6 @@
     if two:
         do_got = to_row(do_rows[:, W:])
         do = ordered(zrow, do_rows[:, :W], do_got, 0)
-        pair = ordered(zrow, y_half[None, :, :Dl], after(y_got, dx_low)[None], 0)
-        layer_out = ordered(zcol, pair[:, None], to_col(pair)[:, None], 1).reshape(S, Dl)
     else:
         do = lax.all_to_all(do_rows, "row", split_axis=1, concat_axis=0, tiled=True)
 
@@ -643,6 +649,8 @@
         proj_got = to_y(product(o_heads, dx_y))
         gate_send = jnp.concatenate([product(da, h_act), product(du, h_lin)], axis=0)
         gate_got = to_row(after(gate_send, do_got))
+        pair = ordered(zrow, y_half[None, :, :Dl], after(y_got, gate_send)[None], 0)
+        layer_out = ordered(zcol, pair[:, None], to_col(pair)[:, None], 1).reshape(S, Dl)
         lower = halved(m, g_y, after(lower_got, gate_send))
         lower_got = to_z(second(lower), 1)
         do, lower, layer_out = lax.optimization_barrier((do, lower, layer_out))

time: 423 us -> 412 us (0.974)
  waiting for transfers between devices: 103 us -> 80 us
  Pallas kernels: 67.5 us -> 82.4 us
  other arithmetic: 69.2 us -> 62.3 us
    ppermute x1, waiting for transfers between devices: 15.2 us -> 2.55 us  [local(): from_left = lax.ppermute(dkv_right, 'dp', up)]
    ppermute x1, waiting for transfers between devices: 15.2 us -> 4.37 us  [local(): kv_left = lax.ppermute(kv[S - H:], 'dp', up)]
    pallas_call x2, Pallas kernels: 38.3 us -> 46.3 us  [attend_back_call(): pl.pallas_call(functools.partial(backward_kernel, heads, sets, final), gr...]
    pallas_call x2, Pallas kernels: 29.3 us -> 36.1 us  [attend_call(): pl.pallas_call(functools.partial(forward_kernel, heads, sets, final), gri...]
    ppermute x14, waiting for transfers between devices: 12 us -> 5.84 us  [to_row(): return lax.ppermute(a, 'row', SWAP)]
    ppermute x10, starting transfers between devices: 10.4 us -> 16.4 us  [to_z(): return lax.ppermute(a, 'dp', [(i, i ^ 2 * j) for i in range(B)])]
    another operation x2 -> x1, other arithmetic: 5.37 us -> 0.34 us
    unnamed x135 -> x145, local copies, waits for them, and re-layouts: 9.74 us -> 9.46 us
  transfers between devices with their start and end apart: 44 -> 44, of which waited for: 16 -> 15; matrix products, arithmetic and copies ran while one was open for 36% -> 35% of each run, Pallas kernels for 16% -> 20%
where the time goes in v5:
time: 412 us; the launch traced here: 405 us
  Pallas kernels  82.4 us (20%)
  waiting for transfers between devices  80 us (19%)
  matrix products  68.7 us (17%)
  starting transfers between devices  66 us (16%)
  other arithmetic  62.3 us (15%)
  local copies, waits for them, and re-layouts  42.9 us (10%)
    pallas_call x2, Pallas kernels, attend_back_call(): pl.pallas_call(functools.partial(backward_kernel, heads, sets, final), gr...  46.3 us
    ppermute x10, waiting for transfers between devices, to_z(): return lax.ppermute(a, 'dp', [(i, i ^ 2 * j) for i in range(B)])  38.1 us
    pallas_call x2, Pallas kernels, attend_call(): pl.pallas_call(functools.partial(forward_kernel, heads, sets, final), gri...  36.1 us
    dot_general x15, matrix products, nn(): return jnp.dot(a, b, preferred_element_type=f32)  31.3 us
    ppermute x5, waiting for transfers between devices, to_y(): return lax.ppermute(a, 'dp', [(i, i ^ 1) for i in range(B)])  29.2 us
    dot_general x8, matrix products, nt(): lax.dot_general(a, b, (((1,), (1,)), ((), ())), preferred_element_type=f32)  17.7 us
    dot_general x10, matrix products, tn(): lax.dot_general(a, b, (((0,), (0,)), ((), ())), preferred_element_type=f32)  17.3 us
    ppermute x10, starting transfers between devices, to_z(): return lax.ppermute(a, 'dp', [(i, i ^ 2 * j) for i in range(B)])  16.4 us
  transfers between devices with their start and end apart: 44, of which 15 were waited for; matrix products, arithmetic and copies ran while one was open for 35% of the time, Pallas kernels for 20%

profile of v5, /device:TPU:3, one launch (start us, length us, event | category | flops | bytes accessed | tf_op | source)
XLA Modules:
  0.0 405.0 jit_solution(16334611717756617279)
XLA Ops:
  10.9 2.8 multiply_sine_fusion
  14.6 3.0 fusion.61
  40.7 2.6 fusion.28
  50.3 5.4 %collective-permute-start.3 = (bf16[1024,512]{1,0:T(8,128)(2,1)}, bf16[1024,512]{1,0:T(8,128)(2,1)}, u32[]{:S(2)}, u32[]{:S(2)}) collective-permute-start(bf16[1024,512]{1,0:T(8,128)(2,1)} %get-tuple-element.221), channel_id=1, source_target_pairs={{0,4},{4,8},{8,12},{12,16},{16,20},{20,24},{24,28},{1,5},{5,9},{9,... | collective-permute-start | bytes 3145736 | tf_op jit(solution)/shard_map/ppermute | solution.py:523
  55.7 5.2 %fusion.16 = bf16[1536,1024]{1,0:T(8,128)(2,1)} fusion(bf16[1536,1024]{1,0:T(8,128)(2,1)S(1)} %fusion.4, s32[1024]{0:T(1024)S(1)} %add_xor_fusion.3), kind=kOutput, calls=%fused_computation.29 | convolution fusion | flops 3223846912 | bytes 6295552 | tf_op jit(solution)/shard_map/dot_general | solution.py:32
  69.3 25.5 %attend_own.1 = (f32[6,256,256]{2,1,0:T(8,128)}, f32[6,2,1024]{2,1,0:T(2,128)}) custom-call(s32[12]{0:T(128)} %reshape.743.bounds, bf16[1536,256]{1,0:T(8,128)(2,1)} %fusion.48.refs_0_, s32[6,1,256]{2,1,0:T(1,128)} %select_n.692.refs_1_.refs_4_, bf16[1536,512]{1,0:T(8,128)(2,1)} %copy-done.4, s32[1536,128]{1,0:T(8,128)} %broadcast_in_dim.134.refs_3_.refs_6_), custom_call_target="tpu_custom_call" | custom-call | flops 6291456 | bytes 3145728 | tf_op jit(solution)/shard_map/attend_own/pallas_call | solution.py:194
  94.9 4.4 %collective-permute-done.3.refs_2_.refs_5_ = bf16[1024,512]{1,0:T(8,128)(2,1)} collective-permute-done((bf16[1024,512]{1,0:T(8,128)(2,1)}, bf16[1024,512]{1,0:T(8,128)(2,1)}, u32[]{:S(2)}, u32[]{:S(2)}) %collective-permute-start.3) | collective-permute-done | bytes 1048608 | tf_op jit(solution)/shard_map/ppermute | solution.py:523
  104.2 10.5 %attend_final.1 = (bf16[1536,256]{1,0:T(8,128)(2,1)}, f32[6,1,1024]{2,1,0:T(1,128)}) custom-call(s32[24]{0:T(128)} %reshape.742.bounds, bf16[1536,256]{1,0:T(8,128)(2,1)} %fusion.48.refs_0_, s32[6,1,256]{2,1,0:T(1,128)} %select_n.692.refs_1_.refs_4_, bf16[1024,512]{1,0:T(8,128)(2,1)} %collective-permute-done.3.refs_2_.refs_5_, ...), custom_call_target="tpu_custom_call" | custom-call | flops 6291456 | bytes 3670016 | tf_op jit(solution)/shard_map/attend_final/pallas_call | solution.py:194
  144.5 3.5 collective-permute-done.13
  147.9 7.1 %multiply_convert_fusion = (bf16[768,1312]{0,1:T(8,128)(2,1)}, bf16[768,1312]{0,1:T(8,128)(2,1)}, bf16[768,1312]{0,1:T(8,128)(2,1)}) fusion(f32[768,1312]{0,1:T(8,128)S(1)} %convolution_add_fusion.1, f32[768,1312]{0,1:T(8,128)S(1)} %convolution_add_fusion, f32[768,1312]{0,1:T(8,128)S(1)} %fusion.80, bf16[656,512]{1,0:T(8,128)(2,1)} %collective-permute-done.13, ...), kind=kOutput, calls=%fused_computation.26 | convolution fusion | flops 1054973952 | bytes 20267008 | tf_op jit(solution)/shard_map/dot_general | solution.py:24
  155.1 3.1 fusion.164
  158.2 3.1 fusion.99
  179.4 2.9 fusion.155
  192.7 12.7 %collective-permute-done.17 = bf16[1312,512]{1,0:T(8,128)(2,1)S(1)} collective-permute-done((bf16[1312,512]{1,0:T(8,128)(2,1)S(1)}, bf16[1312,512]{1,0:T(8,128)(2,1)S(1)}, u32[]{:S(2)}, u32[]{:S(2)}) %collective-permute-start.17) | collective-permute-done | bytes 1343520 | tf_op jit(solution)/shard_map/ppermute | solution.py:480
  218.0 12.8 %back_halo.1 = (f32[6,256,256]{2,1,0:T(8,128)}, bf16[1024,512]{1,0:T(8,128)(2,1)}, bf16[1024,512]{1,0:T(8,128)(2,1)}) custom-call(s32[24]{0:T(128)} %reshape.742.bounds, bf16[1536,256]{1,0:T(8,128)(2,1)} %fusion.48.refs_0_, bf16[1536,256]{1,0:T(8,128)(2,1)} %maximum_select_fusion.7.refs_1_, bf16[1536,256]{1,0:T(8,128)(2,1)} %get-tuple-element.109.refs_2_, ...), custom_call_target="tpu_custom_call" | custom-call | flops 15728640 | bytes 3670016 | tf_op jit(solution)/shard_map/back_halo/pallas_call | solution.py:320
  234.4 4.5 %collective-permute-start.26 = (bf16[1312,128]{1,0:T(8,128)(2,1)}, bf16[1312,128]{1,0:T(8,128)(2,1)S(1)}, u32[]{:S(2)}, u32[]{:S(2)}) collective-permute-start(bf16[1312,128]{1,0:T(8,128)(2,1)} %slice.743), channel_id=1, source_target_pairs={{0,16},{4,20},{8,24},{12,28},{16,0},{20,4},{24,8},{28,12},{1,17},{... | collective-permute-start | bytes 1007624 | tf_op jit(solution)/shard_map/ppermute | solution.py:483
  240.1 5.0 %collective-permute-start.23 = (bf16[1024,512]{1,0:T(8,128)(2,1)}, bf16[1024,512]{1,0:T(8,128)(2,1)}, u32[]{:S(2)}, u32[]{:S(2)}) collective-permute-start(bf16[1024,512]{1,0:T(8,128)(2,1)} %get-tuple-element.133), channel_id=1, source_target_pairs={{0,4},{4,8},{8,12},{12,16},{16,20},{20,24},{24,28},{1,5},{5,9},{9,... | collective-permute-start | bytes 3145736 | tf_op jit(solution)/shard_map/ppermute | solution.py:662
  245.1 33.5 %back_own.1 = (f32[1536,256]{1,0:T(8,128)}, f32[1536,512]{1,0:T(8,128)}) custom-call(s32[12]{0:T(128)} %reshape.743.bounds, bf16[1536,256]{1,0:T(8,128)(2,1)} %fusion.48.refs_0_, bf16[1536,256]{1,0:T(8,128)(2,1)} %maximum_select_fusion.7.refs_1_, bf16[1536,256]{1,0:T(8,128)(2,1)} %get-tuple-element.109.refs_2_, f32[6,1,1024]{2,1,0:T(1,128)} %get-tuple-element.125.refs_3_, ...), custom_call_target="tpu_custom_call" | custom-call | flops 15728640 | bytes 3145728 | tf_op jit(solution)/shard_map/back_own/pallas_call | solution.py:320
  287.2 2.7 fusion.165
  294.5 3.5 collective-permute-start.28
  301.8 2.7 convolution_add_fusion.4
  308.4 2.7 collective-permute-start.36
  313.9 11.6 %collective-permute-done.39 = bf16[1312,256]{1,0:T(8,128)(2,1)} collective-permute-done((bf16[1312,256]{1,0:T(8,128)(2,1)}, bf16[1312,256]{1,0:T(8,128)(2,1)}, u32[]{:S(2)}, u32[]{:S(2)}) %collective-permute-start.39) | collective-permute-done | bytes 671776 | tf_op jit(solution)/shard_map/ppermute | solution.py:480
  327.0 4.5 %collective-permute-done.36 = bf16[1824,256]{1,0:T(8,128)(2,1)S(1)} collective-permute-done((bf16[1824,256]{1,0:T(8,128)(2,1)S(1)}, bf16[1824,256]{1,0:T(8,128)(2,1)S(1)}, u32[]{:S(2)}, u32[]{:S(2)}) %collective-permute-start.36) | collective-permute-done | bytes 933920 | tf_op jit(solution)/shard_map/ppermute | solution.py:483
  331.8 2.8 collective-permute-start.30
  343.3 9.9 %collective-permute-done.40 = bf16[1312,128]{1,0:T(8,128)(2,1)S(1)} collective-permute-done((bf16[1312,128]{1,0:T(8,128)(2,1)S(1)}, bf16[1312,128]{1,0:T(8,128)(2,1)S(1)}, u32[]{:S(2)}, u32[]{:S(2)}) %collective-permute-start.40) | collective-permute-done | bytes 335904 | tf_op jit(solution)/shard_map/ppermute | solution.py:483
  354.1 7.8 %collective-permute-done.33 = bf16[768,256]{1,0:T(8,128)(2,1)S(1)} collective-permute-done((bf16[768,256]{1,0:T(8,128)(2,1)S(1)}, bf16[768,256]{1,0:T(8,128)(2,1)S(1)}, u32[]{:S(2)}, u32[]{:S(2)}) %collective-permute-start.33) | collective-permute-done | bytes 393248 | tf_op jit(solution)/shard_map/ppermute | solution.py:483
  366.0 4.8 %collective-permute-done.38 = bf16[1312,64]{1,0:T(8,128)(2,1)S(1)} collective-permute-done((bf16[1312,64]{1,0:T(8,128)(2,1)S(1)}, bf16[1312,64]{1,0:T(8,128)(2,1)S(1)}, u32[]{:S(2)}, u32[]{:S(2)}) %collective-permute-start.38) | collective-permute-done | bytes 167968 | tf_op jit(solution)/shard_map/ppermute | solution.py:480
  371.6 3.2 collective-permute-start.31
  374.8 8.9 %collective-permute-done.41 = bf16[1312,64]{1,0:T(8,128)(2,1)S(1)} collective-permute-done((bf16[1312,64]{1,0:T(8,128)(2,1)S(1)}, bf16[1312,64]{1,0:T(8,128)(2,1)S(1)}, u32[]{:S(2)}, u32[]{:S(2)}) %collective-permute-start.41) | collective-permute-done | bytes 167968 | tf_op jit(solution)/shard_map/ppermute | solution.py:483
  394.0 3.1 maximum_select_fusion.4
  397.1 3.4 collective-permute-done.35
  (398 shorter events, 183.1 us)
Async XLA Ops:
  2.8 24.6 %collective-permute-start = (bf16[768,512]{1,0:T(8,128)(2,1)}, bf16[768,512]{1,0:T(8,128)(2,1)}, u32[]{:S(2)}, u32[]{:S(2)}) collective-permute-start(bf16[768,512]{1,0:T(8,128)(2,1)} %constant_dynamic-slice_fusion.6), channel_id=1, source_target_pairs={{0,2},{2,0},{1,3},{3,1},{4,6},{6,4},{5,7},{7,5},{8,10},{10,8},{9,1... | collective-permute-start | bytes 2359304 | tf_op jit(solution)/shard_map/ppermute | solution.py:388
  6.2 34.4 %collective-permute-start.2 = (bf16[512,768]{0,1:T(8,128)(2,1)}, bf16[512,768]{0,1:T(8,128)(2,1)}, u32[]{:S(2)}, u32[]{:S(2)}) collective-permute-start(bf16[512,768]{0,1:T(8,128)(2,1)} %get-tuple-element.224), channel_id=1, source_target_pairs={{0,2},{2,0},{1,3},{3,1},{4,6},{6,4},{5,7},{7,5},{8,10},{10,8},{9,1... | collective-permute-start | bytes 2359304 | tf_op jit(solution)/shard_map/ppermute | solution.py:388
  17.6 77.3 %collective-permute-start.7 = (bf16[384,512]{1,0:T(8,128)(2,1)}, bf16[384,512]{1,0:T(8,128)(2,1)S(1)}, u32[]{:S(2)}, u32[]{:S(2)}) collective-permute-start(bf16[384,512]{1,0:T(8,128)(2,1)} %constant_dynamic-slice_fusion.2), channel_id=1, source_target_pairs={{0,2},{2,0},{1,3},{3,1},{4,6},{6,4},{5,7},{7,5},{8,10},{10,8},{9,1... | collective-permute-start | bytes 1179656 | tf_op jit(solution)/shard_map/ppermute | solution.py:388
  17.6 77.3 %collective-permute-start.6 = (bf16[512,512]{1,0:T(8,128)(2,1)}, bf16[512,512]{1,0:T(8,128)(2,1)}, u32[]{:S(2)}, u32[]{:S(2)}) collective-permute-start(bf16[512,512]{1,0:T(8,128)(2,1)} %convert_element_type.238), channel_id=1, source_target_pairs={{0,2},{2,0},{1,3},{3,1},{4,6},{6,4},{5,7},{7,5},{8,10},{10,8},{9,1... | collective-permute-start | bytes 1572872 | tf_op jit(solution)/shard_map/ppermute | solution.py:388
  19.0 75.8 %collective-permute-start.5 = (bf16[512,1312]{0,1:T(8,128)(2,1)}, bf16[512,1312]{0,1:T(8,128)(2,1)}, u32[]{:S(2)}, u32[]{:S(2)}) collective-permute-start(bf16[512,1312]{0,1:T(8,128)(2,1)} %fusion.61), channel_id=1, source_target_pairs={{0,2},{2,0},{1,3},{3,1},{4,6},{6,4},{5,7},{7,5},{8,10},{10,8},{9,1... | collective-permute-start | bytes 4030472 | tf_op jit(solution)/shard_map/ppermute | solution.py:388
  48.9 46.0 %collective-permute-start.4 = (bf16[1024,512]{1,0:T(8,128)(2,1)}, bf16[1024,512]{1,0:T(8,128)(2,1)}, u32[]{:S(2)}, u32[]{:S(2)}) collective-permute-start(bf16[1024,512]{1,0:T(8,128)(2,1)} %get-tuple-element.220), channel_id=1, source_target_pairs={{4,0},{8,4},{12,8},{16,12},{20,16},{24,20},{28,24},{5,1},{9,5},{13... | collective-permute-start | bytes 3145736 | tf_op jit(solution)/shard_map/ppermute | solution.py:524
  50.3 48.9 %collective-permute-start.3 = (bf16[1024,512]{1,0:T(8,128)(2,1)}, bf16[1024,512]{1,0:T(8,128)(2,1)}, u32[]{:S(2)}, u32[]{:S(2)}) collective-permute-start(bf16[1024,512]{1,0:T(8,128)(2,1)} %get-tuple-element.221), channel_id=1, source_target_pairs={{0,4},{4,8},{8,12},{12,16},{16,20},{20,24},{24,28},{1,5},{5,9},{9,... | collective-permute-start | bytes 3145736 | tf_op jit(solution)/shard_map/ppermute | solution.py:523
  99.2 17.2 %collective-permute-start.8 = (bf16[656,512]{1,0:T(8,128)(2,1)}, bf16[656,512]{1,0:T(8,128)(2,1)}, u32[]{:S(2)}, u32[]{:S(2)}) collective-permute-start(bf16[656,512]{1,0:T(8,128)(2,1)} %constant_dynamic-slice_fusion.3), channel_id=1, source_target_pairs={{0,2},{2,0},{1,3},{3,1},{4,6},{6,4},{5,7},{7,5},{8,10},{10,8},{9,1... | collective-permute-start | bytes 2015240 | tf_op jit(solution)/shard_map/ppermute | solution.py:388
  102.9 30.7 %collective-permute-start.14 = (bf16[512,1312]{0,1:T(8,128)(2,1)}, bf16[512,1312]{0,1:T(8,128)(2,1)}, u32[]{:S(2)}, u32[]{:S(2)}) collective-permute-start(bf16[512,1312]{0,1:T(8,128)(2,1)} %collective-permute-done.5), channel_id=1, source_target_pairs={{0,8},{4,12},{8,0},{12,4},{16,24},{20,28},{24,16},{28,20},{1,9},{5... | collective-permute-start | bytes 4030472 | tf_op jit(solution)/shard_map/ppermute | solution.py:483
  121.9 26.0 %collective-permute-start.13 = (bf16[656,512]{1,0:T(8,128)(2,1)}, bf16[656,512]{1,0:T(8,128)(2,1)}, u32[]{:S(2)}, u32[]{:S(2)}) collective-permute-start(bf16[656,512]{1,0:T(8,128)(2,1)} %collective-permute-done.8), channel_id=1, source_target_pairs={{0,8},{4,12},{8,0},{12,4},{16,24},{20,28},{24,16},{28,20},{1,9},{5... | collective-permute-start | bytes 2015240 | tf_op jit(solution)/shard_map/ppermute | solution.py:483
  161.5 15.7 %collective-permute-start.18 = (bf16[384,1024]{1,0:T(8,128)(2,1)S(1)}, bf16[384,1024]{1,0:T(8,128)(2,1)S(1)}, u32[]{:S(2)}, u32[]{:S(2)}) collective-permute-start(bf16[384,1024]{1,0:T(8,128)(2,1)S(1)} %fusion.34), channel_id=1, source_target_pairs={{0,1},{1,0},{2,3},{3,2},{4,5},{5,4},{6,7},{7,6},{8,9},{9,8},{10,11... | collective-permute-start | bytes 2359304 | tf_op jit(solution)/shard_map/ppermute | solution.py:391
  173.7 31.7 %collective-permute-start.17 = (bf16[1312,512]{1,0:T(8,128)(2,1)S(1)}, bf16[1312,512]{1,0:T(8,128)(2,1)S(1)}, u32[]{:S(2)}, u32[]{:S(2)}) collective-permute-start(bf16[1312,512]{1,0:T(8,128)(2,1)S(1)} %convolution_convert_fusion.2), channel_id=1, source_target_pairs={{0,4},{4,0},{8,12},{12,8},{16,20},{20,16},{24,28},{28,24},{1,5},{5... | collective-permute-start | bytes 4030472 | tf_op jit(solution)/shard_map/ppermute | solution.py:480
  177.8 15.0 %collective-permute-start.19 = (bf16[384,512]{1,0:T(8,128)(2,1)S(1)}, bf16[384,512]{1,0:T(8,128)(2,1)S(1)}, u32[]{:S(2)}, u32[]{:S(2)}) collective-permute-start(bf16[384,512]{1,0:T(8,128)(2,1)S(1)} %get-tuple-element.232), channel_id=1, source_target_pairs={{0,2},{2,0},{1,3},{3,1},{4,6},{6,4},{5,7},{7,5},{8,10},{10,8},{9,1... | collective-permute-start | bytes 1179656 | tf_op jit(solution)/shard_map/ppermute | solution.py:388
  183.4 31.8 %collective-permute-start.16 = (bf16[768,256]{1,0:T(8,128)(2,1)S(1)}, bf16[768,256]{1,0:T(8,128)(2,1)S(1)}, u32[]{:S(2)}, u32[]{:S(2)}) collective-permute-start(bf16[768,256]{1,0:T(8,128)(2,1)S(1)} %get-tuple-element.236), channel_id=1, source_target_pairs={{0,2},{2,0},{1,3},{3,1},{4,6},{6,4},{5,7},{7,5},{8,10},{10,8},{9,1... | collective-permute-start | bytes 1179656 | tf_op jit(solution)/shard_map/ppermute | solution.py:388
  210.0 20.8 %collective-permute-start.21 = (bf16[1312,256]{1,0:T(8,128)(2,1)}, bf16[1312,256]{1,0:T(8,128)(2,1)}, u32[]{:S(2)}, u32[]{:S(2)}) collective-permute-start(bf16[1312,256]{1,0:T(8,128)(2,1)} %slice.736), channel_id=1, source_target_pairs={{0,8},{4,12},{8,0},{12,4},{16,24},{20,28},{24,16},{28,20},{1,9},{5... | collective-permute-start | bytes 2015240 | tf_op jit(solution)/shard_map/ppermute | solution.py:483
  213.7 67.3 %collective-permute-start.25 = (bf16[512,512]{1,0:T(8,128)(2,1)}, bf16[512,512]{1,0:T(8,128)(2,1)}, u32[]{:S(2)}, u32[]{:S(2)}) collective-permute-start(bf16[512,512]{1,0:T(8,128)(2,1)} %convolution_convert_fusion.4), channel_id=1, source_target_pairs={{0,4},{4,0},{8,12},{12,8},{16,20},{20,16},{24,28},{28,24},{1,5},{5... | collective-permute-start | bytes 1572872 | tf_op jit(solution)/shard_map/ppermute | solution.py:480
  215.1 68.4 %collective-permute-start.24 = (bf16[2624,512]{1,0:T(8,128)(2,1)}, bf16[2624,512]{1,0:T(8,128)(2,1)}, u32[]{:S(2)}, u32[]{:S(2)}) collective-permute-start(bf16[2624,512]{1,0:T(8,128)(2,1)} %pad_maximum_fusion.1), channel_id=1, source_target_pairs={{0,2},{2,0},{1,3},{3,1},{4,6},{6,4},{5,7},{7,5},{8,10},{10,8},{9,1... | collective-permute-start | bytes 8060936 | tf_op jit(solution)/shard_map/ppermute | solution.py:388
  234.4 46.6 %collective-permute-start.26 = (bf16[1312,128]{1,0:T(8,128)(2,1)}, bf16[1312,128]{1,0:T(8,128)(2,1)S(1)}, u32[]{:S(2)}, u32[]{:S(2)}) collective-permute-start(bf16[1312,128]{1,0:T(8,128)(2,1)} %slice.743), channel_id=1, source_target_pairs={{0,16},{4,20},{8,24},{12,28},{16,0},{20,4},{24,8},{28,12},{1,17},{... | collective-permute-start | bytes 1007624 | tf_op jit(solution)/shard_map/ppermute | solution.py:483
  238.8 42.1 %collective-permute-start.22 = (bf16[1024,512]{1,0:T(8,128)(2,1)}, bf16[1024,512]{1,0:T(8,128)(2,1)}, u32[]{:S(2)}, u32[]{:S(2)}) collective-permute-start(bf16[1024,512]{1,0:T(8,128)(2,1)} %get-tuple-element.132), channel_id=1, source_target_pairs={{4,0},{8,4},{12,8},{16,12},{20,16},{24,20},{28,24},{5,1},{9,5},{13... | collective-permute-start | bytes 3145736 | tf_op jit(solution)/shard_map/ppermute | solution.py:661
  240.1 43.4 %collective-permute-start.23 = (bf16[1024,512]{1,0:T(8,128)(2,1)}, bf16[1024,512]{1,0:T(8,128)(2,1)}, u32[]{:S(2)}, u32[]{:S(2)}) collective-permute-start(bf16[1024,512]{1,0:T(8,128)(2,1)} %get-tuple-element.133), channel_id=1, source_target_pairs={{0,4},{4,8},{8,12},{12,16},{16,20},{20,24},{24,28},{1,5},{5,9},{9,... | collective-permute-start | bytes 3145736 | tf_op jit(solution)/shard_map/ppermute | solution.py:662
  292.3 39.5 %collective-permute-start.32 = (bf16[768,512]{1,0:T(8,128)(2,1)}, bf16[768,512]{1,0:T(8,128)(2,1)}, u32[]{:S(2)}, u32[]{:S(2)}) collective-permute-start(bf16[768,512]{1,0:T(8,128)(2,1)} %fusion.58), channel_id=1, source_target_pairs={{0,4},{4,0},{8,12},{12,8},{16,20},{20,16},{24,28},{28,24},{1,5},{5... | collective-permute-start | bytes 2359304 | tf_op jit(solution)/shard_map/ppermute | solution.py:480
  294.5 46.0 %collective-permute-start.28 = (bf16[768,512]{1,0:T(8,128)(2,1)S(1)}, bf16[768,512]{1,0:T(8,128)(2,1)S(1)}, u32[]{:S(2)}, u32[]{:S(2)}) collective-permute-start(bf16[768,512]{1,0:T(8,128)(2,1)S(1)} %copy-done.31), channel_id=1, source_target_pairs={{0,2},{3,1},{4,6},{7,5},{8,10},{11,9},{12,14},{15,13},{16,18},{19,... | collective-permute-start | bytes 2359304 | tf_op jit(solution)/shard_map/ppermute | solution.py:694
  308.1 17.4 %collective-permute-start.39 = (bf16[1312,256]{1,0:T(8,128)(2,1)}, bf16[1312,256]{1,0:T(8,128)(2,1)}, u32[]{:S(2)}, u32[]{:S(2)}) collective-permute-start(bf16[1312,256]{1,0:T(8,128)(2,1)} %slice.734), channel_id=1, source_target_pairs={{0,4},{4,0},{8,12},{12,8},{16,20},{20,16},{24,28},{28,24},{1,5},{5... | collective-permute-start | bytes 2015240 | tf_op jit(solution)/shard_map/ppermute | solution.py:480
  308.4 23.1 %collective-permute-start.36 = (bf16[1824,256]{1,0:T(8,128)(2,1)S(1)}, bf16[1824,256]{1,0:T(8,128)(2,1)S(1)}, u32[]{:S(2)}, u32[]{:S(2)}) collective-permute-start(bf16[1824,256]{1,0:T(8,128)(2,1)S(1)} %pad_maximum_fusion.5), channel_id=1, source_target_pairs={{0,8},{4,12},{8,0},{12,4},{16,24},{20,28},{24,16},{28,20},{1,9},{5... | collective-permute-start | bytes 2801672 | tf_op jit(solution)/shard_map/ppermute | solution.py:483
  334.8 18.4 %collective-permute-start.40 = (bf16[1312,128]{1,0:T(8,128)(2,1)S(1)}, bf16[1312,128]{1,0:T(8,128)(2,1)S(1)}, u32[]{:S(2)}, u32[]{:S(2)}) collective-permute-start(bf16[1312,128]{1,0:T(8,128)(2,1)S(1)} %slice.740), channel_id=1, source_target_pairs={{0,8},{4,12},{8,0},{12,4},{16,24},{20,28},{24,16},{28,20},{1,9},{5... | collective-permute-start | bytes 1007624 | tf_op jit(solution)/shard_map/ppermute | solution.py:483
  337.6 24.3 %collective-permute-start.33 = (bf16[768,256]{1,0:T(8,128)(2,1)S(1)}, bf16[768,256]{1,0:T(8,128)(2,1)S(1)}, u32[]{:S(2)}, u32[]{:S(2)}) collective-permute-start(bf16[768,256]{1,0:T(8,128)(2,1)S(1)} %slice.737), channel_id=1, source_target_pairs={{0,8},{4,12},{8,0},{12,4},{16,24},{20,28},{24,16},{28,20},{1,9},{5... | collective-permute-start | bytes 1179656 | tf_op jit(solution)/shard_map/ppermute | solution.py:483
  337.9 25.3 %collective-permute-start.37 = (bf16[1824,128]{1,0:T(8,128)(2,1)S(1)}, bf16[1824,128]{1,0:T(8,128)(2,1)S(1)}, u32[]{:S(2)}, u32[]{:S(2)}) collective-permute-start(bf16[1824,128]{1,0:T(8,128)(2,1)S(1)} %pad_maximum_fusion.7), channel_id=1, source_target_pairs={{0,16},{4,20},{8,24},{12,28},{16,0},{20,4},{24,8},{28,12},{1,17},{... | collective-permute-start | bytes 1400840 | tf_op jit(solution)/shard_map/ppermute | solution.py:483
  340.5 30.4 %collective-permute-start.29 = (bf16[768,512]{1,0:T(8,128)(2,1)S(1)}, bf16[768,512]{1,0:T(8,128)(2,1)S(1)}, u32[]{:S(2)}, u32[]{:S(2)}) collective-permute-start(bf16[768,512]{1,0:T(8,128)(2,1)S(1)} %slice.732), channel_id=1, source_target_pairs={{0,2},{2,0},{1,3},{3,1},{4,6},{6,4},{5,7},{7,5},{8,10},{10,8},{9,1... | collective-permute-start | bytes 2359304 | tf_op jit(solution)/shard_map/ppermute | solution.py:388
  353.4 30.3 %collective-permute-start.41 = (bf16[1312,64]{1,0:T(8,128)(2,1)S(1)}, bf16[1312,64]{1,0:T(8,128)(2,1)S(1)}, u32[]{:S(2)}, u32[]{:S(2)}) collective-permute-start(bf16[1312,64]{1,0:T(8,128)(2,1)S(1)} %slice.739), channel_id=1, source_target_pairs={{0,16},{4,20},{8,24},{12,28},{16,0},{20,4},{24,8},{28,12},{1,17},{... | collective-permute-start | bytes 503816 | tf_op jit(solution)/shard_map/ppermute | solution.py:483
  362.8 25.3 %collective-permute-start.34 = (bf16[768,128]{1,0:T(8,128)(2,1)}, bf16[768,128]{1,0:T(8,128)(2,1)}, u32[]{:S(2)}, u32[]{:S(2)}) collective-permute-start(bf16[768,128]{1,0:T(8,128)(2,1)} %slice.745), channel_id=1, source_target_pairs={{0,16},{4,20},{8,24},{12,28},{16,0},{20,4},{24,8},{28,12},{1,17},{... | collective-permute-start | bytes 589832 | tf_op jit(solution)/shard_map/ppermute | solution.py:483
  366.0 22.0 %collective-permute-start.43 = (bf16[1824,64]{1,0:T(8,128)(2,1)}, bf16[1824,64]{1,0:T(8,128)(2,1)S(1)}, u32[]{:S(2)}, u32[]{:S(2)}) collective-permute-start(bf16[1824,64]{1,0:T(8,128)(2,1)} %pad_maximum_fusion.8), channel_id=1, source_target_pairs={{0,2},{2,0},{1,3},{3,1},{4,6},{6,4},{5,7},{7,5},{8,10},{10,8},{9,1... | collective-permute-start | bytes 700424 | tf_op jit(solution)/shard_map/ppermute | solution.py:388
  371.6 22.4 %collective-permute-start.31 = (bf16[768,512]{1,0:T(8,128)(2,1)S(1)}, bf16[768,512]{1,0:T(8,128)(2,1)}, u32[]{:S(2)}, u32[]{:S(2)}) collective-permute-start(bf16[768,512]{1,0:T(8,128)(2,1)S(1)} %fusion.42), channel_id=1, source_target_pairs={{0,1},{1,0},{2,3},{3,2},{4,5},{5,4},{6,7},{7,6},{8,9},{9,8},{10,11... | collective-permute-start | bytes 2359304 | tf_op jit(solution)/shard_map/ppermute | solution.py:391
  (85 other events, 1006.6 us)

commit v6 on v5

--- a/solution.py
+++ b/solution.py
@@ -645,9 +645,9 @@
     if two:
         h2, da, du, o_heads, dx_late = after((h2, da, du, own_first(o_rows, 1), dx_low), do_rows)
         dx_y = relative(dx_late, "yzZx")
-        h_act, h_lin = relative(h2, "xzZy"), relative(h2, "xyzZ")
+        h_x = relative(h2, "xyzZ")
         proj_got = to_y(product(o_heads, dx_y))
-        gate_send = jnp.concatenate([product(da, h_act), product(du, h_lin)], axis=0)
+        gate_send = jnp.concatenate([product(da, h_x), product(du, h_x)], axis=0)
         gate_got = to_row(after(gate_send, do_got))
         pair = ordered(zrow, y_half[None, :, :Dl], after(y_got, gate_send)[None], 0)
         layer_out = ordered(zcol, pair[:, None], to_col(pair)[:, None], 1).reshape(S, Dl)
@@ -711,24 +711,30 @@
 
     if two:
         query = halved(dt, h1_y, after(to_y(query_send), kept))
-        n = F
-        act = halved(da, h_act, gate_got[:n])
-        lin = halved(du, h_lin, gate_got[n:])
+
+        def pair(one, other):
+            return jnp.concatenate([second(one), second(other)], axis=0)
+
+        def joined_pair(one, other, got):
+            n = one.shape[0]
+            return joined(one, got[:n]), joined(other, got[n:])
+
+        gate_got = after(gate_got, kept)
+        act, lin = halved(da, h_x, gate_got[:F]), halved(du, h_x, gate_got[F:])
+        gate_got = to_y(pair(act, lin))
         proj = halved(o_heads, dx_y, proj_got)
-        both_got = after(to_z(jnp.concatenate([second(act), second(proj)], axis=0), 1), kept)
-        lin = joined(lin, after(to_y(second(lin)), kept))
-        act, proj = joined(act, both_got[:n]), joined(proj, both_got[n:])
-        both_got = to_z(jnp.concatenate([second(act), second(proj)], axis=0), 2)
-        lin = joined(lin, to_z(second(lin), 1))
-        act, proj = joined(act, both_got[:n]), joined(proj, both_got[n:])
+        query, proj = joined_pair(query, proj, to_z(pair(query, proj), 1))
+        act, lin = joined_pair(act, lin, after(gate_got, query))
+        gate_got = to_z(pair(act, lin), 1)
+        query, proj = joined_pair(query, proj, to_z(pair(query, proj), 2))
+        act, lin = joined_pair(act, lin, after(gate_got, dx))
         lower = joined(lower, lower_got)
-        last_got = after(to_row(jnp.concatenate([second(lower), second(proj)], axis=0)), dx)
-        lower, proj = joined(lower, last_got[:n]), joined(proj, last_got[n:])
-        act = joined(act, to_y(second(act)))
-        lin = joined(lin, after(to_z(second(lin), 2), dx))
+        last_got = after(to_row(pair(lower, proj)), dx)
+        gate_got = to_z(pair(act, lin).T, 2).T
+        lower, proj = joined_pair(lower, proj, last_got)
+        act, lin = joined_pair(act, lin, gate_got)
         gate = jnp.stack([act.T, lin.T])
-        query = joined(query, to_z(second(query), 1))
-        query = joined(query, after(to_z(second(query), 2), dx)).T
+        query = query.T
         wq_rows = take(wq, b ^ (4 * r), Db)
         place = (2 * b + r) ^ (8 * r)
         wi_rows = jnp.stack(

time: 412 us -> 422 us (1.024)
  Pallas kernels: 82.4 us -> 68.3 us
  waiting for transfers between devices: 80 us -> 91.6 us
  other arithmetic: 62.3 us -> 69.8 us
  local copies, waits for them, and re-layouts: 42.9 us -> 49.7 us
    ppermute x10 -> x8, waiting for transfers between devices: 38.1 us -> 54.5 us  [to_z(): return lax.ppermute(a, 'dp', [(i, i ^ 2 * j) for i in range(B)])]
    ppermute x5 -> x4, waiting for transfers between devices: 29.2 us -> 15.4 us  [to_y(): return lax.ppermute(a, 'dp', [(i, i ^ 1) for i in range(B)])]
    pallas_call x2, Pallas kernels: 46.3 us -> 38.3 us  [attend_back_call(): pl.pallas_call(functools.partial(backward_kernel, heads, sets, final), gr...]
    pallas_call x2, Pallas kernels: 36.1 us -> 30 us  [attend_call(): pl.pallas_call(functools.partial(forward_kernel, heads, sets, final), gri...]
    ppermute x1, waiting for transfers between devices: 4.37 us -> 9.69 us  [local(): kv_left = lax.ppermute(kv[S - H:], 'dp', up)]
    add x11 -> x9, other arithmetic: 3.79 us -> 8.99 us  [joined(): return first(part).astype(f32) + got.astype(f32)]
    dot_general x15 -> x14, matrix products: 31.3 us -> 27.9 us  [nn(): return jnp.dot(a, b, preferred_element_type=f32)]
    ppermute x10 -> x8, starting transfers between devices: 16.4 us -> 18.5 us  [to_z(): return lax.ppermute(a, 'dp', [(i, i ^ 2 * j) for i in range(B)])]
  transfers between devices with their start and end apart: 44 -> 41, of which waited for: 15 -> 11; matrix products, arithmetic and copies ran while one was open for 35% -> 36% of each run, Pallas kernels for 20% -> 16%
where the time goes in v6:
time: 422 us; the launch traced here: 414 us
  waiting for transfers between devices  91.6 us (22%)
  other arithmetic  69.8 us (17%)
  Pallas kernels  68.3 us (16%)
  starting transfers between devices  66.6 us (16%)
  matrix products  65.7 us (16%)
  local copies, waits for them, and re-layouts  49.7 us (12%)
    ppermute x8, waiting for transfers between devices, to_z(): return lax.ppermute(a, 'dp', [(i, i ^ 2 * j) for i in range(B)])  54.5 us
    pallas_call x2, Pallas kernels, attend_back_call(): pl.pallas_call(functools.partial(backward_kernel, heads, sets, final), gr...  38.3 us
    pallas_call x2, Pallas kernels, attend_call(): pl.pallas_call(functools.partial(forward_kernel, heads, sets, final), gri...  30 us
    dot_general x14, matrix products, nn(): return jnp.dot(a, b, preferred_element_type=f32)  27.9 us
    dot_general x8, matrix products, nt(): lax.dot_general(a, b, (((1,), (1,)), ((), ())), preferred_element_type=f32)  19.4 us
    ppermute x8, starting transfers between devices, to_z(): return lax.ppermute(a, 'dp', [(i, i ^ 2 * j) for i in range(B)])  18.5 us
    dot_general x10, matrix products, tn(): lax.dot_general(a, b, (((0,), (0,)), ((), ())), preferred_element_type=f32)  16.9 us
    ppermute x4, waiting for transfers between devices, to_y(): return lax.ppermute(a, 'dp', [(i, i ^ 1) for i in range(B)])  15.4 us
  transfers between devices with their start and end apart: 41, of which 11 were waited for; matrix products, arithmetic and copies ran while one was open for 36% of the time, Pallas kernels for 16%

profile of v6, /device:TPU:3, one launch (start us, length us, event | category | flops | bytes accessed | tf_op | source)
XLA Modules:
  0.0 414.1 jit_solution(9352482440802651742)
XLA Ops:
  8.8 2.8 multiply_sine_fusion
  15.1 3.0 fusion.58
  50.0 4.8 %collective-permute-start.3 = (bf16[1024,512]{1,0:T(8,128)(2,1)}, bf16[1024,512]{1,0:T(8,128)(2,1)}, u32[]{:S(2)}, u32[]{:S(2)}) collective-permute-start(bf16[1024,512]{1,0:T(8,128)(2,1)} %get-tuple-element.227), channel_id=1, source_target_pairs={{0,4},{4,8},{8,12},{12,16},{16,20},{20,24},{24,28},{1,5},{5,9},{9,... | collective-permute-start | bytes 3145736 | tf_op jit(solution)/shard_map/ppermute | solution.py:523
  56.2 5.2 %fusion.15 = bf16[1536,1024]{1,0:T(8,128)(2,1)} fusion(bf16[1536,1024]{1,0:T(8,128)(2,1)S(1)} %fusion.4, s32[1024]{0:T(1024)S(1)} %add_xor_fusion.2), kind=kOutput, calls=%fused_computation.27 | convolution fusion | flops 3223846912 | bytes 6295552 | tf_op jit(solution)/shard_map/dot_general | solution.py:32
  69.9 19.4 %attend_own.1 = (f32[6,256,256]{2,1,0:T(8,128)}, f32[6,2,1024]{2,1,0:T(2,128)}) custom-call(s32[12]{0:T(128)} %reshape.735.bounds, bf16[1536,256]{1,0:T(8,128)(2,1)} %fusion.45.refs_0_, s32[6,1,256]{2,1,0:T(1,128)} %select_n.645.refs_1_.refs_4_, bf16[1536,512]{1,0:T(8,128)(2,1)} %copy-done.4, s32[1536,128]{1,0:T(8,128)} %broadcast_in_dim.132.refs_3_.refs_6_), custom_call_target="tpu_custom_call" | custom-call | flops 6291456 | bytes 3145728 | tf_op jit(solution)/shard_map/attend_own/pallas_call | solution.py:194
  89.4 9.7 %collective-permute-done.3.refs_2_.refs_5_ = bf16[1024,512]{1,0:T(8,128)(2,1)} collective-permute-done((bf16[1024,512]{1,0:T(8,128)(2,1)}, bf16[1024,512]{1,0:T(8,128)(2,1)}, u32[]{:S(2)}, u32[]{:S(2)}) %collective-permute-start.3) | collective-permute-done | bytes 1048608 | tf_op jit(solution)/shard_map/ppermute | solution.py:523
  102.7 3.6 collective-permute-start.14
  106.3 10.6 %attend_final.1 = (bf16[1536,256]{1,0:T(8,128)(2,1)}, f32[6,1,1024]{2,1,0:T(1,128)}) custom-call(s32[24]{0:T(128)} %reshape.734.bounds, bf16[1536,256]{1,0:T(8,128)(2,1)} %fusion.45.refs_0_, s32[6,1,256]{2,1,0:T(1,128)} %select_n.645.refs_1_.refs_4_, bf16[1024,512]{1,0:T(8,128)(2,1)} %collective-permute-done.3.refs_2_.refs_5_, ...), custom_call_target="tpu_custom_call" | custom-call | flops 6291456 | bytes 3670016 | tf_op jit(solution)/shard_map/attend_final/pallas_call | solution.py:194
  125.4 3.7 collective-permute-start.13
  132.9 2.9 collective-permute-done.14
  146.6 3.5 collective-permute-done.13
  150.1 7.1 %multiply_convert_fusion = (bf16[768,1312]{0,1:T(8,128)(2,1)}, bf16[768,1312]{0,1:T(8,128)(2,1)}, bf16[768,1312]{0,1:T(8,128)(2,1)}) fusion(f32[768,1312]{0,1:T(8,128)S(1)} %convolution_add_fusion.1, f32[768,1312]{0,1:T(8,128)S(1)} %convolution_add_fusion, f32[768,1312]{0,1:T(8,128)S(1)} %fusion.73, bf16[656,512]{1,0:T(8,128)(2,1)} %collective-permute-done.13, ...), kind=kOutput, calls=%fused_computation.24 | convolution fusion | flops 1054973952 | bytes 20267008 | tf_op jit(solution)/shard_map/dot_general | solution.py:24
  157.2 3.1 fusion.161
  168.1 3.2 fusion.96
  179.5 3.1 fusion.153
  191.1 15.3 %collective-permute-done.17 = bf16[1312,512]{1,0:T(8,128)(2,1)S(1)} collective-permute-done((bf16[1312,512]{1,0:T(8,128)(2,1)S(1)}, bf16[1312,512]{1,0:T(8,128)(2,1)S(1)}, u32[]{:S(2)}, u32[]{:S(2)}) %collective-permute-start.17) | collective-permute-done | bytes 1343520 | tf_op jit(solution)/shard_map/ppermute | solution.py:480
  218.3 12.3 %back_halo.1 = (f32[6,256,256]{2,1,0:T(8,128)}, bf16[1024,512]{1,0:T(8,128)(2,1)}, bf16[1024,512]{1,0:T(8,128)(2,1)}) custom-call(s32[24]{0:T(128)} %reshape.734.bounds, bf16[1536,256]{1,0:T(8,128)(2,1)} %fusion.45.refs_0_, bf16[1536,256]{1,0:T(8,128)(2,1)} %maximum_select_fusion.7.refs_1_, bf16[1536,256]{1,0:T(8,128)(2,1)} %get-tuple-element.108.refs_2_, ...), custom_call_target="tpu_custom_call" | custom-call | flops 15728640 | bytes 3670016 | tf_op jit(solution)/shard_map/back_halo/pallas_call | solution.py:320
  235.5 8.6 %collective-permute-start.23 = (bf16[1024,512]{1,0:T(8,128)(2,1)}, bf16[1024,512]{1,0:T(8,128)(2,1)}, u32[]{:S(2)}, u32[]{:S(2)}) collective-permute-start(bf16[1024,512]{1,0:T(8,128)(2,1)} %get-tuple-element.132), channel_id=1, source_target_pairs={{0,4},{4,8},{8,12},{12,16},{16,20},{20,24},{24,28},{1,5},{5,9},{9,... | collective-permute-start | bytes 3145736 | tf_op jit(solution)/shard_map/ppermute | solution.py:662
  244.2 4.2 %collective-permute-start.26 = (bf16[1312,128]{1,0:T(8,128)(2,1)}, bf16[1312,128]{1,0:T(8,128)(2,1)S(1)}, u32[]{:S(2)}, u32[]{:S(2)}) collective-permute-start(bf16[1312,128]{1,0:T(8,128)(2,1)} %slice.773), channel_id=1, source_target_pairs={{0,16},{4,20},{8,24},{12,28},{16,0},{20,4},{24,8},{28,12},{1,17},{... | collective-permute-start | bytes 1007624 | tf_op jit(solution)/shard_map/ppermute | solution.py:483
  248.3 26.0 %back_own.1 = (f32[1536,256]{1,0:T(8,128)}, f32[1536,512]{1,0:T(8,128)}) custom-call(s32[12]{0:T(128)} %reshape.735.bounds, bf16[1536,256]{1,0:T(8,128)(2,1)} %fusion.45.refs_0_, bf16[1536,256]{1,0:T(8,128)(2,1)} %maximum_select_fusion.7.refs_1_, bf16[1536,256]{1,0:T(8,128)(2,1)} %get-tuple-element.108.refs_2_, f32[6,1,1024]{2,1,0:T(1,128)} %get-tuple-element.124.refs_3_, ...), custom_call_target="tpu_custom_call" | custom-call | flops 15728640 | bytes 3145728 | tf_op jit(solution)/shard_map/back_own/pallas_call | solution.py:320
  276.6 5.6 %collective-permute-done.26 = bf16[1312,128]{1,0:T(8,128)(2,1)S(1)} collective-permute-done((bf16[1312,128]{1,0:T(8,128)(2,1)}, bf16[1312,128]{1,0:T(8,128)(2,1)S(1)}, u32[]{:S(2)}, u32[]{:S(2)}) %collective-permute-start.26) | collective-permute-done | bytes 335904 | tf_op jit(solution)/shard_map/ppermute | solution.py:483
  282.2 5.8 %collective-permute-done.23 = bf16[1024,512]{1,0:T(8,128)(2,1)} collective-permute-done((bf16[1024,512]{1,0:T(8,128)(2,1)}, bf16[1024,512]{1,0:T(8,128)(2,1)}, u32[]{:S(2)}, u32[]{:S(2)}) %collective-permute-start.23) | collective-permute-done | bytes 1048608 | tf_op jit(solution)/shard_map/ppermute | solution.py:662
  295.6 3.5 collective-permute-start.28
  313.0 3.4 convolution_add_fusion.4
  320.9 2.9 collective-permute-start.33
  328.0 9.0 %collective-permute-done.33 = bf16[1280,256]{1,0:T(8,128)(2,1)S(1)} collective-permute-done((bf16[1280,256]{1,0:T(8,128)(2,1)S(1)}, bf16[1280,256]{1,0:T(8,128)(2,1)S(1)}, u32[]{:S(2)}, u32[]{:S(2)}) %collective-permute-start.33) | collective-permute-done | bytes 655392 | tf_op jit(solution)/shard_map/ppermute | solution.py:483
  342.8 11.5 %collective-permute-done.34 = bf16[1280,128]{1,0:T(8,128)(2,1)S(1)} collective-permute-done((bf16[1280,128]{1,0:T(8,128)(2,1)S(1)}, bf16[1280,128]{1,0:T(8,128)(2,1)S(1)}, u32[]{:S(2)}, u32[]{:S(2)}) %collective-permute-start.34) | collective-permute-done | bytes 327712 | tf_op jit(solution)/shard_map/ppermute | solution.py:483
  360.6 6.2 %collective-permute-done.40 = bf16[1824,64]{1,0:T(8,128)(2,1)S(1)} collective-permute-done((bf16[1824,64]{1,0:T(8,128)(2,1)S(1)}, bf16[1824,64]{1,0:T(8,128)(2,1)S(1)}, u32[]{:S(2)}, u32[]{:S(2)}) %collective-permute-start.40) | collective-permute-done | bytes 233504 | tf_op jit(solution)/shard_map/ppermute | solution.py:388
  366.8 3.6 slice_add_fusion.2
  376.3 9.7 %collective-permute-done.37 = bf16[2624,128]{1,0:T(8,128)(2,1)} collective-permute-done((bf16[2624,128]{1,0:T(8,128)(2,1)}, bf16[2624,128]{1,0:T(8,128)(2,1)}, u32[]{:S(2)}, u32[]{:S(2)}) %collective-permute-start.37) | collective-permute-done | bytes 671776 | tf_op jit(solution)/shard_map/ppermute | solution.py:483
  388.5 3.0 maximum_select_fusion.4
  393.5 12.4 %collective-permute-done.38 = bf16[64,2624]{1,0:T(8,128)(2,1)} collective-permute-done((bf16[64,2624]{1,0:T(8,128)(2,1)S(1)}, bf16[64,2624]{1,0:T(8,128)(2,1)}, u32[]{:S(2)}, u32[]{:S(2)}) %collective-permute-start.38) | collective-permute-done | bytes 335904 | tf_op jit(solution)/shard_map/ppermute | solution.py:483
  (393 shorter events, 182.9 us)
Async XLA Ops:
  2.8 25.1 %collective-permute-start = (bf16[768,512]{1,0:T(8,128)(2,1)}, bf16[768,512]{1,0:T(8,128)(2,1)}, u32[]{:S(2)}, u32[]{:S(2)}) collective-permute-start(bf16[768,512]{1,0:T(8,128)(2,1)} %constant_dynamic-slice_fusion.6), channel_id=1, source_target_pairs={{0,2},{2,0},{1,3},{3,1},{4,6},{6,4},{5,7},{7,5},{8,10},{10,8},{9,1... | collective-permute-start | bytes 2359304 | tf_op jit(solution)/shard_map/ppermute | solution.py:388
  6.2 35.5 %collective-permute-start.2 = (bf16[512,768]{0,1:T(8,128)(2,1)}, bf16[512,768]{0,1:T(8,128)(2,1)}, u32[]{:S(2)}, u32[]{:S(2)}) collective-permute-start(bf16[512,768]{0,1:T(8,128)(2,1)} %get-tuple-element.230), channel_id=1, source_target_pairs={{0,2},{2,0},{1,3},{3,1},{4,6},{6,4},{5,7},{7,5},{8,10},{10,8},{9,1... | collective-permute-start | bytes 2359304 | tf_op jit(solution)/shard_map/ppermute | solution.py:388
  18.1 71.3 %collective-permute-start.5 = (bf16[512,1312]{0,1:T(8,128)(2,1)}, bf16[512,1312]{0,1:T(8,128)(2,1)}, u32[]{:S(2)}, u32[]{:S(2)}) collective-permute-start(bf16[512,1312]{0,1:T(8,128)(2,1)} %fusion.58), channel_id=1, source_target_pairs={{0,2},{2,0},{1,3},{3,1},{4,6},{6,4},{5,7},{7,5},{8,10},{10,8},{9,1... | collective-permute-start | bytes 4030472 | tf_op jit(solution)/shard_map/ppermute | solution.py:388
  18.1 71.3 %collective-permute-start.6 = (bf16[512,512]{1,0:T(8,128)(2,1)}, bf16[512,512]{1,0:T(8,128)(2,1)}, u32[]{:S(2)}, u32[]{:S(2)}) collective-permute-start(bf16[512,512]{1,0:T(8,128)(2,1)} %convert_element_type.234), channel_id=1, source_target_pairs={{0,2},{2,0},{1,3},{3,1},{4,6},{6,4},{5,7},{7,5},{8,10},{10,8},{9,1... | collective-permute-start | bytes 1572872 | tf_op jit(solution)/shard_map/ppermute | solution.py:388
  19.6 69.8 %collective-permute-start.7 = (bf16[384,512]{1,0:T(8,128)(2,1)}, bf16[384,512]{1,0:T(8,128)(2,1)S(1)}, u32[]{:S(2)}, u32[]{:S(2)}) collective-permute-start(bf16[384,512]{1,0:T(8,128)(2,1)} %constant_dynamic-slice_fusion.2), channel_id=1, source_target_pairs={{0,2},{2,0},{1,3},{3,1},{4,6},{6,4},{5,7},{7,5},{8,10},{10,8},{9,1... | collective-permute-start | bytes 1179656 | tf_op jit(solution)/shard_map/ppermute | solution.py:388
  50.0 49.1 %collective-permute-start.3 = (bf16[1024,512]{1,0:T(8,128)(2,1)}, bf16[1024,512]{1,0:T(8,128)(2,1)}, u32[]{:S(2)}, u32[]{:S(2)}) collective-permute-start(bf16[1024,512]{1,0:T(8,128)(2,1)} %get-tuple-element.227), channel_id=1, source_target_pairs={{0,4},{4,8},{8,12},{12,16},{16,20},{20,24},{24,28},{1,5},{5,9},{9,... | collective-permute-start | bytes 3145736 | tf_op jit(solution)/shard_map/ppermute | solution.py:523
  54.8 44.3 %collective-permute-start.4 = (bf16[1024,512]{1,0:T(8,128)(2,1)}, bf16[1024,512]{1,0:T(8,128)(2,1)}, u32[]{:S(2)}, u32[]{:S(2)}) collective-permute-start(bf16[1024,512]{1,0:T(8,128)(2,1)} %get-tuple-element.226), channel_id=1, source_target_pairs={{4,0},{8,4},{12,8},{16,12},{20,16},{24,20},{28,24},{5,1},{9,5},{13... | collective-permute-start | bytes 3145736 | tf_op jit(solution)/shard_map/ppermute | solution.py:524
  99.1 17.9 %collective-permute-start.8 = (bf16[656,512]{1,0:T(8,128)(2,1)}, bf16[656,512]{1,0:T(8,128)(2,1)}, u32[]{:S(2)}, u32[]{:S(2)}) collective-permute-start(bf16[656,512]{1,0:T(8,128)(2,1)} %constant_dynamic-slice_fusion.3), channel_id=1, source_target_pairs={{0,2},{2,0},{1,3},{3,1},{4,6},{6,4},{5,7},{7,5},{8,10},{10,8},{9,1... | collective-permute-start | bytes 2015240 | tf_op jit(solution)/shard_map/ppermute | solution.py:388
  102.7 33.1 %collective-permute-start.14 = (bf16[512,1312]{0,1:T(8,128)(2,1)}, bf16[512,1312]{0,1:T(8,128)(2,1)}, u32[]{:S(2)}, u32[]{:S(2)}) collective-permute-start(bf16[512,1312]{0,1:T(8,128)(2,1)} %collective-permute-done.5), channel_id=1, source_target_pairs={{0,8},{4,12},{8,0},{12,4},{16,24},{20,28},{24,16},{28,20},{1,9},{5... | collective-permute-start | bytes 4030472 | tf_op jit(solution)/shard_map/ppermute | solution.py:483
  125.3 12.4 %collective-permute-start.12 = (bf16[512,1024]{1,0:T(8,128)(2,1)S(1)}, bf16[512,1024]{1,0:T(8,128)(2,1)S(1)}, u32[]{:S(2)}, u32[]{:S(2)}) collective-permute-start(bf16[512,1024]{1,0:T(8,128)(2,1)S(1)} %fusion.62), channel_id=1, source_target_pairs={{0,1},{1,0},{2,3},{3,2},{4,5},{5,4},{6,7},{7,6},{8,9},{9,8},{10,11... | collective-permute-start | bytes 3145736 | tf_op jit(solution)/shard_map/ppermute | solution.py:391
  125.4 24.7 %collective-permute-start.13 = (bf16[656,512]{1,0:T(8,128)(2,1)}, bf16[656,512]{1,0:T(8,128)(2,1)}, u32[]{:S(2)}, u32[]{:S(2)}) collective-permute-start(bf16[656,512]{1,0:T(8,128)(2,1)} %collective-permute-done.8), channel_id=1, source_target_pairs={{0,8},{4,12},{8,0},{12,4},{16,24},{20,28},{24,16},{28,20},{1,9},{5... | collective-permute-start | bytes 2015240 | tf_op jit(solution)/shard_map/ppermute | solution.py:483
  165.0 13.0 %collective-permute-start.15 = (bf16[768,1024]{1,0:T(8,128)(2,1)S(1)}, bf16[768,1024]{1,0:T(8,128)(2,1)S(1)}, u32[]{:S(2)}, u32[]{:S(2)}) collective-permute-start(bf16[768,1024]{1,0:T(8,128)(2,1)S(1)} %fusion.152), channel_id=1, source_target_pairs={{0,1},{1,0},{2,3},{3,2},{4,5},{5,4},{6,7},{7,6},{8,9},{9,8},{10,11... | collective-permute-start | bytes 4718600 | tf_op jit(solution)/shard_map/ppermute | solution.py:391
  175.9 30.6 %collective-permute-start.17 = (bf16[1312,512]{1,0:T(8,128)(2,1)S(1)}, bf16[1312,512]{1,0:T(8,128)(2,1)S(1)}, u32[]{:S(2)}, u32[]{:S(2)}) collective-permute-start(bf16[1312,512]{1,0:T(8,128)(2,1)S(1)} %convolution_convert_fusion.2), channel_id=1, source_target_pairs={{0,4},{4,0},{8,12},{12,8},{16,20},{20,16},{24,28},{28,24},{1,5},{5... | collective-permute-start | bytes 4030472 | tf_op jit(solution)/shard_map/ppermute | solution.py:480
  177.9 28.6 %collective-permute-start.19 = (bf16[384,512]{1,0:T(8,128)(2,1)S(1)}, bf16[384,512]{1,0:T(8,128)(2,1)S(1)}, u32[]{:S(2)}, u32[]{:S(2)}) collective-permute-start(bf16[384,512]{1,0:T(8,128)(2,1)S(1)} %get-tuple-element.240), channel_id=1, source_target_pairs={{0,2},{2,0},{1,3},{3,1},{4,6},{6,4},{5,7},{7,5},{8,10},{10,8},{9,1... | collective-permute-start | bytes 1179656 | tf_op jit(solution)/shard_map/ppermute | solution.py:388
  183.7 31.7 %collective-permute-start.16 = (bf16[768,256]{1,0:T(8,128)(2,1)S(1)}, bf16[768,256]{1,0:T(8,128)(2,1)S(1)}, u32[]{:S(2)}, u32[]{:S(2)}) collective-permute-start(bf16[768,256]{1,0:T(8,128)(2,1)S(1)} %get-tuple-element.244), channel_id=1, source_target_pairs={{0,2},{2,0},{1,3},{3,1},{4,6},{6,4},{5,7},{7,5},{8,10},{10,8},{9,1... | collective-permute-start | bytes 1179656 | tf_op jit(solution)/shard_map/ppermute | solution.py:388
  209.7 21.0 %collective-permute-start.21 = (bf16[1312,256]{1,0:T(8,128)(2,1)}, bf16[1312,256]{1,0:T(8,128)(2,1)}, u32[]{:S(2)}, u32[]{:S(2)}) collective-permute-start(bf16[1312,256]{1,0:T(8,128)(2,1)} %slice.766), channel_id=1, source_target_pairs={{0,8},{4,12},{8,0},{12,4},{16,24},{20,28},{24,16},{28,20},{1,9},{5... | collective-permute-start | bytes 2015240 | tf_op jit(solution)/shard_map/ppermute | solution.py:483
  215.4 61.2 %collective-permute-start.25 = (bf16[512,512]{1,0:T(8,128)(2,1)}, bf16[512,512]{1,0:T(8,128)(2,1)}, u32[]{:S(2)}, u32[]{:S(2)}) collective-permute-start(bf16[512,512]{1,0:T(8,128)(2,1)} %convolution_convert_fusion.4), channel_id=1, source_target_pairs={{0,4},{4,0},{8,12},{12,8},{16,20},{20,16},{24,28},{28,24},{1,5},{5... | collective-permute-start | bytes 1572872 | tf_op jit(solution)/shard_map/ppermute | solution.py:480
  215.4 72.6 %collective-permute-start.24 = (bf16[2624,512]{1,0:T(8,128)(2,1)}, bf16[2624,512]{1,0:T(8,128)(2,1)}, u32[]{:S(2)}, u32[]{:S(2)}) collective-permute-start(bf16[2624,512]{1,0:T(8,128)(2,1)} %pad_maximum_fusion.1), channel_id=1, source_target_pairs={{0,2},{2,0},{1,3},{3,1},{4,6},{6,4},{5,7},{7,5},{8,10},{10,8},{9,1... | collective-permute-start | bytes 8060936 | tf_op jit(solution)/shard_map/ppermute | solution.py:388
  234.2 48.0 %collective-permute-start.22 = (bf16[1024,512]{1,0:T(8,128)(2,1)}, bf16[1024,512]{1,0:T(8,128)(2,1)}, u32[]{:S(2)}, u32[]{:S(2)}) collective-permute-start(bf16[1024,512]{1,0:T(8,128)(2,1)} %get-tuple-element.131), channel_id=1, source_target_pairs={{4,0},{8,4},{12,8},{16,12},{20,16},{24,20},{28,24},{5,1},{9,5},{13... | collective-permute-start | bytes 3145736 | tf_op jit(solution)/shard_map/ppermute | solution.py:661
  235.5 52.4 %collective-permute-start.23 = (bf16[1024,512]{1,0:T(8,128)(2,1)}, bf16[1024,512]{1,0:T(8,128)(2,1)}, u32[]{:S(2)}, u32[]{:S(2)}) collective-permute-start(bf16[1024,512]{1,0:T(8,128)(2,1)} %get-tuple-element.132), channel_id=1, source_target_pairs={{0,4},{4,8},{8,12},{12,16},{16,20},{20,24},{24,28},{1,5},{5,9},{9,... | collective-permute-start | bytes 3145736 | tf_op jit(solution)/shard_map/ppermute | solution.py:662
  244.2 38.0 %collective-permute-start.26 = (bf16[1312,128]{1,0:T(8,128)(2,1)}, bf16[1312,128]{1,0:T(8,128)(2,1)S(1)}, u32[]{:S(2)}, u32[]{:S(2)}) collective-permute-start(bf16[1312,128]{1,0:T(8,128)(2,1)} %slice.773), channel_id=1, source_target_pairs={{0,16},{4,20},{8,24},{12,28},{16,0},{20,4},{24,8},{28,12},{1,17},{... | collective-permute-start | bytes 1007624 | tf_op jit(solution)/shard_map/ppermute | solution.py:483
  295.6 13.0 %collective-permute-start.28 = (bf16[768,512]{1,0:T(8,128)(2,1)S(1)}, bf16[768,512]{1,0:T(8,128)(2,1)S(1)}, u32[]{:S(2)}, u32[]{:S(2)}) collective-permute-start(bf16[768,512]{1,0:T(8,128)(2,1)S(1)} %copy-done.33), channel_id=1, source_target_pairs={{0,2},{3,1},{4,6},{7,5},{8,10},{11,9},{12,14},{15,13},{16,18},{19,... | collective-permute-start | bytes 2359304 | tf_op jit(solution)/shard_map/ppermute | solution.py:694
  300.5 20.0 %collective-permute-start.32 = (bf16[768,512]{1,0:T(8,128)(2,1)S(1)}, bf16[768,512]{1,0:T(8,128)(2,1)S(1)}, u32[]{:S(2)}, u32[]{:S(2)}) collective-permute-start(bf16[768,512]{1,0:T(8,128)(2,1)S(1)} %fusion.55), channel_id=1, source_target_pairs={{0,4},{4,0},{8,12},{12,8},{16,20},{20,16},{24,28},{28,24},{1,5},{5... | collective-permute-start | bytes 2359304 | tf_op jit(solution)/shard_map/ppermute | solution.py:480
  308.6 31.3 %collective-permute-start.29 = (bf16[768,512]{1,0:T(8,128)(2,1)S(1)}, bf16[768,512]{1,0:T(8,128)(2,1)S(1)}, u32[]{:S(2)}, u32[]{:S(2)}) collective-permute-start(bf16[768,512]{1,0:T(8,128)(2,1)S(1)} %slice.762), channel_id=1, source_target_pairs={{0,2},{2,0},{1,3},{3,1},{4,6},{6,4},{5,7},{7,5},{8,10},{10,8},{9,1... | collective-permute-start | bytes 2359304 | tf_op jit(solution)/shard_map/ppermute | solution.py:388
  310.0 18.0 %collective-permute-start.30 = (f32[2,768]{1,0:T(2,128)S(1)}, f32[2,768]{1,0:T(2,128)S(1)}, u32[]{:S(2)}, u32[]{:S(2)}) collective-permute-start(f32[2,768]{1,0:T(2,128)S(1)} %pad_maximum_fusion.12), channel_id=1, source_target_pairs={{0,2},{2,0},{1,3},{3,1},{4,6},{6,4},{5,7},{7,5},{8,10},{10,8},{9,1... | collective-permute-start | bytes 18440 | tf_op jit(solution)/shard_map/ppermute | solution.py:388
  318.5 48.4 %collective-permute-start.36 = (bf16[2624,256]{1,0:T(8,128)(2,1)}, bf16[2624,256]{1,0:T(8,128)(2,1)}, u32[]{:S(2)}, u32[]{:S(2)}) collective-permute-start(bf16[2624,256]{1,0:T(8,128)(2,1)} %pad_maximum_fusion.3), channel_id=1, source_target_pairs={{0,4},{4,0},{8,12},{12,8},{16,20},{20,16},{24,28},{28,24},{1,5},{5... | collective-permute-start | bytes 4030472 | tf_op jit(solution)/shard_map/ppermute | solution.py:480
  320.9 16.1 %collective-permute-start.33 = (bf16[1280,256]{1,0:T(8,128)(2,1)S(1)}, bf16[1280,256]{1,0:T(8,128)(2,1)S(1)}, u32[]{:S(2)}, u32[]{:S(2)}) collective-permute-start(bf16[1280,256]{1,0:T(8,128)(2,1)S(1)} %pad_maximum_fusion.8), channel_id=1, source_target_pairs={{0,8},{4,12},{8,0},{12,4},{16,24},{20,28},{24,16},{28,20},{1,9},{5... | collective-permute-start | bytes 1966088 | tf_op jit(solution)/shard_map/ppermute | solution.py:483
  337.4 17.0 %collective-permute-start.34 = (bf16[1280,128]{1,0:T(8,128)(2,1)S(1)}, bf16[1280,128]{1,0:T(8,128)(2,1)S(1)}, u32[]{:S(2)}, u32[]{:S(2)}) collective-permute-start(bf16[1280,128]{1,0:T(8,128)(2,1)S(1)} %pad_maximum_fusion.11), channel_id=1, source_target_pairs={{0,16},{4,20},{8,24},{12,28},{16,0},{20,4},{24,8},{28,12},{1,17},{... | collective-permute-start | bytes 983048 | tf_op jit(solution)/shard_map/ppermute | solution.py:483
  340.6 47.9 %collective-permute-start.31 = (bf16[768,512]{1,0:T(8,128)(2,1)S(1)}, bf16[768,512]{1,0:T(8,128)(2,1)}, u32[]{:S(2)}, u32[]{:S(2)}) collective-permute-start(bf16[768,512]{1,0:T(8,128)(2,1)S(1)} %fusion.39), channel_id=1, source_target_pairs={{0,1},{1,0},{2,3},{3,2},{4,5},{5,4},{6,7},{7,6},{8,9},{9,8},{10,11... | collective-permute-start | bytes 2359304 | tf_op jit(solution)/shard_map/ppermute | solution.py:391
  359.7 31.8 %collective-permute-start.35 = (f32[64,896]{1,0:T(8,128)}, f32[64,896]{1,0:T(8,128)}, u32[]{:S(2)}, u32[]{:S(2)}) collective-permute-start(f32[64,896]{1,0:T(8,128)} %get-tuple-element.251), channel_id=1, source_target_pairs={{0,2},{2,0},{1,3},{3,1},{4,6},{6,4},{5,7},{7,5},{8,10},{10,8},{9,1... | collective-permute-start | bytes 688136 | tf_op jit(solution)/shard_map/ppermute | solution.py:388
  372.6 13.4 %collective-permute-start.37 = (bf16[2624,128]{1,0:T(8,128)(2,1)}, bf16[2624,128]{1,0:T(8,128)(2,1)}, u32[]{:S(2)}, u32[]{:S(2)}) collective-permute-start(bf16[2624,128]{1,0:T(8,128)(2,1)} %pad_maximum_fusion.7), channel_id=1, source_target_pairs={{0,8},{4,12},{8,0},{12,4},{16,24},{20,28},{24,16},{28,20},{1,9},{5... | collective-permute-start | bytes 2015240 | tf_op jit(solution)/shard_map/ppermute | solution.py:483
  388.4 17.5 %collective-permute-start.38 = (bf16[64,2624]{1,0:T(8,128)(2,1)S(1)}, bf16[64,2624]{1,0:T(8,128)(2,1)}, u32[]{:S(2)}, u32[]{:S(2)}) collective-permute-start(bf16[64,2624]{1,0:T(8,128)(2,1)S(1)} %copy.110), channel_id=1, source_target_pairs={{0,16},{4,20},{8,24},{12,28},{16,0},{20,4},{24,8},{28,12},{1,17},{... | collective-permute-start | bytes 1007624 | tf_op jit(solution)/shard_map/ppermute | solution.py:483
  (82 other events, 890.5 us)

commit v7 on v6

--- a/solution.py
+++ b/solution.py
@@ -540,7 +540,7 @@
         )
         in_got, wo_got, g_got = to_row(in_send), to_row(wo_send), to_row(g_send)
         wd_half = take(wd_low, (b // 2) % 2, F // 2)
-        h1_y = relative(after(h1, kv), "yzZw")
+        h1_y = relative(after(h1, kv), "zZyw")
         q, h1_y, sk_left, sk_right, act_low, lin_low, wd_half = lax.optimization_barrier(
             (q, h1_y, sk_left, sk_right, act_low, lin_low, wd_half)
         )
@@ -644,7 +644,7 @@
 
     if two:
         h2, da, du, o_heads, dx_late = after((h2, da, du, own_first(o_rows, 1), dx_low), do_rows)
-        dx_y = relative(dx_late, "yzZx")
+        dx_y = relative(dx_late, "yxzZ")
         h_x = relative(h2, "xyzZ")
         proj_got = to_y(product(o_heads, dx_y))
         gate_send = jnp.concatenate([product(da, h_x), product(du, h_x)], axis=0)
@@ -666,8 +666,10 @@
         dq_part, lower = lax.optimization_barrier((dq_part, lower))
     dq, dkv = attend_back_call(own_bounds, q, do, o, lse, sq, [kv], [sk_own], heads, [dq_part])
     if two:
-        dkv, from_right, from_left, gate_got, proj_got, lower_got = lax.optimization_barrier(
-            (dkv, from_right, from_left, gate_got, proj_got, lower_got)
+        gate_got = after(gate_got, dq)
+        act, lin = halved(da, h_x, gate_got[:F]), halved(du, h_x, gate_got[F:])
+        dkv, from_right, from_left, act, lin, proj_got, lower_got = lax.optimization_barrier(
+            (dkv, from_right, from_left, act, lin, proj_got, lower_got)
         )
     pad = jnp.zeros((S - H, 2 * W), bf16)
     dkv = (
@@ -680,7 +682,8 @@
     dh1_part = nt(dt, wq)
     if two:
         query_send = product(dt, h1_y)
-        gate_got, proj_got, lower_got = after((gate_got, proj_got, lower_got), query_send, dh1_part)
+        query_got = to_z(query_send, 1)
+        proj_got, lower_got = after((proj_got, lower_got), query_send, dh1_part)
 
     if two:
         n = S // 2
@@ -710,8 +713,6 @@
         ).astype(bf16)
 
     if two:
-        query = halved(dt, h1_y, after(to_y(query_send), kept))
-
         def pair(one, other):
             return jnp.concatenate([second(one), second(other)], axis=0)
 
@@ -719,20 +720,25 @@
             n = one.shape[0]
             return joined(one, got[:n]), joined(other, got[n:])
 
-        gate_got = after(gate_got, kept)
-        act, lin = halved(da, h_x, gate_got[:F]), halved(du, h_x, gate_got[F:])
         gate_got = to_y(pair(act, lin))
+        lower = joined(lower, lower_got)
         proj = halved(o_heads, dx_y, proj_got)
-        query, proj = joined_pair(query, proj, to_z(pair(query, proj), 1))
+        proj = joined(proj, to_row(second(proj)))
+        last_got = to_row(second(lower))
+        query = halved(dt, h1_y, after(query_got, kept))
+        query_got = to_z(second(query), 2)
         act, lin = joined_pair(act, lin, after(gate_got, query))
-        gate_got = to_z(pair(act, lin), 1)
-        query, proj = joined_pair(query, proj, to_z(pair(query, proj), 2))
-        act, lin = joined_pair(act, lin, after(gate_got, dx))
-        lower = joined(lower, lower_got)
-        last_got = after(to_row(pair(lower, proj)), dx)
-        gate_got = to_z(pair(act, lin).T, 2).T
-        lower, proj = joined_pair(lower, proj, last_got)
-        act, lin = joined_pair(act, lin, gate_got)
+        gate_got = to_z(jnp.concatenate([second(act), second(lin), second(proj)], axis=0), 1)
+        query = joined(query, after(query_got, act, lin, proj))
+        query_got = to_y(second(query))
+        n = 2 * F
+        act, lin = joined_pair(act, lin, after(gate_got[:n], dx))
+        proj = joined(proj, after(gate_got[n:], dx))
+        gate_got = to_z(jnp.concatenate([second(act), second(lin), second(proj)], axis=0).T, 2).T
+        query = joined(query, after(query_got, act, lin, proj))
+        lower = joined(lower, after(last_got, dx))
+        act, lin = joined_pair(act, lin, gate_got[:n])
+        proj = joined(proj, gate_got[n:])
         gate = jnp.stack([act.T, lin.T])
         query = query.T
         wq_rows = take(wq, b ^ (4 * r), Db)

time: 422 us -> 418 us (level)
  Pallas kernels: 68.3 us -> 82.1 us
  starting transfers between devices: 66.6 us -> 52.8 us
  waiting for transfers between devices: 91.6 us -> 81.2 us
  local copies, waits for them, and re-layouts: 49.7 us -> 54.1 us
    pallas_call x2, Pallas kernels: 38.3 us -> 46.2 us  [attend_back_call(): pl.pallas_call(functools.partial(backward_kernel, heads, sets, final), gr...]
    ppermute x8, waiting for transfers between devices: 54.5 us -> 46.7 us  [to_z(): return lax.ppermute(a, 'dp', [(i, i ^ 2 * j) for i in range(B)])]
    ppermute x4, waiting for transfers between devices: 15.4 us -> 21.7 us  [to_y(): return lax.ppermute(a, 'dp', [(i, i ^ 1) for i in range(B)])]
    ppermute x8, starting transfers between devices: 18.5 us -> 12.2 us  [to_z(): return lax.ppermute(a, 'dp', [(i, i ^ 2 * j) for i in range(B)])]
    ppermute x1, waiting for transfers between devices: 9.69 us -> 3.71 us  [local(): kv_left = lax.ppermute(kv[S - H:], 'dp', up)]
    pallas_call x2, Pallas kernels: 30 us -> 35.9 us  [attend_call(): pl.pallas_call(functools.partial(forward_kernel, heads, sets, final), gri...]
    ppermute x1, waiting for transfers between devices: 5.76 us -> 0.01 us  [local(): from_left = lax.ppermute(dkv_right, 'dp', up)]
    add x9, other arithmetic: 8.99 us -> 4.69 us  [joined(): return first(part).astype(f32) + got.astype(f32)]
  transfers between devices with their start and end apart: 41 -> 42, of which waited for: 11 -> 10; matrix products, arithmetic and copies ran while one was open for 36% -> 38% of each run, Pallas kernels for 16% -> 20%
where the time goes in v7:
time: 418 us; the launch traced here: 412 us
  Pallas kernels  82.1 us (20%)
  waiting for transfers between devices  81.2 us (19%)
  other arithmetic  70.4 us (17%)
  matrix products  68.4 us (16%)
  local copies, waits for them, and re-layouts  54.1 us (13%)
  starting transfers between devices  52.8 us (13%)
    ppermute x8, waiting for transfers between devices, to_z(): return lax.ppermute(a, 'dp', [(i, i ^ 2 * j) for i in range(B)])  46.7 us
    pallas_call x2, Pallas kernels, attend_back_call(): pl.pallas_call(functools.partial(backward_kernel, heads, sets, final), gr...  46.2 us
    pallas_call x2, Pallas kernels, attend_call(): pl.pallas_call(functools.partial(forward_kernel, heads, sets, final), gri...  35.9 us
    dot_general x14, matrix products, nn(): return jnp.dot(a, b, preferred_element_type=f32)  29.2 us
    ppermute x4, waiting for transfers between devices, to_y(): return lax.ppermute(a, 'dp', [(i, i ^ 1) for i in range(B)])  21.7 us
    dot_general x8, matrix products, nt(): lax.dot_general(a, b, (((1,), (1,)), ((), ())), preferred_element_type=f32)  19.6 us
    dot_general x10, matrix products, tn(): lax.dot_general(a, b, (((0,), (0,)), ((), ())), preferred_element_type=f32)  17 us
    unnamed x133, local copies, waits for them, and re-layouts  13.2 us
  transfers between devices with their start and end apart: 42, of which 10 were waited for; matrix products, arithmetic and copies ran while one was open for 38% of the time, Pallas kernels for 20%

profile of v7, /device:TPU:3, one launch (start us, length us, event | category | flops | bytes accessed | tf_op | source)
XLA Modules:
  0.0 411.7 jit_solution(12852012349340467264)
XLA Ops:
  8.8 2.8 multiply_sine_fusion
  11.7 2.7 convert_element_type.234
  14.3 3.0 fusion.58
  51.2 4.7 %collective-permute-start.3 = (bf16[1024,512]{1,0:T(8,128)(2,1)}, bf16[1024,512]{1,0:T(8,128)(2,1)}, u32[]{:S(2)}, u32[]{:S(2)}) collective-permute-start(bf16[1024,512]{1,0:T(8,128)(2,1)} %get-tuple-element.233), channel_id=1, source_target_pairs={{0,4},{4,8},{8,12},{12,16},{16,20},{20,24},{24,28},{1,5},{5,9},{9,... | collective-permute-start | bytes 3145736 | tf_op jit(solution)/shard_map/ppermute | solution.py:523
  57.3 5.2 %fusion.15 = bf16[1536,1024]{1,0:T(8,128)(2,1)} fusion(bf16[1536,1024]{1,0:T(8,128)(2,1)S(1)} %fusion.4, s32[1024]{0:T(1024)S(1)} %add_xor_fusion.3), kind=kOutput, calls=%fused_computation.28 | convolution fusion | flops 3223846912 | bytes 6295552 | tf_op jit(solution)/shard_map/dot_general | solution.py:32
  70.9 25.5 %attend_own.1 = (f32[6,256,256]{2,1,0:T(8,128)}, f32[6,2,1024]{2,1,0:T(2,128)}) custom-call(s32[12]{0:T(128)} %reshape.752.bounds, bf16[1536,256]{1,0:T(8,128)(2,1)} %fusion.45.refs_0_, s32[6,1,256]{2,1,0:T(1,128)} %select_n.692.refs_1_.refs_4_, bf16[1536,512]{1,0:T(8,128)(2,1)} %copy-done.4, s32[1536,128]{1,0:T(8,128)} %broadcast_in_dim.132.refs_3_.refs_6_), custom_call_target="tpu_custom_call" | custom-call | flops 6291456 | bytes 3145728 | tf_op jit(solution)/shard_map/attend_own/pallas_call | solution.py:194
  96.5 3.7 collective-permute-done.3.refs_2_.refs_5_
  103.6 3.6 collective-permute-start.14
  107.3 10.4 %attend_final.1 = (bf16[1536,256]{1,0:T(8,128)(2,1)}, f32[6,1,1024]{2,1,0:T(1,128)}) custom-call(s32[24]{0:T(128)} %reshape.751.bounds, bf16[1536,256]{1,0:T(8,128)(2,1)} %fusion.45.refs_0_, s32[6,1,256]{2,1,0:T(1,128)} %select_n.692.refs_1_.refs_4_, bf16[1024,512]{1,0:T(8,128)(2,1)} %collective-permute-done.3.refs_2_.refs_5_, ...), custom_call_target="tpu_custom_call" | custom-call | flops 6291456 | bytes 3670016 | tf_op jit(solution)/shard_map/attend_final/pallas_call | solution.py:194
  126.8 3.6 collective-permute-start.13
  139.5 3.2 fusion.163
  151.1 7.3 %multiply_convert_fusion = (bf16[768,1312]{0,1:T(8,128)(2,1)}, bf16[768,1312]{0,1:T(8,128)(2,1)}, bf16[768,1312]{0,1:T(8,128)(2,1)}) fusion(f32[768,1312]{0,1:T(8,128)S(1)} %convolution_add_fusion.1, f32[768,1312]{0,1:T(8,128)S(1)} %convolution_add_fusion, f32[768,1312]{0,1:T(8,128)S(1)} %fusion.73, bf16[656,512]{1,0:T(8,128)(2,1)} %collective-permute-done.13, ...), kind=kOutput, calls=%fused_computation.25 | convolution fusion | flops 1054973952 | bytes 20267008 | tf_op jit(solution)/shard_map/dot_general | solution.py:24
  158.4 3.1 fusion.165
  169.3 3.3 fusion.102
  181.1 2.8 fusion.157
  192.4 15.5 %collective-permute-done.17 = bf16[1312,512]{1,0:T(8,128)(2,1)S(1)} collective-permute-done((bf16[1312,512]{1,0:T(8,128)(2,1)S(1)}, bf16[1312,512]{1,0:T(8,128)(2,1)S(1)}, u32[]{:S(2)}, u32[]{:S(2)}) %collective-permute-start.17) | collective-permute-done | bytes 1343520 | tf_op jit(solution)/shard_map/ppermute | solution.py:480
  220.3 12.4 %back_halo.1 = (f32[6,256,256]{2,1,0:T(8,128)}, bf16[1024,512]{1,0:T(8,128)(2,1)}, bf16[1024,512]{1,0:T(8,128)(2,1)}) custom-call(s32[24]{0:T(128)} %reshape.751.bounds, bf16[1536,256]{1,0:T(8,128)(2,1)} %fusion.45.refs_0_, bf16[1536,256]{1,0:T(8,128)(2,1)} %maximum_select_fusion.7.refs_1_, bf16[1536,256]{1,0:T(8,128)(2,1)} %get-tuple-element.111.refs_2_, ...), custom_call_target="tpu_custom_call" | custom-call | flops 15728640 | bytes 3670016 | tf_op jit(solution)/shard_map/back_halo/pallas_call | solution.py:320
  232.8 2.8 convert_add_fusion.9
  236.8 7.6 %collective-permute-start.23 = (bf16[1024,512]{1,0:T(8,128)(2,1)}, bf16[1024,512]{1,0:T(8,128)(2,1)}, u32[]{:S(2)}, u32[]{:S(2)}) collective-permute-start(bf16[1024,512]{1,0:T(8,128)(2,1)} %get-tuple-element.135), channel_id=1, source_target_pairs={{0,4},{4,8},{8,12},{12,16},{16,20},{20,24},{24,28},{1,5},{5,9},{9,... | collective-permute-start | bytes 3145736 | tf_op jit(solution)/shard_map/ppermute | solution.py:662
  244.4 33.8 %back_own.1 = (f32[1536,256]{1,0:T(8,128)}, f32[1536,512]{1,0:T(8,128)}) custom-call(s32[12]{0:T(128)} %reshape.752.bounds, bf16[1536,256]{1,0:T(8,128)(2,1)} %fusion.45.refs_0_, bf16[1536,256]{1,0:T(8,128)(2,1)} %maximum_select_fusion.7.refs_1_, bf16[1536,256]{1,0:T(8,128)(2,1)} %get-tuple-element.111.refs_2_, f32[6,1,1024]{2,1,0:T(1,128)} %get-tuple-element.127.refs_3_, ...), custom_call_target="tpu_custom_call" | custom-call | flops 15728640 | bytes 3145728 | tf_op jit(solution)/shard_map/back_own/pallas_call | solution.py:320
  285.1 2.7 convert_add_fusion.3
  287.8 9.5 %collective-permute-done.26 = bf16[1312,128]{1,0:T(8,128)(2,1)S(1)} collective-permute-done((bf16[1312,128]{1,0:T(8,128)(2,1)S(1)}, bf16[1312,128]{1,0:T(8,128)(2,1)S(1)}, u32[]{:S(2)}, u32[]{:S(2)}) %collective-permute-start.26) | collective-permute-done | bytes 335904 | tf_op jit(solution)/shard_map/ppermute | solution.py:483
  301.1 2.7 fusion.167
  304.9 2.9 collective-permute-start.28
  316.3 6.0 %collective-permute-done.35 = bf16[512,256]{1,0:T(8,128)(2,1)S(1)} collective-permute-done((bf16[512,256]{1,0:T(8,128)(2,1)S(1)}, bf16[512,256]{1,0:T(8,128)(2,1)S(1)}, u32[]{:S(2)}, u32[]{:S(2)}) %collective-permute-start.35) | collective-permute-done | bytes 262176 | tf_op jit(solution)/shard_map/ppermute | solution.py:388
  327.6 3.9 collective-permute-done.32
  333.0 6.2 %collective-permute-done.34 = bf16[2624,256]{1,0:T(8,128)(2,1)S(1)} collective-permute-done((bf16[2624,256]{1,0:T(8,128)(2,1)S(1)}, bf16[2624,256]{1,0:T(8,128)(2,1)S(1)}, u32[]{:S(2)}, u32[]{:S(2)}) %collective-permute-start.34) | collective-permute-done | bytes 1343520 | tf_op jit(solution)/shard_map/ppermute | solution.py:480
  345.5 3.0 collective-permute-done.30
  348.6 18.6 %collective-permute-done.33 = bf16[768,256]{1,0:T(8,128)(2,1)S(1)} collective-permute-done((bf16[768,256]{1,0:T(8,128)(2,1)S(1)}, bf16[768,256]{1,0:T(8,128)(2,1)S(1)}, u32[]{:S(2)}, u32[]{:S(2)}) %collective-permute-start.33) | collective-permute-done | bytes 393248 | tf_op jit(solution)/shard_map/ppermute | solution.py:483
  375.9 3.1 collective-permute-start.39
  384.7 13.3 %collective-permute-done.39 = bf16[64,3136]{1,0:T(8,128)(2,1)} collective-permute-done((bf16[64,3136]{1,0:T(8,128)(2,1)}, bf16[64,3136]{1,0:T(8,128)(2,1)}, u32[]{:S(2)}, u32[]{:S(2)}) %collective-permute-start.39) | collective-permute-done | bytes 401440 | tf_op jit(solution)/shard_map/ppermute | solution.py:483
  403.0 3.2 maximum_select_fusion.4
  (383 shorter events, 176.9 us)
Async XLA Ops:
  2.8 25.8 %collective-permute-start = (bf16[768,512]{1,0:T(8,128)(2,1)}, bf16[768,512]{1,0:T(8,128)(2,1)}, u32[]{:S(2)}, u32[]{:S(2)}) collective-permute-start(bf16[768,512]{1,0:T(8,128)(2,1)} %constant_dynamic-slice_fusion.6), channel_id=1, source_target_pairs={{0,2},{2,0},{1,3},{3,1},{4,6},{6,4},{5,7},{7,5},{8,10},{10,8},{9,1... | collective-permute-start | bytes 2359304 | tf_op jit(solution)/shard_map/ppermute | solution.py:388
  6.2 36.7 %collective-permute-start.2 = (bf16[512,768]{0,1:T(8,128)(2,1)}, bf16[512,768]{0,1:T(8,128)(2,1)}, u32[]{:S(2)}, u32[]{:S(2)}) collective-permute-start(bf16[512,768]{0,1:T(8,128)(2,1)} %get-tuple-element.236), channel_id=1, source_target_pairs={{0,2},{2,0},{1,3},{3,1},{4,6},{6,4},{5,7},{7,5},{8,10},{10,8},{9,1... | collective-permute-start | bytes 2359304 | tf_op jit(solution)/shard_map/ppermute | solution.py:388
  17.3 79.1 %collective-permute-start.5 = (bf16[512,1312]{0,1:T(8,128)(2,1)}, bf16[512,1312]{0,1:T(8,128)(2,1)}, u32[]{:S(2)}, u32[]{:S(2)}) collective-permute-start(bf16[512,1312]{0,1:T(8,128)(2,1)} %fusion.58), channel_id=1, source_target_pairs={{0,2},{2,0},{1,3},{3,1},{4,6},{6,4},{5,7},{7,5},{8,10},{10,8},{9,1... | collective-permute-start | bytes 4030472 | tf_op jit(solution)/shard_map/ppermute | solution.py:388
  17.4 79.0 %collective-permute-start.6 = (bf16[512,512]{1,0:T(8,128)(2,1)}, bf16[512,512]{1,0:T(8,128)(2,1)}, u32[]{:S(2)}, u32[]{:S(2)}) collective-permute-start(bf16[512,512]{1,0:T(8,128)(2,1)} %convert_element_type.234), channel_id=1, source_target_pairs={{0,2},{2,0},{1,3},{3,1},{4,6},{6,4},{5,7},{7,5},{8,10},{10,8},{9,1... | collective-permute-start | bytes 1572872 | tf_op jit(solution)/shard_map/ppermute | solution.py:388
  18.9 77.6 %collective-permute-start.7 = (bf16[384,512]{1,0:T(8,128)(2,1)S(1)}, bf16[384,512]{1,0:T(8,128)(2,1)}, u32[]{:S(2)}, u32[]{:S(2)}) collective-permute-start(bf16[384,512]{1,0:T(8,128)(2,1)S(1)} %constant_dynamic-slice_fusion.2), channel_id=1, source_target_pairs={{0,2},{2,0},{1,3},{3,1},{4,6},{6,4},{5,7},{7,5},{8,10},{10,8},{9,1... | collective-permute-start | bytes 1179656 | tf_op jit(solution)/shard_map/ppermute | solution.py:388
  51.2 49.0 %collective-permute-start.3 = (bf16[1024,512]{1,0:T(8,128)(2,1)}, bf16[1024,512]{1,0:T(8,128)(2,1)}, u32[]{:S(2)}, u32[]{:S(2)}) collective-permute-start(bf16[1024,512]{1,0:T(8,128)(2,1)} %get-tuple-element.233), channel_id=1, source_target_pairs={{0,4},{4,8},{8,12},{12,16},{16,20},{20,24},{24,28},{1,5},{5,9},{9,... | collective-permute-start | bytes 3145736 | tf_op jit(solution)/shard_map/ppermute | solution.py:523
  55.9 44.3 %collective-permute-start.4 = (bf16[1024,512]{1,0:T(8,128)(2,1)}, bf16[1024,512]{1,0:T(8,128)(2,1)}, u32[]{:S(2)}, u32[]{:S(2)}) collective-permute-start(bf16[1024,512]{1,0:T(8,128)(2,1)} %get-tuple-element.232), channel_id=1, source_target_pairs={{4,0},{8,4},{12,8},{16,12},{20,16},{24,20},{28,24},{5,1},{9,5},{13... | collective-permute-start | bytes 3145736 | tf_op jit(solution)/shard_map/ppermute | solution.py:524
  100.2 17.5 %collective-permute-start.8 = (bf16[656,512]{1,0:T(8,128)(2,1)}, bf16[656,512]{1,0:T(8,128)(2,1)}, u32[]{:S(2)}, u32[]{:S(2)}) collective-permute-start(bf16[656,512]{1,0:T(8,128)(2,1)} %constant_dynamic-slice_fusion.3), channel_id=1, source_target_pairs={{0,2},{2,0},{1,3},{3,1},{4,6},{6,4},{5,7},{7,5},{8,10},{10,8},{9,1... | collective-permute-start | bytes 2015240 | tf_op jit(solution)/shard_map/ppermute | solution.py:388
  103.6 33.1 %collective-permute-start.14 = (bf16[512,1312]{0,1:T(8,128)(2,1)}, bf16[512,1312]{0,1:T(8,128)(2,1)}, u32[]{:S(2)}, u32[]{:S(2)}) collective-permute-start(bf16[512,1312]{0,1:T(8,128)(2,1)} %collective-permute-done.5), channel_id=1, source_target_pairs={{0,8},{4,12},{8,0},{12,4},{16,24},{20,28},{24,16},{28,20},{1,9},{5... | collective-permute-start | bytes 4030472 | tf_op jit(solution)/shard_map/ppermute | solution.py:483
  126.8 24.3 %collective-permute-start.13 = (bf16[656,512]{1,0:T(8,128)(2,1)}, bf16[656,512]{1,0:T(8,128)(2,1)}, u32[]{:S(2)}, u32[]{:S(2)}) collective-permute-start(bf16[656,512]{1,0:T(8,128)(2,1)} %collective-permute-done.8), channel_id=1, source_target_pairs={{0,8},{4,12},{8,0},{12,4},{16,24},{20,28},{24,16},{28,20},{1,9},{5... | collective-permute-start | bytes 2015240 | tf_op jit(solution)/shard_map/ppermute | solution.py:483
  166.2 13.4 %collective-permute-start.15 = (bf16[768,1024]{1,0:T(8,128)(2,1)S(1)}, bf16[768,1024]{1,0:T(8,128)(2,1)S(1)}, u32[]{:S(2)}, u32[]{:S(2)}) collective-permute-start(bf16[768,1024]{1,0:T(8,128)(2,1)S(1)} %fusion.156), channel_id=1, source_target_pairs={{0,1},{1,0},{2,3},{3,2},{4,5},{5,4},{6,7},{7,6},{8,9},{9,8},{10,11... | collective-permute-start | bytes 4718600 | tf_op jit(solution)/shard_map/ppermute | solution.py:391
  177.2 30.6 %collective-permute-start.17 = (bf16[1312,512]{1,0:T(8,128)(2,1)S(1)}, bf16[1312,512]{1,0:T(8,128)(2,1)S(1)}, u32[]{:S(2)}, u32[]{:S(2)}) collective-permute-start(bf16[1312,512]{1,0:T(8,128)(2,1)S(1)} %convolution_convert_fusion.2), channel_id=1, source_target_pairs={{0,4},{4,0},{8,12},{12,8},{16,20},{20,16},{24,28},{28,24},{1,5},{5... | collective-permute-start | bytes 4030472 | tf_op jit(solution)/shard_map/ppermute | solution.py:480
  179.2 28.6 %collective-permute-start.19 = (bf16[384,512]{1,0:T(8,128)(2,1)S(1)}, bf16[384,512]{1,0:T(8,128)(2,1)S(1)}, u32[]{:S(2)}, u32[]{:S(2)}) collective-permute-start(bf16[384,512]{1,0:T(8,128)(2,1)S(1)} %get-tuple-element.248), channel_id=1, source_target_pairs={{0,2},{2,0},{1,3},{3,1},{4,6},{6,4},{5,7},{7,5},{8,10},{10,8},{9,1... | collective-permute-start | bytes 1179656 | tf_op jit(solution)/shard_map/ppermute | solution.py:388
  185.1 32.2 %collective-permute-start.16 = (bf16[768,256]{1,0:T(8,128)(2,1)S(1)}, bf16[768,256]{1,0:T(8,128)(2,1)S(1)}, u32[]{:S(2)}, u32[]{:S(2)}) collective-permute-start(bf16[768,256]{1,0:T(8,128)(2,1)S(1)} %get-tuple-element.252), channel_id=1, source_target_pairs={{0,2},{2,0},{1,3},{3,1},{4,6},{6,4},{5,7},{7,5},{8,10},{10,8},{9,1... | collective-permute-start | bytes 1179656 | tf_op jit(solution)/shard_map/ppermute | solution.py:388
  211.0 21.8 %collective-permute-start.21 = (bf16[1312,256]{1,0:T(8,128)(2,1)}, bf16[1312,256]{1,0:T(8,128)(2,1)}, u32[]{:S(2)}, u32[]{:S(2)}) collective-permute-start(bf16[1312,256]{1,0:T(8,128)(2,1)} %slice.749), channel_id=1, source_target_pairs={{0,8},{4,12},{8,0},{12,4},{16,24},{20,28},{24,16},{28,20},{1,9},{5... | collective-permute-start | bytes 2015240 | tf_op jit(solution)/shard_map/ppermute | solution.py:483
  216.7 71.1 %collective-permute-start.25 = (bf16[512,512]{1,0:T(8,128)(2,1)}, bf16[512,512]{1,0:T(8,128)(2,1)}, u32[]{:S(2)}, u32[]{:S(2)}) collective-permute-start(bf16[512,512]{1,0:T(8,128)(2,1)} %convolution_convert_fusion.4), channel_id=1, source_target_pairs={{0,4},{4,0},{8,12},{12,8},{16,20},{20,16},{24,28},{28,24},{1,5},{5... | collective-permute-start | bytes 1572872 | tf_op jit(solution)/shard_map/ppermute | solution.py:480
  217.3 64.5 %collective-permute-start.24 = (bf16[2624,512]{1,0:T(8,128)(2,1)}, bf16[2624,512]{1,0:T(8,128)(2,1)}, u32[]{:S(2)}, u32[]{:S(2)}) collective-permute-start(bf16[2624,512]{1,0:T(8,128)(2,1)} %pad_maximum_fusion.1), channel_id=1, source_target_pairs={{0,2},{2,0},{1,3},{3,1},{4,6},{6,4},{5,7},{7,5},{8,10},{10,8},{9,1... | collective-permute-start | bytes 8060936 | tf_op jit(solution)/shard_map/ppermute | solution.py:388
  235.5 61.8 %collective-permute-start.22 = (bf16[1024,512]{1,0:T(8,128)(2,1)}, bf16[1024,512]{1,0:T(8,128)(2,1)}, u32[]{:S(2)}, u32[]{:S(2)}) collective-permute-start(bf16[1024,512]{1,0:T(8,128)(2,1)} %get-tuple-element.134), channel_id=1, source_target_pairs={{4,0},{8,4},{12,8},{16,12},{20,16},{24,20},{28,24},{5,1},{9,5},{13... | collective-permute-start | bytes 3145736 | tf_op jit(solution)/shard_map/ppermute | solution.py:661
  236.8 60.5 %collective-permute-start.23 = (bf16[1024,512]{1,0:T(8,128)(2,1)}, bf16[1024,512]{1,0:T(8,128)(2,1)}, u32[]{:S(2)}, u32[]{:S(2)}) collective-permute-start(bf16[1024,512]{1,0:T(8,128)(2,1)} %get-tuple-element.135), channel_id=1, source_target_pairs={{0,4},{4,8},{8,12},{12,16},{16,20},{20,24},{24,28},{1,5},{5,9},{9,... | collective-permute-start | bytes 3145736 | tf_op jit(solution)/shard_map/ppermute | solution.py:662
  281.7 15.6 %collective-permute-start.26 = (bf16[1312,128]{1,0:T(8,128)(2,1)S(1)}, bf16[1312,128]{1,0:T(8,128)(2,1)S(1)}, u32[]{:S(2)}, u32[]{:S(2)}) collective-permute-start(bf16[1312,128]{1,0:T(8,128)(2,1)S(1)} %slice.756), channel_id=1, source_target_pairs={{0,16},{4,20},{8,24},{12,28},{16,0},{20,4},{24,8},{28,12},{1,17},{... | collective-permute-start | bytes 1007624 | tf_op jit(solution)/shard_map/ppermute | solution.py:483
  304.0 20.5 %collective-permute-start.27 = (bf16[768,1024]{1,0:T(8,128)(2,1)S(1)}, bf16[768,1024]{1,0:T(8,128)(2,1)S(1)}, u32[]{:S(2)}, u32[]{:S(2)}) collective-permute-start(bf16[768,1024]{1,0:T(8,128)(2,1)S(1)} %dynamic-slice_convert_fusion), channel_id=1, source_target_pairs={{0,1},{1,0},{2,3},{3,2},{4,5},{5,4},{6,7},{7,6},{8,9},{9,8},{10,11... | collective-permute-start | bytes 4718600 | tf_op jit(solution)/shard_map/ppermute | solution.py:391
  304.9 21.1 %collective-permute-start.28 = (bf16[768,512]{1,0:T(8,128)(2,1)S(1)}, bf16[768,512]{1,0:T(8,128)(2,1)S(1)}, u32[]{:S(2)}, u32[]{:S(2)}) collective-permute-start(bf16[768,512]{1,0:T(8,128)(2,1)S(1)} %copy-done.34), channel_id=1, source_target_pairs={{0,2},{3,1},{4,6},{7,5},{8,10},{11,9},{12,14},{15,13},{16,18},{19,... | collective-permute-start | bytes 2359304 | tf_op jit(solution)/shard_map/ppermute | solution.py:697
  308.1 31.1 %collective-permute-start.34 = (bf16[2624,256]{1,0:T(8,128)(2,1)S(1)}, bf16[2624,256]{1,0:T(8,128)(2,1)S(1)}, u32[]{:S(2)}, u32[]{:S(2)}) collective-permute-start(bf16[2624,256]{1,0:T(8,128)(2,1)S(1)} %pad_maximum_fusion.3), channel_id=1, source_target_pairs={{0,4},{4,0},{8,12},{12,8},{16,20},{20,16},{24,28},{28,24},{1,5},{5... | collective-permute-start | bytes 4030472 | tf_op jit(solution)/shard_map/ppermute | solution.py:480
  312.1 19.4 %collective-permute-start.32 = (bf16[768,512]{1,0:T(8,128)(2,1)}, bf16[768,512]{1,0:T(8,128)(2,1)}, u32[]{:S(2)}, u32[]{:S(2)}) collective-permute-start(bf16[768,512]{1,0:T(8,128)(2,1)} %fusion.55), channel_id=1, source_target_pairs={{0,8},{4,12},{8,0},{12,4},{16,24},{20,28},{24,16},{28,20},{1,9},{5... | collective-permute-start | bytes 2359304 | tf_op jit(solution)/shard_map/ppermute | solution.py:483
  322.3 47.2 %collective-permute-start.41 = (bf16[1312,64]{1,0:T(8,128)(2,1)}, bf16[1312,64]{1,0:T(8,128)(2,1)}, u32[]{:S(2)}, u32[]{:S(2)}) collective-permute-start(bf16[1312,64]{1,0:T(8,128)(2,1)} %slice.751), channel_id=1, source_target_pairs={{0,2},{2,0},{1,3},{3,1},{4,6},{6,4},{5,7},{7,5},{8,10},{10,8},{9,1... | collective-permute-start | bytes 503816 | tf_op jit(solution)/shard_map/ppermute | solution.py:388
  326.0 42.1 %collective-permute-start.29 = (bf16[768,512]{1,0:T(8,128)(2,1)S(1)}, bf16[768,512]{1,0:T(8,128)(2,1)S(1)}, u32[]{:S(2)}, u32[]{:S(2)}) collective-permute-start(bf16[768,512]{1,0:T(8,128)(2,1)S(1)} %slice.745), channel_id=1, source_target_pairs={{0,2},{2,0},{1,3},{3,1},{4,6},{6,4},{5,7},{7,5},{8,10},{10,8},{9,1... | collective-permute-start | bytes 2359304 | tf_op jit(solution)/shard_map/ppermute | solution.py:388
  326.1 22.4 %collective-permute-start.30 = (f32[2,768]{1,0:T(2,128)S(1)}, f32[2,768]{1,0:T(2,128)S(1)}, u32[]{:S(2)}, u32[]{:S(2)}) collective-permute-start(f32[2,768]{1,0:T(2,128)S(1)} %pad_maximum_fusion.9), channel_id=1, source_target_pairs={{0,2},{2,0},{1,3},{3,1},{4,6},{6,4},{5,7},{7,5},{8,10},{10,8},{9,1... | collective-permute-start | bytes 18440 | tf_op jit(solution)/shard_map/ppermute | solution.py:388
  341.0 30.6 %collective-permute-start.37 = (bf16[3136,128]{1,0:T(8,128)(2,1)}, bf16[3136,128]{1,0:T(8,128)(2,1)}, u32[]{:S(2)}, u32[]{:S(2)}) collective-permute-start(bf16[3136,128]{1,0:T(8,128)(2,1)} %pad_maximum_fusion.6), channel_id=1, source_target_pairs={{0,8},{4,12},{8,0},{12,4},{16,24},{20,28},{24,16},{28,20},{1,9},{5... | collective-permute-start | bytes 2408456 | tf_op jit(solution)/shard_map/ppermute | solution.py:483
  341.0 26.2 %collective-permute-start.33 = (bf16[768,256]{1,0:T(8,128)(2,1)S(1)}, bf16[768,256]{1,0:T(8,128)(2,1)S(1)}, u32[]{:S(2)}, u32[]{:S(2)}) collective-permute-start(bf16[768,256]{1,0:T(8,128)(2,1)S(1)} %slice.750), channel_id=1, source_target_pairs={{0,16},{4,20},{8,24},{12,28},{16,0},{20,4},{24,8},{28,12},{1,17},{... | collective-permute-start | bytes 1179656 | tf_op jit(solution)/shard_map/ppermute | solution.py:483
  368.9 34.0 %collective-permute-start.31 = (bf16[768,512]{1,0:T(8,128)(2,1)S(1)}, bf16[768,512]{1,0:T(8,128)(2,1)}, u32[]{:S(2)}, u32[]{:S(2)}) collective-permute-start(bf16[768,512]{1,0:T(8,128)(2,1)S(1)} %fusion.39), channel_id=1, source_target_pairs={{0,1},{1,0},{2,3},{3,2},{4,5},{5,4},{6,7},{7,6},{8,9},{9,8},{10,11... | collective-permute-start | bytes 2359304 | tf_op jit(solution)/shard_map/ppermute | solution.py:391
  375.9 22.0 %collective-permute-start.39 = (bf16[64,3136]{1,0:T(8,128)(2,1)}, bf16[64,3136]{1,0:T(8,128)(2,1)}, u32[]{:S(2)}, u32[]{:S(2)}) collective-permute-start(bf16[64,3136]{1,0:T(8,128)(2,1)} %copy.110), channel_id=1, source_target_pairs={{0,16},{4,20},{8,24},{12,28},{16,0},{20,4},{24,8},{28,12},{1,17},{... | collective-permute-start | bytes 1204232 | tf_op jit(solution)/shard_map/ppermute | solution.py:483
  383.7 22.4 %collective-permute-start.38 = (f32[64,896]{1,0:T(8,128)}, f32[64,896]{1,0:T(8,128)}, u32[]{:S(2)}, u32[]{:S(2)}) collective-permute-start(f32[64,896]{1,0:T(8,128)} %get-tuple-element.257), channel_id=1, source_target_pairs={{0,2},{2,0},{1,3},{3,1},{4,6},{6,4},{5,7},{7,5},{8,10},{10,8},{9,1... | collective-permute-start | bytes 688136 | tf_op jit(solution)/shard_map/ppermute | solution.py:388
  (77 other events, 875.2 us)

commit v8 on v7

--- a/solution.py
+++ b/solution.py
@@ -540,7 +540,7 @@
         )
         in_got, wo_got, g_got = to_row(in_send), to_row(wo_send), to_row(g_send)
         wd_half = take(wd_low, (b // 2) % 2, F // 2)
-        h1_y = relative(after(h1, kv), "zZyw")
+        h1_y = relative(after(h1, kv), "zyZw")
         q, h1_y, sk_left, sk_right, act_low, lin_low, wd_half = lax.optimization_barrier(
             (q, h1_y, sk_left, sk_right, act_low, lin_low, wd_half)
         )
@@ -726,11 +726,11 @@
         proj = joined(proj, to_row(second(proj)))
         last_got = to_row(second(lower))
         query = halved(dt, h1_y, after(query_got, kept))
-        query_got = to_z(second(query), 2)
+        query_got = to_y(second(query))
         act, lin = joined_pair(act, lin, after(gate_got, query))
         gate_got = to_z(jnp.concatenate([second(act), second(lin), second(proj)], axis=0), 1)
         query = joined(query, after(query_got, act, lin, proj))
-        query_got = to_y(second(query))
+        query_got = to_z(second(query), 2)
         n = 2 * F
         act, lin = joined_pair(act, lin, after(gate_got[:n], dx))
         proj = joined(proj, after(gate_got[n:], dx))

time: 418 us -> 408 us (0.976)
  waiting for transfers between devices: 81.2 us -> 74.1 us
    ppermute x8, waiting for transfers between devices: 46.7 us -> 36.4 us  [to_z(): return lax.ppermute(a, 'dp', [(i, i ^ 2 * j) for i in range(B)])]
  transfers between devices with their start and end apart: 42 -> 42, of which waited for: 10 -> 11; matrix products, arithmetic and copies ran while one was open for 38% -> 39% of each run, Pallas kernels for 20% -> 20%
where the time goes in v8:
time: 408 us; the launch traced here: 404 us
  Pallas kernels  82.1 us (20%)
  waiting for transfers between devices  74.1 us (18%)
  other arithmetic  70.4 us (17%)
  matrix products  68.4 us (17%)
  starting transfers between devices  53.3 us (13%)
  local copies, waits for them, and re-layouts  52.5 us (13%)
    pallas_call x2, Pallas kernels, attend_back_call(): pl.pallas_call(functools.partial(backward_kernel, heads, sets, final), gr...  46.2 us
    ppermute x8, waiting for transfers between devices, to_z(): return lax.ppermute(a, 'dp', [(i, i ^ 2 * j) for i in range(B)])  36.4 us
    pallas_call x2, Pallas kernels, attend_call(): pl.pallas_call(functools.partial(forward_kernel, heads, sets, final), gri...  35.9 us
    dot_general x14, matrix products, nn(): return jnp.dot(a, b, preferred_element_type=f32)  29.2 us
    ppermute x4, waiting for transfers between devices, to_y(): return lax.ppermute(a, 'dp', [(i, i ^ 1) for i in range(B)])  25.8 us
    dot_general x8, matrix products, nt(): lax.dot_general(a, b, (((1,), (1,)), ((), ())), preferred_element_type=f32)  19.6 us
    dot_general x10, matrix products, tn(): lax.dot_general(a, b, (((0,), (0,)), ((), ())), preferred_element_type=f32)  17 us
    ppermute x8, starting transfers between devices, to_z(): return lax.ppermute(a, 'dp', [(i, i ^ 2 * j) for i in range(B)])  13.4 us
  transfers between devices with their start and end apart: 42, of which 11 were waited for; matrix products, arithmetic and copies ran while one was open for 39% of the time, Pallas kernels for 20%

profile of v8, /device:TPU:3, one launch (start us, length us, event | category | flops | bytes accessed | tf_op | source)
XLA Modules:
  0.0 403.5 jit_solution(8390749493949550021)
XLA Ops:
  8.8 2.8 multiply_sine_fusion
  11.7 2.7 convert_element_type.234
  14.3 3.0 fusion.58
  51.2 4.7 %collective-permute-start.3 = (bf16[1024,512]{1,0:T(8,128)(2,1)}, bf16[1024,512]{1,0:T(8,128)(2,1)}, u32[]{:S(2)}, u32[]{:S(2)}) collective-permute-start(bf16[1024,512]{1,0:T(8,128)(2,1)} %get-tuple-element.233), channel_id=1, source_target_pairs={{0,4},{4,8},{8,12},{12,16},{16,20},{20,24},{24,28},{1,5},{5,9},{9,... | collective-permute-start | bytes 3145736 | tf_op jit(solution)/shard_map/ppermute | solution.py:523
  57.3 5.2 %fusion.15 = bf16[1536,1024]{1,0:T(8,128)(2,1)} fusion(bf16[1536,1024]{1,0:T(8,128)(2,1)S(1)} %fusion.4, s32[1024]{0:T(1024)S(1)} %add_xor_fusion.3), kind=kOutput, calls=%fused_computation.28 | convolution fusion | flops 3223846912 | bytes 6295552 | tf_op jit(solution)/shard_map/dot_general | solution.py:32
  70.9 25.5 %attend_own.1 = (f32[6,256,256]{2,1,0:T(8,128)}, f32[6,2,1024]{2,1,0:T(2,128)}) custom-call(s32[12]{0:T(128)} %reshape.750.bounds, bf16[1536,256]{1,0:T(8,128)(2,1)} %fusion.45.refs_0_, s32[6,1,256]{2,1,0:T(1,128)} %select_n.688.refs_1_.refs_4_, bf16[1536,512]{1,0:T(8,128)(2,1)} %copy-done.4, s32[1536,128]{1,0:T(8,128)} %broadcast_in_dim.132.refs_3_.refs_6_), custom_call_target="tpu_custom_call" | custom-call | flops 6291456 | bytes 3145728 | tf_op jit(solution)/shard_map/attend_own/pallas_call | solution.py:194
  96.5 3.7 collective-permute-done.3.refs_2_.refs_5_
  103.6 3.6 collective-permute-start.14
  107.3 10.4 %attend_final.1 = (bf16[1536,256]{1,0:T(8,128)(2,1)}, f32[6,1,1024]{2,1,0:T(1,128)}) custom-call(s32[24]{0:T(128)} %reshape.749.bounds, bf16[1536,256]{1,0:T(8,128)(2,1)} %fusion.45.refs_0_, s32[6,1,256]{2,1,0:T(1,128)} %select_n.688.refs_1_.refs_4_, bf16[1024,512]{1,0:T(8,128)(2,1)} %collective-permute-done.3.refs_2_.refs_5_, ...), custom_call_target="tpu_custom_call" | custom-call | flops 6291456 | bytes 3670016 | tf_op jit(solution)/shard_map/attend_final/pallas_call | solution.py:194
  126.8 3.6 collective-permute-start.13
  139.5 3.2 fusion.163
  151.1 7.3 %multiply_convert_fusion = (bf16[768,1312]{0,1:T(8,128)(2,1)}, bf16[768,1312]{0,1:T(8,128)(2,1)}, bf16[768,1312]{0,1:T(8,128)(2,1)}) fusion(f32[768,1312]{0,1:T(8,128)S(1)} %convolution_add_fusion.1, f32[768,1312]{0,1:T(8,128)S(1)} %convolution_add_fusion, f32[768,1312]{0,1:T(8,128)S(1)} %fusion.73, bf16[656,512]{1,0:T(8,128)(2,1)} %collective-permute-done.13, ...), kind=kOutput, calls=%fused_computation.25 | convolution fusion | flops 1054973952 | bytes 20267008 | tf_op jit(solution)/shard_map/dot_general | solution.py:24
  158.4 3.1 fusion.165
  169.3 3.3 fusion.102
  181.1 2.8 fusion.157
  192.4 15.5 %collective-permute-done.17 = bf16[1312,512]{1,0:T(8,128)(2,1)S(1)} collective-permute-done((bf16[1312,512]{1,0:T(8,128)(2,1)S(1)}, bf16[1312,512]{1,0:T(8,128)(2,1)S(1)}, u32[]{:S(2)}, u32[]{:S(2)}) %collective-permute-start.17) | collective-permute-done | bytes 1343520 | tf_op jit(solution)/shard_map/ppermute | solution.py:480
  220.3 12.4 %back_halo.1 = (f32[6,256,256]{2,1,0:T(8,128)}, bf16[1024,512]{1,0:T(8,128)(2,1)}, bf16[1024,512]{1,0:T(8,128)(2,1)}) custom-call(s32[24]{0:T(128)} %reshape.749.bounds, bf16[1536,256]{1,0:T(8,128)(2,1)} %fusion.45.refs_0_, bf16[1536,256]{1,0:T(8,128)(2,1)} %maximum_select_fusion.7.refs_1_, bf16[1536,256]{1,0:T(8,128)(2,1)} %get-tuple-element.111.refs_2_, ...), custom_call_target="tpu_custom_call" | custom-call | flops 15728640 | bytes 3670016 | tf_op jit(solution)/shard_map/back_halo/pallas_call | solution.py:320
  232.8 2.8 convert_add_fusion.9
  236.8 5.0 %collective-permute-start.23 = (bf16[1024,512]{1,0:T(8,128)(2,1)}, bf16[1024,512]{1,0:T(8,128)(2,1)}, u32[]{:S(2)}, u32[]{:S(2)}) collective-permute-start(bf16[1024,512]{1,0:T(8,128)(2,1)} %get-tuple-element.135), channel_id=1, source_target_pairs={{0,4},{4,8},{8,12},{12,16},{16,20},{20,24},{24,28},{1,5},{5,9},{9,... | collective-permute-start | bytes 3145736 | tf_op jit(solution)/shard_map/ppermute | solution.py:662
  241.9 33.8 %back_own.1 = (f32[1536,256]{1,0:T(8,128)}, f32[1536,512]{1,0:T(8,128)}) custom-call(s32[12]{0:T(128)} %reshape.750.bounds, bf16[1536,256]{1,0:T(8,128)(2,1)} %fusion.45.refs_0_, bf16[1536,256]{1,0:T(8,128)(2,1)} %maximum_select_fusion.7.refs_1_, bf16[1536,256]{1,0:T(8,128)(2,1)} %get-tuple-element.111.refs_2_, f32[6,1,1024]{2,1,0:T(1,128)} %get-tuple-element.127.refs_3_, ...), custom_call_target="tpu_custom_call" | custom-call | flops 15728640 | bytes 3145728 | tf_op jit(solution)/shard_map/back_own/pallas_call | solution.py:320
  279.2 3.5 collective-permute-start.26
  285.3 2.7 convert_add_fusion.3
  288.0 9.1 %collective-permute-done.26 = bf16[1312,128]{1,0:T(8,128)(2,1)S(1)} collective-permute-done((bf16[1312,128]{1,0:T(8,128)(2,1)S(1)}, bf16[1312,128]{1,0:T(8,128)(2,1)S(1)}, u32[]{:S(2)}, u32[]{:S(2)}) %collective-permute-start.26) | collective-permute-done | bytes 335904 | tf_op jit(solution)/shard_map/ppermute | solution.py:483
  300.8 2.7 fusion.167
  305.5 2.9 collective-permute-start.28
  316.9 6.0 %collective-permute-done.35 = bf16[512,256]{1,0:T(8,128)(2,1)S(1)} collective-permute-done((bf16[512,256]{1,0:T(8,128)(2,1)S(1)}, bf16[512,256]{1,0:T(8,128)(2,1)S(1)}, u32[]{:S(2)}, u32[]{:S(2)}) %collective-permute-start.35) | collective-permute-done | bytes 262176 | tf_op jit(solution)/shard_map/ppermute | solution.py:388
  328.0 4.5 %collective-permute-done.32 = bf16[768,512]{1,0:T(8,128)(2,1)} collective-permute-done((bf16[768,512]{1,0:T(8,128)(2,1)}, bf16[768,512]{1,0:T(8,128)(2,1)}, u32[]{:S(2)}, u32[]{:S(2)}) %collective-permute-start.32) | collective-permute-done | bytes 786464 | tf_op jit(solution)/shard_map/ppermute | solution.py:483
  333.9 6.2 %collective-permute-done.34 = bf16[2624,256]{1,0:T(8,128)(2,1)S(1)} collective-permute-done((bf16[2624,256]{1,0:T(8,128)(2,1)S(1)}, bf16[2624,256]{1,0:T(8,128)(2,1)S(1)}, u32[]{:S(2)}, u32[]{:S(2)}) %collective-permute-start.34) | collective-permute-done | bytes 1343520 | tf_op jit(solution)/shard_map/ppermute | solution.py:480
  348.4 4.0 collective-permute-done.33
  358.8 6.8 %collective-permute-done.37 = bf16[3136,128]{1,0:T(8,128)(2,1)} collective-permute-done((bf16[3136,128]{1,0:T(8,128)(2,1)}, bf16[3136,128]{1,0:T(8,128)(2,1)}, u32[]{:S(2)}, u32[]{:S(2)}) %collective-permute-start.37) | collective-permute-done | bytes 802848 | tf_op jit(solution)/shard_map/ppermute | solution.py:483
  375.2 14.7 %collective-permute-done.39 = bf16[64,3136]{1,0:T(8,128)(2,1)} collective-permute-done((bf16[64,3136]{1,0:T(8,128)(2,1)}, bf16[64,3136]{1,0:T(8,128)(2,1)}, u32[]{:S(2)}, u32[]{:S(2)}) %collective-permute-start.39) | collective-permute-done | bytes 401440 | tf_op jit(solution)/shard_map/ppermute | solution.py:483
  395.0 3.2 maximum_select_fusion.4
  (383 shorter events, 180.1 us)
Async XLA Ops:
  2.8 25.8 %collective-permute-start = (bf16[768,512]{1,0:T(8,128)(2,1)}, bf16[768,512]{1,0:T(8,128)(2,1)}, u32[]{:S(2)}, u32[]{:S(2)}) collective-permute-start(bf16[768,512]{1,0:T(8,128)(2,1)} %constant_dynamic-slice_fusion.6), channel_id=1, source_target_pairs={{0,2},{2,0},{1,3},{3,1},{4,6},{6,4},{5,7},{7,5},{8,10},{10,8},{9,1... | collective-permute-start | bytes 2359304 | tf_op jit(solution)/shard_map/ppermute | solution.py:388
  6.2 36.7 %collective-permute-start.2 = (bf16[512,768]{0,1:T(8,128)(2,1)}, bf16[512,768]{0,1:T(8,128)(2,1)}, u32[]{:S(2)}, u32[]{:S(2)}) collective-permute-start(bf16[512,768]{0,1:T(8,128)(2,1)} %get-tuple-element.236), channel_id=1, source_target_pairs={{0,2},{2,0},{1,3},{3,1},{4,6},{6,4},{5,7},{7,5},{8,10},{10,8},{9,1... | collective-permute-start | bytes 2359304 | tf_op jit(solution)/shard_map/ppermute | solution.py:388
  17.3 79.1 %collective-permute-start.5 = (bf16[512,1312]{0,1:T(8,128)(2,1)}, bf16[512,1312]{0,1:T(8,128)(2,1)}, u32[]{:S(2)}, u32[]{:S(2)}) collective-permute-start(bf16[512,1312]{0,1:T(8,128)(2,1)} %fusion.58), channel_id=1, source_target_pairs={{0,2},{2,0},{1,3},{3,1},{4,6},{6,4},{5,7},{7,5},{8,10},{10,8},{9,1... | collective-permute-start | bytes 4030472 | tf_op jit(solution)/shard_map/ppermute | solution.py:388
  17.4 79.0 %collective-permute-start.6 = (bf16[512,512]{1,0:T(8,128)(2,1)}, bf16[512,512]{1,0:T(8,128)(2,1)}, u32[]{:S(2)}, u32[]{:S(2)}) collective-permute-start(bf16[512,512]{1,0:T(8,128)(2,1)} %convert_element_type.234), channel_id=1, source_target_pairs={{0,2},{2,0},{1,3},{3,1},{4,6},{6,4},{5,7},{7,5},{8,10},{10,8},{9,1... | collective-permute-start | bytes 1572872 | tf_op jit(solution)/shard_map/ppermute | solution.py:388
  18.9 77.6 %collective-permute-start.7 = (bf16[384,512]{1,0:T(8,128)(2,1)S(1)}, bf16[384,512]{1,0:T(8,128)(2,1)}, u32[]{:S(2)}, u32[]{:S(2)}) collective-permute-start(bf16[384,512]{1,0:T(8,128)(2,1)S(1)} %constant_dynamic-slice_fusion.2), channel_id=1, source_target_pairs={{0,2},{2,0},{1,3},{3,1},{4,6},{6,4},{5,7},{7,5},{8,10},{10,8},{9,1... | collective-permute-start | bytes 1179656 | tf_op jit(solution)/shard_map/ppermute | solution.py:388
  51.2 49.0 %collective-permute-start.3 = (bf16[1024,512]{1,0:T(8,128)(2,1)}, bf16[1024,512]{1,0:T(8,128)(2,1)}, u32[]{:S(2)}, u32[]{:S(2)}) collective-permute-start(bf16[1024,512]{1,0:T(8,128)(2,1)} %get-tuple-element.233), channel_id=1, source_target_pairs={{0,4},{4,8},{8,12},{12,16},{16,20},{20,24},{24,28},{1,5},{5,9},{9,... | collective-permute-start | bytes 3145736 | tf_op jit(solution)/shard_map/ppermute | solution.py:523
  55.9 44.3 %collective-permute-start.4 = (bf16[1024,512]{1,0:T(8,128)(2,1)}, bf16[1024,512]{1,0:T(8,128)(2,1)}, u32[]{:S(2)}, u32[]{:S(2)}) collective-permute-start(bf16[1024,512]{1,0:T(8,128)(2,1)} %get-tuple-element.232), channel_id=1, source_target_pairs={{4,0},{8,4},{12,8},{16,12},{20,16},{24,20},{28,24},{5,1},{9,5},{13... | collective-permute-start | bytes 3145736 | tf_op jit(solution)/shard_map/ppermute | solution.py:524
  100.2 17.5 %collective-permute-start.8 = (bf16[656,512]{1,0:T(8,128)(2,1)}, bf16[656,512]{1,0:T(8,128)(2,1)}, u32[]{:S(2)}, u32[]{:S(2)}) collective-permute-start(bf16[656,512]{1,0:T(8,128)(2,1)} %constant_dynamic-slice_fusion.3), channel_id=1, source_target_pairs={{0,2},{2,0},{1,3},{3,1},{4,6},{6,4},{5,7},{7,5},{8,10},{10,8},{9,1... | collective-permute-start | bytes 2015240 | tf_op jit(solution)/shard_map/ppermute | solution.py:388
  103.6 33.1 %collective-permute-start.14 = (bf16[512,1312]{0,1:T(8,128)(2,1)}, bf16[512,1312]{0,1:T(8,128)(2,1)}, u32[]{:S(2)}, u32[]{:S(2)}) collective-permute-start(bf16[512,1312]{0,1:T(8,128)(2,1)} %collective-permute-done.5), channel_id=1, source_target_pairs={{0,8},{4,12},{8,0},{12,4},{16,24},{20,28},{24,16},{28,20},{1,9},{5... | collective-permute-start | bytes 4030472 | tf_op jit(solution)/shard_map/ppermute | solution.py:483
  126.8 24.3 %collective-permute-start.13 = (bf16[656,512]{1,0:T(8,128)(2,1)}, bf16[656,512]{1,0:T(8,128)(2,1)}, u32[]{:S(2)}, u32[]{:S(2)}) collective-permute-start(bf16[656,512]{1,0:T(8,128)(2,1)} %collective-permute-done.8), channel_id=1, source_target_pairs={{0,8},{4,12},{8,0},{12,4},{16,24},{20,28},{24,16},{28,20},{1,9},{5... | collective-permute-start | bytes 2015240 | tf_op jit(solution)/shard_map/ppermute | solution.py:483
  166.2 13.4 %collective-permute-start.15 = (bf16[768,1024]{1,0:T(8,128)(2,1)S(1)}, bf16[768,1024]{1,0:T(8,128)(2,1)S(1)}, u32[]{:S(2)}, u32[]{:S(2)}) collective-permute-start(bf16[768,1024]{1,0:T(8,128)(2,1)S(1)} %fusion.156), channel_id=1, source_target_pairs={{0,1},{1,0},{2,3},{3,2},{4,5},{5,4},{6,7},{7,6},{8,9},{9,8},{10,11... | collective-permute-start | bytes 4718600 | tf_op jit(solution)/shard_map/ppermute | solution.py:391
  177.2 30.6 %collective-permute-start.17 = (bf16[1312,512]{1,0:T(8,128)(2,1)S(1)}, bf16[1312,512]{1,0:T(8,128)(2,1)S(1)}, u32[]{:S(2)}, u32[]{:S(2)}) collective-permute-start(bf16[1312,512]{1,0:T(8,128)(2,1)S(1)} %convolution_convert_fusion.2), channel_id=1, source_target_pairs={{0,4},{4,0},{8,12},{12,8},{16,20},{20,16},{24,28},{28,24},{1,5},{5... | collective-permute-start | bytes 4030472 | tf_op jit(solution)/shard_map/ppermute | solution.py:480
  179.2 28.6 %collective-permute-start.19 = (bf16[384,512]{1,0:T(8,128)(2,1)S(1)}, bf16[384,512]{1,0:T(8,128)(2,1)S(1)}, u32[]{:S(2)}, u32[]{:S(2)}) collective-permute-start(bf16[384,512]{1,0:T(8,128)(2,1)S(1)} %get-tuple-element.248), channel_id=1, source_target_pairs={{0,2},{2,0},{1,3},{3,1},{4,6},{6,4},{5,7},{7,5},{8,10},{10,8},{9,1... | collective-permute-start | bytes 1179656 | tf_op jit(solution)/shard_map/ppermute | solution.py:388
  185.1 31.6 %collective-permute-start.16 = (bf16[768,256]{1,0:T(8,128)(2,1)S(1)}, bf16[768,256]{1,0:T(8,128)(2,1)S(1)}, u32[]{:S(2)}, u32[]{:S(2)}) collective-permute-start(bf16[768,256]{1,0:T(8,128)(2,1)S(1)} %get-tuple-element.252), channel_id=1, source_target_pairs={{0,2},{2,0},{1,3},{3,1},{4,6},{6,4},{5,7},{7,5},{8,10},{10,8},{9,1... | collective-permute-start | bytes 1179656 | tf_op jit(solution)/shard_map/ppermute | solution.py:388
  211.0 21.8 %collective-permute-start.21 = (bf16[1312,256]{1,0:T(8,128)(2,1)}, bf16[1312,256]{1,0:T(8,128)(2,1)}, u32[]{:S(2)}, u32[]{:S(2)}) collective-permute-start(bf16[1312,256]{1,0:T(8,128)(2,1)} %slice.749), channel_id=1, source_target_pairs={{0,8},{4,12},{8,0},{12,4},{16,24},{20,28},{24,16},{28,20},{1,9},{5... | collective-permute-start | bytes 2015240 | tf_op jit(solution)/shard_map/ppermute | solution.py:483
  216.7 71.3 %collective-permute-start.25 = (bf16[512,512]{1,0:T(8,128)(2,1)}, bf16[512,512]{1,0:T(8,128)(2,1)}, u32[]{:S(2)}, u32[]{:S(2)}) collective-permute-start(bf16[512,512]{1,0:T(8,128)(2,1)} %convolution_convert_fusion.4), channel_id=1, source_target_pairs={{0,4},{4,0},{8,12},{12,8},{16,20},{20,16},{24,28},{28,24},{1,5},{5... | collective-permute-start | bytes 1572872 | tf_op jit(solution)/shard_map/ppermute | solution.py:480
  216.7 66.0 %collective-permute-start.24 = (bf16[2624,512]{1,0:T(8,128)(2,1)}, bf16[2624,512]{1,0:T(8,128)(2,1)}, u32[]{:S(2)}, u32[]{:S(2)}) collective-permute-start(bf16[2624,512]{1,0:T(8,128)(2,1)} %pad_maximum_fusion.1), channel_id=1, source_target_pairs={{0,2},{2,0},{1,3},{3,1},{4,6},{6,4},{5,7},{7,5},{8,10},{10,8},{9,1... | collective-permute-start | bytes 8060936 | tf_op jit(solution)/shard_map/ppermute | solution.py:388
  235.5 61.6 %collective-permute-start.22 = (bf16[1024,512]{1,0:T(8,128)(2,1)}, bf16[1024,512]{1,0:T(8,128)(2,1)}, u32[]{:S(2)}, u32[]{:S(2)}) collective-permute-start(bf16[1024,512]{1,0:T(8,128)(2,1)} %get-tuple-element.134), channel_id=1, source_target_pairs={{4,0},{8,4},{12,8},{16,12},{20,16},{24,20},{28,24},{5,1},{9,5},{13... | collective-permute-start | bytes 3145736 | tf_op jit(solution)/shard_map/ppermute | solution.py:661
  236.8 60.3 %collective-permute-start.23 = (bf16[1024,512]{1,0:T(8,128)(2,1)}, bf16[1024,512]{1,0:T(8,128)(2,1)}, u32[]{:S(2)}, u32[]{:S(2)}) collective-permute-start(bf16[1024,512]{1,0:T(8,128)(2,1)} %get-tuple-element.135), channel_id=1, source_target_pairs={{0,4},{4,8},{8,12},{12,16},{16,20},{20,24},{24,28},{1,5},{5,9},{9,... | collective-permute-start | bytes 3145736 | tf_op jit(solution)/shard_map/ppermute | solution.py:662
  279.2 17.9 %collective-permute-start.26 = (bf16[1312,128]{1,0:T(8,128)(2,1)S(1)}, bf16[1312,128]{1,0:T(8,128)(2,1)S(1)}, u32[]{:S(2)}, u32[]{:S(2)}) collective-permute-start(bf16[1312,128]{1,0:T(8,128)(2,1)S(1)} %slice.756), channel_id=1, source_target_pairs={{0,16},{4,20},{8,24},{12,28},{16,0},{20,4},{24,8},{28,12},{1,17},{... | collective-permute-start | bytes 1007624 | tf_op jit(solution)/shard_map/ppermute | solution.py:483
  303.8 21.0 %collective-permute-start.27 = (bf16[768,1024]{1,0:T(8,128)(2,1)S(1)}, bf16[768,1024]{1,0:T(8,128)(2,1)S(1)}, u32[]{:S(2)}, u32[]{:S(2)}) collective-permute-start(bf16[768,1024]{1,0:T(8,128)(2,1)S(1)} %dynamic-slice_convert_fusion), channel_id=1, source_target_pairs={{0,1},{1,0},{2,3},{3,2},{4,5},{5,4},{6,7},{7,6},{8,9},{9,8},{10,11... | collective-permute-start | bytes 4718600 | tf_op jit(solution)/shard_map/ppermute | solution.py:391
  305.5 20.9 %collective-permute-start.28 = (bf16[768,512]{1,0:T(8,128)(2,1)S(1)}, bf16[768,512]{1,0:T(8,128)(2,1)S(1)}, u32[]{:S(2)}, u32[]{:S(2)}) collective-permute-start(bf16[768,512]{1,0:T(8,128)(2,1)S(1)} %copy-done.34), channel_id=1, source_target_pairs={{0,2},{3,1},{4,6},{7,5},{8,10},{11,9},{12,14},{15,13},{16,18},{19,... | collective-permute-start | bytes 2359304 | tf_op jit(solution)/shard_map/ppermute | solution.py:697
  308.7 31.4 %collective-permute-start.34 = (bf16[2624,256]{1,0:T(8,128)(2,1)S(1)}, bf16[2624,256]{1,0:T(8,128)(2,1)S(1)}, u32[]{:S(2)}, u32[]{:S(2)}) collective-permute-start(bf16[2624,256]{1,0:T(8,128)(2,1)S(1)} %pad_maximum_fusion.3), channel_id=1, source_target_pairs={{0,4},{4,0},{8,12},{12,8},{16,20},{20,16},{24,28},{28,24},{1,5},{5... | collective-permute-start | bytes 4030472 | tf_op jit(solution)/shard_map/ppermute | solution.py:480
  312.7 19.8 %collective-permute-start.32 = (bf16[768,512]{1,0:T(8,128)(2,1)}, bf16[768,512]{1,0:T(8,128)(2,1)}, u32[]{:S(2)}, u32[]{:S(2)}) collective-permute-start(bf16[768,512]{1,0:T(8,128)(2,1)} %fusion.55), channel_id=1, source_target_pairs={{0,8},{4,12},{8,0},{12,4},{16,24},{20,28},{24,16},{28,20},{1,9},{5... | collective-permute-start | bytes 2359304 | tf_op jit(solution)/shard_map/ppermute | solution.py:483
  322.9 33.8 %collective-permute-start.41 = (bf16[1312,64]{1,0:T(8,128)(2,1)}, bf16[1312,64]{1,0:T(8,128)(2,1)}, u32[]{:S(2)}, u32[]{:S(2)}) collective-permute-start(bf16[1312,64]{1,0:T(8,128)(2,1)} %slice.751), channel_id=1, source_target_pairs={{0,2},{2,0},{1,3},{3,1},{4,6},{6,4},{5,7},{7,5},{8,10},{10,8},{9,1... | collective-permute-start | bytes 503816 | tf_op jit(solution)/shard_map/ppermute | solution.py:388
  326.4 28.1 %collective-permute-start.29 = (bf16[768,512]{1,0:T(8,128)(2,1)S(1)}, bf16[768,512]{1,0:T(8,128)(2,1)S(1)}, u32[]{:S(2)}, u32[]{:S(2)}) collective-permute-start(bf16[768,512]{1,0:T(8,128)(2,1)S(1)} %slice.745), channel_id=1, source_target_pairs={{0,2},{2,0},{1,3},{3,1},{4,6},{6,4},{5,7},{7,5},{8,10},{10,8},{9,1... | collective-permute-start | bytes 2359304 | tf_op jit(solution)/shard_map/ppermute | solution.py:388
  326.5 21.9 %collective-permute-start.30 = (f32[2,768]{1,0:T(2,128)S(1)}, f32[2,768]{1,0:T(2,128)S(1)}, u32[]{:S(2)}, u32[]{:S(2)}) collective-permute-start(f32[2,768]{1,0:T(2,128)S(1)} %pad_maximum_fusion.9), channel_id=1, source_target_pairs={{0,2},{2,0},{1,3},{3,1},{4,6},{6,4},{5,7},{7,5},{8,10},{10,8},{9,1... | collective-permute-start | bytes 18440 | tf_op jit(solution)/shard_map/ppermute | solution.py:388
  341.9 23.7 %collective-permute-start.37 = (bf16[3136,128]{1,0:T(8,128)(2,1)}, bf16[3136,128]{1,0:T(8,128)(2,1)}, u32[]{:S(2)}, u32[]{:S(2)}) collective-permute-start(bf16[3136,128]{1,0:T(8,128)(2,1)} %pad_maximum_fusion.6), channel_id=1, source_target_pairs={{0,8},{4,12},{8,0},{12,4},{16,24},{20,28},{24,16},{28,20},{1,9},{5... | collective-permute-start | bytes 2408456 | tf_op jit(solution)/shard_map/ppermute | solution.py:483
  353.3 16.3 %collective-permute-start.36 = (bf16[768,128]{1,0:T(8,128)(2,1)}, bf16[768,128]{1,0:T(8,128)(2,1)}, u32[]{:S(2)}, u32[]{:S(2)}) collective-permute-start(bf16[768,128]{1,0:T(8,128)(2,1)} %slice.758), channel_id=1, source_target_pairs={{0,16},{4,20},{8,24},{12,28},{16,0},{20,4},{24,8},{28,12},{1,17},{... | collective-permute-start | bytes 589832 | tf_op jit(solution)/shard_map/ppermute | solution.py:483
  355.1 39.9 %collective-permute-start.31 = (bf16[768,512]{1,0:T(8,128)(2,1)S(1)}, bf16[768,512]{1,0:T(8,128)(2,1)}, u32[]{:S(2)}, u32[]{:S(2)}) collective-permute-start(bf16[768,512]{1,0:T(8,128)(2,1)S(1)} %fusion.39), channel_id=1, source_target_pairs={{0,1},{1,0},{2,3},{3,2},{4,5},{5,4},{6,7},{7,6},{8,9},{9,8},{10,11... | collective-permute-start | bytes 2359304 | tf_op jit(solution)/shard_map/ppermute | solution.py:391
  369.5 20.4 %collective-permute-start.39 = (bf16[64,3136]{1,0:T(8,128)(2,1)}, bf16[64,3136]{1,0:T(8,128)(2,1)}, u32[]{:S(2)}, u32[]{:S(2)}) collective-permute-start(bf16[64,3136]{1,0:T(8,128)(2,1)} %copy.110), channel_id=1, source_target_pairs={{0,16},{4,20},{8,24},{12,28},{16,0},{20,4},{24,8},{28,12},{1,17},{... | collective-permute-start | bytes 1204232 | tf_op jit(solution)/shard_map/ppermute | solution.py:483
  374.3 23.8 %collective-permute-start.38 = (f32[64,896]{1,0:T(8,128)}, f32[64,896]{1,0:T(8,128)}, u32[]{:S(2)}, u32[]{:S(2)}) collective-permute-start(f32[64,896]{1,0:T(8,128)} %get-tuple-element.257), channel_id=1, source_target_pairs={{0,2},{2,0},{1,3},{3,1},{4,6},{6,4},{5,7},{7,5},{8,10},{10,8},{9,1... | collective-permute-start | bytes 688136 | tf_op jit(solution)/shard_map/ppermute | solution.py:388
  (77 other events, 860.1 us)

commit v9 on v8

--- a/solution.py
+++ b/solution.py
@@ -644,16 +644,13 @@
 
     if two:
         h2, da, du, o_heads, dx_late = after((h2, da, du, own_first(o_rows, 1), dx_low), do_rows)
-        dx_y = relative(dx_late, "yxzZ")
+        dx_y = relative(dx_late, "xyzZ")
         h_x = relative(h2, "xyzZ")
-        proj_got = to_y(product(o_heads, dx_y))
-        gate_send = jnp.concatenate([product(da, h_x), product(du, h_x)], axis=0)
+        gate_send = jnp.concatenate([product(da, h_x), product(du, h_x), product(o_heads, dx_y)], axis=0)
         gate_got = to_row(after(gate_send, do_got))
         pair = ordered(zrow, y_half[None, :, :Dl], after(y_got, gate_send)[None], 0)
         layer_out = ordered(zcol, pair[:, None], to_col(pair)[:, None], 1).reshape(S, Dl)
-        lower = halved(m, g_y, after(lower_got, gate_send))
-        lower_got = to_z(second(lower), 1)
-        do, lower, layer_out = lax.optimization_barrier((do, lower, layer_out))
+        do, layer_out = lax.optimization_barrier((do, layer_out))
 
     dq_part, dkv_left, dkv_right = attend_back_call(
         halo_bounds, q, do, o, lse, sq, [kv_left, kv_right], [sk_left, sk_right], heads
@@ -661,15 +658,16 @@
     from_right = lax.ppermute(dkv_left, "dp", down)
     from_left = lax.ppermute(dkv_right, "dp", up)
     if two:
-        lower = joined(lower, after(lower_got, dq_part))
-        lower_got = to_z(second(lower), 2)
+        lower = halved(m, g_y, after(lower_got, dq_part))
+        lower_got = to_z(second(lower), 1)
         dq_part, lower = lax.optimization_barrier((dq_part, lower))
     dq, dkv = attend_back_call(own_bounds, q, do, o, lse, sq, [kv], [sk_own], heads, [dq_part])
     if two:
         gate_got = after(gate_got, dq)
-        act, lin = halved(da, h_x, gate_got[:F]), halved(du, h_x, gate_got[F:])
-        dkv, from_right, from_left, act, lin, proj_got, lower_got = lax.optimization_barrier(
-            (dkv, from_right, from_left, act, lin, proj_got, lower_got)
+        act, lin = halved(da, h_x, gate_got[:F]), halved(du, h_x, gate_got[F : 2 * F])
+        proj = halved(o_heads, dx_y, gate_got[2 * F :])
+        dkv, from_right, from_left, act, lin, proj, lower_got = lax.optimization_barrier(
+            (dkv, from_right, from_left, act, lin, proj, lower_got)
         )
     pad = jnp.zeros((S - H, 2 * W), bf16)
     dkv = (
@@ -683,7 +681,7 @@
     if two:
         query_send = product(dt, h1_y)
         query_got = to_z(query_send, 1)
-        proj_got, lower_got = after((proj_got, lower_got), query_send, dh1_part)
+        lower_got = after(lower_got, query_send, dh1_part)
 
     if two:
         n = S // 2
@@ -713,32 +711,29 @@
         ).astype(bf16)
 
     if two:
-        def pair(one, other):
-            return jnp.concatenate([second(one), second(other)], axis=0)
-
-        def joined_pair(one, other, got):
-            n = one.shape[0]
-            return joined(one, got[:n]), joined(other, got[n:])
-
-        gate_got = to_y(pair(act, lin))
+        def three(*parts):
+            return jnp.concatenate([second(a) for a in parts], axis=0)
+
+        def joined_three(parts, got):
+            n = F
+            return [joined(a, g) for a, g in zip(parts, (got[:n], got[n : 2 * n], got[2 * n :]))]
+
+        gate_got = to_y(three(act, lin, proj))
         lower = joined(lower, lower_got)
-        proj = halved(o_heads, dx_y, proj_got)
-        proj = joined(proj, to_row(second(proj)))
-        last_got = to_row(second(lower))
+        lower_got = to_z(second(lower), 2)
         query = halved(dt, h1_y, after(query_got, kept))
         query_got = to_y(second(query))
-        act, lin = joined_pair(act, lin, after(gate_got, query))
-        gate_got = to_z(jnp.concatenate([second(act), second(lin), second(proj)], axis=0), 1)
+        act, lin, proj = joined_three((act, lin, proj), after(gate_got, query))
+        gate_got = to_z(three(act, lin, proj), 1)
+        lower = joined(lower, after(lower_got, act, lin, proj))
+        last_got = to_row(second(lower))
         query = joined(query, after(query_got, act, lin, proj))
         query_got = to_z(second(query), 2)
-        n = 2 * F
-        act, lin = joined_pair(act, lin, after(gate_got[:n], dx))
-        proj = joined(proj, after(gate_got[n:], dx))
-        gate_got = to_z(jnp.concatenate([second(act), second(lin), second(proj)], axis=0).T, 2).T
+        act, lin, proj = joined_three((act, lin, proj), after(gate_got, dx))
+        gate_got = to_z(three(act, lin, proj).T, 2).T
         query = joined(query, after(query_got, act, lin, proj))
         lower = joined(lower, after(last_got, dx))
-        act, lin = joined_pair(act, lin, gate_got[:n])
-        proj = joined(proj, gate_got[n:])
+        act, lin, proj = joined_three((act, lin, proj), gate_got)
         gate = jnp.stack([act.T, lin.T])
         query = query.T
         wq_rows = take(wq, b ^ (4 * r), Db)

time: 408 us -> 403 us (0.988)
  waiting for transfers between devices: 74.1 us -> 62.6 us
  other arithmetic: 70.4 us -> 76.3 us
    ppermute x4 -> x3, waiting for transfers between devices: 25.8 us -> 5.86 us  [to_y(): return lax.ppermute(a, 'dp', [(i, i ^ 1) for i in range(B)])]
    ppermute x8, waiting for transfers between devices: 36.4 us -> 50.1 us  [to_z(): return lax.ppermute(a, 'dp', [(i, i ^ 2 * j) for i in range(B)])]
    ppermute x15 -> x14, waiting for transfers between devices: 8.19 us -> 3.11 us  [to_row(): return lax.ppermute(a, 'row', SWAP)]
    ppermute x1, starting transfers between devices: 5.05 us -> 9.53 us  [local(): from_left = lax.ppermute(dkv_right, 'dp', up)]
    dot_general x10, matrix products: 17 us -> 21.2 us  [tn(): lax.dot_general(a, b, (((0,), (0,)), ((), ())), preferred_element_type=f32)]
    unnamed x133 -> x193, local copies, waits for them, and re-layouts: 11.6 us -> 15.2 us
    ppermute x15 -> x14, starting transfers between devices: 11.2 us -> 9.13 us  [to_row(): return lax.ppermute(a, 'row', SWAP)]
  transfers between devices with their start and end apart: 42 -> 40, of which waited for: 11 -> 10; matrix products, arithmetic and copies ran while one was open for 39% -> 41% of each run, Pallas kernels for 20% -> 20%
where the time goes in v9:
time: 403 us; the launch traced here: 395 us
  Pallas kernels  78.3 us (19%)
  other arithmetic  76.3 us (19%)
  matrix products  71.2 us (18%)
  waiting for transfers between devices  62.6 us (16%)
  local copies, waits for them, and re-layouts  53.8 us (13%)
  starting transfers between devices  50.2 us (12%)
    ppermute x8, waiting for transfers between devices, to_z(): return lax.ppermute(a, 'dp', [(i, i ^ 2 * j) for i in range(B)])  50.1 us
    pallas_call x2, Pallas kernels, attend_back_call(): pl.pallas_call(functools.partial(backward_kernel, heads, sets, final), gr...  44 us
    pallas_call x2, Pallas kernels, attend_call(): pl.pallas_call(functools.partial(forward_kernel, heads, sets, final), gri...  34.4 us
    dot_general x14, matrix products, nn(): return jnp.dot(a, b, preferred_element_type=f32)  30.4 us
    dot_general x10, matrix products, tn(): lax.dot_general(a, b, (((0,), (0,)), ((), ())), preferred_element_type=f32)  21.2 us
    dot_general x8, matrix products, nt(): lax.dot_general(a, b, (((1,), (1,)), ((), ())), preferred_element_type=f32)  17 us
    unnamed x193, local copies, waits for them, and re-layouts  15.2 us
    ppermute x8, starting transfers between devices, to_z(): return lax.ppermute(a, 'dp', [(i, i ^ 2 * j) for i in range(B)])  10.4 us
  transfers between devices with their start and end apart: 40, of which 10 were waited for; matrix products, arithmetic and copies ran while one was open for 41% of the time, Pallas kernels for 20%

profile of v9, /device:TPU:3, one launch (start us, length us, event | category | flops | bytes accessed | tf_op | source)
XLA Modules:
  0.0 395.3 jit_solution(6426366174310870326)
XLA Ops:
  8.8 2.8 multiply_sine_fusion
  11.7 2.7 convert_element_type.234
  15.1 3.0 fusion.58
  40.9 2.6 fusion.26
  49.1 4.8 %collective-permute-start.3 = (bf16[1024,512]{1,0:T(8,128)(2,1)}, bf16[1024,512]{1,0:T(8,128)(2,1)}, u32[]{:S(2)}, u32[]{:S(2)}) collective-permute-start(bf16[1024,512]{1,0:T(8,128)(2,1)} %get-tuple-element.229), channel_id=1, source_target_pairs={{0,4},{4,8},{8,12},{12,16},{16,20},{20,24},{24,28},{1,5},{5,9},{9,... | collective-permute-start | bytes 3145736 | tf_op jit(solution)/shard_map/ppermute | solution.py:523
  55.4 5.2 %fusion.15 = bf16[1536,1024]{1,0:T(8,128)(2,1)} fusion(bf16[1536,1024]{1,0:T(8,128)(2,1)S(1)} %fusion.4, s32[1024]{0:T(1024)S(1)} %add_xor_fusion.2), kind=kOutput, calls=%fused_computation.27 | convolution fusion | flops 3223846912 | bytes 6295552 | tf_op jit(solution)/shard_map/dot_general | solution.py:32
  69.1 25.5 %attend_own.1 = (f32[6,256,256]{2,1,0:T(8,128)}, f32[6,2,1024]{2,1,0:T(2,128)}) custom-call(s32[12]{0:T(128)} %reshape.741.bounds, bf16[1536,256]{1,0:T(8,128)(2,1)} %fusion.45.refs_0_, s32[6,1,256]{2,1,0:T(1,128)} %select_n.655.refs_1_.refs_4_, bf16[1536,512]{1,0:T(8,128)(2,1)} %copy-done.5, s32[1536,128]{1,0:T(8,128)} %broadcast_in_dim.132.refs_3_.refs_6_), custom_call_target="tpu_custom_call" | custom-call | flops 6291456 | bytes 3145728 | tf_op jit(solution)/shard_map/attend_own/pallas_call | solution.py:194
  94.6 3.6 collective-permute-done.3.refs_2_.refs_5_
  100.9 3.6 collective-permute-start.14
  104.5 8.8 %attend_final.1 = (bf16[1536,256]{1,0:T(8,128)(2,1)}, f32[6,1,1024]{2,1,0:T(1,128)}) custom-call(s32[24]{0:T(128)} %reshape.740.bounds, bf16[1536,256]{1,0:T(8,128)(2,1)} %fusion.45.refs_0_, s32[6,1,256]{2,1,0:T(1,128)} %select_n.655.refs_1_.refs_4_, bf16[1024,512]{1,0:T(8,128)(2,1)} %collective-permute-done.3.refs_2_.refs_5_, ...), custom_call_target="tpu_custom_call" | custom-call | flops 6291456 | bytes 3670016 | tf_op jit(solution)/shard_map/attend_final/pallas_call | solution.py:194
  124.7 3.6 collective-permute-start.13
  136.2 3.2 fusion.164
  148.2 6.5 %multiply_convert_fusion = (bf16[768,1312]{0,1:T(8,128)(2,1)}, bf16[768,1312]{0,1:T(8,128)(2,1)S(1)}, bf16[768,1312]{0,1:T(8,128)(2,1)S(1)}) fusion(f32[768,1312]{0,1:T(8,128)S(1)} %convolution_add_fusion.1, f32[768,1312]{0,1:T(8,128)S(1)} %convolution_add_fusion, f32[768,1312]{0,1:T(8,128)S(1)} %fusion.74, ...), kind=kOutput, calls=%fused_computation.24 | convolution fusion | flops 1054973952 | bytes 20267008 | tf_op jit(solution)/shard_map/dot_general | solution.py:24
  163.5 2.8 fusion.103
  170.2 3.4 fusion.27
  179.8 2.6 fusion.65
  182.4 4.0 %fusion.158 = (bf16[768,1024]{1,0:T(8,128)(2,1)S(1)}, f32[768,1024]{1,0:T(8,128)}) fusion(f32[768]{0:T(1024)S(1)} %broadcast_multiply_fusion.2, f32[768,1024]{1,0:T(8,128)S(1)} %get-tuple-element.272, f32[768]{0:T(1024)S(1)} %broadcast_multiply_fusion.4, f32[768]{0:T(1024)S(1)} %broadcast_multiply_fusion.3, f32[1024]{0:T(1024)S(1)} %maximum_select_fusion.15, ...), kind=kLoop, calls=%fused_computation.380 | loop fusion | flops 10223616 | bytes 14172160 | tf_op jit(solution)/shard_map/convert_element_type | solution.py:637
  200.4 4.4 %fusion.70 = f32[1312,512]{1,0:T(8,128)} fusion(bf16[768,1312]{0,1:T(8,128)(2,1)} %get-tuple-element.214, bf16[768,1024]{1,0:T(8,128)(2,1)} %copy-done.89), kind=kOutput, calls=%fused_computation.151 | convolution fusion | flops 1031798784 | bytes 5488640 | tf_op jit(solution)/shard_map/dot_general | solution.py:28
  209.9 10.5 %back_halo.1 = (f32[6,256,256]{2,1,0:T(8,128)}, bf16[1024,512]{1,0:T(8,128)(2,1)}, bf16[1024,512]{1,0:T(8,128)(2,1)}) custom-call(s32[24]{0:T(128)} %reshape.740.bounds, bf16[1536,256]{1,0:T(8,128)(2,1)} %fusion.45.refs_0_, bf16[1536,256]{1,0:T(8,128)(2,1)} %maximum_select_fusion.7.refs_1_, bf16[1536,256]{1,0:T(8,128)(2,1)} %get-tuple-element.108.refs_2_, ...), custom_call_target="tpu_custom_call" | custom-call | flops 15728640 | bytes 3670016 | tf_op jit(solution)/shard_map/back_halo/pallas_call | solution.py:320
  225.2 9.5 %collective-permute-start.22 = (bf16[1024,512]{1,0:T(8,128)(2,1)}, bf16[1024,512]{1,0:T(8,128)(2,1)}, u32[]{:S(2)}, u32[]{:S(2)}) collective-permute-start(bf16[1024,512]{1,0:T(8,128)(2,1)} %get-tuple-element.132), channel_id=1, source_target_pairs={{0,4},{4,8},{8,12},{12,16},{16,20},{20,24},{24,28},{1,5},{5,9},{9,... | collective-permute-start | bytes 3145736 | tf_op jit(solution)/shard_map/ppermute | solution.py:659
  236.1 33.5 %back_own.1 = (f32[1536,256]{1,0:T(8,128)}, f32[1536,512]{1,0:T(8,128)}) custom-call(s32[12]{0:T(128)} %reshape.741.bounds, bf16[1536,256]{1,0:T(8,128)(2,1)} %fusion.45.refs_0_, bf16[1536,256]{1,0:T(8,128)(2,1)} %maximum_select_fusion.7.refs_1_, bf16[1536,256]{1,0:T(8,128)(2,1)} %get-tuple-element.108.refs_2_, f32[6,1,1024]{2,1,0:T(1,128)} %get-tuple-element.124.refs_3_, ...), custom_call_target="tpu_custom_call" | custom-call | flops 15728640 | bytes 3145728 | tf_op jit(solution)/shard_map/back_own/pallas_call | solution.py:320
  273.5 2.6 convert_add_fusion.4
  278.8 3.0 convert_add_fusion.3
  281.8 3.2 convert_add_fusion.1
  286.7 2.6 fusion.168
  291.0 3.0 collective-permute-start.26
  305.2 20.1 %collective-permute-done.30 = bf16[768,512]{1,0:T(8,128)(2,1)S(1)} collective-permute-done((bf16[768,512]{1,0:T(8,128)(2,1)}, bf16[768,512]{1,0:T(8,128)(2,1)S(1)}, u32[]{:S(2)}, u32[]{:S(2)}) %collective-permute-start.30) | collective-permute-done | bytes 786464 | tf_op jit(solution)/shard_map/ppermute | solution.py:483
  334.6 5.3 %collective-permute-done.31 = bf16[768,256]{1,0:T(8,128)(2,1)S(1)} collective-permute-done((bf16[768,256]{1,0:T(8,128)(2,1)S(1)}, bf16[768,256]{1,0:T(8,128)(2,1)S(1)}, u32[]{:S(2)}, u32[]{:S(2)}) %collective-permute-start.31) | collective-permute-done | bytes 393248 | tf_op jit(solution)/shard_map/ppermute | solution.py:480
  344.3 13.0 %collective-permute-done.34 = bf16[3136,128]{1,0:T(8,128)(2,1)} collective-permute-done((bf16[3136,128]{1,0:T(8,128)(2,1)}, bf16[3136,128]{1,0:T(8,128)(2,1)}, u32[]{:S(2)}, u32[]{:S(2)}) %collective-permute-start.34) | collective-permute-done | bytes 802848 | tf_op jit(solution)/shard_map/ppermute | solution.py:483
  361.4 2.6 fusion.16
  367.0 14.7 %collective-permute-done.36 = bf16[64,3136]{1,0:T(8,128)(2,1)} collective-permute-done((bf16[64,3136]{1,0:T(8,128)(2,1)}, bf16[64,3136]{1,0:T(8,128)(2,1)}, u32[]{:S(2)}, u32[]{:S(2)}) %collective-permute-start.36) | collective-permute-done | bytes 401440 | tf_op jit(solution)/shard_map/ppermute | solution.py:483
  386.8 3.2 maximum_select_fusion.4
  (436 shorter events, 172.7 us)
Async XLA Ops:
  2.8 25.2 %collective-permute-start = (bf16[768,512]{1,0:T(8,128)(2,1)}, bf16[768,512]{1,0:T(8,128)(2,1)}, u32[]{:S(2)}, u32[]{:S(2)}) collective-permute-start(bf16[768,512]{1,0:T(8,128)(2,1)} %constant_dynamic-slice_fusion.6), channel_id=1, source_target_pairs={{0,2},{2,0},{1,3},{3,1},{4,6},{6,4},{5,7},{7,5},{8,10},{10,8},{9,1... | collective-permute-start | bytes 2359304 | tf_op jit(solution)/shard_map/ppermute | solution.py:388
  6.2 34.7 %collective-permute-start.2 = (bf16[512,768]{0,1:T(8,128)(2,1)}, bf16[512,768]{0,1:T(8,128)(2,1)}, u32[]{:S(2)}, u32[]{:S(2)}) collective-permute-start(bf16[512,768]{0,1:T(8,128)(2,1)} %get-tuple-element.232), channel_id=1, source_target_pairs={{0,2},{2,0},{1,3},{3,1},{4,6},{6,4},{5,7},{7,5},{8,10},{10,8},{9,1... | collective-permute-start | bytes 2359304 | tf_op jit(solution)/shard_map/ppermute | solution.py:388
  18.1 76.5 %collective-permute-start.5 = (bf16[512,1312]{0,1:T(8,128)(2,1)}, bf16[512,1312]{0,1:T(8,128)(2,1)}, u32[]{:S(2)}, u32[]{:S(2)}) collective-permute-start(bf16[512,1312]{0,1:T(8,128)(2,1)} %fusion.58), channel_id=1, source_target_pairs={{0,2},{2,0},{1,3},{3,1},{4,6},{6,4},{5,7},{7,5},{8,10},{10,8},{9,1... | collective-permute-start | bytes 4030472 | tf_op jit(solution)/shard_map/ppermute | solution.py:388
  18.1 76.5 %collective-permute-start.6 = (bf16[512,512]{1,0:T(8,128)(2,1)}, bf16[512,512]{1,0:T(8,128)(2,1)}, u32[]{:S(2)}, u32[]{:S(2)}) collective-permute-start(bf16[512,512]{1,0:T(8,128)(2,1)} %convert_element_type.234), channel_id=1, source_target_pairs={{0,2},{2,0},{1,3},{3,1},{4,6},{6,4},{5,7},{7,5},{8,10},{10,8},{9,1... | collective-permute-start | bytes 1572872 | tf_op jit(solution)/shard_map/ppermute | solution.py:388
  19.6 75.0 %collective-permute-start.7 = (bf16[384,512]{1,0:T(8,128)(2,1)}, bf16[384,512]{1,0:T(8,128)(2,1)S(1)}, u32[]{:S(2)}, u32[]{:S(2)}) collective-permute-start(bf16[384,512]{1,0:T(8,128)(2,1)} %constant_dynamic-slice_fusion.2), channel_id=1, source_target_pairs={{0,2},{2,0},{1,3},{3,1},{4,6},{6,4},{5,7},{7,5},{8,10},{10,8},{9,1... | collective-permute-start | bytes 1179656 | tf_op jit(solution)/shard_map/ppermute | solution.py:388
  49.1 49.0 %collective-permute-start.3 = (bf16[1024,512]{1,0:T(8,128)(2,1)}, bf16[1024,512]{1,0:T(8,128)(2,1)}, u32[]{:S(2)}, u32[]{:S(2)}) collective-permute-start(bf16[1024,512]{1,0:T(8,128)(2,1)} %get-tuple-element.229), channel_id=1, source_target_pairs={{0,4},{4,8},{8,12},{12,16},{16,20},{20,24},{24,28},{1,5},{5,9},{9,... | collective-permute-start | bytes 3145736 | tf_op jit(solution)/shard_map/ppermute | solution.py:523
  54.0 44.2 %collective-permute-start.4 = (bf16[1024,512]{1,0:T(8,128)(2,1)}, bf16[1024,512]{1,0:T(8,128)(2,1)}, u32[]{:S(2)}, u32[]{:S(2)}) collective-permute-start(bf16[1024,512]{1,0:T(8,128)(2,1)} %get-tuple-element.228), channel_id=1, source_target_pairs={{4,0},{8,4},{12,8},{16,12},{20,16},{24,20},{28,24},{5,1},{9,5},{13... | collective-permute-start | bytes 3145736 | tf_op jit(solution)/shard_map/ppermute | solution.py:524
  98.2 16.8 %collective-permute-start.8 = (bf16[656,512]{1,0:T(8,128)(2,1)}, bf16[656,512]{1,0:T(8,128)(2,1)}, u32[]{:S(2)}, u32[]{:S(2)}) collective-permute-start(bf16[656,512]{1,0:T(8,128)(2,1)} %constant_dynamic-slice_fusion.3), channel_id=1, source_target_pairs={{0,2},{2,0},{1,3},{3,1},{4,6},{6,4},{5,7},{7,5},{8,10},{10,8},{9,1... | collective-permute-start | bytes 2015240 | tf_op jit(solution)/shard_map/ppermute | solution.py:388
  100.9 33.0 %collective-permute-start.14 = (bf16[512,1312]{0,1:T(8,128)(2,1)}, bf16[512,1312]{0,1:T(8,128)(2,1)}, u32[]{:S(2)}, u32[]{:S(2)}) collective-permute-start(bf16[512,1312]{0,1:T(8,128)(2,1)} %collective-permute-done.5), channel_id=1, source_target_pairs={{0,8},{4,12},{8,0},{12,4},{16,24},{20,28},{24,16},{28,20},{1,9},{5... | collective-permute-start | bytes 4030472 | tf_op jit(solution)/shard_map/ppermute | solution.py:483
  119.7 11.7 %collective-permute-start.9 = (bf16[384,512]{1,0:T(8,128)(2,1)}, bf16[384,512]{1,0:T(8,128)(2,1)S(1)}, u32[]{:S(2)}, u32[]{:S(2)}) collective-permute-start(bf16[384,512]{1,0:T(8,128)(2,1)} %copy-done.58), channel_id=1, source_target_pairs={{0,1},{1,0},{2,3},{3,2},{4,5},{5,4},{6,7},{7,6},{8,9},{9,8},{10,11... | collective-permute-start | bytes 1179656 | tf_op jit(solution)/shard_map/ppermute | solution.py:391
  124.7 23.5 %collective-permute-start.13 = (bf16[656,512]{1,0:T(8,128)(2,1)}, bf16[656,512]{1,0:T(8,128)(2,1)S(1)}, u32[]{:S(2)}, u32[]{:S(2)}) collective-permute-start(bf16[656,512]{1,0:T(8,128)(2,1)} %collective-permute-done.8), channel_id=1, source_target_pairs={{0,8},{4,12},{8,0},{12,4},{16,24},{20,28},{24,16},{28,20},{1,9},{5... | collective-permute-start | bytes 2015240 | tf_op jit(solution)/shard_map/ppermute | solution.py:483
  162.2 17.0 %collective-permute-start.15 = (bf16[768,1024]{1,0:T(8,128)(2,1)}, bf16[768,1024]{1,0:T(8,128)(2,1)}, u32[]{:S(2)}, u32[]{:S(2)}) collective-permute-start(bf16[768,1024]{1,0:T(8,128)(2,1)} %fusion.157), channel_id=1, source_target_pairs={{0,1},{1,0},{2,3},{3,2},{4,5},{5,4},{6,7},{7,6},{8,9},{9,8},{10,11... | collective-permute-start | bytes 4718600 | tf_op jit(solution)/shard_map/ppermute | solution.py:391
  175.9 44.5 %collective-permute-start.20 = (bf16[1312,512]{1,0:T(8,128)(2,1)}, bf16[1312,512]{1,0:T(8,128)(2,1)}, u32[]{:S(2)}, u32[]{:S(2)}) collective-permute-start(bf16[1312,512]{1,0:T(8,128)(2,1)} %convolution_convert_fusion), channel_id=1, source_target_pairs={{0,4},{4,0},{8,12},{12,8},{16,20},{20,16},{24,28},{28,24},{1,5},{5... | collective-permute-start | bytes 4030472 | tf_op jit(solution)/shard_map/ppermute | solution.py:480
  179.1 19.9 %collective-permute-start.18 = (bf16[384,512]{1,0:T(8,128)(2,1)S(1)}, bf16[384,512]{1,0:T(8,128)(2,1)S(1)}, u32[]{:S(2)}, u32[]{:S(2)}) collective-permute-start(bf16[384,512]{1,0:T(8,128)(2,1)S(1)} %get-tuple-element.244), channel_id=1, source_target_pairs={{0,2},{2,0},{1,3},{3,1},{4,6},{6,4},{5,7},{7,5},{8,10},{10,8},{9,1... | collective-permute-start | bytes 1179656 | tf_op jit(solution)/shard_map/ppermute | solution.py:388
  188.2 11.6 %collective-permute-start.16 = (bf16[768,256]{1,0:T(8,128)(2,1)}, bf16[768,256]{1,0:T(8,128)(2,1)}, u32[]{:S(2)}, u32[]{:S(2)}) collective-permute-start(bf16[768,256]{1,0:T(8,128)(2,1)} %get-tuple-element.248), channel_id=1, source_target_pairs={{0,2},{2,0},{1,3},{3,1},{4,6},{6,4},{5,7},{7,5},{8,10},{10,8},{9,1... | collective-permute-start | bytes 1179656 | tf_op jit(solution)/shard_map/ppermute | solution.py:388
  199.9 72.0 %collective-permute-start.23 = (bf16[3136,512]{1,0:T(8,128)(2,1)}, bf16[3136,512]{1,0:T(8,128)(2,1)}, u32[]{:S(2)}, u32[]{:S(2)}) collective-permute-start(bf16[3136,512]{1,0:T(8,128)(2,1)} %pad_maximum_fusion), channel_id=1, source_target_pairs={{0,2},{2,0},{1,3},{3,1},{4,6},{6,4},{5,7},{7,5},{8,10},{10,8},{9,1... | collective-permute-start | bytes 9633800 | tf_op jit(solution)/shard_map/ppermute | solution.py:388
  223.9 57.9 %collective-permute-start.21 = (bf16[1024,512]{1,0:T(8,128)(2,1)}, bf16[1024,512]{1,0:T(8,128)(2,1)}, u32[]{:S(2)}, u32[]{:S(2)}) collective-permute-start(bf16[1024,512]{1,0:T(8,128)(2,1)} %get-tuple-element.131), channel_id=1, source_target_pairs={{4,0},{8,4},{12,8},{16,12},{20,16},{24,20},{28,24},{5,1},{9,5},{13... | collective-permute-start | bytes 3145736 | tf_op jit(solution)/shard_map/ppermute | solution.py:658
  225.2 56.6 %collective-permute-start.22 = (bf16[1024,512]{1,0:T(8,128)(2,1)}, bf16[1024,512]{1,0:T(8,128)(2,1)}, u32[]{:S(2)}, u32[]{:S(2)}) collective-permute-start(bf16[1024,512]{1,0:T(8,128)(2,1)} %get-tuple-element.132), channel_id=1, source_target_pairs={{0,4},{4,8},{8,12},{12,16},{16,20},{20,24},{24,28},{1,5},{5,9},{9,... | collective-permute-start | bytes 3145736 | tf_op jit(solution)/shard_map/ppermute | solution.py:659
  234.7 47.1 %collective-permute-start.24 = (bf16[1312,256]{1,0:T(8,128)(2,1)}, bf16[1312,256]{1,0:T(8,128)(2,1)S(1)}, u32[]{:S(2)}, u32[]{:S(2)}) collective-permute-start(bf16[1312,256]{1,0:T(8,128)(2,1)} %slice.751), channel_id=1, source_target_pairs={{0,8},{4,12},{8,0},{12,4},{16,24},{20,28},{24,16},{28,20},{1,9},{5... | collective-permute-start | bytes 2015240 | tf_op jit(solution)/shard_map/ppermute | solution.py:483
  289.6 12.3 %collective-permute-start.25 = (bf16[768,1024]{1,0:T(8,128)(2,1)S(1)}, bf16[768,1024]{1,0:T(8,128)(2,1)S(1)}, u32[]{:S(2)}, u32[]{:S(2)}) collective-permute-start(bf16[768,1024]{1,0:T(8,128)(2,1)S(1)} %dynamic-slice_convert_fusion), channel_id=1, source_target_pairs={{0,1},{1,0},{2,3},{3,2},{4,5},{5,4},{6,7},{7,6},{8,9},{9,8},{10,11... | collective-permute-start | bytes 4718600 | tf_op jit(solution)/shard_map/ppermute | solution.py:391
  291.0 12.5 %collective-permute-start.26 = (bf16[768,512]{1,0:T(8,128)(2,1)S(1)}, bf16[768,512]{1,0:T(8,128)(2,1)S(1)}, u32[]{:S(2)}, u32[]{:S(2)}) collective-permute-start(bf16[768,512]{1,0:T(8,128)(2,1)S(1)} %copy-done.52), channel_id=1, source_target_pairs={{0,2},{3,1},{4,6},{7,5},{8,10},{11,9},{12,14},{15,13},{16,18},{19,... | collective-permute-start | bytes 2359304 | tf_op jit(solution)/shard_map/ppermute | solution.py:695
  294.4 37.2 %collective-permute-start.32 = (bf16[3136,256]{1,0:T(8,128)(2,1)S(1)}, bf16[3136,256]{1,0:T(8,128)(2,1)S(1)}, u32[]{:S(2)}, u32[]{:S(2)}) collective-permute-start(bf16[3136,256]{1,0:T(8,128)(2,1)S(1)} %pad_maximum_fusion.2), channel_id=1, source_target_pairs={{0,4},{4,0},{8,12},{12,8},{16,20},{20,16},{24,28},{28,24},{1,5},{5... | collective-permute-start | bytes 4816904 | tf_op jit(solution)/shard_map/ppermute | solution.py:480
  298.4 26.8 %collective-permute-start.30 = (bf16[768,512]{1,0:T(8,128)(2,1)}, bf16[768,512]{1,0:T(8,128)(2,1)S(1)}, u32[]{:S(2)}, u32[]{:S(2)}) collective-permute-start(bf16[768,512]{1,0:T(8,128)(2,1)} %fusion.55), channel_id=1, source_target_pairs={{0,8},{4,12},{8,0},{12,4},{16,24},{20,28},{24,16},{28,20},{1,9},{5... | collective-permute-start | bytes 2359304 | tf_op jit(solution)/shard_map/ppermute | solution.py:483
  300.1 34.2 %collective-permute-start.38 = (bf16[1312,128]{1,0:T(8,128)(2,1)}, bf16[1312,128]{1,0:T(8,128)(2,1)S(1)}, u32[]{:S(2)}, u32[]{:S(2)}) collective-permute-start(bf16[1312,128]{1,0:T(8,128)(2,1)} %slice.754), channel_id=1, source_target_pairs={{0,16},{4,20},{8,24},{12,28},{16,0},{20,4},{24,8},{28,12},{1,17},{... | collective-permute-start | bytes 1007624 | tf_op jit(solution)/shard_map/ppermute | solution.py:483
  303.5 37.3 %collective-permute-start.27 = (bf16[768,512]{1,0:T(8,128)(2,1)S(1)}, bf16[768,512]{1,0:T(8,128)(2,1)S(1)}, u32[]{:S(2)}, u32[]{:S(2)}) collective-permute-start(bf16[768,512]{1,0:T(8,128)(2,1)S(1)} %slice.747), channel_id=1, source_target_pairs={{0,2},{2,0},{1,3},{3,1},{4,6},{6,4},{5,7},{7,5},{8,10},{10,8},{9,1... | collective-permute-start | bytes 2359304 | tf_op jit(solution)/shard_map/ppermute | solution.py:388
  304.8 26.1 %collective-permute-start.28 = (f32[2,768]{1,0:T(2,128)S(1)}, f32[2,768]{1,0:T(2,128)S(1)}, u32[]{:S(2)}, u32[]{:S(2)}) collective-permute-start(f32[2,768]{1,0:T(2,128)S(1)} %pad_maximum_fusion.9), channel_id=1, source_target_pairs={{0,2},{2,0},{1,3},{3,1},{4,6},{6,4},{5,7},{7,5},{8,10},{10,8},{9,1... | collective-permute-start | bytes 18440 | tf_op jit(solution)/shard_map/ppermute | solution.py:388
  325.6 14.3 %collective-permute-start.31 = (bf16[768,256]{1,0:T(8,128)(2,1)S(1)}, bf16[768,256]{1,0:T(8,128)(2,1)S(1)}, u32[]{:S(2)}, u32[]{:S(2)}) collective-permute-start(bf16[768,256]{1,0:T(8,128)(2,1)S(1)} %slice.752), channel_id=1, source_target_pairs={{0,4},{4,0},{8,12},{12,8},{16,20},{20,16},{24,28},{28,24},{1,5},{5... | collective-permute-start | bytes 1179656 | tf_op jit(solution)/shard_map/ppermute | solution.py:480
  333.6 23.8 %collective-permute-start.34 = (bf16[3136,128]{1,0:T(8,128)(2,1)}, bf16[3136,128]{1,0:T(8,128)(2,1)}, u32[]{:S(2)}, u32[]{:S(2)}) collective-permute-start(bf16[3136,128]{1,0:T(8,128)(2,1)} %pad_maximum_fusion.6), channel_id=1, source_target_pairs={{0,8},{4,12},{8,0},{12,4},{16,24},{20,28},{24,16},{28,20},{1,9},{5... | collective-permute-start | bytes 2408456 | tf_op jit(solution)/shard_map/ppermute | solution.py:483
  340.9 20.5 %collective-permute-start.33 = (bf16[768,128]{1,0:T(8,128)(2,1)}, bf16[768,128]{1,0:T(8,128)(2,1)}, u32[]{:S(2)}, u32[]{:S(2)}) collective-permute-start(bf16[768,128]{1,0:T(8,128)(2,1)} %slice.760), channel_id=1, source_target_pairs={{0,16},{4,20},{8,24},{12,28},{16,0},{20,4},{24,8},{28,12},{1,17},{... | collective-permute-start | bytes 589832 | tf_op jit(solution)/shard_map/ppermute | solution.py:483
  341.5 45.3 %collective-permute-start.29 = (bf16[768,512]{1,0:T(8,128)(2,1)S(1)}, bf16[768,512]{1,0:T(8,128)(2,1)}, u32[]{:S(2)}, u32[]{:S(2)}) collective-permute-start(bf16[768,512]{1,0:T(8,128)(2,1)S(1)} %fusion.39), channel_id=1, source_target_pairs={{0,1},{1,0},{2,3},{3,2},{4,5},{5,4},{6,7},{7,6},{8,9},{9,8},{10,11... | collective-permute-start | bytes 2359304 | tf_op jit(solution)/shard_map/ppermute | solution.py:391
  361.4 20.4 %collective-permute-start.36 = (bf16[64,3136]{1,0:T(8,128)(2,1)}, bf16[64,3136]{1,0:T(8,128)(2,1)}, u32[]{:S(2)}, u32[]{:S(2)}) collective-permute-start(bf16[64,3136]{1,0:T(8,128)(2,1)} %copy.105), channel_id=1, source_target_pairs={{0,16},{4,20},{8,24},{12,28},{16,0},{20,4},{24,8},{28,12},{1,17},{... | collective-permute-start | bytes 1204232 | tf_op jit(solution)/shard_map/ppermute | solution.py:483
  366.1 23.9 %collective-permute-start.35 = (f32[64,896]{1,0:T(8,128)}, f32[64,896]{1,0:T(8,128)}, u32[]{:S(2)}, u32[]{:S(2)}) collective-permute-start(f32[64,896]{1,0:T(8,128)} %get-tuple-element.251), channel_id=1, source_target_pairs={{0,2},{2,0},{1,3},{3,1},{4,6},{6,4},{5,7},{7,5},{8,10},{10,8},{9,1... | collective-permute-start | bytes 688136 | tf_op jit(solution)/shard_map/ppermute | solution.py:388
  (105 other events, 715.2 us)

commit v10 on v9

--- a/solution.py
+++ b/solution.py
@@ -644,6 +644,13 @@
 
     if two:
         h2, da, du, o_heads, dx_late = after((h2, da, du, own_first(o_rows, 1), dx_low), do_rows)
+        def three(*parts):
+            return jnp.concatenate([second(a) for a in parts], axis=0)
+
+        def joined_three(parts, got):
+            n = F
+            return [joined(a, g) for a, g in zip(parts, (got[:n], got[n : 2 * n], got[2 * n :]))]
+
         dx_y = relative(dx_late, "xyzZ")
         h_x = relative(h2, "xyzZ")
         gate_send = jnp.concatenate([product(da, h_x), product(du, h_x), product(o_heads, dx_y)], axis=0)
@@ -666,9 +673,11 @@
         gate_got = after(gate_got, dq)
         act, lin = halved(da, h_x, gate_got[:F]), halved(du, h_x, gate_got[F : 2 * F])
         proj = halved(o_heads, dx_y, gate_got[2 * F :])
-        dkv, from_right, from_left, act, lin, proj, lower_got = lax.optimization_barrier(
-            (dkv, from_right, from_left, act, lin, proj, lower_got)
+        gate_send = three(act, lin, proj)
+        dkv, from_right, from_left, act, lin, proj, gate_send, lower_got = lax.optimization_barrier(
+            (dkv, from_right, from_left, act, lin, proj, gate_send, lower_got)
         )
+        gate_got = to_y(gate_send)
     pad = jnp.zeros((S - H, 2 * W), bf16)
     dkv = (
         dkv
@@ -711,14 +720,6 @@
         ).astype(bf16)
 
     if two:
-        def three(*parts):
-            return jnp.concatenate([second(a) for a in parts], axis=0)
-
-        def joined_three(parts, got):
-            n = F
-            return [joined(a, g) for a, g in zip(parts, (got[:n], got[n : 2 * n], got[2 * n :]))]
-
-        gate_got = to_y(three(act, lin, proj))
         lower = joined(lower, lower_got)
         lower_got = to_z(second(lower), 2)
         query = halved(dt, h1_y, after(query_got, kept))
@@ -730,7 +731,7 @@
         query = joined(query, after(query_got, act, lin, proj))
         query_got = to_z(second(query), 2)
         act, lin, proj = joined_three((act, lin, proj), after(gate_got, dx))
-        gate_got = to_z(three(act, lin, proj).T, 2).T
+        gate_got = after(to_z(three(act, lin, proj).T, 2), tokens_grad).T
         query = joined(query, after(query_got, act, lin, proj))
         lower = joined(lower, after(last_got, dx))
         act, lin, proj = joined_three((act, lin, proj), gate_got)

time: 403 us -> 408 us (1.012)
  Pallas kernels: 78.3 us -> 70.1 us
  starting transfers between devices: 50.2 us -> 55.9 us
    ppermute x14, waiting for transfers between devices: 3.11 us -> 15.3 us  [to_row(): return lax.ppermute(a, 'row', SWAP)]
    ppermute x8, waiting for transfers between devices: 50.1 us -> 39.2 us  [to_z(): return lax.ppermute(a, 'dp', [(i, i ^ 2 * j) for i in range(B)])]
    ppermute x1, waiting for transfers between devices: 3.56 us -> 9.87 us  [local(): kv_left = lax.ppermute(kv[S - H:], 'dp', up)]
    ppermute x8, starting transfers between devices: 10.4 us -> 16 us  [to_z(): return lax.ppermute(a, 'dp', [(i, i ^ 2 * j) for i in range(B)])]
    pallas_call x2, Pallas kernels: 44 us -> 39.6 us  [attend_back_call(): pl.pallas_call(functools.partial(backward_kernel, heads, sets, final), gr...]
  transfers between devices with their start and end apart: 40 -> 40, of which waited for: 10 -> 10; matrix products, arithmetic and copies ran while one was open for 41% -> 42% of each run, Pallas kernels for 20% -> 17%
where the time goes in v10:
time: 408 us; the launch traced here: 403 us
  other arithmetic  77.5 us (19%)
  matrix products  74.1 us (18%)
  Pallas kernels  70.1 us (17%)
  waiting for transfers between devices  66.5 us (16%)
  local copies, waits for them, and re-layouts  56.1 us (14%)
  starting transfers between devices  55.9 us (14%)
    pallas_call x2, Pallas kernels, attend_back_call(): pl.pallas_call(functools.partial(backward_kernel, heads, sets, final), gr...  39.6 us
    ppermute x8, waiting for transfers between devices, to_z(): return lax.ppermute(a, 'dp', [(i, i ^ 2 * j) for i in range(B)])  39.2 us
    pallas_call x2, Pallas kernels, attend_call(): pl.pallas_call(functools.partial(forward_kernel, heads, sets, final), gri...  30.5 us
    dot_general x14, matrix products, nn(): return jnp.dot(a, b, preferred_element_type=f32)  30.3 us
    dot_general x10, matrix products, tn(): lax.dot_general(a, b, (((0,), (0,)), ((), ())), preferred_element_type=f32)  24.1 us
    dot_general x8, matrix products, nt(): lax.dot_general(a, b, (((1,), (1,)), ((), ())), preferred_element_type=f32)  17.1 us
    unnamed x193, local copies, waits for them, and re-layouts  16.3 us
    ppermute x8, starting transfers between devices, to_z(): return lax.ppermute(a, 'dp', [(i, i ^ 2 * j) for i in range(B)])  16 us
  transfers between devices with their start and end apart: 40, of which 10 were waited for; matrix products, arithmetic and copies ran while one was open for 42% of the time, Pallas kernels for 17%

profile of v10, /device:TPU:3, one launch (start us, length us, event | category | flops | bytes accessed | tf_op | source)
XLA Modules:
  0.0 403.2 jit_solution(14647277153128342809)
XLA Ops:
  8.8 2.8 multiply_sine_fusion
  11.7 2.7 convert_element_type.234
  15.1 3.0 fusion.58
  49.3 4.7 %collective-permute-start.3 = (bf16[1024,512]{1,0:T(8,128)(2,1)}, bf16[1024,512]{1,0:T(8,128)(2,1)}, u32[]{:S(2)}, u32[]{:S(2)}) collective-permute-start(bf16[1024,512]{1,0:T(8,128)(2,1)} %get-tuple-element.233), channel_id=1, source_target_pairs={{0,4},{4,8},{8,12},{12,16},{16,20},{20,24},{24,28},{1,5},{5,9},{9,... | collective-permute-start | bytes 3145736 | tf_op jit(solution)/shard_map/ppermute | solution.py:523
  55.5 5.2 %fusion.15 = bf16[1536,1024]{1,0:T(8,128)(2,1)} fusion(bf16[1536,1024]{1,0:T(8,128)(2,1)S(1)} %fusion.4, s32[1024]{0:T(1024)S(1)} %add_xor_fusion.2), kind=kOutput, calls=%fused_computation.27 | convolution fusion | flops 3223846912 | bytes 6295552 | tf_op jit(solution)/shard_map/dot_general | solution.py:32
  69.1 19.4 %attend_own.1 = (f32[6,256,256]{2,1,0:T(8,128)}, f32[6,2,1024]{2,1,0:T(2,128)}) custom-call(s32[12]{0:T(128)} %reshape.741.bounds, bf16[1536,256]{1,0:T(8,128)(2,1)} %fusion.45.refs_0_, s32[6,1,256]{2,1,0:T(1,128)} %select_n.655.refs_1_.refs_4_, bf16[1536,512]{1,0:T(8,128)(2,1)} %copy-done.5, s32[1536,128]{1,0:T(8,128)} %broadcast_in_dim.132.refs_3_.refs_6_), custom_call_target="tpu_custom_call" | custom-call | flops 6291456 | bytes 3145728 | tf_op jit(solution)/shard_map/attend_own/pallas_call | solution.py:194
  88.5 9.9 %collective-permute-done.3.refs_2_.refs_5_ = bf16[1024,512]{1,0:T(8,128)(2,1)} collective-permute-done((bf16[1024,512]{1,0:T(8,128)(2,1)}, bf16[1024,512]{1,0:T(8,128)(2,1)}, u32[]{:S(2)}, u32[]{:S(2)}) %collective-permute-start.3) | collective-permute-done | bytes 1048608 | tf_op jit(solution)/shard_map/ppermute | solution.py:523
  101.1 3.6 collective-permute-start.14
  104.7 11.1 %attend_final.1 = (bf16[1536,256]{1,0:T(8,128)(2,1)}, f32[6,1,1024]{2,1,0:T(1,128)}) custom-call(s32[24]{0:T(128)} %reshape.740.bounds, bf16[1536,256]{1,0:T(8,128)(2,1)} %fusion.45.refs_0_, s32[6,1,256]{2,1,0:T(1,128)} %select_n.655.refs_1_.refs_4_, bf16[1024,512]{1,0:T(8,128)(2,1)} %collective-permute-done.3.refs_2_.refs_5_, ...), custom_call_target="tpu_custom_call" | custom-call | flops 6291456 | bytes 3670016 | tf_op jit(solution)/shard_map/attend_final/pallas_call | solution.py:194
  124.9 3.6 collective-permute-start.13
  136.5 3.2 fusion.164
  148.4 6.5 %multiply_convert_fusion = (bf16[768,1312]{0,1:T(8,128)(2,1)}, bf16[768,1312]{0,1:T(8,128)(2,1)S(1)}, bf16[768,1312]{0,1:T(8,128)(2,1)S(1)}) fusion(f32[768,1312]{0,1:T(8,128)S(1)} %convolution_add_fusion.1, f32[768,1312]{0,1:T(8,128)S(1)} %convolution_add_fusion, f32[768,1312]{0,1:T(8,128)S(1)} %fusion.74, ...), kind=kOutput, calls=%fused_computation.24 | convolution fusion | flops 1054973952 | bytes 20267008 | tf_op jit(solution)/shard_map/dot_general | solution.py:24
  163.6 2.9 fusion.103
  170.4 3.4 fusion.27
  183.7 4.0 fusion.158
  202.1 4.4 %fusion.70 = f32[1312,512]{1,0:T(8,128)} fusion(bf16[768,1312]{0,1:T(8,128)(2,1)} %get-tuple-element.218, bf16[768,1024]{1,0:T(8,128)(2,1)} %copy-done.87), kind=kOutput, calls=%fused_computation.151 | convolution fusion | flops 1031798784 | bytes 5488640 | tf_op jit(solution)/shard_map/dot_general | solution.py:28
  210.5 13.5 %back_halo.1 = (f32[6,256,256]{2,1,0:T(8,128)}, bf16[1024,512]{1,0:T(8,128)(2,1)}, bf16[1024,512]{1,0:T(8,128)(2,1)}) custom-call(s32[24]{0:T(128)} %reshape.740.bounds, bf16[1536,256]{1,0:T(8,128)(2,1)} %fusion.45.refs_0_, bf16[1536,256]{1,0:T(8,128)(2,1)} %maximum_select_fusion.7.refs_1_, bf16[1536,256]{1,0:T(8,128)(2,1)} %get-tuple-element.110.refs_2_, ...), custom_call_target="tpu_custom_call" | custom-call | flops 15728640 | bytes 3670016 | tf_op jit(solution)/shard_map/back_halo/pallas_call | solution.py:320
  228.8 9.4 %collective-permute-start.22 = (bf16[1024,512]{1,0:T(8,128)(2,1)}, bf16[1024,512]{1,0:T(8,128)(2,1)}, u32[]{:S(2)}, u32[]{:S(2)}) collective-permute-start(bf16[1024,512]{1,0:T(8,128)(2,1)} %get-tuple-element.134), channel_id=1, source_target_pairs={{0,4},{4,8},{8,12},{12,16},{16,20},{20,24},{24,28},{1,5},{5,9},{9,... | collective-permute-start | bytes 3145736 | tf_op jit(solution)/shard_map/ppermute | solution.py:666
  238.5 26.1 %back_own.1 = (f32[1536,256]{1,0:T(8,128)}, f32[1536,512]{1,0:T(8,128)}) custom-call(s32[12]{0:T(128)} %reshape.741.bounds, bf16[1536,256]{1,0:T(8,128)(2,1)} %fusion.45.refs_0_, bf16[1536,256]{1,0:T(8,128)(2,1)} %maximum_select_fusion.7.refs_1_, bf16[1536,256]{1,0:T(8,128)(2,1)} %get-tuple-element.110.refs_2_, f32[6,1,1024]{2,1,0:T(1,128)} %get-tuple-element.126.refs_3_, ...), custom_call_target="tpu_custom_call" | custom-call | flops 15728640 | bytes 3145728 | tf_op jit(solution)/shard_map/back_own/pallas_call | solution.py:320
  266.9 6.2 %collective-permute-done.23 = bf16[3136,512]{1,0:T(8,128)(2,1)} collective-permute-done((bf16[3136,512]{1,0:T(8,128)(2,1)}, bf16[3136,512]{1,0:T(8,128)(2,1)}, u32[]{:S(2)}, u32[]{:S(2)}) %collective-permute-start.23) | collective-permute-done | bytes 3211296 | tf_op jit(solution)/shard_map/ppermute | solution.py:388
  275.7 3.6 convert_add_fusion.3
  288.8 2.7 fusion.168
  300.7 4.6 %fusion.55 = bf16[768,512]{1,0:T(8,128)(2,1)} fusion(bf16[1536,768]{1,0:T(8,128)(2,1)} %copy-done.58, bf16[1536,1024]{1,0:T(8,128)(2,1)} %fusion.15), kind=kOutput, calls=%fused_computation.111 | convolution fusion | flops 1208352768 | bytes 4718592 | tf_op jit(solution)/shard_map/dot_general | solution.py:28
  305.3 6.4 %collective-permute-start.30 = (bf16[768,512]{1,0:T(8,128)(2,1)}, bf16[768,512]{1,0:T(8,128)(2,1)S(1)}, u32[]{:S(2)}, u32[]{:S(2)}) collective-permute-start(bf16[768,512]{1,0:T(8,128)(2,1)} %fusion.55), channel_id=1, source_target_pairs={{0,8},{4,12},{8,0},{12,4},{16,24},{20,28},{24,16},{28,20},{1,9},{5... | collective-permute-start | bytes 2359304 | tf_op jit(solution)/shard_map/ppermute | solution.py:483
  313.9 2.8 multiply_reduce_fusion.3
  318.4 17.8 %collective-permute-done.30 = bf16[768,512]{1,0:T(8,128)(2,1)S(1)} collective-permute-done((bf16[768,512]{1,0:T(8,128)(2,1)}, bf16[768,512]{1,0:T(8,128)(2,1)S(1)}, u32[]{:S(2)}, u32[]{:S(2)}) %collective-permute-start.30) | collective-permute-done | bytes 786464 | tf_op jit(solution)/shard_map/ppermute | solution.py:483
  349.3 5.7 %collective-permute-done.39 = bf16[1312,64]{1,0:T(8,128)(2,1)S(1)} collective-permute-done((bf16[1312,64]{1,0:T(8,128)(2,1)S(1)}, bf16[1312,64]{1,0:T(8,128)(2,1)S(1)}, u32[]{:S(2)}, u32[]{:S(2)}) %collective-permute-start.39) | collective-permute-done | bytes 167968 | tf_op jit(solution)/shard_map/ppermute | solution.py:388
  356.1 11.0 %collective-permute-done.34 = bf16[3136,128]{1,0:T(8,128)(2,1)} collective-permute-done((bf16[3136,128]{1,0:T(8,128)(2,1)}, bf16[3136,128]{1,0:T(8,128)(2,1)}, u32[]{:S(2)}, u32[]{:S(2)}) %collective-permute-start.34) | collective-permute-done | bytes 802848 | tf_op jit(solution)/shard_map/ppermute | solution.py:483
  372.4 2.6 fusion.16
  376.2 3.0 maximum_select_fusion.4
  379.2 3.3 collective-permute-done.35
  383.3 8.5 %collective-permute-done.36 = bf16[64,3136]{1,0:T(8,128)(2,1)} collective-permute-done((bf16[64,3136]{1,0:T(8,128)(2,1)}, bf16[64,3136]{1,0:T(8,128)(2,1)}, u32[]{:S(2)}, u32[]{:S(2)}) %collective-permute-start.36) | collective-permute-done | bytes 401440 | tf_op jit(solution)/shard_map/ppermute | solution.py:483
  (437 shorter events, 182.7 us)
Async XLA Ops:
  2.8 25.1 %collective-permute-start = (bf16[768,512]{1,0:T(8,128)(2,1)}, bf16[768,512]{1,0:T(8,128)(2,1)}, u32[]{:S(2)}, u32[]{:S(2)}) collective-permute-start(bf16[768,512]{1,0:T(8,128)(2,1)} %constant_dynamic-slice_fusion.6), channel_id=1, source_target_pairs={{0,2},{2,0},{1,3},{3,1},{4,6},{6,4},{5,7},{7,5},{8,10},{10,8},{9,1... | collective-permute-start | bytes 2359304 | tf_op jit(solution)/shard_map/ppermute | solution.py:388
  6.2 34.9 %collective-permute-start.2 = (bf16[512,768]{0,1:T(8,128)(2,1)}, bf16[512,768]{0,1:T(8,128)(2,1)}, u32[]{:S(2)}, u32[]{:S(2)}) collective-permute-start(bf16[512,768]{0,1:T(8,128)(2,1)} %get-tuple-element.236), channel_id=1, source_target_pairs={{0,2},{2,0},{1,3},{3,1},{4,6},{6,4},{5,7},{7,5},{8,10},{10,8},{9,1... | collective-permute-start | bytes 2359304 | tf_op jit(solution)/shard_map/ppermute | solution.py:388
  18.1 70.4 %collective-permute-start.5 = (bf16[512,1312]{0,1:T(8,128)(2,1)}, bf16[512,1312]{0,1:T(8,128)(2,1)}, u32[]{:S(2)}, u32[]{:S(2)}) collective-permute-start(bf16[512,1312]{0,1:T(8,128)(2,1)} %fusion.58), channel_id=1, source_target_pairs={{0,2},{2,0},{1,3},{3,1},{4,6},{6,4},{5,7},{7,5},{8,10},{10,8},{9,1... | collective-permute-start | bytes 4030472 | tf_op jit(solution)/shard_map/ppermute | solution.py:388
  18.1 70.4 %collective-permute-start.6 = (bf16[512,512]{1,0:T(8,128)(2,1)}, bf16[512,512]{1,0:T(8,128)(2,1)}, u32[]{:S(2)}, u32[]{:S(2)}) collective-permute-start(bf16[512,512]{1,0:T(8,128)(2,1)} %convert_element_type.234), channel_id=1, source_target_pairs={{0,2},{2,0},{1,3},{3,1},{4,6},{6,4},{5,7},{7,5},{8,10},{10,8},{9,1... | collective-permute-start | bytes 1572872 | tf_op jit(solution)/shard_map/ppermute | solution.py:388
  19.5 68.9 %collective-permute-start.7 = (bf16[384,512]{1,0:T(8,128)(2,1)}, bf16[384,512]{1,0:T(8,128)(2,1)S(1)}, u32[]{:S(2)}, u32[]{:S(2)}) collective-permute-start(bf16[384,512]{1,0:T(8,128)(2,1)} %constant_dynamic-slice_fusion.2), channel_id=1, source_target_pairs={{0,2},{2,0},{1,3},{3,1},{4,6},{6,4},{5,7},{7,5},{8,10},{10,8},{9,1... | collective-permute-start | bytes 1179656 | tf_op jit(solution)/shard_map/ppermute | solution.py:388
  49.3 49.1 %collective-permute-start.3 = (bf16[1024,512]{1,0:T(8,128)(2,1)}, bf16[1024,512]{1,0:T(8,128)(2,1)}, u32[]{:S(2)}, u32[]{:S(2)}) collective-permute-start(bf16[1024,512]{1,0:T(8,128)(2,1)} %get-tuple-element.233), channel_id=1, source_target_pairs={{0,4},{4,8},{8,12},{12,16},{16,20},{20,24},{24,28},{1,5},{5,9},{9,... | collective-permute-start | bytes 3145736 | tf_op jit(solution)/shard_map/ppermute | solution.py:523
  54.1 44.3 %collective-permute-start.4 = (bf16[1024,512]{1,0:T(8,128)(2,1)}, bf16[1024,512]{1,0:T(8,128)(2,1)}, u32[]{:S(2)}, u32[]{:S(2)}) collective-permute-start(bf16[1024,512]{1,0:T(8,128)(2,1)} %get-tuple-element.232), channel_id=1, source_target_pairs={{4,0},{8,4},{12,8},{16,12},{20,16},{24,20},{28,24},{5,1},{9,5},{13... | collective-permute-start | bytes 3145736 | tf_op jit(solution)/shard_map/ppermute | solution.py:524
  98.4 17.4 %collective-permute-start.8 = (bf16[656,512]{1,0:T(8,128)(2,1)}, bf16[656,512]{1,0:T(8,128)(2,1)}, u32[]{:S(2)}, u32[]{:S(2)}) collective-permute-start(bf16[656,512]{1,0:T(8,128)(2,1)} %constant_dynamic-slice_fusion.3), channel_id=1, source_target_pairs={{0,2},{2,0},{1,3},{3,1},{4,6},{6,4},{5,7},{7,5},{8,10},{10,8},{9,1... | collective-permute-start | bytes 2015240 | tf_op jit(solution)/shard_map/ppermute | solution.py:388
  101.1 33.1 %collective-permute-start.14 = (bf16[512,1312]{0,1:T(8,128)(2,1)}, bf16[512,1312]{0,1:T(8,128)(2,1)}, u32[]{:S(2)}, u32[]{:S(2)}) collective-permute-start(bf16[512,1312]{0,1:T(8,128)(2,1)} %collective-permute-done.5), channel_id=1, source_target_pairs={{0,8},{4,12},{8,0},{12,4},{16,24},{20,28},{24,16},{28,20},{1,9},{5... | collective-permute-start | bytes 4030472 | tf_op jit(solution)/shard_map/ppermute | solution.py:483
  119.9 12.0 %collective-permute-start.9 = (bf16[384,512]{1,0:T(8,128)(2,1)}, bf16[384,512]{1,0:T(8,128)(2,1)S(1)}, u32[]{:S(2)}, u32[]{:S(2)}) collective-permute-start(bf16[384,512]{1,0:T(8,128)(2,1)} %copy-done.54), channel_id=1, source_target_pairs={{0,1},{1,0},{2,3},{3,2},{4,5},{5,4},{6,7},{7,6},{8,9},{9,8},{10,11... | collective-permute-start | bytes 1179656 | tf_op jit(solution)/shard_map/ppermute | solution.py:391
  124.8 11.4 %collective-permute-start.12 = (bf16[512,1024]{1,0:T(8,128)(2,1)S(1)}, bf16[512,1024]{1,0:T(8,128)(2,1)S(1)}, u32[]{:S(2)}, u32[]{:S(2)}) collective-permute-start(bf16[512,1024]{1,0:T(8,128)(2,1)S(1)} %fusion.62), channel_id=1, source_target_pairs={{0,1},{1,0},{2,3},{3,2},{4,5},{5,4},{6,7},{7,6},{8,9},{9,8},{10,11... | collective-permute-start | bytes 3145736 | tf_op jit(solution)/shard_map/ppermute | solution.py:391
  124.9 23.5 %collective-permute-start.13 = (bf16[656,512]{1,0:T(8,128)(2,1)}, bf16[656,512]{1,0:T(8,128)(2,1)S(1)}, u32[]{:S(2)}, u32[]{:S(2)}) collective-permute-start(bf16[656,512]{1,0:T(8,128)(2,1)} %collective-permute-done.8), channel_id=1, source_target_pairs={{0,8},{4,12},{8,0},{12,4},{16,24},{20,28},{24,16},{28,20},{1,9},{5... | collective-permute-start | bytes 2015240 | tf_op jit(solution)/shard_map/ppermute | solution.py:483
  162.3 18.1 %collective-permute-start.15 = (bf16[768,1024]{1,0:T(8,128)(2,1)}, bf16[768,1024]{1,0:T(8,128)(2,1)}, u32[]{:S(2)}, u32[]{:S(2)}) collective-permute-start(bf16[768,1024]{1,0:T(8,128)(2,1)} %fusion.157), channel_id=1, source_target_pairs={{0,1},{1,0},{2,3},{3,2},{4,5},{5,4},{6,7},{7,6},{8,9},{9,8},{10,11... | collective-permute-start | bytes 4718600 | tf_op jit(solution)/shard_map/ppermute | solution.py:391
  176.2 47.8 %collective-permute-start.20 = (bf16[1312,512]{1,0:T(8,128)(2,1)}, bf16[1312,512]{1,0:T(8,128)(2,1)}, u32[]{:S(2)}, u32[]{:S(2)}) collective-permute-start(bf16[1312,512]{1,0:T(8,128)(2,1)} %convolution_convert_fusion), channel_id=1, source_target_pairs={{0,4},{4,0},{8,12},{12,8},{16,20},{20,16},{24,28},{28,24},{1,5},{5... | collective-permute-start | bytes 4030472 | tf_op jit(solution)/shard_map/ppermute | solution.py:480
  180.4 19.8 %collective-permute-start.18 = (bf16[384,512]{1,0:T(8,128)(2,1)S(1)}, bf16[384,512]{1,0:T(8,128)(2,1)S(1)}, u32[]{:S(2)}, u32[]{:S(2)}) collective-permute-start(bf16[384,512]{1,0:T(8,128)(2,1)S(1)} %get-tuple-element.248), channel_id=1, source_target_pairs={{0,2},{2,0},{1,3},{3,1},{4,6},{6,4},{5,7},{7,5},{8,10},{10,8},{9,1... | collective-permute-start | bytes 1179656 | tf_op jit(solution)/shard_map/ppermute | solution.py:388
  189.5 12.2 %collective-permute-start.16 = (bf16[768,256]{1,0:T(8,128)(2,1)}, bf16[768,256]{1,0:T(8,128)(2,1)}, u32[]{:S(2)}, u32[]{:S(2)}) collective-permute-start(bf16[768,256]{1,0:T(8,128)(2,1)} %get-tuple-element.252), channel_id=1, source_target_pairs={{0,2},{2,0},{1,3},{3,1},{4,6},{6,4},{5,7},{7,5},{8,10},{10,8},{9,1... | collective-permute-start | bytes 1179656 | tf_op jit(solution)/shard_map/ppermute | solution.py:388
  201.8 71.3 %collective-permute-start.23 = (bf16[3136,512]{1,0:T(8,128)(2,1)}, bf16[3136,512]{1,0:T(8,128)(2,1)}, u32[]{:S(2)}, u32[]{:S(2)}) collective-permute-start(bf16[3136,512]{1,0:T(8,128)(2,1)} %pad_maximum_fusion), channel_id=1, source_target_pairs={{0,2},{2,0},{1,3},{3,1},{4,6},{6,4},{5,7},{7,5},{8,10},{10,8},{9,1... | collective-permute-start | bytes 9633800 | tf_op jit(solution)/shard_map/ppermute | solution.py:388
  227.5 56.4 %collective-permute-start.21 = (bf16[1024,512]{1,0:T(8,128)(2,1)}, bf16[1024,512]{1,0:T(8,128)(2,1)}, u32[]{:S(2)}, u32[]{:S(2)}) collective-permute-start(bf16[1024,512]{1,0:T(8,128)(2,1)} %get-tuple-element.133), channel_id=1, source_target_pairs={{4,0},{8,4},{12,8},{16,12},{20,16},{24,20},{28,24},{5,1},{9,5},{13... | collective-permute-start | bytes 3145736 | tf_op jit(solution)/shard_map/ppermute | solution.py:665
  228.8 55.1 %collective-permute-start.22 = (bf16[1024,512]{1,0:T(8,128)(2,1)}, bf16[1024,512]{1,0:T(8,128)(2,1)}, u32[]{:S(2)}, u32[]{:S(2)}) collective-permute-start(bf16[1024,512]{1,0:T(8,128)(2,1)} %get-tuple-element.134), channel_id=1, source_target_pairs={{0,4},{4,8},{8,12},{12,16},{16,20},{20,24},{24,28},{1,5},{5,9},{9,... | collective-permute-start | bytes 3145736 | tf_op jit(solution)/shard_map/ppermute | solution.py:666
  238.3 45.6 %collective-permute-start.24 = (bf16[1312,256]{1,0:T(8,128)(2,1)}, bf16[1312,256]{1,0:T(8,128)(2,1)S(1)}, u32[]{:S(2)}, u32[]{:S(2)}) collective-permute-start(bf16[1312,256]{1,0:T(8,128)(2,1)} %slice.749), channel_id=1, source_target_pairs={{0,8},{4,12},{8,0},{12,4},{16,24},{20,28},{24,16},{28,20},{1,9},{5... | collective-permute-start | bytes 2015240 | tf_op jit(solution)/shard_map/ppermute | solution.py:483
  295.5 18.0 %collective-permute-start.25 = (bf16[768,1024]{1,0:T(8,128)(2,1)}, bf16[768,1024]{1,0:T(8,128)(2,1)}, u32[]{:S(2)}, u32[]{:S(2)}) collective-permute-start(bf16[768,1024]{1,0:T(8,128)(2,1)} %dynamic-slice_convert_fusion), channel_id=1, source_target_pairs={{0,1},{1,0},{2,3},{3,2},{4,5},{5,4},{6,7},{7,6},{8,9},{9,8},{10,11... | collective-permute-start | bytes 4718600 | tf_op jit(solution)/shard_map/ppermute | solution.py:391
  297.8 18.9 %collective-permute-start.26 = (bf16[768,512]{1,0:T(8,128)(2,1)S(1)}, bf16[768,512]{1,0:T(8,128)(2,1)S(1)}, u32[]{:S(2)}, u32[]{:S(2)}) collective-permute-start(bf16[768,512]{1,0:T(8,128)(2,1)S(1)} %slice.533), channel_id=1, source_target_pairs={{0,2},{3,1},{4,6},{7,5},{8,10},{11,9},{12,14},{15,13},{16,18},{19,... | collective-permute-start | bytes 2359304 | tf_op jit(solution)/shard_map/ppermute | solution.py:704
  300.4 40.6 %collective-permute-start.32 = (bf16[3136,256]{1,0:T(8,128)(2,1)}, bf16[3136,256]{1,0:T(8,128)(2,1)S(1)}, u32[]{:S(2)}, u32[]{:S(2)}) collective-permute-start(bf16[3136,256]{1,0:T(8,128)(2,1)} %pad_maximum_fusion.2), channel_id=1, source_target_pairs={{0,4},{4,0},{8,12},{12,8},{16,20},{20,16},{24,28},{28,24},{1,5},{5... | collective-permute-start | bytes 4816904 | tf_op jit(solution)/shard_map/ppermute | solution.py:480
  305.3 30.9 %collective-permute-start.30 = (bf16[768,512]{1,0:T(8,128)(2,1)}, bf16[768,512]{1,0:T(8,128)(2,1)S(1)}, u32[]{:S(2)}, u32[]{:S(2)}) collective-permute-start(bf16[768,512]{1,0:T(8,128)(2,1)} %fusion.55), channel_id=1, source_target_pairs={{0,8},{4,12},{8,0},{12,4},{16,24},{20,28},{24,16},{28,20},{1,9},{5... | collective-permute-start | bytes 2359304 | tf_op jit(solution)/shard_map/ppermute | solution.py:483
  312.0 33.1 %collective-permute-start.38 = (bf16[1312,128]{1,0:T(8,128)(2,1)S(1)}, bf16[1312,128]{1,0:T(8,128)(2,1)S(1)}, u32[]{:S(2)}, u32[]{:S(2)}) collective-permute-start(bf16[1312,128]{1,0:T(8,128)(2,1)S(1)} %slice.754), channel_id=1, source_target_pairs={{0,16},{4,20},{8,24},{12,28},{16,0},{20,4},{24,8},{28,12},{1,17},{... | collective-permute-start | bytes 1007624 | tf_op jit(solution)/shard_map/ppermute | solution.py:483
  316.8 31.7 %collective-permute-start.27 = (bf16[768,512]{1,0:T(8,128)(2,1)S(1)}, bf16[768,512]{1,0:T(8,128)(2,1)S(1)}, u32[]{:S(2)}, u32[]{:S(2)}) collective-permute-start(bf16[768,512]{1,0:T(8,128)(2,1)S(1)} %slice.747), channel_id=1, source_target_pairs={{0,2},{2,0},{1,3},{3,1},{4,6},{6,4},{5,7},{7,5},{8,10},{10,8},{9,1... | collective-permute-start | bytes 2359304 | tf_op jit(solution)/shard_map/ppermute | solution.py:388
  316.9 24.0 %collective-permute-start.28 = (f32[2,768]{1,0:T(2,128)S(1)}, f32[2,768]{1,0:T(2,128)S(1)}, u32[]{:S(2)}, u32[]{:S(2)}) collective-permute-start(f32[2,768]{1,0:T(2,128)S(1)} %pad_maximum_fusion.9), channel_id=1, source_target_pairs={{0,2},{2,0},{1,3},{3,1},{4,6},{6,4},{5,7},{7,5},{8,10},{10,8},{9,1... | collective-permute-start | bytes 18440 | tf_op jit(solution)/shard_map/ppermute | solution.py:388
  336.5 11.1 %collective-permute-start.31 = (bf16[768,256]{1,0:T(8,128)(2,1)S(1)}, bf16[768,256]{1,0:T(8,128)(2,1)S(1)}, u32[]{:S(2)}, u32[]{:S(2)}) collective-permute-start(bf16[768,256]{1,0:T(8,128)(2,1)S(1)} %slice.752), channel_id=1, source_target_pairs={{0,4},{4,0},{8,12},{12,8},{16,20},{20,16},{24,28},{28,24},{1,5},{5... | collective-permute-start | bytes 1179656 | tf_op jit(solution)/shard_map/ppermute | solution.py:480
  343.1 23.9 %collective-permute-start.34 = (bf16[3136,128]{1,0:T(8,128)(2,1)}, bf16[3136,128]{1,0:T(8,128)(2,1)}, u32[]{:S(2)}, u32[]{:S(2)}) collective-permute-start(bf16[3136,128]{1,0:T(8,128)(2,1)} %pad_maximum_fusion.6), channel_id=1, source_target_pairs={{0,8},{4,12},{8,0},{12,4},{16,24},{20,28},{24,16},{28,20},{1,9},{5... | collective-permute-start | bytes 2408456 | tf_op jit(solution)/shard_map/ppermute | solution.py:483
  348.5 22.6 %collective-permute-start.33 = (bf16[768,128]{1,0:T(8,128)(2,1)}, bf16[768,128]{1,0:T(8,128)(2,1)}, u32[]{:S(2)}, u32[]{:S(2)}) collective-permute-start(bf16[768,128]{1,0:T(8,128)(2,1)} %slice.760), channel_id=1, source_target_pairs={{0,16},{4,20},{8,24},{12,28},{16,0},{20,4},{24,8},{28,12},{1,17},{... | collective-permute-start | bytes 589832 | tf_op jit(solution)/shard_map/ppermute | solution.py:483
  349.1 27.0 %collective-permute-start.29 = (bf16[768,512]{1,0:T(8,128)(2,1)S(1)}, bf16[768,512]{1,0:T(8,128)(2,1)}, u32[]{:S(2)}, u32[]{:S(2)}) collective-permute-start(bf16[768,512]{1,0:T(8,128)(2,1)S(1)} %fusion.39), channel_id=1, source_target_pairs={{0,1},{1,0},{2,3},{3,2},{4,5},{5,4},{6,7},{7,6},{8,9},{9,8},{10,11... | collective-permute-start | bytes 2359304 | tf_op jit(solution)/shard_map/ppermute | solution.py:391
  371.1 20.7 %collective-permute-start.36 = (bf16[64,3136]{1,0:T(8,128)(2,1)}, bf16[64,3136]{1,0:T(8,128)(2,1)}, u32[]{:S(2)}, u32[]{:S(2)}) collective-permute-start(bf16[64,3136]{1,0:T(8,128)(2,1)} %copy.105), channel_id=1, source_target_pairs={{0,16},{4,20},{8,24},{12,28},{16,0},{20,4},{24,8},{28,12},{1,17},{... | collective-permute-start | bytes 1204232 | tf_op jit(solution)/shard_map/ppermute | solution.py:483
  (105 other events, 716.0 us)

commit v11 on v9

--- a/solution.py
+++ b/solution.py
@@ -730,7 +730,7 @@
         query = joined(query, after(query_got, act, lin, proj))
         query_got = to_z(second(query), 2)
         act, lin, proj = joined_three((act, lin, proj), after(gate_got, dx))
-        gate_got = to_z(three(act, lin, proj).T, 2).T
+        gate_got = after(to_z(three(act, lin, proj).T, 2), tokens_grad).T
         query = joined(query, after(query_got, act, lin, proj))
         lower = joined(lower, after(last_got, dx))
         act, lin, proj = joined_three((act, lin, proj), gate_got)

time: 403 us -> 399 us (0.990)
  Pallas kernels: 78.3 us -> 67.3 us
  waiting for transfers between devices: 62.6 us -> 68.3 us
    ppermute x14, waiting for transfers between devices: 3.11 us -> 13.5 us  [to_row(): return lax.ppermute(a, 'row', SWAP)]
    ppermute x8, waiting for transfers between devices: 50.1 us -> 41.5 us  [to_z(): return lax.ppermute(a, 'dp', [(i, i ^ 2 * j) for i in range(B)])]
    ppermute x1, waiting for transfers between devices: 3.56 us -> 11.2 us  [local(): kv_left = lax.ppermute(kv[S - H:], 'dp', up)]
    pallas_call x2, Pallas kernels: 44 us -> 38 us  [attend_back_call(): pl.pallas_call(functools.partial(backward_kernel, heads, sets, final), gr...]
    ppermute x8, starting transfers between devices: 10.4 us -> 15.7 us  [to_z(): return lax.ppermute(a, 'dp', [(i, i ^ 2 * j) for i in range(B)])]
    pallas_call x2, Pallas kernels: 34.4 us -> 29.4 us  [attend_call(): pl.pallas_call(functools.partial(forward_kernel, heads, sets, final), gri...]
    unnamed x193 -> x191, local copies, waits for them, and re-layouts: 15.2 us -> 14.1 us
  transfers between devices with their start and end apart: 40 -> 40, of which waited for: 10 -> 9; matrix products, arithmetic and copies ran while one was open for 41% -> 42% of each run, Pallas kernels for 20% -> 17%
where the time goes in v11:
time: 399 us; the launch traced here: 393 us
  other arithmetic  75.8 us (19%)
  matrix products  71.2 us (18%)
  waiting for transfers between devices  68.3 us (17%)
  Pallas kernels  67.3 us (17%)
  starting transfers between devices  54.1 us (14%)
  local copies, waits for them, and re-layouts  53.5 us (13%)
    ppermute x8, waiting for transfers between devices, to_z(): return lax.ppermute(a, 'dp', [(i, i ^ 2 * j) for i in range(B)])  41.5 us
    pallas_call x2, Pallas kernels, attend_back_call(): pl.pallas_call(functools.partial(backward_kernel, heads, sets, final), gr...  38 us
    dot_general x14, matrix products, nn(): return jnp.dot(a, b, preferred_element_type=f32)  30.3 us
    pallas_call x2, Pallas kernels, attend_call(): pl.pallas_call(functools.partial(forward_kernel, heads, sets, final), gri...  29.4 us
    dot_general x10, matrix products, tn(): lax.dot_general(a, b, (((0,), (0,)), ((), ())), preferred_element_type=f32)  21.2 us
    dot_general x8, matrix products, nt(): lax.dot_general(a, b, (((1,), (1,)), ((), ())), preferred_element_type=f32)  17 us
    ppermute x8, starting transfers between devices, to_z(): return lax.ppermute(a, 'dp', [(i, i ^ 2 * j) for i in range(B)])  15.7 us
    unnamed x191, local copies, waits for them, and re-layouts  14.1 us
  transfers between devices with their start and end apart: 40, of which 9 were waited for; matrix products, arithmetic and copies ran while one was open for 42% of the time, Pallas kernels for 17%

profile of v11, /device:TPU:3, one launch (start us, length us, event | category | flops | bytes accessed | tf_op | source)
XLA Modules:
  0.0 393.2 jit_solution(11979759000882494222)
XLA Ops:
  8.8 2.8 multiply_sine_fusion
  11.6 2.7 convert_element_type.234
  15.1 3.0 fusion.58
  40.9 2.6 fusion.26
  49.1 4.8 %collective-permute-start.3 = (bf16[1024,512]{1,0:T(8,128)(2,1)}, bf16[1024,512]{1,0:T(8,128)(2,1)}, u32[]{:S(2)}, u32[]{:S(2)}) collective-permute-start(bf16[1024,512]{1,0:T(8,128)(2,1)} %get-tuple-element.231), channel_id=1, source_target_pairs={{0,4},{4,8},{8,12},{12,16},{16,20},{20,24},{24,28},{1,5},{5,9},{9,... | collective-permute-start | bytes 3145736 | tf_op jit(solution)/shard_map/ppermute | solution.py:523
  55.3 5.2 %fusion.15 = bf16[1536,1024]{1,0:T(8,128)(2,1)} fusion(bf16[1536,1024]{1,0:T(8,128)(2,1)S(1)} %fusion.4, s32[1024]{0:T(1024)S(1)} %add_xor_fusion.2), kind=kOutput, calls=%fused_computation.27 | convolution fusion | flops 3223846912 | bytes 6295552 | tf_op jit(solution)/shard_map/dot_general | solution.py:32
  69.0 17.9 %attend_own.1 = (f32[6,256,256]{2,1,0:T(8,128)}, f32[6,2,1024]{2,1,0:T(2,128)}) custom-call(s32[12]{0:T(128)} %reshape.741.bounds, bf16[1536,256]{1,0:T(8,128)(2,1)} %fusion.45.refs_0_, s32[6,1,256]{2,1,0:T(1,128)} %select_n.655.refs_1_.refs_4_, bf16[1536,512]{1,0:T(8,128)(2,1)} %copy-done.5, s32[1536,128]{1,0:T(8,128)} %broadcast_in_dim.132.refs_3_.refs_6_), custom_call_target="tpu_custom_call" | custom-call | flops 6291456 | bytes 3145728 | tf_op jit(solution)/shard_map/attend_own/pallas_call | solution.py:194
  86.9 11.2 %collective-permute-done.3.refs_2_.refs_5_ = bf16[1024,512]{1,0:T(8,128)(2,1)} collective-permute-done((bf16[1024,512]{1,0:T(8,128)(2,1)}, bf16[1024,512]{1,0:T(8,128)(2,1)}, u32[]{:S(2)}, u32[]{:S(2)}) %collective-permute-start.3) | collective-permute-done | bytes 1048608 | tf_op jit(solution)/shard_map/ppermute | solution.py:523
  100.8 3.6 collective-permute-start.14
  104.4 11.5 %attend_final.1 = (bf16[1536,256]{1,0:T(8,128)(2,1)}, f32[6,1,1024]{2,1,0:T(1,128)}) custom-call(s32[24]{0:T(128)} %reshape.740.bounds, bf16[1536,256]{1,0:T(8,128)(2,1)} %fusion.45.refs_0_, s32[6,1,256]{2,1,0:T(1,128)} %select_n.655.refs_1_.refs_4_, bf16[1024,512]{1,0:T(8,128)(2,1)} %collective-permute-done.3.refs_2_.refs_5_, ...), custom_call_target="tpu_custom_call" | custom-call | flops 6291456 | bytes 3670016 | tf_op jit(solution)/shard_map/attend_final/pallas_call | solution.py:194
  124.6 3.6 collective-permute-start.13
  136.7 3.2 fusion.164
  148.1 6.5 %multiply_convert_fusion = (bf16[768,1312]{0,1:T(8,128)(2,1)}, bf16[768,1312]{0,1:T(8,128)(2,1)S(1)}, bf16[768,1312]{0,1:T(8,128)(2,1)S(1)}) fusion(f32[768,1312]{0,1:T(8,128)S(1)} %convolution_add_fusion.1, f32[768,1312]{0,1:T(8,128)S(1)} %convolution_add_fusion, f32[768,1312]{0,1:T(8,128)S(1)} %fusion.74, ...), kind=kOutput, calls=%fused_computation.24 | convolution fusion | flops 1054973952 | bytes 20267008 | tf_op jit(solution)/shard_map/dot_general | solution.py:24
  163.4 2.8 fusion.103
  170.1 3.4 fusion.27
  179.7 2.6 fusion.65
  182.3 4.0 %fusion.158 = (bf16[768,1024]{1,0:T(8,128)(2,1)S(1)}, f32[768,1024]{1,0:T(8,128)}) fusion(f32[768]{0:T(1024)S(1)} %broadcast_multiply_fusion.2, f32[768,1024]{1,0:T(8,128)S(1)} %get-tuple-element.274, f32[768]{0:T(1024)S(1)} %broadcast_multiply_fusion.4, f32[768]{0:T(1024)S(1)} %broadcast_multiply_fusion.3, f32[1024]{0:T(1024)S(1)} %maximum_select_fusion.15, ...), kind=kLoop, calls=%fused_computation.380 | loop fusion | flops 10223616 | bytes 14172160 | tf_op jit(solution)/shard_map/convert_element_type | solution.py:637
  200.4 4.4 %fusion.70 = f32[1312,512]{1,0:T(8,128)} fusion(bf16[768,1312]{0,1:T(8,128)(2,1)} %get-tuple-element.216, bf16[768,1024]{1,0:T(8,128)(2,1)} %copy-done.88), kind=kOutput, calls=%fused_computation.151 | convolution fusion | flops 1031798784 | bytes 5488640 | tf_op jit(solution)/shard_map/dot_general | solution.py:28
  209.8 14.0 %back_halo.1 = (f32[6,256,256]{2,1,0:T(8,128)}, bf16[1024,512]{1,0:T(8,128)(2,1)}, bf16[1024,512]{1,0:T(8,128)(2,1)}) custom-call(s32[24]{0:T(128)} %reshape.740.bounds, bf16[1536,256]{1,0:T(8,128)(2,1)} %fusion.45.refs_0_, bf16[1536,256]{1,0:T(8,128)(2,1)} %maximum_select_fusion.7.refs_1_, bf16[1536,256]{1,0:T(8,128)(2,1)} %get-tuple-element.109.refs_2_, ...), custom_call_target="tpu_custom_call" | custom-call | flops 15728640 | bytes 3670016 | tf_op jit(solution)/shard_map/back_halo/pallas_call | solution.py:320
  228.6 6.8 %collective-permute-start.22 = (bf16[1024,512]{1,0:T(8,128)(2,1)}, bf16[1024,512]{1,0:T(8,128)(2,1)}, u32[]{:S(2)}, u32[]{:S(2)}) collective-permute-start(bf16[1024,512]{1,0:T(8,128)(2,1)} %get-tuple-element.133), channel_id=1, source_target_pairs={{0,4},{4,8},{8,12},{12,16},{16,20},{20,24},{24,28},{1,5},{5,9},{9,... | collective-permute-start | bytes 3145736 | tf_op jit(solution)/shard_map/ppermute | solution.py:659
  235.7 24.0 %back_own.1 = (f32[1536,256]{1,0:T(8,128)}, f32[1536,512]{1,0:T(8,128)}) custom-call(s32[12]{0:T(128)} %reshape.741.bounds, bf16[1536,256]{1,0:T(8,128)(2,1)} %fusion.45.refs_0_, bf16[1536,256]{1,0:T(8,128)(2,1)} %maximum_select_fusion.7.refs_1_, bf16[1536,256]{1,0:T(8,128)(2,1)} %get-tuple-element.109.refs_2_, f32[6,1,1024]{2,1,0:T(1,128)} %get-tuple-element.125.refs_3_, ...), custom_call_target="tpu_custom_call" | custom-call | flops 15728640 | bytes 3145728 | tf_op jit(solution)/shard_map/back_own/pallas_call | solution.py:320
  262.0 8.7 %collective-permute-done.23 = bf16[3136,512]{1,0:T(8,128)(2,1)} collective-permute-done((bf16[3136,512]{1,0:T(8,128)(2,1)}, bf16[3136,512]{1,0:T(8,128)(2,1)}, u32[]{:S(2)}, u32[]{:S(2)}) %collective-permute-start.23) | collective-permute-done | bytes 3211296 | tf_op jit(solution)/shard_map/ppermute | solution.py:388
  276.0 3.0 convert_add_fusion.3
  279.1 3.2 convert_add_fusion.1
  284.0 2.6 fusion.168
  288.3 2.8 collective-permute-start.26
  295.5 4.0 %collective-permute-start.30 = (bf16[768,512]{1,0:T(8,128)(2,1)}, bf16[768,512]{1,0:T(8,128)(2,1)S(1)}, u32[]{:S(2)}, u32[]{:S(2)}) collective-permute-start(bf16[768,512]{1,0:T(8,128)(2,1)} %fusion.55), channel_id=1, source_target_pairs={{0,8},{4,12},{8,0},{12,4},{16,24},{20,28},{24,16},{28,20},{1,9},{5... | collective-permute-start | bytes 2359304 | tf_op jit(solution)/shard_map/ppermute | solution.py:483
  305.6 19.0 %collective-permute-done.30 = bf16[768,512]{1,0:T(8,128)(2,1)S(1)} collective-permute-done((bf16[768,512]{1,0:T(8,128)(2,1)}, bf16[768,512]{1,0:T(8,128)(2,1)S(1)}, u32[]{:S(2)}, u32[]{:S(2)}) %collective-permute-start.30) | collective-permute-done | bytes 786464 | tf_op jit(solution)/shard_map/ppermute | solution.py:483
  345.1 12.4 %collective-permute-done.34 = bf16[3136,128]{1,0:T(8,128)(2,1)} collective-permute-done((bf16[3136,128]{1,0:T(8,128)(2,1)}, bf16[3136,128]{1,0:T(8,128)(2,1)}, u32[]{:S(2)}, u32[]{:S(2)}) %collective-permute-start.34) | collective-permute-done | bytes 802848 | tf_op jit(solution)/shard_map/ppermute | solution.py:483
  362.8 2.6 fusion.16
  366.6 3.0 maximum_select_fusion.4
  373.0 8.9 %collective-permute-done.36 = bf16[64,3136]{1,0:T(8,128)(2,1)} collective-permute-done((bf16[64,3136]{1,0:T(8,128)(2,1)}, bf16[64,3136]{1,0:T(8,128)(2,1)}, u32[]{:S(2)}, u32[]{:S(2)}) %collective-permute-start.36) | collective-permute-done | bytes 401440 | tf_op jit(solution)/shard_map/ppermute | solution.py:483
  (434 shorter events, 179.5 us)
Async XLA Ops:
  2.8 25.1 %collective-permute-start = (bf16[768,512]{1,0:T(8,128)(2,1)}, bf16[768,512]{1,0:T(8,128)(2,1)}, u32[]{:S(2)}, u32[]{:S(2)}) collective-permute-start(bf16[768,512]{1,0:T(8,128)(2,1)} %constant_dynamic-slice_fusion.6), channel_id=1, source_target_pairs={{0,2},{2,0},{1,3},{3,1},{4,6},{6,4},{5,7},{7,5},{8,10},{10,8},{9,1... | collective-permute-start | bytes 2359304 | tf_op jit(solution)/shard_map/ppermute | solution.py:388
  6.2 34.6 %collective-permute-start.2 = (bf16[512,768]{0,1:T(8,128)(2,1)}, bf16[512,768]{0,1:T(8,128)(2,1)}, u32[]{:S(2)}, u32[]{:S(2)}) collective-permute-start(bf16[512,768]{0,1:T(8,128)(2,1)} %get-tuple-element.234), channel_id=1, source_target_pairs={{0,2},{2,0},{1,3},{3,1},{4,6},{6,4},{5,7},{7,5},{8,10},{10,8},{9,1... | collective-permute-start | bytes 2359304 | tf_op jit(solution)/shard_map/ppermute | solution.py:388
  18.1 68.8 %collective-permute-start.5 = (bf16[512,1312]{0,1:T(8,128)(2,1)}, bf16[512,1312]{0,1:T(8,128)(2,1)}, u32[]{:S(2)}, u32[]{:S(2)}) collective-permute-start(bf16[512,1312]{0,1:T(8,128)(2,1)} %fusion.58), channel_id=1, source_target_pairs={{0,2},{2,0},{1,3},{3,1},{4,6},{6,4},{5,7},{7,5},{8,10},{10,8},{9,1... | collective-permute-start | bytes 4030472 | tf_op jit(solution)/shard_map/ppermute | solution.py:388
  18.1 68.8 %collective-permute-start.6 = (bf16[512,512]{1,0:T(8,128)(2,1)}, bf16[512,512]{1,0:T(8,128)(2,1)}, u32[]{:S(2)}, u32[]{:S(2)}) collective-permute-start(bf16[512,512]{1,0:T(8,128)(2,1)} %convert_element_type.234), channel_id=1, source_target_pairs={{0,2},{2,0},{1,3},{3,1},{4,6},{6,4},{5,7},{7,5},{8,10},{10,8},{9,1... | collective-permute-start | bytes 1572872 | tf_op jit(solution)/shard_map/ppermute | solution.py:388
  19.6 67.3 %collective-permute-start.7 = (bf16[384,512]{1,0:T(8,128)(2,1)}, bf16[384,512]{1,0:T(8,128)(2,1)S(1)}, u32[]{:S(2)}, u32[]{:S(2)}) collective-permute-start(bf16[384,512]{1,0:T(8,128)(2,1)} %constant_dynamic-slice_fusion.2), channel_id=1, source_target_pairs={{0,2},{2,0},{1,3},{3,1},{4,6},{6,4},{5,7},{7,5},{8,10},{10,8},{9,1... | collective-permute-start | bytes 1179656 | tf_op jit(solution)/shard_map/ppermute | solution.py:388
  49.1 49.1 %collective-permute-start.3 = (bf16[1024,512]{1,0:T(8,128)(2,1)}, bf16[1024,512]{1,0:T(8,128)(2,1)}, u32[]{:S(2)}, u32[]{:S(2)}) collective-permute-start(bf16[1024,512]{1,0:T(8,128)(2,1)} %get-tuple-element.231), channel_id=1, source_target_pairs={{0,4},{4,8},{8,12},{12,16},{16,20},{20,24},{24,28},{1,5},{5,9},{9,... | collective-permute-start | bytes 3145736 | tf_op jit(solution)/shard_map/ppermute | solution.py:523
  53.9 44.2 %collective-permute-start.4 = (bf16[1024,512]{1,0:T(8,128)(2,1)}, bf16[1024,512]{1,0:T(8,128)(2,1)}, u32[]{:S(2)}, u32[]{:S(2)}) collective-permute-start(bf16[1024,512]{1,0:T(8,128)(2,1)} %get-tuple-element.230), channel_id=1, source_target_pairs={{4,0},{8,4},{12,8},{16,12},{20,16},{24,20},{28,24},{5,1},{9,5},{13... | collective-permute-start | bytes 3145736 | tf_op jit(solution)/shard_map/ppermute | solution.py:524
  98.1 17.8 %collective-permute-start.8 = (bf16[656,512]{1,0:T(8,128)(2,1)}, bf16[656,512]{1,0:T(8,128)(2,1)}, u32[]{:S(2)}, u32[]{:S(2)}) collective-permute-start(bf16[656,512]{1,0:T(8,128)(2,1)} %constant_dynamic-slice_fusion.3), channel_id=1, source_target_pairs={{0,2},{2,0},{1,3},{3,1},{4,6},{6,4},{5,7},{7,5},{8,10},{10,8},{9,1... | collective-permute-start | bytes 2015240 | tf_op jit(solution)/shard_map/ppermute | solution.py:388
  100.8 33.2 %collective-permute-start.14 = (bf16[512,1312]{0,1:T(8,128)(2,1)}, bf16[512,1312]{0,1:T(8,128)(2,1)}, u32[]{:S(2)}, u32[]{:S(2)}) collective-permute-start(bf16[512,1312]{0,1:T(8,128)(2,1)} %collective-permute-done.5), channel_id=1, source_target_pairs={{0,8},{4,12},{8,0},{12,4},{16,24},{20,28},{24,16},{28,20},{1,9},{5... | collective-permute-start | bytes 4030472 | tf_op jit(solution)/shard_map/ppermute | solution.py:483
  119.6 12.4 %collective-permute-start.9 = (bf16[384,512]{1,0:T(8,128)(2,1)}, bf16[384,512]{1,0:T(8,128)(2,1)S(1)}, u32[]{:S(2)}, u32[]{:S(2)}) collective-permute-start(bf16[384,512]{1,0:T(8,128)(2,1)} %copy-done.57), channel_id=1, source_target_pairs={{0,1},{1,0},{2,3},{3,2},{4,5},{5,4},{6,7},{7,6},{8,9},{9,8},{10,11... | collective-permute-start | bytes 1179656 | tf_op jit(solution)/shard_map/ppermute | solution.py:391
  124.6 11.6 %collective-permute-start.12 = (bf16[512,1024]{1,0:T(8,128)(2,1)S(1)}, bf16[512,1024]{1,0:T(8,128)(2,1)S(1)}, u32[]{:S(2)}, u32[]{:S(2)}) collective-permute-start(bf16[512,1024]{1,0:T(8,128)(2,1)S(1)} %fusion.62), channel_id=1, source_target_pairs={{0,1},{1,0},{2,3},{3,2},{4,5},{5,4},{6,7},{7,6},{8,9},{9,8},{10,11... | collective-permute-start | bytes 3145736 | tf_op jit(solution)/shard_map/ppermute | solution.py:391
  124.6 23.5 %collective-permute-start.13 = (bf16[656,512]{1,0:T(8,128)(2,1)}, bf16[656,512]{1,0:T(8,128)(2,1)S(1)}, u32[]{:S(2)}, u32[]{:S(2)}) collective-permute-start(bf16[656,512]{1,0:T(8,128)(2,1)} %collective-permute-done.8), channel_id=1, source_target_pairs={{0,8},{4,12},{8,0},{12,4},{16,24},{20,28},{24,16},{28,20},{1,9},{5... | collective-permute-start | bytes 2015240 | tf_op jit(solution)/shard_map/ppermute | solution.py:483
  162.1 17.0 %collective-permute-start.15 = (bf16[768,1024]{1,0:T(8,128)(2,1)}, bf16[768,1024]{1,0:T(8,128)(2,1)}, u32[]{:S(2)}, u32[]{:S(2)}) collective-permute-start(bf16[768,1024]{1,0:T(8,128)(2,1)} %fusion.157), channel_id=1, source_target_pairs={{0,1},{1,0},{2,3},{3,2},{4,5},{5,4},{6,7},{7,6},{8,9},{9,8},{10,11... | collective-permute-start | bytes 4718600 | tf_op jit(solution)/shard_map/ppermute | solution.py:391
  175.8 48.0 %collective-permute-start.20 = (bf16[1312,512]{1,0:T(8,128)(2,1)}, bf16[1312,512]{1,0:T(8,128)(2,1)}, u32[]{:S(2)}, u32[]{:S(2)}) collective-permute-start(bf16[1312,512]{1,0:T(8,128)(2,1)} %convolution_convert_fusion), channel_id=1, source_target_pairs={{0,4},{4,0},{8,12},{12,8},{16,20},{20,16},{24,28},{28,24},{1,5},{5... | collective-permute-start | bytes 4030472 | tf_op jit(solution)/shard_map/ppermute | solution.py:480
  179.0 19.8 %collective-permute-start.18 = (bf16[384,512]{1,0:T(8,128)(2,1)S(1)}, bf16[384,512]{1,0:T(8,128)(2,1)S(1)}, u32[]{:S(2)}, u32[]{:S(2)}) collective-permute-start(bf16[384,512]{1,0:T(8,128)(2,1)S(1)} %get-tuple-element.246), channel_id=1, source_target_pairs={{0,2},{2,0},{1,3},{3,1},{4,6},{6,4},{5,7},{7,5},{8,10},{10,8},{9,1... | collective-permute-start | bytes 1179656 | tf_op jit(solution)/shard_map/ppermute | solution.py:388
  188.2 11.6 %collective-permute-start.16 = (bf16[768,256]{1,0:T(8,128)(2,1)}, bf16[768,256]{1,0:T(8,128)(2,1)}, u32[]{:S(2)}, u32[]{:S(2)}) collective-permute-start(bf16[768,256]{1,0:T(8,128)(2,1)} %get-tuple-element.250), channel_id=1, source_target_pairs={{0,2},{2,0},{1,3},{3,1},{4,6},{6,4},{5,7},{7,5},{8,10},{10,8},{9,1... | collective-permute-start | bytes 1179656 | tf_op jit(solution)/shard_map/ppermute | solution.py:388
  199.8 70.9 %collective-permute-start.23 = (bf16[3136,512]{1,0:T(8,128)(2,1)}, bf16[3136,512]{1,0:T(8,128)(2,1)}, u32[]{:S(2)}, u32[]{:S(2)}) collective-permute-start(bf16[3136,512]{1,0:T(8,128)(2,1)} %pad_maximum_fusion), channel_id=1, source_target_pairs={{0,2},{2,0},{1,3},{3,1},{4,6},{6,4},{5,7},{7,5},{8,10},{10,8},{9,1... | collective-permute-start | bytes 9633800 | tf_op jit(solution)/shard_map/ppermute | solution.py:388
  227.3 51.7 %collective-permute-start.21 = (bf16[1024,512]{1,0:T(8,128)(2,1)}, bf16[1024,512]{1,0:T(8,128)(2,1)}, u32[]{:S(2)}, u32[]{:S(2)}) collective-permute-start(bf16[1024,512]{1,0:T(8,128)(2,1)} %get-tuple-element.132), channel_id=1, source_target_pairs={{4,0},{8,4},{12,8},{16,12},{20,16},{24,20},{28,24},{5,1},{9,5},{13... | collective-permute-start | bytes 3145736 | tf_op jit(solution)/shard_map/ppermute | solution.py:658
  228.6 50.4 %collective-permute-start.22 = (bf16[1024,512]{1,0:T(8,128)(2,1)}, bf16[1024,512]{1,0:T(8,128)(2,1)}, u32[]{:S(2)}, u32[]{:S(2)}) collective-permute-start(bf16[1024,512]{1,0:T(8,128)(2,1)} %get-tuple-element.133), channel_id=1, source_target_pairs={{0,4},{4,8},{8,12},{12,16},{16,20},{20,24},{24,28},{1,5},{5,9},{9,... | collective-permute-start | bytes 3145736 | tf_op jit(solution)/shard_map/ppermute | solution.py:659
  235.4 43.6 %collective-permute-start.24 = (bf16[1312,256]{1,0:T(8,128)(2,1)}, bf16[1312,256]{1,0:T(8,128)(2,1)S(1)}, u32[]{:S(2)}, u32[]{:S(2)}) collective-permute-start(bf16[1312,256]{1,0:T(8,128)(2,1)} %slice.751), channel_id=1, source_target_pairs={{0,8},{4,12},{8,0},{12,4},{16,24},{20,28},{24,16},{28,20},{1,9},{5... | collective-permute-start | bytes 2015240 | tf_op jit(solution)/shard_map/ppermute | solution.py:483
  286.9 15.1 %collective-permute-start.25 = (bf16[768,1024]{1,0:T(8,128)(2,1)S(1)}, bf16[768,1024]{1,0:T(8,128)(2,1)S(1)}, u32[]{:S(2)}, u32[]{:S(2)}) collective-permute-start(bf16[768,1024]{1,0:T(8,128)(2,1)S(1)} %dynamic-slice_convert_fusion), channel_id=1, source_target_pairs={{0,1},{1,0},{2,3},{3,2},{4,5},{5,4},{6,7},{7,6},{8,9},{9,8},{10,11... | collective-permute-start | bytes 4718600 | tf_op jit(solution)/shard_map/ppermute | solution.py:391
  288.3 15.7 %collective-permute-start.26 = (bf16[768,512]{1,0:T(8,128)(2,1)S(1)}, bf16[768,512]{1,0:T(8,128)(2,1)S(1)}, u32[]{:S(2)}, u32[]{:S(2)}) collective-permute-start(bf16[768,512]{1,0:T(8,128)(2,1)S(1)} %copy-done.51), channel_id=1, source_target_pairs={{0,2},{3,1},{4,6},{7,5},{8,10},{11,9},{12,14},{15,13},{16,18},{19,... | collective-permute-start | bytes 2359304 | tf_op jit(solution)/shard_map/ppermute | solution.py:695
  291.5 39.1 %collective-permute-start.32 = (bf16[3136,256]{1,0:T(8,128)(2,1)S(1)}, bf16[3136,256]{1,0:T(8,128)(2,1)S(1)}, u32[]{:S(2)}, u32[]{:S(2)}) collective-permute-start(bf16[3136,256]{1,0:T(8,128)(2,1)S(1)} %pad_maximum_fusion.2), channel_id=1, source_target_pairs={{0,4},{4,0},{8,12},{12,8},{16,20},{20,16},{24,28},{28,24},{1,5},{5... | collective-permute-start | bytes 4816904 | tf_op jit(solution)/shard_map/ppermute | solution.py:480
  295.5 29.1 %collective-permute-start.30 = (bf16[768,512]{1,0:T(8,128)(2,1)}, bf16[768,512]{1,0:T(8,128)(2,1)S(1)}, u32[]{:S(2)}, u32[]{:S(2)}) collective-permute-start(bf16[768,512]{1,0:T(8,128)(2,1)} %fusion.55), channel_id=1, source_target_pairs={{0,8},{4,12},{8,0},{12,4},{16,24},{20,28},{24,16},{28,20},{1,9},{5... | collective-permute-start | bytes 2359304 | tf_op jit(solution)/shard_map/ppermute | solution.py:483
  300.6 34.2 %collective-permute-start.38 = (bf16[1312,128]{1,0:T(8,128)(2,1)}, bf16[1312,128]{1,0:T(8,128)(2,1)S(1)}, u32[]{:S(2)}, u32[]{:S(2)}) collective-permute-start(bf16[1312,128]{1,0:T(8,128)(2,1)} %slice.754), channel_id=1, source_target_pairs={{0,16},{4,20},{8,24},{12,28},{16,0},{20,4},{24,8},{28,12},{1,17},{... | collective-permute-start | bytes 1007624 | tf_op jit(solution)/shard_map/ppermute | solution.py:483
  304.0 36.6 %collective-permute-start.27 = (bf16[768,512]{1,0:T(8,128)(2,1)S(1)}, bf16[768,512]{1,0:T(8,128)(2,1)S(1)}, u32[]{:S(2)}, u32[]{:S(2)}) collective-permute-start(bf16[768,512]{1,0:T(8,128)(2,1)S(1)} %slice.747), channel_id=1, source_target_pairs={{0,2},{2,0},{1,3},{3,1},{4,6},{6,4},{5,7},{7,5},{8,10},{10,8},{9,1... | collective-permute-start | bytes 2359304 | tf_op jit(solution)/shard_map/ppermute | solution.py:388
  304.1 26.4 %collective-permute-start.28 = (f32[2,768]{1,0:T(2,128)S(1)}, f32[2,768]{1,0:T(2,128)S(1)}, u32[]{:S(2)}, u32[]{:S(2)}) collective-permute-start(f32[2,768]{1,0:T(2,128)S(1)} %pad_maximum_fusion.9), channel_id=1, source_target_pairs={{0,2},{2,0},{1,3},{3,1},{4,6},{6,4},{5,7},{7,5},{8,10},{10,8},{9,1... | collective-permute-start | bytes 18440 | tf_op jit(solution)/shard_map/ppermute | solution.py:388
  324.9 12.2 %collective-permute-start.31 = (bf16[768,256]{1,0:T(8,128)(2,1)S(1)}, bf16[768,256]{1,0:T(8,128)(2,1)S(1)}, u32[]{:S(2)}, u32[]{:S(2)}) collective-permute-start(bf16[768,256]{1,0:T(8,128)(2,1)S(1)} %slice.752), channel_id=1, source_target_pairs={{0,4},{4,0},{8,12},{12,8},{16,20},{20,16},{24,28},{28,24},{1,5},{5... | collective-permute-start | bytes 1179656 | tf_op jit(solution)/shard_map/ppermute | solution.py:480
  333.2 24.3 %collective-permute-start.34 = (bf16[3136,128]{1,0:T(8,128)(2,1)}, bf16[3136,128]{1,0:T(8,128)(2,1)}, u32[]{:S(2)}, u32[]{:S(2)}) collective-permute-start(bf16[3136,128]{1,0:T(8,128)(2,1)} %pad_maximum_fusion.6), channel_id=1, source_target_pairs={{0,8},{4,12},{8,0},{12,4},{16,24},{20,28},{24,16},{28,20},{1,9},{5... | collective-permute-start | bytes 2408456 | tf_op jit(solution)/shard_map/ppermute | solution.py:483
  338.1 23.5 %collective-permute-start.33 = (bf16[768,128]{1,0:T(8,128)(2,1)}, bf16[768,128]{1,0:T(8,128)(2,1)}, u32[]{:S(2)}, u32[]{:S(2)}) collective-permute-start(bf16[768,128]{1,0:T(8,128)(2,1)} %slice.760), channel_id=1, source_target_pairs={{0,16},{4,20},{8,24},{12,28},{16,0},{20,4},{24,8},{28,12},{1,17},{... | collective-permute-start | bytes 589832 | tf_op jit(solution)/shard_map/ppermute | solution.py:483
  341.2 25.3 %collective-permute-start.29 = (bf16[768,512]{1,0:T(8,128)(2,1)S(1)}, bf16[768,512]{1,0:T(8,128)(2,1)}, u32[]{:S(2)}, u32[]{:S(2)}) collective-permute-start(bf16[768,512]{1,0:T(8,128)(2,1)S(1)} %fusion.39), channel_id=1, source_target_pairs={{0,1},{1,0},{2,3},{3,2},{4,5},{5,4},{6,7},{7,6},{8,9},{9,8},{10,11... | collective-permute-start | bytes 2359304 | tf_op jit(solution)/shard_map/ppermute | solution.py:391
  361.5 20.4 %collective-permute-start.36 = (bf16[64,3136]{1,0:T(8,128)(2,1)}, bf16[64,3136]{1,0:T(8,128)(2,1)}, u32[]{:S(2)}, u32[]{:S(2)}) collective-permute-start(bf16[64,3136]{1,0:T(8,128)(2,1)} %copy.105), channel_id=1, source_target_pairs={{0,16},{4,20},{8,24},{12,28},{16,0},{20,4},{24,8},{28,12},{1,17},{... | collective-permute-start | bytes 1204232 | tf_op jit(solution)/shard_map/ppermute | solution.py:483
  (104 other events, 733.4 us)

commit v12 on v11

--- a/solution.py
+++ b/solution.py
@@ -730,11 +730,16 @@
         query = joined(query, after(query_got, act, lin, proj))
         query_got = to_z(second(query), 2)
         act, lin, proj = joined_three((act, lin, proj), after(gate_got, dx))
-        gate_got = after(to_z(three(act, lin, proj).T, 2), tokens_grad).T
+        gate_got = after(to_z(three(act, lin, proj).T, 2), tokens_grad)
         query = joined(query, after(query_got, act, lin, proj))
         lower = joined(lower, after(last_got, dx))
-        act, lin, proj = joined_three((act, lin, proj), gate_got)
-        gate = jnp.stack([act.T, lin.T])
+        gate = jnp.stack(
+            [
+                first(w).astype(f32).T + gate_got[:, i * F : (i + 1) * F].astype(f32)
+                for i, w in enumerate((act, lin))
+            ]
+        )
+        proj = joined(proj, gate_got[:, 2 * F :].T)
         query = query.T
         wq_rows = take(wq, b ^ (4 * r), Db)
         place = (2 * b + r) ^ (8 * r)

time: 399 us -> 398 us (level)
  transfers between devices with their start and end apart: 40 -> 40, of which waited for: 9 -> 11; matrix products, arithmetic and copies ran while one was open for 42% -> 42% of each run, Pallas kernels for 17% -> 17%
where the time goes in v12:
time: 398 us; the launch traced here: 391 us
  other arithmetic  76 us (19%)
  matrix products  71.2 us (18%)
  Pallas kernels  67.3 us (17%)
  waiting for transfers between devices  66.4 us (17%)
  starting transfers between devices  55.2 us (14%)
  local copies, waits for them, and re-layouts  52.1 us (13%)
    ppermute x8, waiting for transfers between devices, to_z(): return lax.ppermute(a, 'dp', [(i, i ^ 2 * j) for i in range(B)])  39.6 us
    pallas_call x2, Pallas kernels, attend_back_call(): pl.pallas_call(functools.partial(backward_kernel, heads, sets, final), gr...  38 us
    dot_general x14, matrix products, nn(): return jnp.dot(a, b, preferred_element_type=f32)  30.4 us
    pallas_call x2, Pallas kernels, attend_call(): pl.pallas_call(functools.partial(forward_kernel, heads, sets, final), gri...  29.4 us
    dot_general x10, matrix products, tn(): lax.dot_general(a, b, (((0,), (0,)), ((), ())), preferred_element_type=f32)  21.2 us
    ppermute x8, starting transfers between devices, to_z(): return lax.ppermute(a, 'dp', [(i, i ^ 2 * j) for i in range(B)])  17.2 us
    dot_general x8, matrix products, nt(): lax.dot_general(a, b, (((1,), (1,)), ((), ())), preferred_element_type=f32)  17 us
    unnamed x191, local copies, waits for them, and re-layouts  12.7 us
  transfers between devices with their start and end apart: 40, of which 11 were waited for; matrix products, arithmetic and copies ran while one was open for 42% of the time, Pallas kernels for 17%

profile of v12, /device:TPU:3, one launch (start us, length us, event | category | flops | bytes accessed | tf_op | source)
XLA Modules:
  0.0 391.1 jit_solution(11979759000882494222)
XLA Ops:
  8.8 2.8 multiply_sine_fusion
  11.6 2.7 convert_element_type.237
  15.1 3.0 fusion.58
  40.9 2.6 fusion.26
  49.1 4.8 %collective-permute-start.3 = (bf16[1024,512]{1,0:T(8,128)(2,1)}, bf16[1024,512]{1,0:T(8,128)(2,1)}, u32[]{:S(2)}, u32[]{:S(2)}) collective-permute-start(bf16[1024,512]{1,0:T(8,128)(2,1)} %get-tuple-element.231), channel_id=1, source_target_pairs={{0,4},{4,8},{8,12},{12,16},{16,20},{20,24},{24,28},{1,5},{5,9},{9,... | collective-permute-start | bytes 3145736 | tf_op jit(solution)/shard_map/ppermute | solution.py:523
  55.3 5.2 %fusion.15 = bf16[1536,1024]{1,0:T(8,128)(2,1)} fusion(bf16[1536,1024]{1,0:T(8,128)(2,1)S(1)} %fusion.4, s32[1024]{0:T(1024)S(1)} %add_xor_fusion.2), kind=kOutput, calls=%fused_computation.27 | convolution fusion | flops 3223846912 | bytes 6295552 | tf_op jit(solution)/shard_map/dot_general | solution.py:32
  69.0 19.4 %attend_own.1 = (f32[6,256,256]{2,1,0:T(8,128)}, f32[6,2,1024]{2,1,0:T(2,128)}) custom-call(s32[12]{0:T(128)} %reshape.741.bounds, bf16[1536,256]{1,0:T(8,128)(2,1)} %fusion.45.refs_0_, s32[6,1,256]{2,1,0:T(1,128)} %select_n.655.refs_1_.refs_4_, bf16[1536,512]{1,0:T(8,128)(2,1)} %copy-done.5, s32[1536,128]{1,0:T(8,128)} %broadcast_in_dim.132.refs_3_.refs_6_), custom_call_target="tpu_custom_call" | custom-call | flops 6291456 | bytes 3145728 | tf_op jit(solution)/shard_map/attend_own/pallas_call | solution.py:194
  88.4 9.7 %collective-permute-done.3.refs_2_.refs_5_ = bf16[1024,512]{1,0:T(8,128)(2,1)} collective-permute-done((bf16[1024,512]{1,0:T(8,128)(2,1)}, bf16[1024,512]{1,0:T(8,128)(2,1)}, u32[]{:S(2)}, u32[]{:S(2)}) %collective-permute-start.3) | collective-permute-done | bytes 1048608 | tf_op jit(solution)/shard_map/ppermute | solution.py:523
  100.8 3.6 collective-permute-start.14
  104.4 10.0 %attend_final.1 = (bf16[1536,256]{1,0:T(8,128)(2,1)}, f32[6,1,1024]{2,1,0:T(1,128)}) custom-call(s32[24]{0:T(128)} %reshape.740.bounds, bf16[1536,256]{1,0:T(8,128)(2,1)} %fusion.45.refs_0_, s32[6,1,256]{2,1,0:T(1,128)} %select_n.655.refs_1_.refs_4_, bf16[1024,512]{1,0:T(8,128)(2,1)} %collective-permute-done.3.refs_2_.refs_5_, ...), custom_call_target="tpu_custom_call" | custom-call | flops 6291456 | bytes 3670016 | tf_op jit(solution)/shard_map/attend_final/pallas_call | solution.py:194
  124.6 3.6 collective-permute-start.13
  136.1 3.2 fusion.166
  148.1 6.5 %multiply_convert_fusion = (bf16[768,1312]{0,1:T(8,128)(2,1)}, bf16[768,1312]{0,1:T(8,128)(2,1)S(1)}, bf16[768,1312]{0,1:T(8,128)(2,1)S(1)}) fusion(f32[768,1312]{0,1:T(8,128)S(1)} %convolution_add_fusion.1, f32[768,1312]{0,1:T(8,128)S(1)} %convolution_add_fusion, f32[768,1312]{0,1:T(8,128)S(1)} %fusion.74, ...), kind=kOutput, calls=%fused_computation.24 | convolution fusion | flops 1054973952 | bytes 20267008 | tf_op jit(solution)/shard_map/dot_general | solution.py:24
  163.4 2.8 fusion.105
  170.1 3.4 fusion.27
  179.7 2.6 fusion.65
  182.3 4.0 %fusion.160 = (bf16[768,1024]{1,0:T(8,128)(2,1)S(1)}, f32[768,1024]{1,0:T(8,128)}) fusion(f32[768]{0:T(1024)S(1)} %broadcast_multiply_fusion.2, f32[768,1024]{1,0:T(8,128)S(1)} %get-tuple-element.274, f32[768]{0:T(1024)S(1)} %broadcast_multiply_fusion.4, f32[768]{0:T(1024)S(1)} %broadcast_multiply_fusion.3, f32[1024]{0:T(1024)S(1)} %maximum_select_fusion.15, ...), kind=kLoop, calls=%fused_computation.382 | loop fusion | flops 10223616 | bytes 14172160 | tf_op jit(solution)/shard_map/convert_element_type | solution.py:637
  200.4 4.4 %fusion.70 = f32[1312,512]{1,0:T(8,128)} fusion(bf16[768,1312]{0,1:T(8,128)(2,1)} %get-tuple-element.216, bf16[768,1024]{1,0:T(8,128)(2,1)} %copy-done.88), kind=kOutput, calls=%fused_computation.151 | convolution fusion | flops 1031798784 | bytes 5488640 | tf_op jit(solution)/shard_map/dot_general | solution.py:28
  209.8 12.1 %back_halo.1 = (f32[6,256,256]{2,1,0:T(8,128)}, bf16[1024,512]{1,0:T(8,128)(2,1)}, bf16[1024,512]{1,0:T(8,128)(2,1)}) custom-call(s32[24]{0:T(128)} %reshape.740.bounds, bf16[1536,256]{1,0:T(8,128)(2,1)} %fusion.45.refs_0_, bf16[1536,256]{1,0:T(8,128)(2,1)} %maximum_select_fusion.7.refs_1_, bf16[1536,256]{1,0:T(8,128)(2,1)} %get-tuple-element.109.refs_2_, ...), custom_call_target="tpu_custom_call" | custom-call | flops 15728640 | bytes 3670016 | tf_op jit(solution)/shard_map/back_halo/pallas_call | solution.py:320
  226.7 5.2 %collective-permute-start.22 = (bf16[1024,512]{1,0:T(8,128)(2,1)}, bf16[1024,512]{1,0:T(8,128)(2,1)}, u32[]{:S(2)}, u32[]{:S(2)}) collective-permute-start(bf16[1024,512]{1,0:T(8,128)(2,1)} %get-tuple-element.133), channel_id=1, source_target_pairs={{0,4},{4,8},{8,12},{12,16},{16,20},{20,24},{24,28},{1,5},{5,9},{9,... | collective-permute-start | bytes 3145736 | tf_op jit(solution)/shard_map/ppermute | solution.py:659
  232.6 25.9 %back_own.1 = (f32[1536,256]{1,0:T(8,128)}, f32[1536,512]{1,0:T(8,128)}) custom-call(s32[12]{0:T(128)} %reshape.741.bounds, bf16[1536,256]{1,0:T(8,128)(2,1)} %fusion.45.refs_0_, bf16[1536,256]{1,0:T(8,128)(2,1)} %maximum_select_fusion.7.refs_1_, bf16[1536,256]{1,0:T(8,128)(2,1)} %get-tuple-element.109.refs_2_, f32[6,1,1024]{2,1,0:T(1,128)} %get-tuple-element.125.refs_3_, ...), custom_call_target="tpu_custom_call" | custom-call | flops 15728640 | bytes 3145728 | tf_op jit(solution)/shard_map/back_own/pallas_call | solution.py:320
  260.8 9.9 %collective-permute-done.23 = bf16[3136,512]{1,0:T(8,128)(2,1)} collective-permute-done((bf16[3136,512]{1,0:T(8,128)(2,1)}, bf16[3136,512]{1,0:T(8,128)(2,1)}, u32[]{:S(2)}, u32[]{:S(2)}) %collective-permute-start.23) | collective-permute-done | bytes 3211296 | tf_op jit(solution)/shard_map/ppermute | solution.py:388
  276.0 3.0 convert_add_fusion.3
  279.1 3.2 convert_add_fusion.1
  284.0 2.6 fusion.170
  288.3 2.8 collective-permute-start.26
  305.0 17.5 %collective-permute-done.30 = bf16[768,512]{1,0:T(8,128)(2,1)S(1)} collective-permute-done((bf16[768,512]{1,0:T(8,128)(2,1)}, bf16[768,512]{1,0:T(8,128)(2,1)S(1)}, u32[]{:S(2)}, u32[]{:S(2)}) %collective-permute-start.30) | collective-permute-done | bytes 786464 | tf_op jit(solution)/shard_map/ppermute | solution.py:483
  332.4 4.7 %collective-permute-done.31 = bf16[768,256]{1,0:T(8,128)(2,1)S(1)} collective-permute-done((bf16[768,256]{1,0:T(8,128)(2,1)S(1)}, bf16[768,256]{1,0:T(8,128)(2,1)S(1)}, u32[]{:S(2)}, u32[]{:S(2)}) %collective-permute-start.31) | collective-permute-done | bytes 393248 | tf_op jit(solution)/shard_map/ppermute | solution.py:480
  342.8 11.6 %collective-permute-done.34 = bf16[3136,128]{1,0:T(8,128)(2,1)} collective-permute-done((bf16[3136,128]{1,0:T(8,128)(2,1)}, bf16[3136,128]{1,0:T(8,128)(2,1)}, u32[]{:S(2)}, u32[]{:S(2)}) %collective-permute-start.34) | collective-permute-done | bytes 802848 | tf_op jit(solution)/shard_map/ppermute | solution.py:483
  361.3 2.6 fusion.16
  365.0 3.0 maximum_select_fusion.4
  370.5 8.2 %collective-permute-done.36 = bf16[64,3136]{1,0:T(8,128)(2,1)} collective-permute-done((bf16[64,3136]{1,0:T(8,128)(2,1)}, bf16[64,3136]{1,0:T(8,128)(2,1)}, u32[]{:S(2)}, u32[]{:S(2)}) %collective-permute-start.36) | collective-permute-done | bytes 401440 | tf_op jit(solution)/shard_map/ppermute | solution.py:483
  (434 shorter events, 181.7 us)
Async XLA Ops:
  2.8 25.1 %collective-permute-start = (bf16[768,512]{1,0:T(8,128)(2,1)}, bf16[768,512]{1,0:T(8,128)(2,1)}, u32[]{:S(2)}, u32[]{:S(2)}) collective-permute-start(bf16[768,512]{1,0:T(8,128)(2,1)} %constant_dynamic-slice_fusion.6), channel_id=1, source_target_pairs={{0,2},{2,0},{1,3},{3,1},{4,6},{6,4},{5,7},{7,5},{8,10},{10,8},{9,1... | collective-permute-start | bytes 2359304 | tf_op jit(solution)/shard_map/ppermute | solution.py:388
  6.2 34.6 %collective-permute-start.2 = (bf16[512,768]{0,1:T(8,128)(2,1)}, bf16[512,768]{0,1:T(8,128)(2,1)}, u32[]{:S(2)}, u32[]{:S(2)}) collective-permute-start(bf16[512,768]{0,1:T(8,128)(2,1)} %get-tuple-element.234), channel_id=1, source_target_pairs={{0,2},{2,0},{1,3},{3,1},{4,6},{6,4},{5,7},{7,5},{8,10},{10,8},{9,1... | collective-permute-start | bytes 2359304 | tf_op jit(solution)/shard_map/ppermute | solution.py:388
  18.1 70.3 %collective-permute-start.5 = (bf16[512,1312]{0,1:T(8,128)(2,1)}, bf16[512,1312]{0,1:T(8,128)(2,1)}, u32[]{:S(2)}, u32[]{:S(2)}) collective-permute-start(bf16[512,1312]{0,1:T(8,128)(2,1)} %fusion.58), channel_id=1, source_target_pairs={{0,2},{2,0},{1,3},{3,1},{4,6},{6,4},{5,7},{7,5},{8,10},{10,8},{9,1... | collective-permute-start | bytes 4030472 | tf_op jit(solution)/shard_map/ppermute | solution.py:388
  18.1 70.3 %collective-permute-start.6 = (bf16[512,512]{1,0:T(8,128)(2,1)}, bf16[512,512]{1,0:T(8,128)(2,1)}, u32[]{:S(2)}, u32[]{:S(2)}) collective-permute-start(bf16[512,512]{1,0:T(8,128)(2,1)} %convert_element_type.237), channel_id=1, source_target_pairs={{0,2},{2,0},{1,3},{3,1},{4,6},{6,4},{5,7},{7,5},{8,10},{10,8},{9,1... | collective-permute-start | bytes 1572872 | tf_op jit(solution)/shard_map/ppermute | solution.py:388
  19.6 68.8 %collective-permute-start.7 = (bf16[384,512]{1,0:T(8,128)(2,1)}, bf16[384,512]{1,0:T(8,128)(2,1)S(1)}, u32[]{:S(2)}, u32[]{:S(2)}) collective-permute-start(bf16[384,512]{1,0:T(8,128)(2,1)} %constant_dynamic-slice_fusion.2), channel_id=1, source_target_pairs={{0,2},{2,0},{1,3},{3,1},{4,6},{6,4},{5,7},{7,5},{8,10},{10,8},{9,1... | collective-permute-start | bytes 1179656 | tf_op jit(solution)/shard_map/ppermute | solution.py:388
  49.1 49.1 %collective-permute-start.3 = (bf16[1024,512]{1,0:T(8,128)(2,1)}, bf16[1024,512]{1,0:T(8,128)(2,1)}, u32[]{:S(2)}, u32[]{:S(2)}) collective-permute-start(bf16[1024,512]{1,0:T(8,128)(2,1)} %get-tuple-element.231), channel_id=1, source_target_pairs={{0,4},{4,8},{8,12},{12,16},{16,20},{20,24},{24,28},{1,5},{5,9},{9,... | collective-permute-start | bytes 3145736 | tf_op jit(solution)/shard_map/ppermute | solution.py:523
  53.9 44.2 %collective-permute-start.4 = (bf16[1024,512]{1,0:T(8,128)(2,1)}, bf16[1024,512]{1,0:T(8,128)(2,1)}, u32[]{:S(2)}, u32[]{:S(2)}) collective-permute-start(bf16[1024,512]{1,0:T(8,128)(2,1)} %get-tuple-element.230), channel_id=1, source_target_pairs={{4,0},{8,4},{12,8},{16,12},{20,16},{24,20},{28,24},{5,1},{9,5},{13... | collective-permute-start | bytes 3145736 | tf_op jit(solution)/shard_map/ppermute | solution.py:524
  98.1 16.8 %collective-permute-start.8 = (bf16[656,512]{1,0:T(8,128)(2,1)}, bf16[656,512]{1,0:T(8,128)(2,1)}, u32[]{:S(2)}, u32[]{:S(2)}) collective-permute-start(bf16[656,512]{1,0:T(8,128)(2,1)} %constant_dynamic-slice_fusion.3), channel_id=1, source_target_pairs={{0,2},{2,0},{1,3},{3,1},{4,6},{6,4},{5,7},{7,5},{8,10},{10,8},{9,1... | collective-permute-start | bytes 2015240 | tf_op jit(solution)/shard_map/ppermute | solution.py:388
  100.8 33.1 %collective-permute-start.14 = (bf16[512,1312]{0,1:T(8,128)(2,1)}, bf16[512,1312]{0,1:T(8,128)(2,1)}, u32[]{:S(2)}, u32[]{:S(2)}) collective-permute-start(bf16[512,1312]{0,1:T(8,128)(2,1)} %collective-permute-done.5), channel_id=1, source_target_pairs={{0,8},{4,12},{8,0},{12,4},{16,24},{20,28},{24,16},{28,20},{1,9},{5... | collective-permute-start | bytes 4030472 | tf_op jit(solution)/shard_map/ppermute | solution.py:483
  119.6 11.7 %collective-permute-start.9 = (bf16[384,512]{1,0:T(8,128)(2,1)}, bf16[384,512]{1,0:T(8,128)(2,1)S(1)}, u32[]{:S(2)}, u32[]{:S(2)}) collective-permute-start(bf16[384,512]{1,0:T(8,128)(2,1)} %copy-done.57), channel_id=1, source_target_pairs={{0,1},{1,0},{2,3},{3,2},{4,5},{5,4},{6,7},{7,6},{8,9},{9,8},{10,11... | collective-permute-start | bytes 1179656 | tf_op jit(solution)/shard_map/ppermute | solution.py:391
  124.6 11.5 %collective-permute-start.12 = (bf16[512,1024]{1,0:T(8,128)(2,1)S(1)}, bf16[512,1024]{1,0:T(8,128)(2,1)S(1)}, u32[]{:S(2)}, u32[]{:S(2)}) collective-permute-start(bf16[512,1024]{1,0:T(8,128)(2,1)S(1)} %fusion.62), channel_id=1, source_target_pairs={{0,1},{1,0},{2,3},{3,2},{4,5},{5,4},{6,7},{7,6},{8,9},{9,8},{10,11... | collective-permute-start | bytes 3145736 | tf_op jit(solution)/shard_map/ppermute | solution.py:391
  124.6 23.5 %collective-permute-start.13 = (bf16[656,512]{1,0:T(8,128)(2,1)}, bf16[656,512]{1,0:T(8,128)(2,1)S(1)}, u32[]{:S(2)}, u32[]{:S(2)}) collective-permute-start(bf16[656,512]{1,0:T(8,128)(2,1)} %collective-permute-done.8), channel_id=1, source_target_pairs={{0,8},{4,12},{8,0},{12,4},{16,24},{20,28},{24,16},{28,20},{1,9},{5... | collective-permute-start | bytes 2015240 | tf_op jit(solution)/shard_map/ppermute | solution.py:483
  162.1 17.0 %collective-permute-start.15 = (bf16[768,1024]{1,0:T(8,128)(2,1)}, bf16[768,1024]{1,0:T(8,128)(2,1)}, u32[]{:S(2)}, u32[]{:S(2)}) collective-permute-start(bf16[768,1024]{1,0:T(8,128)(2,1)} %fusion.159), channel_id=1, source_target_pairs={{0,1},{1,0},{2,3},{3,2},{4,5},{5,4},{6,7},{7,6},{8,9},{9,8},{10,11... | collective-permute-start | bytes 4718600 | tf_op jit(solution)/shard_map/ppermute | solution.py:391
  175.8 46.1 %collective-permute-start.20 = (bf16[1312,512]{1,0:T(8,128)(2,1)}, bf16[1312,512]{1,0:T(8,128)(2,1)}, u32[]{:S(2)}, u32[]{:S(2)}) collective-permute-start(bf16[1312,512]{1,0:T(8,128)(2,1)} %convolution_convert_fusion), channel_id=1, source_target_pairs={{0,4},{4,0},{8,12},{12,8},{16,20},{20,16},{24,28},{28,24},{1,5},{5... | collective-permute-start | bytes 4030472 | tf_op jit(solution)/shard_map/ppermute | solution.py:480
  179.0 19.8 %collective-permute-start.18 = (bf16[384,512]{1,0:T(8,128)(2,1)S(1)}, bf16[384,512]{1,0:T(8,128)(2,1)S(1)}, u32[]{:S(2)}, u32[]{:S(2)}) collective-permute-start(bf16[384,512]{1,0:T(8,128)(2,1)S(1)} %get-tuple-element.246), channel_id=1, source_target_pairs={{0,2},{2,0},{1,3},{3,1},{4,6},{6,4},{5,7},{7,5},{8,10},{10,8},{9,1... | collective-permute-start | bytes 1179656 | tf_op jit(solution)/shard_map/ppermute | solution.py:388
  188.2 11.6 %collective-permute-start.16 = (bf16[768,256]{1,0:T(8,128)(2,1)}, bf16[768,256]{1,0:T(8,128)(2,1)}, u32[]{:S(2)}, u32[]{:S(2)}) collective-permute-start(bf16[768,256]{1,0:T(8,128)(2,1)} %get-tuple-element.250), channel_id=1, source_target_pairs={{0,2},{2,0},{1,3},{3,1},{4,6},{6,4},{5,7},{7,5},{8,10},{10,8},{9,1... | collective-permute-start | bytes 1179656 | tf_op jit(solution)/shard_map/ppermute | solution.py:388
  199.8 70.9 %collective-permute-start.23 = (bf16[3136,512]{1,0:T(8,128)(2,1)}, bf16[3136,512]{1,0:T(8,128)(2,1)}, u32[]{:S(2)}, u32[]{:S(2)}) collective-permute-start(bf16[3136,512]{1,0:T(8,128)(2,1)} %pad_maximum_fusion), channel_id=1, source_target_pairs={{0,2},{2,0},{1,3},{3,1},{4,6},{6,4},{5,7},{7,5},{8,10},{10,8},{9,1... | collective-permute-start | bytes 9633800 | tf_op jit(solution)/shard_map/ppermute | solution.py:388
  225.4 53.6 %collective-permute-start.21 = (bf16[1024,512]{1,0:T(8,128)(2,1)}, bf16[1024,512]{1,0:T(8,128)(2,1)}, u32[]{:S(2)}, u32[]{:S(2)}) collective-permute-start(bf16[1024,512]{1,0:T(8,128)(2,1)} %get-tuple-element.132), channel_id=1, source_target_pairs={{4,0},{8,4},{12,8},{16,12},{20,16},{24,20},{28,24},{5,1},{9,5},{13... | collective-permute-start | bytes 3145736 | tf_op jit(solution)/shard_map/ppermute | solution.py:658
  226.7 52.3 %collective-permute-start.22 = (bf16[1024,512]{1,0:T(8,128)(2,1)}, bf16[1024,512]{1,0:T(8,128)(2,1)}, u32[]{:S(2)}, u32[]{:S(2)}) collective-permute-start(bf16[1024,512]{1,0:T(8,128)(2,1)} %get-tuple-element.133), channel_id=1, source_target_pairs={{0,4},{4,8},{8,12},{12,16},{16,20},{20,24},{24,28},{1,5},{5,9},{9,... | collective-permute-start | bytes 3145736 | tf_op jit(solution)/shard_map/ppermute | solution.py:659
  231.9 47.1 %collective-permute-start.24 = (bf16[1312,256]{1,0:T(8,128)(2,1)}, bf16[1312,256]{1,0:T(8,128)(2,1)S(1)}, u32[]{:S(2)}, u32[]{:S(2)}) collective-permute-start(bf16[1312,256]{1,0:T(8,128)(2,1)} %slice.755), channel_id=1, source_target_pairs={{0,8},{4,12},{8,0},{12,4},{16,24},{20,28},{24,16},{28,20},{1,9},{5... | collective-permute-start | bytes 2015240 | tf_op jit(solution)/shard_map/ppermute | solution.py:483
  286.9 15.0 %collective-permute-start.25 = (bf16[768,1024]{1,0:T(8,128)(2,1)S(1)}, bf16[768,1024]{1,0:T(8,128)(2,1)S(1)}, u32[]{:S(2)}, u32[]{:S(2)}) collective-permute-start(bf16[768,1024]{1,0:T(8,128)(2,1)S(1)} %dynamic-slice_convert_fusion), channel_id=1, source_target_pairs={{0,1},{1,0},{2,3},{3,2},{4,5},{5,4},{6,7},{7,6},{8,9},{9,8},{10,11... | collective-permute-start | bytes 4718600 | tf_op jit(solution)/shard_map/ppermute | solution.py:391
  288.3 15.1 %collective-permute-start.26 = (bf16[768,512]{1,0:T(8,128)(2,1)S(1)}, bf16[768,512]{1,0:T(8,128)(2,1)S(1)}, u32[]{:S(2)}, u32[]{:S(2)}) collective-permute-start(bf16[768,512]{1,0:T(8,128)(2,1)S(1)} %copy-done.51), channel_id=1, source_target_pairs={{0,2},{3,1},{4,6},{7,5},{8,10},{11,9},{12,14},{15,13},{16,18},{19,... | collective-permute-start | bytes 2359304 | tf_op jit(solution)/shard_map/ppermute | solution.py:695
  291.5 37.2 %collective-permute-start.32 = (bf16[3136,256]{1,0:T(8,128)(2,1)S(1)}, bf16[3136,256]{1,0:T(8,128)(2,1)S(1)}, u32[]{:S(2)}, u32[]{:S(2)}) collective-permute-start(bf16[3136,256]{1,0:T(8,128)(2,1)S(1)} %pad_maximum_fusion.2), channel_id=1, source_target_pairs={{0,4},{4,0},{8,12},{12,8},{16,20},{20,16},{24,28},{28,24},{1,5},{5... | collective-permute-start | bytes 4816904 | tf_op jit(solution)/shard_map/ppermute | solution.py:480
  295.5 27.0 %collective-permute-start.30 = (bf16[768,512]{1,0:T(8,128)(2,1)}, bf16[768,512]{1,0:T(8,128)(2,1)S(1)}, u32[]{:S(2)}, u32[]{:S(2)}) collective-permute-start(bf16[768,512]{1,0:T(8,128)(2,1)} %fusion.55), channel_id=1, source_target_pairs={{0,8},{4,12},{8,0},{12,4},{16,24},{20,28},{24,16},{28,20},{1,9},{5... | collective-permute-start | bytes 2359304 | tf_op jit(solution)/shard_map/ppermute | solution.py:483
  298.1 34.0 %collective-permute-start.38 = (bf16[1312,128]{1,0:T(8,128)(2,1)}, bf16[1312,128]{1,0:T(8,128)(2,1)S(1)}, u32[]{:S(2)}, u32[]{:S(2)}) collective-permute-start(bf16[1312,128]{1,0:T(8,128)(2,1)} %slice.758), channel_id=1, source_target_pairs={{0,16},{4,20},{8,24},{12,28},{16,0},{20,4},{24,8},{28,12},{1,17},{... | collective-permute-start | bytes 1007624 | tf_op jit(solution)/shard_map/ppermute | solution.py:483
  303.4 37.2 %collective-permute-start.27 = (bf16[768,512]{1,0:T(8,128)(2,1)S(1)}, bf16[768,512]{1,0:T(8,128)(2,1)S(1)}, u32[]{:S(2)}, u32[]{:S(2)}) collective-permute-start(bf16[768,512]{1,0:T(8,128)(2,1)S(1)} %slice.751), channel_id=1, source_target_pairs={{0,2},{2,0},{1,3},{3,1},{4,6},{6,4},{5,7},{7,5},{8,10},{10,8},{9,1... | collective-permute-start | bytes 2359304 | tf_op jit(solution)/shard_map/ppermute | solution.py:388
  303.5 24.7 %collective-permute-start.28 = (f32[2,768]{1,0:T(2,128)S(1)}, f32[2,768]{1,0:T(2,128)S(1)}, u32[]{:S(2)}, u32[]{:S(2)}) collective-permute-start(f32[2,768]{1,0:T(2,128)S(1)} %pad_maximum_fusion.9), channel_id=1, source_target_pairs={{0,2},{2,0},{1,3},{3,1},{4,6},{6,4},{5,7},{7,5},{8,10},{10,8},{9,1... | collective-permute-start | bytes 18440 | tf_op jit(solution)/shard_map/ppermute | solution.py:388
  322.9 14.3 %collective-permute-start.31 = (bf16[768,256]{1,0:T(8,128)(2,1)S(1)}, bf16[768,256]{1,0:T(8,128)(2,1)S(1)}, u32[]{:S(2)}, u32[]{:S(2)}) collective-permute-start(bf16[768,256]{1,0:T(8,128)(2,1)S(1)} %slice.756), channel_id=1, source_target_pairs={{0,4},{4,0},{8,12},{12,8},{16,20},{20,16},{24,28},{28,24},{1,5},{5... | collective-permute-start | bytes 1179656 | tf_op jit(solution)/shard_map/ppermute | solution.py:480
  330.9 23.5 %collective-permute-start.34 = (bf16[3136,128]{1,0:T(8,128)(2,1)}, bf16[3136,128]{1,0:T(8,128)(2,1)}, u32[]{:S(2)}, u32[]{:S(2)}) collective-permute-start(bf16[3136,128]{1,0:T(8,128)(2,1)} %pad_maximum_fusion.6), channel_id=1, source_target_pairs={{0,8},{4,12},{8,0},{12,4},{16,24},{20,28},{24,16},{28,20},{1,9},{5... | collective-permute-start | bytes 2408456 | tf_op jit(solution)/shard_map/ppermute | solution.py:483
  338.1 21.9 %collective-permute-start.33 = (bf16[768,128]{1,0:T(8,128)(2,1)}, bf16[768,128]{1,0:T(8,128)(2,1)}, u32[]{:S(2)}, u32[]{:S(2)}) collective-permute-start(bf16[768,128]{1,0:T(8,128)(2,1)} %slice.764), channel_id=1, source_target_pairs={{0,16},{4,20},{8,24},{12,28},{16,0},{20,4},{24,8},{28,12},{1,17},{... | collective-permute-start | bytes 589832 | tf_op jit(solution)/shard_map/ppermute | solution.py:483
  341.2 23.8 %collective-permute-start.29 = (bf16[768,512]{1,0:T(8,128)(2,1)S(1)}, bf16[768,512]{1,0:T(8,128)(2,1)}, u32[]{:S(2)}, u32[]{:S(2)}) collective-permute-start(bf16[768,512]{1,0:T(8,128)(2,1)S(1)} %fusion.39), channel_id=1, source_target_pairs={{0,1},{1,0},{2,3},{3,2},{4,5},{5,4},{6,7},{7,6},{8,9},{9,8},{10,11... | collective-permute-start | bytes 2359304 | tf_op jit(solution)/shard_map/ppermute | solution.py:391
  358.4 20.2 %collective-permute-start.36 = (bf16[64,3136]{1,0:T(8,128)(2,1)}, bf16[64,3136]{1,0:T(8,128)(2,1)}, u32[]{:S(2)}, u32[]{:S(2)}) collective-permute-start(bf16[64,3136]{1,0:T(8,128)(2,1)} %copy.107), channel_id=1, source_target_pairs={{0,16},{4,20},{8,24},{12,28},{16,0},{20,4},{24,8},{28,12},{1,17},{... | collective-permute-start | bytes 1204232 | tf_op jit(solution)/shard_map/ppermute | solution.py:483
  (104 other events, 748.0 us)
